TPU v7x, 32 devices: a whole 2x2x4 slice. The times are simulated.
32 devices in a mesh: dp: 8 (over y, x, core), ctx: 4 (over z).
Axes of the slice: x: 2, y: 2, z: 4, core: 2. Of those that a mesh axis runs over, the one named last changes fastest.
Arguments:
- tokens: bfloat16 [8, 2048, 1024], P('dp', 'ctx'), may hold values from -6 to 6
- first_values: bfloat16 [8, 2048, 1024], P('dp', 'ctx'), may hold values from -6 to 6
- v1_accum: float32 [8, 2048, 1024], P('dp', 'ctx'), may hold values from -6 to 6
- segment_ids: int32 [8, 2048], P('dp', 'ctx'), may hold values from 0 to 3, as said below
- positions: int32 [8, 2048], P('dp', 'ctx'), may hold values from 0 to 2047, as said below
- cotangent: bfloat16 [8, 2048, 1024], P('dp', 'ctx'), may hold values from -6 to 6
- attn_gain: bfloat16 [1024], P(('dp', 'ctx')), may hold values from 0.25 to 1.75
- w_query: bfloat16 [1024, 1024], P(('dp', 'ctx')), may hold values from -0.1875 to 0.1875
- w_key: bfloat16 [1024, 1024], P(('dp', 'ctx')), may hold values from -0.1875 to 0.1875
- w_value: bfloat16 [1024, 1024], P(('dp', 'ctx')), may hold values from -0.1875 to 0.1875
- w_out: bfloat16 [1024, 1024], P(('dp', 'ctx')), may hold values from -2 to 2
- mlp_gain: bfloat16 [1024], P(('dp', 'ctx')), may hold values from 0.25 to 1.75
- w_gate: bfloat16 [1024, 2816], P(('dp', 'ctx')), may hold values from -0.1875 to 0.1875
- w_up: bfloat16 [1024, 2816], P(('dp', 'ctx')), may hold values from -0.1875 to 0.1875
- w_down: bfloat16 [2816, 1024], P(('dp', 'ctx')), may hold values from -0.109375 to 0.109375
Outputs:
- output: bfloat16 [8, 2048, 1024], P('dp', 'ctx')
- input_grad: float32 [8, 2048, 1024], P('dp', 'ctx')
- v1_grad: float32 [8, 2048, 1024], P('dp', 'ctx')
- attn_gain_grad: float32 [1024], P(('dp', 'ctx'))
- w_query_grad: float32 [1024, 1024], P(('dp', 'ctx'))
- w_key_grad: float32 [1024, 1024], P(('dp', 'ctx'))
- w_value_grad: float32 [1024, 1024], P(('dp', 'ctx'))
- w_out_grad: float32 [1024, 1024], P(('dp', 'ctx'))
- mlp_gain_grad: float32 [1024], P(('dp', 'ctx'))
- w_gate_grad: float32 [1024, 2816], P(('dp', 'ctx'))
- w_up_grad: float32 [1024, 2816], P(('dp', 'ctx'))
- w_down_grad: float32 [2816, 1024], P(('dp', 'ctx'))
Inputs may be any that keep to these rules, and one draw needn't show every extreme that they name: `segment_ids`: in each packed row the ids start at 0 and never fall; a row holds at most 4 documents, and one row of every draw holds a single one. `positions`: 0 at the start of a row or where the segment id changes, else one more than the token before; one row of every draw is a single document.
All inputs are finite; a program needn't handle non-finite values.
Results may differ from a plain program's by a relative error of at most 0.015.
Values may be sent and summed in bfloat16 or wider, within the bound.
A program may use at most 256 MiB of HBM per device.

v0:
```python
import jax
import jax.numpy as jnp
from jax import lax
from jax.sharding import PartitionSpec as P

HEADS = 16
HEAD_DIM = 64
HEAD_BLOCK = 4


epsilon = 1e-05


def rms_scale(values):
    return lax.rsqrt(jnp.mean(values * values, axis=-1, keepdims=True) + epsilon)


def angle_tables(position_rows):
    freqs = 10000.0 ** (-jnp.arange(HEAD_DIM // 2).astype(jnp.float32) * (2.0 / HEAD_DIM))
    angles = position_rows.astype(jnp.float32)[..., None] * freqs
    return (jnp.cos(angles)[..., None, :], jnp.sin(angles)[..., None, :])


def rotate(heads_in, cosine_table, sine_table):
    half_dim = heads_in.shape[-1] // 2
    first_half = heads_in[..., :half_dim]
    second_half = heads_in[..., half_dim:]
    return jnp.concatenate(
        [
            first_half * cosine_table - second_half * sine_table,
            second_half * cosine_table + first_half * sine_table,
        ],
        axis=-1,
    )


def norm_back(grad_normed, normed, inv_root, norm_gain):
    grad_scaled = grad_normed * norm_gain.astype(jnp.float32)
    grad_input = inv_root * (
        grad_scaled - normed * jnp.mean(grad_scaled * normed, axis=-1, keepdims=True)
    )
    return (grad_input, jnp.sum(grad_normed * normed, axis=0))


def attn_front(flat_tokens, first_flat, attn_set, cosine_table, sine_table, row_count, seq_piece):
    inv_root = rms_scale(flat_tokens)
    normed = flat_tokens * inv_root
    normed_in = (normed * attn_set[0].astype(jnp.float32)).astype(jnp.bfloat16)
    query_proj = jnp.dot(normed_in, attn_set[1], preferred_element_type=jnp.float32)
    key_proj = jnp.dot(normed_in, attn_set[2], preferred_element_type=jnp.float32)
    value_proj = jnp.dot(normed_in, attn_set[3], preferred_element_type=jnp.float32)
    query_rot = rotate(
        query_proj.reshape(row_count, seq_piece, HEADS, HEAD_DIM), cosine_table, sine_table
    )
    key_rot = rotate(
        key_proj.reshape(row_count, seq_piece, HEADS, HEAD_DIM), cosine_table, sine_table
    )
    query_rot = query_rot.astype(jnp.bfloat16).reshape(row_count, seq_piece, -1)
    key_rot = key_rot.astype(jnp.bfloat16).reshape(row_count, seq_piece, -1)
    value_mix = (
        (0.5 * value_proj + 0.5 * first_flat).astype(jnp.bfloat16).reshape(row_count, seq_piece, -1)
    )
    return (normed, inv_root, normed_in, query_rot, key_rot, value_mix)


def mlp_block(flat_tokens, attended_low, out_weight, mlp_set):
    middle = flat_tokens + jnp.dot(attended_low, out_weight, preferred_element_type=jnp.float32)
    inv_root_two = rms_scale(middle)
    normed_two = middle * inv_root_two
    mlp_in = (normed_two * mlp_set[0].astype(jnp.float32)).astype(jnp.bfloat16)
    gate_proj = jnp.dot(mlp_in, mlp_set[1], preferred_element_type=jnp.float32)
    up_proj = jnp.dot(mlp_in, mlp_set[2], preferred_element_type=jnp.float32)
    hidden = (gate_proj * jax.nn.sigmoid(gate_proj) * up_proj).astype(jnp.bfloat16)
    result = middle + jnp.dot(hidden, mlp_set[3], preferred_element_type=jnp.float32)
    return (normed_two, inv_root_two, mlp_in, gate_proj, up_proj, hidden, result)


def split_groups(row_block):
    tok_count = row_block.shape[0]
    return row_block.reshape(tok_count, HEADS // HEAD_BLOCK, HEAD_BLOCK * HEAD_DIM).transpose(
        1, 0, 2
    )


def join_groups(group_block):
    return group_block.transpose(1, 0, 2).reshape(group_block.shape[1], -1)


def as_heads(block):
    return block.reshape(block.shape[0], HEAD_BLOCK, HEAD_DIM)


def attend_row(members):
    query_row, key_row, value_row, allowed = members

    def per_group(pieces):
        query_block, key_block, value_block = pieces
        scores = (
            jnp.einsum(
                "qhd,khd->hqk",
                as_heads(query_block),
                as_heads(key_block),
                preferred_element_type=jnp.float32,
            )
            * 0.125
        )
        scores = jnp.where(allowed[None], scores, -1e30)
        highest = jnp.max(scores, axis=-1, keepdims=True)
        exp_scores = jnp.exp(scores - highest)
        denominator = jnp.sum(exp_scores, axis=-1, keepdims=True)
        soft_low = (exp_scores / denominator).astype(jnp.bfloat16)
        attended = jnp.einsum(
            "hqk,khd->qhd", soft_low, as_heads(value_block), preferred_element_type=jnp.float32
        )
        return (
            attended.reshape(query_block.shape[0], -1),
            (highest + jnp.log(denominator))[..., 0],
        )

    attended, log_total = lax.map(
        per_group, (split_groups(query_row), split_groups(key_row), split_groups(value_row))
    )
    return (join_groups(attended), log_total)


def attend_back(members):
    query_row, key_row, value_row, grad_row, log_total, allowed = members

    def per_group(pieces):
        query_block, key_block, value_block, grad_block, log_block = pieces
        query_heads = as_heads(query_block)
        key_heads = as_heads(key_block)
        grad_heads = as_heads(grad_block)
        scores = (
            jnp.einsum("qhd,khd->hqk", query_heads, key_heads, preferred_element_type=jnp.float32)
            * 0.125
        )
        soft_weights = jnp.where(allowed[None], jnp.exp(scores - log_block[..., None]), 0.0)
        soft_low = soft_weights.astype(jnp.bfloat16)
        grad_probs = jnp.einsum(
            "qhd,khd->hqk", grad_heads, as_heads(value_block), preferred_element_type=jnp.float32
        )
        row_delta = jnp.sum(soft_weights * grad_probs, axis=-1, keepdims=True)
        grad_scores = (soft_weights * (grad_probs - row_delta)).astype(jnp.bfloat16)
        grad_query = (
            jnp.einsum("hqk,khd->qhd", grad_scores, key_heads, preferred_element_type=jnp.float32)
            * 0.125
        )
        grad_key = (
            jnp.einsum("hqk,qhd->khd", grad_scores, query_heads, preferred_element_type=jnp.float32)
            * 0.125
        )
        grad_value = jnp.einsum(
            "hqk,qhd->khd", soft_low, grad_heads, preferred_element_type=jnp.float32
        )
        return (
            grad_query.reshape(query_block.shape[0], -1),
            grad_key.reshape(key_block.shape[0], -1),
            grad_value.reshape(key_block.shape[0], -1),
        )

    grad_query, grad_key, grad_value = lax.map(
        per_group,
        (
            split_groups(query_row),
            split_groups(key_row),
            split_groups(value_row),
            split_groups(grad_row),
            log_total,
        ),
    )
    return (join_groups(grad_query), join_groups(grad_key), join_groups(grad_value))


def local(
    tokens,
    first_values,
    v1_accum,
    segment_ids,
    positions,
    cotangent,
    attn_gain,
    w_query,
    w_key,
    w_value,
    w_out,
    mlp_gain,
    w_gate,
    w_up,
    w_down,
):
    row_count, seq_piece, model_width = tokens.shape
    token_count = row_count * seq_piece
    flat_tokens = tokens.astype(jnp.float32).reshape(token_count, model_width)
    first_flat = first_values.astype(jnp.float32).reshape(token_count, model_width)
    cosine_table, sine_table = angle_tables(positions)
    segment_low = segment_ids.astype(jnp.bfloat16)
    attn_set = (
        lax.all_gather(attn_gain, ("dp", "ctx"), axis=0, tiled=True),
        lax.all_gather(w_query, ("dp", "ctx"), axis=0, tiled=True),
        lax.all_gather(w_key, ("dp", "ctx"), axis=0, tiled=True),
        lax.all_gather(w_value, ("dp", "ctx"), axis=0, tiled=True),
        lax.all_gather(w_out, ("dp", "ctx"), axis=0, tiled=True),
    )
    normed, inv_root, normed_in, query_rot, key_rot, value_mix = attn_front(
        flat_tokens, first_flat, attn_set, cosine_table, sine_table, row_count, seq_piece
    )
    key_full, value_full, segment_full = (
        lax.all_gather(key_rot, "ctx", axis=1, tiled=True),
        lax.all_gather(value_mix, "ctx", axis=1, tiled=True),
        lax.all_gather(segment_low, "ctx", axis=1, tiled=True),
    )
    query_order = lax.axis_index("ctx") * seq_piece + jnp.arange(seq_piece, dtype=jnp.int32)
    full_order = jnp.arange(key_full.shape[1], dtype=jnp.int32)
    segment_own = segment_ids.astype(jnp.float32)
    segment_all = segment_full.astype(jnp.float32)
    allowed = (segment_own[:, :, None] == segment_all[:, None, :]) & (
        query_order[None, :, None] >= full_order[None, None, :]
    )
    attended, log_total = lax.map(attend_row, (query_rot, key_full, value_full, allowed))
    attended_low = attended.reshape(token_count, model_width).astype(jnp.bfloat16)
    mlp_set = (
        lax.all_gather(mlp_gain, ("dp", "ctx"), axis=0, tiled=True),
        lax.all_gather(w_gate, ("dp", "ctx"), axis=0, tiled=True),
        lax.all_gather(w_up, ("dp", "ctx"), axis=0, tiled=True),
        lax.all_gather(w_down, ("dp", "ctx"), axis=0, tiled=True),
    )
    normed_two, inv_root_two, mlp_in, gate_proj, up_proj, hidden, output_flat = mlp_block(
        flat_tokens, attended_low, attn_set[4], mlp_set
    )
    output = output_flat.reshape(tokens.shape).astype(jnp.bfloat16)
    attn_set = (
        lax.all_gather(attn_gain, ("dp", "ctx"), axis=0, tiled=True),
        lax.all_gather(w_query, ("dp", "ctx"), axis=0, tiled=True),
        lax.all_gather(w_key, ("dp", "ctx"), axis=0, tiled=True),
        lax.all_gather(w_value, ("dp", "ctx"), axis=0, tiled=True),
        lax.all_gather(w_out, ("dp", "ctx"), axis=0, tiled=True),
    )
    mlp_set = (
        lax.all_gather(mlp_gain, ("dp", "ctx"), axis=0, tiled=True),
        lax.all_gather(w_gate, ("dp", "ctx"), axis=0, tiled=True),
        lax.all_gather(w_up, ("dp", "ctx"), axis=0, tiled=True),
        lax.all_gather(w_down, ("dp", "ctx"), axis=0, tiled=True),
    )
    normed, inv_root, normed_in, query_rot, key_rot, value_mix = attn_front(
        flat_tokens, first_flat, attn_set, cosine_table, sine_table, row_count, seq_piece
    )
    key_full, value_full = (
        lax.all_gather(key_rot, "ctx", axis=1, tiled=True),
        lax.all_gather(value_mix, "ctx", axis=1, tiled=True),
    )
    normed_two, inv_root_two, mlp_in, gate_proj, up_proj, hidden, output_flat = mlp_block(
        flat_tokens, attended_low, attn_set[4], mlp_set
    )
    cot_low = cotangent.reshape(token_count, model_width)
    cot_float = cot_low.astype(jnp.float32)
    grad_hidden = jnp.einsum("td,fd->tf", cot_low, mlp_set[3], preferred_element_type=jnp.float32)
    sigma = jax.nn.sigmoid(gate_proj)
    grad_gate_low = (grad_hidden * up_proj * sigma * (1.0 + gate_proj * (1.0 - sigma))).astype(
        jnp.bfloat16
    )
    grad_up_low = (grad_hidden * gate_proj * sigma).astype(jnp.bfloat16)
    grad_mlp_in = jnp.einsum(
        "tf,df->td", grad_gate_low, mlp_set[1], preferred_element_type=jnp.float32
    )
    grad_mlp_in = grad_mlp_in + jnp.einsum(
        "tf,df->td", grad_up_low, mlp_set[2], preferred_element_type=jnp.float32
    )
    grad_middle_norm, grad_gain_two = norm_back(grad_mlp_in, normed_two, inv_root_two, mlp_set[0])
    grad_middle = cot_float + grad_middle_norm
    grad_branch_low = grad_middle.astype(jnp.bfloat16)
    grad_attended = jnp.einsum(
        "te,de->td", grad_branch_low, attn_set[4], preferred_element_type=jnp.float32
    )
    grad_attended = grad_attended.astype(jnp.bfloat16).reshape(row_count, seq_piece, model_width)
    grad_query_rot, grad_key_full, grad_value_full = lax.map(
        attend_back, (query_rot, key_full, value_full, grad_attended, log_total, allowed)
    )
    grad_key_rot, grad_value_mix = (
        lax.psum_scatter(
            grad_key_full.astype(jnp.bfloat16), "ctx", scatter_dimension=1, tiled=True
        ).astype(jnp.float32),
        lax.psum_scatter(
            grad_value_full.astype(jnp.bfloat16), "ctx", scatter_dimension=1, tiled=True
        ).astype(jnp.float32),
    )
    v1_grad = v1_accum + 0.5 * grad_value_mix
    grad_query_low = rotate(
        grad_query_rot.reshape(row_count, seq_piece, HEADS, HEAD_DIM), cosine_table, -sine_table
    )
    grad_query_low = grad_query_low.astype(jnp.bfloat16).reshape(token_count, model_width)
    grad_key_low = rotate(
        grad_key_rot.reshape(row_count, seq_piece, HEADS, HEAD_DIM), cosine_table, -sine_table
    )
    grad_key_low = grad_key_low.astype(jnp.bfloat16).reshape(token_count, model_width)
    grad_value_low = (0.5 * grad_value_mix).astype(jnp.bfloat16).reshape(token_count, model_width)
    grad_normed_in = jnp.einsum(
        "te,de->td", grad_query_low, attn_set[1], preferred_element_type=jnp.float32
    )
    grad_normed_in = grad_normed_in + jnp.einsum(
        "te,de->td", grad_key_low, attn_set[2], preferred_element_type=jnp.float32
    )
    grad_normed_in = grad_normed_in + jnp.einsum(
        "te,de->td", grad_value_low, attn_set[3], preferred_element_type=jnp.float32
    )
    grad_input_norm, grad_gain_one = norm_back(grad_normed_in, normed, inv_root, attn_set[0])
    input_grad = (grad_middle + grad_input_norm).reshape(tokens.shape)
    attn_right = jnp.concatenate([grad_query_low, grad_key_low, grad_value_low], axis=1)
    left_in = normed_in
    projections = jnp.einsum("td,te->de", left_in, attn_right, preferred_element_type=jnp.float32)
    out_part = jnp.einsum(
        "td,te->de", attended_low, grad_branch_low, preferred_element_type=jnp.float32
    )
    attn_matrix = lax.psum_scatter(
        jnp.concatenate([projections, out_part], axis=1),
        ("dp", "ctx"),
        scatter_dimension=0,
        tiled=True,
    )
    mlp_right = jnp.concatenate([grad_gate_low, grad_up_low], axis=1)
    left_in = mlp_in
    gate_up_matrix = lax.psum_scatter(
        jnp.einsum("td,tf->df", left_in, mlp_right, preferred_element_type=jnp.float32),
        ("dp", "ctx"),
        scatter_dimension=0,
        tiled=True,
    )
    down_matrix = lax.psum_scatter(
        jnp.einsum("tf,td->fd", hidden, cot_low, preferred_element_type=jnp.float32),
        ("dp", "ctx"),
        scatter_dimension=0,
        tiled=True,
    )
    gain_one, gain_two = (
        lax.psum_scatter(grad_gain_one, ("dp", "ctx"), scatter_dimension=0, tiled=True),
        lax.psum_scatter(grad_gain_two, ("dp", "ctx"), scatter_dimension=0, tiled=True),
    )
    ff_width = w_gate.shape[1]
    return (
        output,
        input_grad,
        v1_grad,
        gain_one,
        attn_matrix[:, 0:model_width],
        attn_matrix[:, model_width : 2 * model_width],
        attn_matrix[:, 2 * model_width : 3 * model_width],
        attn_matrix[:, 3 * model_width : 4 * model_width],
        gain_two,
        gate_up_matrix[:, 0:ff_width],
        gate_up_matrix[:, ff_width : 2 * ff_width],
        down_matrix,
    )


def solution(mesh):
    placed = (
        P("dp", "ctx", None),
        P("dp", "ctx", None),
        P("dp", "ctx", None),
        P("dp", "ctx"),
        P("dp", "ctx"),
        P("dp", "ctx", None),
        P(("dp", "ctx")),
        P(("dp", "ctx"), None),
        P(("dp", "ctx"), None),
        P(("dp", "ctx"), None),
        P(("dp", "ctx"), None),
        P(("dp", "ctx")),
        P(("dp", "ctx"), None),
        P(("dp", "ctx"), None),
        P(("dp", "ctx"), None),
    )
    return jax.shard_map(
        local,
        mesh=mesh,
        in_specs=placed,
        out_specs=(
            P("dp", "ctx", None),
            P("dp", "ctx", None),
            P("dp", "ctx", None),
            P(("dp", "ctx")),
            P(("dp", "ctx"), None),
            P(("dp", "ctx"), None),
            P(("dp", "ctx"), None),
            P(("dp", "ctx"), None),
            P(("dp", "ctx")),
            P(("dp", "ctx"), None),
            P(("dp", "ctx"), None),
            P(("dp", "ctx"), None),
        ),
        check_vma=False,
    )
```

profile of v0, /device:TPU:27, one launch (start us, length us, event | category | flops | bytes accessed | tf_op | source)
XLA Modules:
  0.0 2115.0 jit_solution(10984931252567152281)
XLA Ops:
  11.1 38.3 %all-reduce.5 = (bf16[1024]{0:T(1024)(128)(2,1)S(1)}, bf16[1024]{0:T(1024)(128)(2,1)S(1)}) all-reduce(bf16[1024]{0:T(1024)(128)(2,1)S(1)} %dynamic-update-slice, bf16[1024]{0:T(1024)(128)(2,1)S(1)} %dynamic-update-slice.1), channel_id=1, replica_groups=mesh['dp'=8,'ctx'=4] {'dp','ctx'}, use_global_device_ids=true, to_apply=%add | all-reduce | flops 2048 | bytes 8192
  51.0 16.7 all-gather.11.cloned.1.call-done
  67.7 4.4 fusion.45
  73.2 52.8 %all-gather.15.cloned.1.call-done = bf16[1024,1024]{1,0:T(8,128)(2,1)} async-done(((bf16[32,1024]{1,0:T(8,128)(2,1)}), bf16[1024,1024]{1,0:T(8,128)(2,1)}) %all-gather.15.cloned.1.call-update) | async-done | bytes 2097168 | tf_op jit(solution)/shard_map/all_gather | solution.py:201
  128.9 55.4 %all-gather.13.cloned.1.call-done = bf16[1024,1024]{1,0:T(8,128)(2,1)} async-done(((bf16[32,1024]{1,0:T(8,128)(2,1)}), bf16[1024,1024]{1,0:T(8,128)(2,1)}) %all-gather.13.cloned.1.call-update) | async-done | bytes 2097168 | tf_op jit(solution)/shard_map/all_gather | solution.py:200
  184.3 3.9 copy.36
  196.0 11.6 all_gather.50
  208.4 56.2 %all-gather.27.cloned.1.call-done = bf16[2048,1024]{1,0:T(8,128)(2,1)} async-done(((bf16[512,1024]{1,0:T(8,128)(2,1)}), bf16[2048,1024]{1,0:T(8,128)(2,1)}) %all-gather.27.cloned.1.call-update) | async-done | bytes 4194320 | tf_op jit(solution)/shard_map/all_gather | solution.py:210
  264.6 6.5 copy.44
  271.1 74.8 %all-gather.17.cloned.1.call-done = bf16[1,2048,1024]{1,2,0:T(8,128)(2,1)} async-done(((bf16[1,512,1024]{1,2,0:T(8,128)(2,1)}), bf16[1,2048,1024]{1,2,0:T(8,128)(2,1)}) %all-gather.17.cloned.1.call-update) | async-done | bytes 4194320 | tf_op jit(solution)/shard_map/all_gather | solution.py:209
  345.9 65.4 %while.50 = (s32[]{:T(128)}, bf16[4,512,256]{1,2,0:T(8,128)(2,1)S(1)}, f32[4,4,512]{2,1,0:T(4,128)}, bf16[4,2048,256]{1,2,0:T(8,128)(2,1)}, bf16[4,512,256]{1,2,...) while((s32[]{:T(128)}, ...), condition=%wide.region_4.5_spmd.clone.clone, body=%wide.region_1.4_spmd.clone.sunk.clone | while | flops 1127217152 | bytes 62468212 | solution.py:120
  348.9 3.3 fusion.156
  352.2 4.4 fusion.157
  356.6 5.0 fusion.158
  365.2 3.3 fusion.156
  368.5 4.4 fusion.157
  372.9 5.0 fusion.158
  381.6 3.3 fusion.156
  384.9 4.4 fusion.157
  389.3 5.0 fusion.158
  397.9 3.3 fusion.156
  401.2 4.4 fusion.157
  405.6 5.0 fusion.158
  412.6 3.3 multiply_reduce_fusion.3
  416.2 58.0 %all-gather.21.cloned.1.call-done = bf16[1024,2816]{1,0:T(8,128)(2,1)} async-done(((bf16[32,2816]{1,0:T(8,128)(2,1)}), bf16[1024,2816]{1,0:T(8,128)(2,1)}) %all-gather.21.cloned.1.call-update) | async-done | bytes 5767184 | tf_op jit(solution)/shard_map/all_gather | solution.py:224
  474.2 7.5 fusion.70
  481.7 61.6 %all-gather.23.cloned.1.call-done = bf16[1024,2816]{1,0:T(8,128)(2,1)} async-done(((bf16[32,2816]{1,0:T(8,128)(2,1)}), bf16[1024,2816]{1,0:T(8,128)(2,1)}) %all-gather.23.cloned.1.call-update) | async-done | bytes 5767184 | tf_op jit(solution)/shard_map/all_gather | solution.py:225
  543.4 8.0 fusion.71
  551.3 61.2 %all-gather.25.cloned.1.call-done = bf16[2816,1024]{1,0:T(8,128)(2,1)} async-done(((bf16[88,1024]{1,0:T(8,128)(2,1)}), bf16[2816,1024]{1,0:T(8,128)(2,1)}) %all-gather.25.cloned.1.call-update) | async-done | bytes 5767184 | tf_op jit(solution)/shard_map/all_gather | solution.py:226
  612.5 11.3 multiply_convert_fusion.1
  623.8 7.3 fusion.72
  631.2 4.0 multiply_reduce_fusion.1
  639.8 187.9 %while.51 = (s32[]{:T(128)}, f32[4,512,256]{1,2,0:T(8,128)}, bf16[4,2048,256]{1,2,0:T(8,128)(2,1)}, bf16[4,2048,256]{1,2,0:T(8,128)(2,1)}, bf16[4,2048,256]{1,2,...) while((s32[]{:T(128)}, f32[4,512,256]{1,2,0:T(8,128)}, ...), condition=%wide.region_9.10_spmd.clone.clone, body=%wide.region_7.9_spmd.clone.sunk.clone | while | flops 2751592448 | bytes 188371376 | solution.py:162
  652.2 11.7 multiply_reduce_fusion.6
  663.9 8.5 multiply_convert_fusion.7
  676.5 3.8 fusion.171
  680.4 5.0 convolution_multiply_fusion.7
  699.2 11.7 multiply_reduce_fusion.6
  710.8 8.5 multiply_convert_fusion.7
  723.5 3.8 fusion.171
  727.3 5.0 convolution_multiply_fusion.7
  746.0 11.7 multiply_reduce_fusion.6
  757.6 8.5 multiply_convert_fusion.7
  770.3 3.8 fusion.171
  774.2 5.0 convolution_multiply_fusion.7
  792.9 11.6 multiply_reduce_fusion.6
  804.5 8.5 multiply_convert_fusion.7
  817.2 3.8 fusion.171
  821.0 5.0 convolution_multiply_fusion.7
  827.7 6.4 copy.46
  836.4 3.2 fusion.55
  839.6 64.3 %reduce-scatter.6.cloned.1.call-done = bf16[1,512,1024]{1,2,0:T(8,128)(2,1)} async-done(((bf16[1,2048,1024]{1,2,0:T(8,128)(2,1)}), bf16[1,512,1024]{1,2,0:T(8,128)(2,1)}) %reduce-scatter.6.cloned.1.call-update) | async-done | bytes 1048592 | tf_op jit(solution)/shard_map/reduce_scatter | solution.py:280
  911.3 72.3 %reduce-scatter.8.cloned.1.call-done = bf16[1,512,1024]{2,1,0:T(8,128)(2,1)} async-done(((bf16[1,2048,1024]{2,1,0:T(8,128)(2,1)}), bf16[1,512,1024]{2,1,0:T(8,128)(2,1)}) %reduce-scatter.8.cloned.1.call-update) | async-done | bytes 1048592 | tf_op jit(solution)/shard_map/reduce_scatter | solution.py:283
  983.6 3.9 fusion.49
  987.6 3.6 fusion.21
  991.2 6.1 pad_maximum_fusion
  997.4 13.8 fusion.17
  1011.5 9.5 fusion.51
  1021.1 8.4 fusion.48
  1036.4 42.1 %all-reduce.4 = (f32[1024]{0:T(1024)S(1)}, f32[1024]{0:T(1024)S(1)}) all-reduce(f32[1024]{0:T(1024)S(1)} %get-tuple-element.214, f32[1024]{0:T(1024)S(1)} %copy-done.43), channel_id=5, replica_groups=mesh['dp'=8,'ctx'=4] {'dp','ctx'}, use_global_device_ids=true, to_apply=%region_14.15.clone | all-reduce | flops 2048 | bytes 16384
  1079.6 3.5 fusion.39
  1083.1 278.1 %reduce-scatter.10.cloned.1.call-done = f32[32,4096]{1,0:T(8,128)} async-done(((f32[1024,4096]{1,0:T(8,128)}), f32[32,4096]{1,0:T(8,128)}) %reduce-scatter.10.cloned.1.call-update) | async-done | bytes 524304 | tf_op jit(solution)/shard_map/reduce_scatter | solution.py:314
  1363.1 494.0 %reduce-scatter.12.cloned.1.call-done = f32[32,5632]{1,0:T(8,128)} async-done(((f32[1024,5632]{1,0:T(8,128)}), f32[32,5632]{1,0:T(8,128)}) %reduce-scatter.12.cloned.1.call-update) | async-done | bytes 720912 | tf_op jit(solution)/shard_map/reduce_scatter | solution.py:322
  1859.1 249.0 %reduce-scatter.14.cloned.1.call-done = f32[88,1024]{1,0:T(8,128)} async-done(((f32[2816,1024]{1,0:T(8,128)}), f32[88,1024]{1,0:T(8,128)}) %reduce-scatter.14.cloned.1.call-update) | async-done | bytes 360464 | tf_op jit(solution)/shard_map/reduce_scatter | solution.py:328
  (281 shorter events, 131.2 us)
Async XLA Ops:
  7.2 60.5 %all-gather.11.cloned.1.call-start = ((), (), s32[]{:S(2)}) async-start(), calls=%async_computation.5 | async-start | bytes 2162688 | tf_op jit(solution)/shard_map/all_gather | solution.py:202
  7.9 118.1 %all-gather.15.cloned.1.call-start = ((), (), s32[]{:S(2)}) async-start(), calls=%async_computation.7 | async-start | bytes 2162688 | tf_op jit(solution)/shard_map/all_gather | solution.py:201
  8.7 175.6 %all-gather.13.cloned.1.call-start = ((), (), s32[]{:S(2)}) async-start(), calls=%async_computation.6 | async-start | bytes 2162688 | tf_op jit(solution)/shard_map/all_gather | solution.py:200
  9.4 255.2 %all-gather.27.cloned.1.call-start = ((), (), s32[]{:S(2)}) async-start(), calls=%async_computation.18 | async-start | bytes 5242880 | tf_op jit(solution)/shard_map/all_gather | solution.py:210
  49.5 140.1 %copy-start.35 = (f32[1024]{0:T(1024)}, f32[1024]{0:T(1024)S(1)}, u32[]{:S(2)}) copy-start(f32[1024]{0:T(1024)S(1)} %convert_element_type.172) | copy-start | bytes 12292
  51.0 138.6 %copy-start.40 = (f32[512]{0:T(512)}, f32[512]{0:T(512)S(1)}, u32[]{:S(2)}) copy-start(f32[512]{0:T(512)S(1)} %add_rsqrt_fusion.1) | copy-start | bytes 6148
  51.0 21.2 %copy-start.45 = (s32[1,512]{1,0:T(1,128)S(1)}, s32[1,512]{1,0:T(1,128)}, u32[]{:S(2)}) copy-start(s32[1,512]{1,0:T(1,128)} %param.23) | copy-start | bytes 6148
  72.1 273.7 %all-gather.17.cloned.1.call-start = ((), (), s32[]{:S(2)}) async-start(), calls=%async_computation.8 | async-start | bytes 5242880 | tf_op jit(solution)/shard_map/all_gather | solution.py:209
  73.2 118.0 %copy-start.33 = (f32[512,32]{0,1:T(8,128)}, f32[512,32]{0,1:T(8,128)S(1)}, u32[]{:S(2)}) copy-start(f32[512,32]{0,1:T(8,128)S(1)} %get-tuple-element.295) | copy-start | bytes 196612
  128.9 59.4 %copy-start.5 = (bf16[1,512,1024]{2,1,0:T(8,128)(2,1)S(1)}, bf16[1,512,1024]{2,1,0:T(8,128)(2,1)}, u32[]{:S(2)}) copy-start(bf16[1,512,1024]{2,1,0:T(8,128)(2,1)} %param.19) | copy-start | bytes 3145732
  191.9 4.1 copy-start.44
  193.0 218.3 %all-gather.19.cloned.1.call-start = ((), (), s32[]{:S(2)}) async-start(), calls=%async_computation.9 | async-start | bytes 2162688 | tf_op jit(solution)/shard_map/all_gather | solution.py:203
  193.6 280.6 %all-gather.21.cloned.1.call-start = ((), (), s32[]{:S(2)}) async-start(), calls=%async_computation.10 | async-start | bytes 5947392 | tf_op jit(solution)/shard_map/all_gather | solution.py:224
  194.3 349.0 %all-gather.23.cloned.1.call-start = ((), (), s32[]{:S(2)}) async-start(), calls=%async_computation.11 | async-start | bytes 5947392 | tf_op jit(solution)/shard_map/all_gather | solution.py:225
  195.1 417.5 %all-gather.25.cloned.1.call-start = ((), (), s32[]{:S(2)}) async-start(), calls=%async_computation.12 | async-start | bytes 5947392 | tf_op jit(solution)/shard_map/all_gather | solution.py:226
  195.8 708.1 %reduce-scatter.6.cloned.1.call-start = ((), (), s32[]{:S(2)}) async-start(), calls=%async_computation.13 | async-start | bytes 5242880 | tf_op jit(solution)/shard_map/reduce_scatter | solution.py:280
  345.9 66.7 %copy-start.6 = (bf16[1,512,1024]{2,1,0:T(8,128)(2,1)S(1)}, bf16[1,512,1024]{2,1,0:T(8,128)(2,1)}, u32[]{:S(2)}) copy-start(bf16[1,512,1024]{2,1,0:T(8,128)(2,1)} %param.19) | copy-start | bytes 3145732
  412.6 3.3 copy-start.42
  415.9 219.4 %copy-start.11 = (f32[512,1024]{1,0:T(8,128)}, f32[512,1024]{1,0:T(8,128)S(1)}, u32[]{:S(2)}) copy-start(f32[512,1024]{1,0:T(8,128)S(1)} %get-tuple-element.299) | copy-start | bytes 6291460
  416.2 127.2 %copy-start.15 = (bf16[512,1024]{1,0:T(8,128)(2,1)}, bf16[512,1024]{1,0:T(8,128)(2,1)S(1)}, u32[]{:S(2)}) copy-start(bf16[512,1024]{1,0:T(8,128)(2,1)S(1)} %multiply_convert_fusion.4) | copy-start | bytes 3145732
  623.8 7.4 copy-start.23
  623.8 7.4 copy-start.22
  623.8 7.4 copy-start.46
  631.2 4.1 copy-start.30
  639.9 2.3 copy-start.31
  640.0 2.3 copy-start.38
  642.3 2.4 copy-start.2
  672.4 3.3 copy-start
  672.4 4.1 copy-start.1
  672.4 4.1 copy-start.4
  676.5 3.8 copy-start.3
  686.9 2.3 copy-start.38
  689.2 2.4 copy-start.2
  719.3 3.3 copy-start
  719.3 4.1 copy-start.1
  719.4 4.1 copy-start.4
  723.5 3.8 copy-start.3
  733.7 2.3 copy-start.38
  736.0 2.4 copy-start.2
  766.2 3.3 copy-start
  766.2 4.2 copy-start.1
  766.2 4.2 copy-start.4
  770.3 3.8 copy-start.3
  780.6 2.3 copy-start.38
  782.9 2.4 copy-start.2
  813.0 3.3 copy-start
  813.1 4.1 copy-start.1
  813.1 4.1 copy-start.4
  817.2 3.8 copy-start.3
  827.7 155.9 %reduce-scatter.8.cloned.1.call-start = ((), (), s32[]{:S(2)}) async-start(), calls=%async_computation.14 | async-start | bytes 5242880 | tf_op jit(solution)/shard_map/reduce_scatter | solution.py:283
  834.2 527.1 %reduce-scatter.10.cloned.1.call-start = ((), (), s32[]{:S(2)}) async-start(), calls=%async_computation.15 | async-start | bytes 17301504 | tf_op jit(solution)/shard_map/reduce_scatter | solution.py:314
  839.6 66.0 %copy-start.34 = (f32[512,32]{0,1:T(8,128)S(1)}, f32[512,32]{0,1:T(8,128)}, u32[]{:S(2)}) copy-start(f32[512,32]{0,1:T(8,128)} %copy-done.33) | copy-start | bytes 196612
  839.6 66.0 %copy-start.37 = (f32[512,32]{0,1:T(8,128)S(1)}, f32[512,32]{0,1:T(8,128)}, u32[]{:S(2)}) copy-start(f32[512,32]{0,1:T(8,128)} %get-tuple-element.293) | copy-start | bytes 196612
  911.3 76.3 %copy-start.7 = (bf16[1,512,1024]{2,1,0:T(8,128)(2,1)S(1)}, bf16[1,512,1024]{2,1,0:T(8,128)(2,1)}, u32[]{:S(2)}) copy-start(bf16[1,512,1024]{2,1,0:T(8,128)(2,1)} %param.19) | copy-start | bytes 3145732
  911.3 76.3 %copy-start.36 = (f32[1024]{0:T(1024)S(1)}, f32[1024]{0:T(1024)}, u32[]{:S(2)}) copy-start(f32[1024]{0:T(1024)} %copy-done.35) | copy-start | bytes 12292
  911.3 76.3 %copy-start.41 = (f32[512]{0:T(512)S(1)}, f32[512]{0:T(512)}, u32[]{:S(2)}) copy-start(f32[512]{0:T(512)} %copy-done.40) | copy-start | bytes 6148
  983.6 3.9 copy-start.16
  983.6 4.0 copy-start.17
  987.6 3.6 copy-start.8
  997.3 859.8 %reduce-scatter.12.cloned.1.call-start = ((), (), s32[]{:S(2)}) async-start(), calls=%async_computation.16 | async-start | bytes 23789568 | tf_op jit(solution)/shard_map/reduce_scatter | solution.py:322
  1011.2 1096.9 %reduce-scatter.14.cloned.1.call-start = ((), (), s32[]{:S(2)}) async-start(), calls=%async_computation.17 | async-start | bytes 11894784 | tf_op jit(solution)/shard_map/reduce_scatter | solution.py:328
  1021.1 8.4 copy-start.20
  1021.1 8.4 copy-start.26
  1033.4 3.0 copy-start.43
  (24 other events, 39.9 us)
Sparse Core Ops, SparseCore 0:
  10.9 56.6 all-gather.10
  70.6 55.3 all-gather.14
  128.9 55.3 all-gather.12
  186.3 78.2 all-gather.26
  266.6 79.2 all-gather.16
  348.7 56.5 all-gather.18
  408.0 66.1 all-gather.20
  477.0 66.2 all-gather.22
  546.2 66.2 all-gather.24
  827.8 76.0 reduce-scatter.5
  906.3 77.2 reduce-scatter.7
  997.4 363.7 reduce-scatter.9
  1363.5 493.5 reduce-scatter.11
  1859.9 248.1 reduce-scatter.13
where the time goes:
time: 2130 us; the launch traced here: 2120 us
  waiting for transfers between devices  1600 us (75%)
  matrix products  229 us (11%)
  other arithmetic  93.1 us (4%)
  blocking collectives  92 us (4%)
  local copies, waits for them, and re-layouts  84.8 us (4%)
    reduce_scatter x1, waiting for transfers between devices, local(): lax.psum_scatter(jnp.einsum('td,tf->df', left_in, mlp_right, preferred_el...  494 us
    reduce_scatter x1, waiting for transfers between devices, local(): lax.psum_scatter(jnp.concatenate([projections, out_part], axis=1), ('dp',...  278 us
    reduce_scatter x1, waiting for transfers between devices, local(): lax.psum_scatter(jnp.einsum('tf,td->fd', hidden, cot_low, preferred_eleme...  249 us
    unnamed x2, blocking collectives  80.4 us
    all_gather x1, waiting for transfers between devices, local(): lax.all_gather(key_rot, 'ctx', axis=1, tiled=True)  74.8 us
    reduce_scatter x1, waiting for transfers between devices, local(): lax.psum_scatter(grad_value_full.astype(jnp.bfloat16), 'ctx', scatter_dim...  72.3 us
    reduce_scatter x1, waiting for transfers between devices, local(): lax.psum_scatter(grad_key_full.astype(jnp.bfloat16), 'ctx', scatter_dimen...  64.3 us
    all_gather x1, waiting for transfers between devices, local(): lax.all_gather(w_up, ('dp', 'ctx'), axis=0, tiled=True)  61.6 us
  transfers between devices with their start and end apart: 14, of which 13 were waited for; matrix products, arithmetic and copies ran while one was open for 8% of the time, Pallas kernels for 0%

commit v1 on v0

--- a/solution.py
+++ b/solution.py
@@ -1,14 +1,25 @@
+import functools
+
 import jax
 import jax.numpy as jnp
 from jax import lax
+from jax.experimental import pallas as pl
+from jax.experimental.pallas import tpu as pltpu
 from jax.sharding import PartitionSpec as P
 
 HEADS = 16
 HEAD_DIM = 64
+LANES = 128
+TOKEN_BLOCK = 512
+FF_BLOCK = 256
+NEG = -1e30
+F32 = jnp.float32
+LOW = jnp.bfloat16
+BYTES = 60 * 2**20
+epsilon = 1e-05
+
+
 HEAD_BLOCK = 4
-
-
-epsilon = 1e-05
 
 
 def rms_scale(values):
@@ -172,7 +183,7 @@
     return (join_groups(grad_query), join_groups(grad_key), join_groups(grad_value))
 
 
-def local(
+def plain_local(
     tokens,
     first_values,
     v1_accum,
@@ -352,6 +363,628 @@
     )
 
 
+def params(**kw):
+    return pltpu.CompilerParams(vmem_limit_bytes=BYTES, **kw)
+
+
+def dot(a, b, da, db):
+    return lax.dot_general(a, b, (((da,), (db,)), ((), ())), preferred_element_type=F32)
+
+
+def lane_block(index):
+    return pl.ds(pl.multiple_of(index * LANES, LANES), LANES)
+
+
+def half_swap(x):
+    lane = lax.broadcasted_iota(jnp.int32, x.shape, 1)
+    left = pltpu.roll(x, LANES - HEAD_DIM // 2, 1)
+    right = pltpu.roll(x, HEAD_DIM // 2, 1)
+    return jnp.where(lane % HEAD_DIM < HEAD_DIM // 2, left, right)
+
+
+def head_lanes(x, head):
+    lane = lax.broadcasted_iota(jnp.int32, x.shape, 1)
+    return jnp.where(lane // HEAD_DIM == head, x, jnp.zeros_like(x))
+
+
+def qkv_kernel(blocks, x_ref, w_ref, gain_ref, fv_ref, cos_ref, sin_ref, xn_ref, q_ref, k_ref, v_ref, rel):
+    dp = lax.axis_index("dp")
+    for d in range(blocks):
+        rel[:, d * LANES : (d + 1) * LANES] = x_ref[:, lane_block(dp ^ d)].astype(F32)
+    x = rel[...]
+    inv = lax.rsqrt(jnp.mean(x * x, axis=-1, keepdims=True) + epsilon)
+    xn = (x * inv * gain_ref[...]).astype(LOW)
+    xn_ref[...] = xn
+    width = q_ref.shape[1]
+    proj = dot(xn, w_ref[...], 1, 0)
+    cos, sin = cos_ref[...], sin_ref[...]
+    for b in range(width // LANES):
+        at = slice(b * LANES, (b + 1) * LANES)
+        qb = proj[:, b * LANES : (b + 1) * LANES]
+        q_ref[:, at] = ((qb * cos + half_swap(qb) * sin) * 0.125).astype(LOW)
+        kb = proj[:, width + b * LANES : width + (b + 1) * LANES]
+        k_ref[:, at] = (kb * cos + half_swap(kb) * sin).astype(LOW)
+    v_ref[...] = (0.5 * proj[:, 2 * width :] + 0.5 * fv_ref[...].astype(F32)).astype(LOW)
+
+
+def qkv_call(x, w, gain, fv, cos, sin):
+    length, model = x.shape
+    width = fv.shape[1]
+    tb = TOKEN_BLOCK
+    row = lambda cols: pl.BlockSpec((tb, cols), lambda i: (i, 0))
+    whole = lambda a: pl.BlockSpec(a.shape, lambda i: (0, 0))
+    return pl.pallas_call(
+        functools.partial(qkv_kernel, model // LANES),
+        grid=(length // tb,),
+        in_specs=[row(model), whole(w), whole(gain), row(width), row(LANES), row(LANES)],
+        out_specs=[row(model), row(width), row(width), row(width)],
+        out_shape=[jax.ShapeDtypeStruct((length, model), LOW)]
+        + [jax.ShapeDtypeStruct((length, width), LOW)] * 3,
+        scratch_shapes=[pltpu.VMEM((tb, model), F32)],
+        compiler_params=params(),
+        cost_estimate=pl.CostEstimate(
+            flops=2 * length * model * 3 * width, bytes_accessed=10 * 2**20, transcendentals=0
+        ),
+        name="qkv",
+    )(x, w, gain, fv, cos, sin)
+
+
+def attend_kernel(q_ref, k_ref, v_ref, sq_ref, sk_ref, o_ref, of_ref, lse_ref, s_ref, m_ref, l_ref, acc_ref):
+    i = pl.program_id(0)
+    tb = q_ref.shape[0]
+    q = q_ref[...]
+    seg_q = sq_ref[:, 0:1]
+    lane = lax.broadcasted_iota(jnp.int32, (tb, LANES), 1)
+
+    def fold(x, op):
+        r = x[:, 0:LANES]
+        for b in range(1, tb // LANES):
+            r = op(r, x[:, b * LANES : (b + 1) * LANES])
+        return r
+
+    for head in range(2):
+        qm = head_lanes(q, head)
+        m_ref[...] = jnp.full_like(m_ref, NEG)
+
+        def score(j, causal):
+            at = pl.ds(pl.multiple_of(j * tb, tb), tb)
+            s = dot(qm, k_ref[at, :], 1, 1)
+            ok = seg_q == sk_ref[0:1, at]
+            if causal:
+                r = lax.broadcasted_iota(jnp.int32, (tb, tb), 0)
+                c = lax.broadcasted_iota(jnp.int32, (tb, tb), 1)
+                ok = ok & (r >= c)
+            s = jnp.where(ok, s, NEG)
+            s_ref[:, at] = s
+            m_ref[...] = jnp.maximum(m_ref[...], fold(s, jnp.maximum))
+
+        def score_step(j, carry):
+            score(j, False)
+            return carry
+
+        lax.fori_loop(0, i, score_step, 0)
+        score(i, True)
+        top = jnp.max(m_ref[...], axis=1, keepdims=True)
+        l_ref[...] = jnp.zeros_like(l_ref)
+        acc_ref[...] = jnp.zeros_like(acc_ref)
+
+        def value_step(j, carry):
+            at = pl.ds(pl.multiple_of(j * tb, tb), tb)
+            p = jnp.exp(s_ref[:, at] - top)
+            l_ref[...] += fold(p, jnp.add)
+            acc_ref[...] += dot(p.astype(LOW), v_ref[at, :], 1, 0)
+            return carry
+
+        lax.fori_loop(0, i + 1, value_step, 0)
+        total = jnp.sum(l_ref[...], axis=1, keepdims=True)
+        out = acc_ref[...] / total
+        lse = jnp.broadcast_to(top + jnp.log(total), (tb, LANES))
+        if head == 0:
+            of_ref[...] = out
+            lse_ref[...] = lse
+        else:
+            of_ref[...] = jnp.where(lane < HEAD_DIM, of_ref[...], out)
+            lse_ref[...] = jnp.where(lane < HEAD_DIM, lse_ref[...], lse)
+    o_ref[...] = of_ref[...].astype(LOW)
+
+
+def attend_call(pair, q, k, v, seg_col, seg_row):
+    length = q.shape[0]
+    tb = TOKEN_BLOCK
+    rows = pl.BlockSpec((tb, LANES), lambda i: (i, 0))
+    full = pl.BlockSpec((length, LANES), lambda i: (0, pair))
+    return pl.pallas_call(
+        attend_kernel,
+        grid=(length // tb,),
+        in_specs=[
+            pl.BlockSpec((tb, LANES), lambda i: (i, pair)),
+            full,
+            full,
+            rows,
+            pl.BlockSpec((8, length), lambda i: (0, 0)),
+        ],
+        out_specs=[rows, rows, rows],
+        out_shape=[
+            jax.ShapeDtypeStruct((length, LANES), LOW),
+            jax.ShapeDtypeStruct((length, LANES), F32),
+            jax.ShapeDtypeStruct((length, LANES), F32),
+        ],
+        scratch_shapes=[
+            pltpu.VMEM((tb, length), F32),
+            pltpu.VMEM((tb, LANES), F32),
+            pltpu.VMEM((tb, LANES), F32),
+            pltpu.VMEM((tb, LANES), F32),
+        ],
+        compiler_params=params(),
+        cost_estimate=pl.CostEstimate(
+            flops=8 * 10**9, bytes_accessed=6 * 2**20, transcendentals=length * length
+        ),
+        name="attend",
+    )(q, k, v, seg_col, seg_row)
+
+
+def attend_back_kernel(
+    q_ref, k_ref, v_ref, g_ref, of_ref, lse_ref, sc_ref, sr_ref, cos_ref, sin_ref, out_ref,
+    lse_row, delta_row, dq_acc, dk_acc, dv_acc,
+):
+    j = pl.program_id(0)
+    steps = pl.num_programs(0)
+    tb = dk_acc.shape[0]
+
+    @pl.when(j == 0)
+    def _():
+        dq_acc[...] = jnp.zeros_like(dq_acc)
+        r = lax.broadcasted_iota(jnp.int32, (8, LANES), 0)
+        lane = lax.broadcasted_iota(jnp.int32, (8, LANES), 1)
+        first = jnp.where(lane == r * HEAD_DIM, 1.0, 0.0)
+        group = jnp.where(lane // HEAD_DIM == r, 1.0, 0.0)
+        exact = lax.Precision.HIGHEST
+        for b in range(lse_ref.shape[0] // tb):
+            at = slice(b * tb, (b + 1) * tb)
+            dims = (((1,), (1,)), ((), ()))
+            lse_row[:, at] = lax.dot_general(first, lse_ref[at, :], dims, precision=exact, preferred_element_type=F32)
+            prod = g_ref[at, :].astype(F32) * of_ref[at, :]
+            delta_row[:, at] = lax.dot_general(group, prod, dims, precision=exact, preferred_element_type=F32)
+
+    dk_acc[...] = jnp.zeros_like(dk_acc)
+    dv_acc[...] = jnp.zeros_like(dv_acc)
+    mine = pl.ds(pl.multiple_of(j * tb, tb), tb)
+    k = k_ref[mine, :]
+    v = v_ref[mine, :]
+    seg_k = sc_ref[mine, 0:1]
+
+    def block(i, causal):
+        at = pl.ds(pl.multiple_of(i * tb, tb), tb)
+        q = q_ref[at, :]
+        g = g_ref[at, :]
+        ok = seg_k == sr_ref[0:1, at]
+        if causal:
+            r = lax.broadcasted_iota(jnp.int32, (tb, tb), 0)
+            c = lax.broadcasted_iota(jnp.int32, (tb, tb), 1)
+            ok = ok & (r <= c)
+        for head in range(2):
+            qm = head_lanes(q, head)
+            gm = head_lanes(g, head)
+            s = dot(k, qm, 1, 1)
+            p = jnp.where(ok, jnp.exp(s - lse_row[head : head + 1, at]), 0.0)
+            dp = dot(v, gm, 1, 1)
+            ds = (p * (dp - delta_row[head : head + 1, at])).astype(LOW)
+            dv_acc[...] += dot(p.astype(LOW), gm, 1, 0)
+            dk_acc[...] += dot(ds, qm, 1, 0)
+            dq_acc[at, :] += dot(ds, head_lanes(k, head), 0, 0)
+
+    block(j, True)
+
+    def step(i, carry):
+        block(i, False)
+        return carry
+
+    lax.fori_loop(j + 1, steps, step, 0)
+    dk = dk_acc[...]
+    dk = dk * cos_ref[mine, :] - half_swap(dk) * sin_ref[mine, :]
+    out_ref[mine, LANES : 2 * LANES] = dk.astype(LOW)
+    out_ref[mine, 2 * LANES : 3 * LANES] = dv_acc[...].astype(LOW)
+
+    @pl.when(j == steps - 1)
+    def _():
+        for b in range(dq_acc.shape[0] // tb):
+            at = slice(b * tb, (b + 1) * tb)
+            dq = dq_acc[at, :] * 0.125
+            dq = dq * cos_ref[at, :] - half_swap(dq) * sin_ref[at, :]
+            out_ref[at, 0:LANES] = dq.astype(LOW)
+
+
+def attend_back_call(pair, q, k, v, g, of, lse, seg_col, seg_row, cos, sin):
+    length = q.shape[0]
+    tb = TOKEN_BLOCK
+    full = pl.BlockSpec((length, LANES), lambda j: (0, pair))
+    own = pl.BlockSpec((length, LANES), lambda j: (0, 0))
+    return pl.pallas_call(
+        attend_back_kernel,
+        grid=(length // tb,),
+        in_specs=[full] * 4 + [own] * 3 + [pl.BlockSpec((8, length), lambda j: (0, 0))] + [own] * 2,
+        out_specs=pl.BlockSpec((length, 3 * LANES), lambda j: (0, 0)),
+        out_shape=jax.ShapeDtypeStruct((length, 3 * LANES), LOW),
+        scratch_shapes=[
+            pltpu.VMEM((8, length), F32),
+            pltpu.VMEM((8, length), F32),
+            pltpu.VMEM((length, LANES), F32),
+            pltpu.VMEM((tb, LANES), F32),
+            pltpu.VMEM((tb, LANES), F32),
+        ],
+        compiler_params=params(),
+        cost_estimate=pl.CostEstimate(
+            flops=20 * 10**9, bytes_accessed=8 * 2**20, transcendentals=length * length
+        ),
+        name="attend_back",
+    )(q, k, v, g, of, lse, seg_col, seg_row, cos, sin)
+
+
+def mlp_kernel(blocks, tok_ref, att_ref, cot_ref, gain_ref, *refs):
+    pieces, refs = refs[: 3 * blocks], refs[3 * blocks :]
+    go_in, up_in, dn_in = pieces[:blocks], pieces[blocks : 2 * blocks], pieces[2 * blocks :]
+    out_ref, gm_ref, ga_ref, gk, gs, uk, us, ok, os, dk, ds = refs[:11]
+    wo, wg, wu, wd, att, nat, n2, mi, mit, inv_ref, oacc, dacc, dwd, sem, osem = refs[11:]
+    dp = lax.axis_index("dp")
+    u = pl.program_id(0)
+    last = pl.num_programs(0) - 1
+    ff = wu.shape[1]
+    down = dn_in[0].shape[0]
+
+    def copies():
+        made = []
+        for d in range(blocks):
+            at = pl.ds(d * LANES, LANES)
+            made.append(pltpu.make_async_copy(go_in[d].at[:, pl.ds(ff, wo.shape[1])], wo.at[at, :], sem.at[0, d]))
+        for d in range(blocks):
+            at = pl.ds(d * LANES, LANES)
+            made.append(pltpu.make_async_copy(go_in[d].at[:, pl.ds(0, ff)], wg.at[at, :], sem.at[1, d]))
+            made.append(pltpu.make_async_copy(up_in[d], wu.at[at, :], sem.at[2, d]))
+            rows = pl.ds(pl.multiple_of((dp ^ d) * down, 32), down)
+            made.append(pltpu.make_async_copy(dn_in[d], wd.at[rows, :], sem.at[3, d]))
+        return made
+
+    def out_copies():
+        made = []
+        for d in range(blocks):
+            rows = pl.ds(pl.multiple_of((dp ^ d) * down, 32), down)
+            made.append(pltpu.make_async_copy(dwd.at[rows, :], (ds if d % 2 else dk).at[d // 2], osem.at[d]))
+        return made
+
+    @pl.when(u == 0)
+    def _():
+        made = copies()
+        for c in made:
+            c.start()
+        for d in range(blocks):
+            att[:, d * LANES : (d + 1) * LANES] = att_ref[:, lane_block(dp ^ d)]
+        for c in made[:blocks]:
+            c.wait()
+        mid = tok_ref[...].astype(F32) + dot(att[...], wo[...], 1, 0)
+        inv = lax.rsqrt(jnp.mean(mid * mid, axis=-1, keepdims=True) + epsilon)
+        oacc[...] = mid
+        nat[...] = mid * inv
+        inv_ref[...] = jnp.broadcast_to(inv, inv_ref.shape)
+        for d in range(blocks):
+            n2[:, d * LANES : (d + 1) * LANES] = nat[:, lane_block(dp ^ d)]
+        mi[...] = (n2[...] * gain_ref[...]).astype(LOW)
+        mit[...] = mi[...].T
+        dacc[...] = jnp.zeros_like(dacc)
+        for c in made[blocks:]:
+            c.wait()
+
+    cols = pl.ds(pl.multiple_of(u * FF_BLOCK, FF_BLOCK), FF_BLOCK)
+    x = mi[...]
+    cot = cot_ref[...]
+    wgu, wuu, wdu = wg[:, cols], wu[:, cols], wd[cols, :]
+    gate = dot(x, wgu, 1, 0)
+    up = dot(x, wuu, 1, 0)
+    grad_hidden = dot(cot, wdu, 1, 1)
+    sig = jax.nn.sigmoid(gate)
+    hidden = (gate * sig * up).astype(LOW)
+    dg = (grad_hidden * up * sig * (1.0 + gate * (1.0 - sig))).astype(LOW)
+    du = (grad_hidden * gate * sig).astype(LOW)
+    oacc[...] += dot(hidden, wdu, 1, 0)
+    dacc[...] += dot(dg, wgu, 1, 1) + dot(du, wuu, 1, 1)
+    xt = mit[...]
+    dwg = dot(xt, dg, 1, 0).astype(LOW)
+    dwu = dot(xt, du, 1, 0).astype(LOW)
+    for d in range(blocks):
+        (gs if d % 2 else gk)[d // 2] = dwg[d * LANES : (d + 1) * LANES]
+        (us if d % 2 else uk)[d // 2] = dwu[d * LANES : (d + 1) * LANES]
+    dwd[cols, :] = dot(hidden, cot, 0, 0).astype(LOW)
+
+    @pl.when(u == last)
+    def _():
+        made = out_copies()
+        for c in made:
+            c.start()
+        out_ref[...] = oacc[...].astype(LOW)
+        scaled = dacc[...] * gain_ref[...]
+        norm = n2[...]
+        mean = jnp.mean(scaled * norm, axis=-1, keepdims=True)
+        n2[...] = inv_ref[:, 0:1] * (scaled - norm * mean)
+        for d in range(blocks):
+            nat[:, lane_block(dp ^ d)] = n2[:, d * LANES : (d + 1) * LANES]
+        gm = cot.astype(F32) + nat[...]
+        gm_ref[...] = gm
+        gb = gm.astype(LOW)
+        n2[...] = dot(gb, wo[...], 1, 1)
+        for d in range(blocks):
+            ga_ref[:, lane_block(dp ^ d)] = n2[:, d * LANES : (d + 1) * LANES].astype(LOW)
+        dwo = dot(att[...], gb, 0, 0).astype(LOW)
+        for d in range(blocks):
+            (os if d % 2 else ok)[d // 2] = dwo[d * LANES : (d + 1) * LANES]
+        for c in made:
+            c.wait()
+
+
+def mlp_call(tok, att, cot, gain, go, up, dn):
+    tb, model = tok.shape
+    blocks = len(go)
+    ff = up[0].shape[1]
+    half = blocks // 2
+    down = dn[0].shape[0]
+    whole = lambda a: pl.BlockSpec(a.shape, lambda u: (0, 0))
+    anyspace = pl.BlockSpec(memory_space=pl.ANY)
+    half_cols = pl.BlockSpec((half, LANES, FF_BLOCK), lambda u: (0, 0, u))
+    half_out = pl.BlockSpec((half, LANES, model), lambda u: (0, 0, 0))
+    tokens = pl.BlockSpec((tb, model), lambda u: (0, 0))
+    shape = jax.ShapeDtypeStruct
+    return pl.pallas_call(
+        functools.partial(mlp_kernel, blocks),
+        grid=(ff // FF_BLOCK,),
+        in_specs=[whole(tok), whole(att), whole(cot), whole(gain)] + [anyspace] * (3 * blocks),
+        out_specs=[tokens, tokens, tokens] + [half_cols] * 4 + [half_out] * 2 + [anyspace] * 2,
+        out_shape=[shape((tb, model), LOW), shape((tb, model), F32), shape((tb, model), LOW)]
+        + [shape((half, LANES, ff), LOW)] * 4
+        + [shape((half, LANES, model), LOW)] * 2
+        + [shape((half, down, model), LOW)] * 2,
+        scratch_shapes=[
+            pltpu.VMEM((model, model), LOW),
+            pltpu.VMEM((model, ff), LOW),
+            pltpu.VMEM((model, ff), LOW),
+            pltpu.VMEM((ff, model), LOW),
+            pltpu.VMEM((tb, model), LOW),
+            pltpu.VMEM((tb, model), F32),
+            pltpu.VMEM((tb, model), F32),
+            pltpu.VMEM((tb, model), LOW),
+            pltpu.VMEM((model, tb), LOW),
+            pltpu.VMEM((tb, LANES), F32),
+            pltpu.VMEM((tb, model), F32),
+            pltpu.VMEM((tb, model), F32),
+            pltpu.VMEM((ff, model), LOW),
+            pltpu.SemaphoreType.DMA((4, blocks)),
+            pltpu.SemaphoreType.DMA((blocks,)),
+        ],
+        compiler_params=params(),
+        cost_estimate=pl.CostEstimate(
+            flops=2 * tb * model * (8 * ff + 3 * model), bytes_accessed=50 * 2**20, transcendentals=0
+        ),
+        name="mlp",
+    )(tok, att, cot, gain, *go, *up, *dn)
+
+
+def input_kernel(blocks, parts, tok_ref, gm_ref, v1_ref, gain_ref, *refs):
+    w_in, refs = refs[:blocks], refs[blocks:]
+    g_in, refs = refs[: 2 * parts], refs[2 * parts :]
+    ig_ref, vg_ref, w, g, rel, nat, sem = refs
+    dp = lax.axis_index("dp")
+    c = lax.axis_index("ctx")
+    model = tok_ref.shape[1]
+    made = [pltpu.make_async_copy(w_in[d], w.at[pl.ds(d * LANES, LANES), :], sem.at[d]) for d in range(blocks)]
+    for m in made:
+        m.start()
+    for d in range(blocks):
+        rel[:, d * LANES : (d + 1) * LANES] = tok_ref[:, lane_block(dp ^ d)].astype(F32)
+    for k in range(parts):
+        source = lax.rem(c + parts - k, parts)
+        for pair in range(2):
+            for t in range(3):
+                block = g_in[2 * k + pair][:, t * LANES : (t + 1) * LANES]
+                g[:, pl.ds(pl.multiple_of(t * model + source * 2 * LANES + pair * LANES, LANES), LANES)] = block
+    gv = g[:, 2 * model :].astype(F32)
+    vg_ref[...] = v1_ref[...] + 0.5 * gv
+    x = rel[...]
+    inv = lax.rsqrt(jnp.mean(x * x, axis=-1, keepdims=True) + epsilon)
+    norm = x * inv
+    for m in made:
+        m.wait()
+    grad = dot(g[:, : 2 * model], w[:, : 2 * model], 1, 1)
+    grad = grad + 0.5 * dot(g[:, 2 * model :], w[:, 2 * model :], 1, 1)
+    scaled = grad * gain_ref[...]
+    mean = jnp.mean(scaled * norm, axis=-1, keepdims=True)
+    rel[...] = inv * (scaled - norm * mean)
+    for d in range(blocks):
+        nat[:, lane_block(dp ^ d)] = rel[:, d * LANES : (d + 1) * LANES]
+    ig_ref[...] = gm_ref[...] + nat[...]
+
+
+def input_call(tok, gm, v1, gain, ws, gs):
+    tb, model = tok.shape
+    blocks = len(ws)
+    parts = len(gs) // 2
+    vmem = pl.BlockSpec(memory_space=pltpu.VMEM)
+    shape = jax.ShapeDtypeStruct
+    return pl.pallas_call(
+        functools.partial(input_kernel, blocks, parts),
+        in_specs=[vmem] * 4 + [pl.BlockSpec(memory_space=pl.ANY)] * blocks + [vmem] * len(gs),
+        out_specs=[vmem, vmem],
+        out_shape=[shape((tb, model), F32)] * 2,
+        scratch_shapes=[
+            pltpu.VMEM((model, 3 * model), LOW),
+            pltpu.VMEM((tb, 3 * model), LOW),
+            pltpu.VMEM((tb, model), F32),
+            pltpu.VMEM((tb, model), F32),
+            pltpu.SemaphoreType.DMA((blocks,)),
+        ],
+        compiler_params=params(),
+        cost_estimate=pl.CostEstimate(
+            flops=2 * tb * model * 3 * model, bytes_accessed=20 * 2**20, transcendentals=0
+        ),
+        name="input_grad",
+    )(tok, gm, v1, gain, *ws, *gs)
+
+
+def fast_local(
+    n_dp, n_ctx, tokens, first_values, v1_accum, segment_ids, positions, cotangent,
+    attn_gain, w_query, w_key, w_value, w_out, mlp_gain, w_gate, w_up, w_down,
+):
+    c = lax.axis_index("ctx")
+    seq, model = tokens.shape[1:]
+    width = model // n_ctx
+    length = seq * n_ctx
+    ff = w_gate.shape[1]
+    own_rows = w_query.shape[0]
+    down_rows = w_down.shape[0]
+    bits = [1 << b for b in range(n_dp.bit_length() - 1)]
+    plane = bits[1:]
+
+    def shift(x, k):
+        return lax.ppermute(x, "ctx", [(i, (i + k) % n_ctx) for i in range(n_ctx)])
+
+    def flip(x, bit):
+        return lax.ppermute(x, "dp", [(i, i ^ bit) for i in range(n_dp)])
+
+    def cut(x, index, size, axis):
+        return lax.dynamic_slice_in_dim(x, index * size, size, axis)
+
+    def swap_ctx(x, axis):
+        size = x.shape[axis] // n_ctx
+        return [cut(x, c, size, axis)] + [shift(cut(x, (c + k) % n_ctx, size, axis), k) for k in range(1, n_ctx)]
+
+    def place(slots, axis):
+        size = slots[0].shape[axis]
+        dims = list(slots[0].shape)
+        dims[axis] = size * n_ctx
+        out = jnp.zeros(dims, slots[0].dtype)
+        for k, slot in enumerate(slots):
+            out = lax.dynamic_update_slice_in_dim(out, slot, ((c + n_ctx - k) % n_ctx) * size, axis)
+        return out
+
+    def gather_dp(x, order):
+        got = {0: x}
+        for bit in order:
+            for d in sorted(got):
+                got[d ^ bit] = flip(got[d], bit)
+        return [got[d] for d in range(n_dp)]
+
+    def gather_ctx(x):
+        return lax.all_gather(x, "ctx", axis=0, tiled=True)
+
+    tok = tokens[0]
+    row_tokens = gather_ctx(tok)
+    marks = jnp.concatenate([segment_ids, positions], axis=0)
+    marks = place([marks] + [shift(marks, k) for k in range(1, n_ctx)], 1)
+    head_first = place(swap_ctx(first_values[0], 1), 0)
+
+    gains = jnp.stack([attn_gain, mlp_gain], axis=1)
+    gains = jnp.tile(jnp.pad(gains, ((0, 0), (0, width - 2))), (1, n_ctx))
+    packed = jnp.stack([w_query, w_key, w_value, gains])
+    slots = jnp.stack(swap_ctx(packed, 2))
+    slots = place([slots[k : k + 1] for k in range(n_ctx)], 0)
+    slots = jnp.stack(gather_dp(slots, plane + bits[:1]))
+    packed_all = slots.reshape(n_dp * n_ctx, 4, own_rows, width)
+    head_weights = packed_all[:, :3].transpose(0, 2, 1, 3).reshape(model, 3 * width)
+    gain_rel = packed_all[:, 3, :, 0].reshape(1, model).astype(F32)
+    gain_two_rel = packed_all[:, 3, :, 1].reshape(1, model).astype(F32)
+
+    go = gather_ctx(jnp.concatenate([w_gate, w_out], axis=1))
+    up = gather_ctx(w_up)
+    dn = gather_ctx(w_down)
+    go = gather_dp(go, plane + bits[:1])
+    up = gather_dp(up, plane[::-1] + bits[:1])
+    dn = gather_dp(dn, plane[::-1] + bits[:1])
+
+    seg_row = jnp.broadcast_to(marks[0:1], (8, length))
+    seg_col = jnp.broadcast_to(marks[0][:, None], (length, LANES))
+    freqs = 10000.0 ** (-jnp.arange(HEAD_DIM // 2).astype(F32) * (2.0 / HEAD_DIM))
+    angles = marks[1].astype(F32)[:, None] * freqs
+    cos, sin = jnp.cos(angles), jnp.sin(angles)
+    cos = jnp.concatenate([cos] * 4, axis=1)
+    sin = jnp.concatenate([-sin, sin] * 2, axis=1)
+    xn, q, k, v = qkv_call(row_tokens, head_weights, gain_rel, head_first, cos, sin)
+    pairs = width // LANES
+    outs = [attend_call(p, q, k, v, seg_col, seg_row) for p in range(pairs)]
+    attended = jnp.zeros((seq, model), LOW)
+    for p in range(pairs):
+        for s, slot in enumerate(swap_ctx(outs[p][0], 0)):
+            at = ((c + n_ctx - s) % n_ctx) * width + p * LANES
+            attended = lax.dynamic_update_slice_in_dim(attended, slot, at, 1)
+    cot = cotangent[0]
+    (output, grad_middle, grad_attended, gate_keep, gate_send, up_keep, up_send, out_keep, out_send,
+     down_keep, down_send) = mlp_call(tok, attended, cot, gain_two_rel, go, up, dn)
+
+    head_grad = place(swap_ctx(grad_attended, 1), 0)
+
+    qkv_all = gather_dp(gather_ctx(jnp.concatenate([w_query, w_key, w_value], axis=1)), plane + bits[:1])
+
+    back = [
+        attend_back_call(p, q, k, v, head_grad, outs[p][1], outs[p][2], seg_col, seg_row, cos, sin)
+        for p in range(pairs)
+    ]
+
+    def scatter_dp(keep, send, order):
+        terms = [keep, flip(send, bits[0])]
+        count = keep.shape[0]
+        names = list(range(count))
+        for bit in order:
+            near = bit >> 1
+            stay = [n for n in names if not n & near]
+            leave = [n for n in names if n & near]
+
+            def pick(which):
+                return sum(
+                    jnp.stack([t[names.index(n)] for n in which]).astype(F32) for t in terms
+                )
+
+            got = flip(pick(leave).astype(LOW), bit)
+            terms = [jnp.stack([t[names.index(n)] for n in stay]) for t in terms] + [got]
+            names = stay
+        return sum(t[0].astype(F32) for t in terms)
+
+    def scatter_ctx(x):
+        size = x.shape[0] // n_ctx
+        got = cut(x, c, size, 0)
+        for k in range(1, n_ctx):
+            got = got + shift(cut(x, (c + k) % n_ctx, size, 0).astype(LOW), k).astype(F32)
+        return got
+
+    gate_grad = scatter_ctx(scatter_dp(gate_keep, gate_send, plane))
+    up_grad = scatter_ctx(scatter_dp(up_keep, up_send, plane[::-1]))
+    down_grad = scatter_ctx(scatter_dp(down_keep, down_send, plane))
+    out_grad = scatter_ctx(scatter_dp(out_keep, out_send, plane[::-1]))
+
+    grads = [swap_ctx(b, 0) for b in back]
+    qkv_grad = jnp.zeros((3, own_rows, model), F32)
+    for p in range(pairs):
+        product = lax.dot_general(
+            xn, back[p], (((0,), (0,)), ((), ())), preferred_element_type=F32
+        ).astype(LOW).reshape(n_dp // 2, 2, model // n_dp, 3 * LANES)
+        total = scatter_dp(product[:, 0], product[:, 1], plane)
+        for s, slot in enumerate(swap_ctx(total.astype(LOW), 0)):
+            block = slot.astype(F32).reshape(own_rows, 3, LANES).transpose(1, 0, 2)
+            at = ((c + n_ctx - s) % n_ctx) * width + p * LANES
+            qkv_grad = lax.dynamic_update_slice_in_dim(qkv_grad, block, at, 2)
+    query_grad, key_grad, value_grad = qkv_grad[0], qkv_grad[1], 0.5 * qkv_grad[2]
+
+    input_grad, v1_grad = input_call(
+        tok, grad_middle, v1_accum[0], gain_rel, qkv_all, [grads[p][s] for s in range(n_ctx) for p in range(pairs)]
+    )
+
+    def row_dot(a, w):
+        return jnp.sum(a * w.astype(F32), axis=1)
+
+    gain_one = (
+        row_dot(query_grad, w_query) + row_dot(key_grad, w_key) + row_dot(value_grad, w_value)
+    ) / attn_gain.astype(F32)
+    gain_two = (row_dot(gate_grad, w_gate) + row_dot(up_grad, w_up)) / mlp_gain.astype(F32)
+    return (
+        output[None], input_grad[None], v1_grad[None], gain_one, query_grad, key_grad, value_grad,
+        out_grad, gain_two, gate_grad, up_grad, down_grad,
+    )
+
+
 def solution(mesh):
     placed = (
         P("dp", "ctx", None),
@@ -370,6 +1003,19 @@
         P(("dp", "ctx"), None),
         P(("dp", "ctx"), None),
     )
+    n_dp, n_ctx = mesh.shape["dp"], mesh.shape["ctx"]
+
+    def local(*args):
+        rows, seq, model = args[0].shape
+        fits = (
+            rows == 1
+            and seq == TOKEN_BLOCK
+            and model == n_dp * LANES
+            and model == 2 * LANES * n_ctx
+            and args[12].shape[1] % FF_BLOCK == 0
+        )
+        return fast_local(n_dp, n_ctx, *args) if fits else plain_local(*args)
+
     return jax.shard_map(
         local,
         mesh=mesh,

time: 2130 us -> 724 us (0.34)
  waiting for transfers between devices: 1600 us -> 243 us
  matrix products: 229 us -> 10.2 us
  Pallas kernels: 0 us -> 151 us
  starting transfers between devices: 0.81 us -> 103 us
  other arithmetic: 93.1 us -> 36.1 us
  local copies, waits for them, and re-layouts: 84.8 us -> 42 us
    reduce_scatter x5 -> x0, waiting for transfers between devices: 1160 us -> none  [the longest x1 494 us: local(): lax.psum_scatter(jnp.einsum('td,tf->df', left_in, mlp_right, preferred_el...]
    all_gather x9 -> x1, waiting for transfers between devices: 437 us -> 0.01 us  [gather_ctx(): return lax.all_gather(x, 'ctx', axis=0, tiled=True)]
    ppermute x0 -> x95, waiting for transfers between devices: none -> 243 us  [the longest x53 131 us: flip(): return lax.ppermute(x, 'dp', [(i, i ^ bit) for i in range(n_dp)])]
    dot_general x46 -> x2, matrix products: 229 us -> 10.2 us  [fast_local(): lax.dot_general(xn, back[p], (((0,), (0,)), ((), ())), preferred_element_...]
    pallas_call x0 -> x7, Pallas kernels: none -> 151 us  [the longest x2 47.4 us: attend_back_call(): pl.pallas_call(attend_back_kernel, grid=(length // tb,), in_specs=[full]...]
    ppermute x0 -> x95, starting transfers between devices: none -> 103 us  [the longest x53 57.4 us: flip(): return lax.ppermute(x, 'dp', [(i, i ^ bit) for i in range(n_dp)])]
    all_gather x1 -> x4, blocking collectives: 11.6 us -> 111 us  [gather_ctx(): return lax.all_gather(x, 'ctx', axis=0, tiled=True)]
    unnamed x2 -> x0, blocking collectives: 80.4 us -> none
  transfers between devices with their start and end apart: 14 -> 96, of which waited for: 13 -> 27; matrix products, arithmetic and copies ran while one was open for 8% -> 12% of each run, Pallas kernels for 0% -> 21%
where the time goes in v1:
time: 724 us; the launch traced here: 712 us
  waiting for transfers between devices  243 us (34%)
  Pallas kernels  151 us (21%)
  blocking collectives  111 us (15%)
  starting transfers between devices  103 us (14%)
  local copies, waits for them, and re-layouts  42 us (6%)
  other arithmetic  36.1 us (5%)
  between operations  15.6 us (2%)
  matrix products  10.2 us (1%)
    ppermute x53, waiting for transfers between devices, flip(): return lax.ppermute(x, 'dp', [(i, i ^ bit) for i in range(n_dp)])  131 us
    ppermute x42, waiting for transfers between devices, shift(): return lax.ppermute(x, 'ctx', [(i, (i + k) % n_ctx) for i in range(n_ctx)])  112 us
    all_gather x4, blocking collectives, gather_ctx(): return lax.all_gather(x, 'ctx', axis=0, tiled=True)  111 us
    ppermute x53, starting transfers between devices, flip(): return lax.ppermute(x, 'dp', [(i, i ^ bit) for i in range(n_dp)])  57.4 us
    pallas_call x2, Pallas kernels, attend_back_call(): pl.pallas_call(attend_back_kernel, grid=(length // tb,), in_specs=[full]...  47.4 us
    pallas_call x1, Pallas kernels, mlp_call(): pl.pallas_call(functools.partial(mlp_kernel, blocks), grid=(ff // FF_BLOC...  47.3 us
    ppermute x42, starting transfers between devices, shift(): return lax.ppermute(x, 'ctx', [(i, (i + k) % n_ctx) for i in range(n_ctx)])  45.9 us
    pallas_call x2, Pallas kernels, attend_call(): pl.pallas_call(attend_kernel, grid=(length // tb,), in_specs=[pl.BlockSpe...  34.2 us
  transfers between devices with their start and end apart: 96, of which 27 were waited for; matrix products, arithmetic and copies ran while one was open for 12% of the time, Pallas kernels for 21%

profile of v1, /device:TPU:27, one launch (start us, length us, event | category | flops | bytes accessed | tf_op | source)
XLA Modules:
  0.0 712.0 jit_solution(16113248632045803048)
XLA Ops:
  12.7 3.1 collective-permute-start
  16.8 20.0 %all_gather.17.refs_8_ = bf16[128,2816]{1,0:T(8,128)(2,1)} all-gather(bf16[32,2816]{1,0:T(8,128)(2,1)S(1)} %copy-done.21), channel_id=1, replica_groups=mesh['dp'=8,'ctx'=4] {'ctx'}, dimensions={0}, use_global_device_ids=true | all-gather | bytes 901120 | tf_op jit(solution)/shard_map/all_gather | solution.py:873
  37.0 28.5 %all_gather.18.refs_16_ = bf16[352,1024]{1,0:T(8,128)(2,1)} all-gather(bf16[88,1024]{1,0:T(8,128)(2,1)} %param.29), channel_id=1, replica_groups=mesh['dp'=8,'ctx'=4] {'ctx'}, dimensions={0}, use_global_device_ids=true | all-gather | bytes 901120 | tf_op jit(solution)/shard_map/all_gather | solution.py:873
  65.5 28.1 %all_gather.19.refs_0_ = bf16[128,3072]{1,0:T(8,128)(2,1)S(1)} all-gather(bf16[32,3072]{1,0:T(8,128)(2,1)S(1)} %pad_maximum_fusion.4), channel_id=1, replica_groups=mesh['dp'=8,'ctx'=4] {'ctx'}, dimensions={0}, use_global_device_ids=true | all-gather | bytes 983040 | tf_op jit(solution)/shard_map/all_gather | solution.py:873
  93.7 34.5 %all_gather.16.refs_0_ = bf16[128,3840]{1,0:T(8,128)(2,1)S(1)} all-gather(bf16[32,3840]{1,0:T(8,128)(2,1)S(1)} %pad_maximum_fusion.3), channel_id=1, replica_groups=mesh['dp'=8,'ctx'=4] {'ctx'}, dimensions={0}, use_global_device_ids=true | all-gather | bytes 1228800 | tf_op jit(solution)/shard_map/all_gather | solution.py:873
  128.9 3.2 collective-permute-start.10
  133.5 3.7 fusion.6
  137.3 3.1 pad_maximum_fusion
  143.8 9.8 %collective-permute-start.3 = (bf16[4,4,32,256]{3,2,1,0:T(8,128)(2,1)S(1)}, bf16[4,4,32,256]{3,2,1,0:T(8,128)(2,1)S(1)}, u32[]{:S(2)}, u32[]{:S(2)}) collective-permute-start(bf16[4,4,32,256]{3,2,1,0:T(8,128)(2,1)S(1)} %bitcast_dynamic-update-slice_fusion.9), channel_id=1, source_target_pairs={{0,4},{4,0},{8,12},{12,8},{16,20},{20,16},{24,28},{28,24},{1,5},{5... | collective-permute-start | bytes 786440 | tf_op jit(solution)/shard_map/ppermute | solution.py:847
  153.9 10.7 %collective-permute-done.11 = bf16[512,256]{1,0:T(8,128)(2,1)S(1)} collective-permute-done((bf16[512,256]{1,0:T(8,128)(2,1)}, bf16[512,256]{1,0:T(8,128)(2,1)S(1)}, u32[]{:S(2)}, u32[]{:S(2)}) %collective-permute-start.11) | collective-permute-done | bytes 262176 | tf_op jit(solution)/shard_map/ppermute | solution.py:844
  166.5 2.7 collective-permute-start.5
  169.2 17.0 %collective-permute-done.6 = bf16[4,4,32,256]{3,2,1,0:T(8,128)(2,1)S(1)} collective-permute-done((bf16[4,4,32,256]{3,2,1,0:T(8,128)(2,1)S(1)}, bf16[4,4,32,256]{3,2,1,0:T(8,128)(2,1)S(1)}, u32[]{:S(2)}, u32[]{:S(2)}) %collective-permute-start.6) | collective-permute-done | bytes 262176 | tf_op jit(solution)/shard_map/ppermute | solution.py:847
  187.5 3.3 collective-permute-start.7
  193.2 2.5 collective-permute-start.29
  198.1 1.5 copy.61
  199.6 1.5 copy.65
  203.4 6.3 collective-permute-done.37.refs_18_
  209.9 2.3 collective-permute-start.22
  212.2 9.6 %qkv.1 = (bf16[2048,1024]{1,0:T(8,128)(2,1)}, bf16[2048,256]{1,0:T(8,128)(2,1)}, bf16[2048,256]{1,0:T(8,128)(2,1)}, bf16[2048,256]{1,0:T(8,128)(2,1)}) custom-call(bf16[2048,1024]{1,0:T(8,128)(2,1)} %bitcast.221, bf16[1024,768]{1,0:T(8,128)(2,1)} %bitcast.196, f32[1,1024]{1,0:T(1,128)} %reshape.244.gain_ref, bf16[2048,256]{1,0:T(8,128)(2,1)} %copy-done.15, ...), custom_call_target="tpu_custom_call" | custom-call | flops 3221225472 | bytes 10485760 | tf_op jit(solution)/shard_map/qkv/pallas_call | solution.py:416
  223.0 3.5 collective-permute-done.44.refs_2_
  229.7 17.1 %attend.2 = (bf16[2048,128]{1,0:T(8,128)(2,1)}, f32[2048,128]{1,0:T(8,128)}, f32[2048,128]{1,0:T(8,128)}) custom-call(bf16[2048,256]{1,0:T(8,128)(2,1)} %get-tuple-element.35.q_ref, bf16[2048,256]{1,0:T(8,128)(2,1)} %get-tuple-element.36.k_ref, bf16[2048,256]{1,0:T(8,128)(2,1)} %get-tuple-element.37.v_ref, s32[2048,128]{1,0:T(8,128)} %broadcast_in_dim.39.sq_ref.sc_ref, ...), custom_call_target="tpu_custom_call" | custom-call | flops 8000000000 | bytes 6291456 | tf_op jit(solution)/shard_map/attend/pallas_call | solution.py:496
  246.9 1.9 constant_dynamic-slice_fusion.20
  250.3 12.7 %collective-permute-done.34.refs_14_ = bf16[128,2816]{1,0:T(8,128)(2,1)} collective-permute-done((bf16[128,2816]{1,0:T(8,128)(2,1)}, bf16[128,2816]{1,0:T(8,128)(2,1)}, u32[]{:S(2)}, u32[]{:S(2)}) %collective-permute-start.34) | collective-permute-done | bytes 720928 | tf_op jit(solution)/shard_map/ppermute | solution.py:847
  263.0 2.0 collective-permute-start.33
  265.0 13.4 %collective-permute-done.41.refs_22_ = bf16[352,1024]{1,0:T(8,128)(2,1)} collective-permute-done((bf16[352,1024]{1,0:T(8,128)(2,1)}, bf16[352,1024]{1,0:T(8,128)(2,1)}, u32[]{:S(2)}, u32[]{:S(2)}) %collective-permute-start.41) | collective-permute-done | bytes 720928 | tf_op jit(solution)/shard_map/ppermute | solution.py:847
  280.4 17.1 %attend.3 = (bf16[2048,128]{1,0:T(8,128)(2,1)}, f32[2048,128]{1,0:T(8,128)}, f32[2048,128]{1,0:T(8,128)}) custom-call(bf16[2048,256]{1,0:T(8,128)(2,1)} %get-tuple-element.35.q_ref, bf16[2048,256]{1,0:T(8,128)(2,1)} %get-tuple-element.36.k_ref, bf16[2048,256]{1,0:T(8,128)(2,1)} %get-tuple-element.37.v_ref, s32[2048,128]{1,0:T(8,128)} %broadcast_in_dim.39.sq_ref.sc_ref, ...), custom_call_target="tpu_custom_call" | custom-call | flops 8000000000 | bytes 6291456 | tf_op jit(solution)/shard_map/attend/pallas_call | solution.py:496
  299.5 4.4 collective-permute-done.27.refs_6_
  305.4 9.4 %collective-permute-done.20 = bf16[512,128]{1,0:T(8,128)(2,1)S(1)} collective-permute-done((bf16[512,128]{1,0:T(8,128)(2,1)S(1)}, bf16[512,128]{1,0:T(8,128)(2,1)S(1)}, u32[]{:S(2)}, u32[]{:S(2)}) %collective-permute-start.20) | collective-permute-done | bytes 131104 | tf_op jit(solution)/shard_map/ppermute | solution.py:844
  318.8 47.3 %mlp.1 = (bf16[512,1024]{1,0:T(8,128)(2,1)}, f32[512,1024]{1,0:T(8,128)}, bf16[512,1024]{1,0:T(8,128)(2,1)}, bf16[4,128,2816]{2,1,0:T(8,128)(2,1)}, bf16[4,128,2...) custom-call(bf16[512,1024]{1,0:T(8,128)(2,1)} %bitcast.191, ...), custom_call_target="tpu_custom_call" | custom-call | flops 26843545600 | bytes 52428800 | tf_op jit(solution)/shard_map/mlp/pallas_call | solution.py:734
  366.2 1.4 constant_dynamic-slice_fusion.14
  371.7 3.4 collective-permute-done.50
  375.1 2.4 collective-permute-start.43
  378.1 11.9 %collective-permute-done.51 = bf16[512,256]{1,0:T(8,128)(2,1)S(1)} collective-permute-done((bf16[512,256]{1,0:T(8,128)(2,1)S(1)}, bf16[512,256]{1,0:T(8,128)(2,1)S(1)}, u32[]{:S(2)}, u32[]{:S(2)}) %collective-permute-start.51) | collective-permute-done | bytes 262176 | tf_op jit(solution)/shard_map/ppermute | solution.py:844
  392.5 23.6 %attend_back.3 = bf16[2048,384]{1,0:T(8,128)(2,1)} custom-call(bf16[2048,256]{1,0:T(8,128)(2,1)} %get-tuple-element.35.q_ref, bf16[2048,256]{1,0:T(8,128)(2,1)} %get-tuple-element.36.k_ref, bf16[2048,256]{1,0:T(8,128)(2,1)} %get-tuple-element.37.v_ref, bf16[2048,256]{1,0:T(8,128)(2,1)} %copy-done.13, f32[2048,128]{1,0:T(8,128)} %get-tuple-element.45.of_ref, ...), custom_call_target="tpu_custom_call" | custom-call | flops 20000000000 | bytes 8388608 | tf_op jit(solution)/shard_map/attend_back/pallas_call | solution.py:602
  416.2 5.0 convolution_convert_fusion
  421.3 23.8 %attend_back.2 = bf16[2048,384]{1,0:T(8,128)(2,1)} custom-call(bf16[2048,256]{1,0:T(8,128)(2,1)} %get-tuple-element.35.q_ref, bf16[2048,256]{1,0:T(8,128)(2,1)} %get-tuple-element.36.k_ref, bf16[2048,256]{1,0:T(8,128)(2,1)} %get-tuple-element.37.v_ref, bf16[2048,256]{1,0:T(8,128)(2,1)} %copy-done.13, f32[2048,128]{1,0:T(8,128)} %get-tuple-element.43.of_ref, ...), custom_call_target="tpu_custom_call" | custom-call | flops 20000000000 | bytes 8388608 | tf_op jit(solution)/shard_map/attend_back/pallas_call | solution.py:602
  445.1 5.1 convolution_convert_fusion.1
  454.0 2.6 collective-permute-start.56
  457.6 2.4 collective-permute-start.53
  460.0 2.3 collective-permute-done.54.refs_11_
  465.0 23.5 %collective-permute-done.56.refs_13_ = bf16[512,384]{1,0:T(8,128)(2,1)S(1)} collective-permute-done((bf16[512,384]{1,0:T(8,128)(2,1)S(1)}, bf16[512,384]{1,0:T(8,128)(2,1)S(1)}, u32[]{:S(2)}, u32[]{:S(2)}) %collective-permute-start.56) | collective-permute-done | bytes 393248 | tf_op jit(solution)/shard_map/ppermute | solution.py:844
  491.4 30.9 %collective-permute-done.55.refs_12_ = bf16[512,384]{1,0:T(8,128)(2,1)S(1)} collective-permute-done((bf16[512,384]{1,0:T(8,128)(2,1)S(1)}, bf16[512,384]{1,0:T(8,128)(2,1)S(1)}, u32[]{:S(2)}, u32[]{:S(2)}) %collective-permute-start.55) | collective-permute-done | bytes 393248 | tf_op jit(solution)/shard_map/ppermute | solution.py:844
  523.6 12.1 %input_grad.1 = (f32[512,1024]{1,0:T(8,128)}, f32[512,1024]{1,0:T(8,128)}) custom-call(bf16[512,1024]{1,0:T(8,128)(2,1)} %bitcast.192, f32[512,1024]{1,0:T(8,128)} %get-tuple-element.41.gm_ref, f32[512,1024]{1,0:T(8,128)} %bitcast.195, f32[1,1024]{1,0:T(1,128)} %reshape.244.gain_ref, bf16[128,3072]{1,0:T(8,128)(2,1)} %copy-done, ...), custom_call_target="tpu_custom_call" | custom-call | flops 3221225472 | bytes 20971520 | tf_op jit(solution)/shard_map/input_grad/pallas_call | solution.py:809
  547.6 3.6 collective-permute-start.83
  553.5 2.1 collective-permute-start.68
  559.2 2.2 add_convert_fusion.6
  561.4 1.5 collective-permute-start.70
  568.8 6.5 collective-permute-done.72
  578.2 3.6 collective-permute-done.73
  583.1 1.9 collective-permute-start.74
  587.7 1.7 add_convert_fusion.1
  594.1 21.6 %collective-permute-done.90 = bf16[2,352,1024]{2,1,0:T(8,128)(2,1)S(1)} collective-permute-done((bf16[2,352,1024]{2,1,0:T(8,128)(2,1)S(1)}, bf16[2,352,1024]{2,1,0:T(8,128)(2,1)S(1)}, u32[]{:S(2)}, u32[]{:S(2)}) %collective-permute-start.90) | collective-permute-done | bytes 1441824 | tf_op jit(solution)/shard_map/ppermute | solution.py:847
  616.6 2.0 collective-permute-done.84
  620.8 25.8 %collective-permute-done.78 = bf16[2,128,2816]{2,1,0:T(8,128)(2,1)S(1)} collective-permute-done((bf16[2,128,2816]{2,1,0:T(8,128)(2,1)S(1)}, bf16[2,128,2816]{2,1,0:T(8,128)(2,1)S(1)}, u32[]{:S(2)}, u32[]{:S(2)}) %collective-permute-start.78) | collective-permute-done | bytes 1441824 | tf_op jit(solution)/shard_map/ppermute | solution.py:847
  649.1 3.1 collective-permute-start.92
  652.2 9.8 %collective-permute-done.85 = bf16[1,128,2816]{2,1,0:T(8,128)(2,1)S(1)} collective-permute-done((bf16[1,128,2816]{2,1,0:T(8,128)(2,1)S(1)}, bf16[1,128,2816]{2,1,0:T(8,128)(2,1)S(1)}, u32[]{:S(2)}, u32[]{:S(2)}) %collective-permute-start.85) | collective-permute-done | bytes 720928 | tf_op jit(solution)/shard_map/ppermute | solution.py:847
  662.0 1.4 convert_add_fusion.1
  663.6 3.1 collective-permute-start.86
  667.1 1.5 convert_add_fusion.2
  669.1 3.8 collective-permute-start.80
  672.9 10.1 %collective-permute-done.87 = bf16[32,2816]{1,0:T(8,128)(2,1)S(1)} collective-permute-done((bf16[32,2816]{1,0:T(8,128)(2,1)S(1)}, bf16[32,2816]{1,0:T(8,128)(2,1)S(1)}, u32[]{:S(2)}, u32[]{:S(2)}) %collective-permute-start.87) | collective-permute-done | bytes 180256 | tf_op jit(solution)/shard_map/ppermute | solution.py:844
  683.0 6.4 collective-permute-start.82
  690.5 2.3 collective-permute-start.94
  692.7 9.6 %collective-permute-done.81 = bf16[32,2816]{1,0:T(8,128)(2,1)S(1)} collective-permute-done((bf16[32,2816]{1,0:T(8,128)(2,1)S(1)}, bf16[32,2816]{1,0:T(8,128)(2,1)S(1)}, u32[]{:S(2)}, u32[]{:S(2)}) %collective-permute-start.81) | collective-permute-done | bytes 180256 | tf_op jit(solution)/shard_map/ppermute | solution.py:844
  (349 shorter events, 102.2 us)
Async XLA Ops:
  7.2 205.0 %all-gather.3.cloned.1.call-start = ((), (), s32[]{:S(2)}) async-start(), calls=%async_computation | async-start | bytes 5242880 | tf_op jit(solution)/shard_map/all_gather | solution.py:873
  8.7 119.4 %collective-permute-start.13 = (s32[2,512]{1,0:T(2,128)}, s32[2,512]{1,0:T(2,128)}, u32[]{:S(2)}, u32[]{:S(2)}) collective-permute-start(s32[2,512]{1,0:T(2,128)} %get-tuple-element.141), channel_id=1, source_target_pairs={{0,1},{1,2},{2,3},{3,0},{4,5},{5,6},{6,7},{7,4},{8,9},{9,10},{10,1... | collective-permute-start | bytes 12296 | tf_op jit(solution)/shard_map/ppermute | solution.py:844
  8.7 120.2 %collective-permute-start.14 = (s32[2,512]{1,0:T(2,128)}, s32[2,512]{1,0:T(2,128)}, u32[]{:S(2)}, u32[]{:S(2)}) collective-permute-start(s32[2,512]{1,0:T(2,128)} %get-tuple-element.141), channel_id=1, source_target_pairs={{0,2},{1,3},{2,0},{3,1},{4,6},{5,7},{6,4},{7,5},{8,10},{9,11},{10,... | collective-permute-start | bytes 12296 | tf_op jit(solution)/shard_map/ppermute | solution.py:844
  10.1 122.8 %collective-permute-start.15 = (s32[2,512]{1,0:T(2,128)}, s32[2,512]{1,0:T(2,128)}, u32[]{:S(2)}, u32[]{:S(2)}) collective-permute-start(s32[2,512]{1,0:T(2,128)} %get-tuple-element.141), channel_id=1, source_target_pairs={{0,3},{1,0},{2,1},{3,2},{4,7},{5,4},{6,5},{7,6},{8,11},{9,8},{10,9... | collective-permute-start | bytes 12296 | tf_op jit(solution)/shard_map/ppermute | solution.py:844
  12.7 127.6 %collective-permute-start = (bf16[4,32,256]{2,1,0:T(8,128)(2,1)}, bf16[4,32,256]{2,1,0:T(8,128)(2,1)}, u32[]{:S(2)}, u32[]{:S(2)}) collective-permute-start(bf16[4,32,256]{2,1,0:T(8,128)(2,1)} %get-tuple-element.127), channel_id=1, source_target_pairs={{0,1},{1,2},{2,3},{3,0},{4,5},{5,6},{6,7},{7,4},{8,9},{9,10},{10,1... | collective-permute-start | bytes 196616 | tf_op jit(solution)/shard_map/ppermute | solution.py:844
  15.8 125.8 %collective-permute-start.1 = (bf16[4,32,256]{2,1,0:T(8,128)(2,1)}, bf16[4,32,256]{2,1,0:T(8,128)(2,1)}, u32[]{:S(2)}, u32[]{:S(2)}) collective-permute-start(bf16[4,32,256]{2,1,0:T(8,128)(2,1)} %get-tuple-element.126), channel_id=1, source_target_pairs={{0,2},{1,3},{2,0},{3,1},{4,6},{5,7},{6,4},{7,5},{8,10},{9,11},{10,... | collective-permute-start | bytes 196616 | tf_op jit(solution)/shard_map/ppermute | solution.py:844
  128.9 24.7 %collective-permute-start.10 = (bf16[512,256]{1,0:T(8,128)(2,1)}, bf16[512,256]{1,0:T(8,128)(2,1)S(1)}, u32[]{:S(2)}, u32[]{:S(2)}) collective-permute-start(bf16[512,256]{1,0:T(8,128)(2,1)} %get-tuple-element.100), channel_id=1, source_target_pairs={{0,1},{1,2},{2,3},{3,0},{4,5},{5,6},{6,7},{7,4},{8,9},{9,10},{10,1... | collective-permute-start | bytes 786440 | tf_op jit(solution)/shard_map/ppermute | solution.py:844
  132.8 31.7 %collective-permute-start.11 = (bf16[512,256]{1,0:T(8,128)(2,1)}, bf16[512,256]{1,0:T(8,128)(2,1)S(1)}, u32[]{:S(2)}, u32[]{:S(2)}) collective-permute-start(bf16[512,256]{1,0:T(8,128)(2,1)} %get-tuple-element.101), channel_id=1, source_target_pairs={{0,2},{1,3},{2,0},{3,1},{4,6},{5,7},{6,4},{7,5},{8,10},{9,11},{10,... | collective-permute-start | bytes 786440 | tf_op jit(solution)/shard_map/ppermute | solution.py:844
  140.3 24.5 %collective-permute-start.12 = (bf16[512,256]{1,0:T(8,128)(2,1)S(1)}, bf16[512,256]{1,0:T(8,128)(2,1)S(1)}, u32[]{:S(2)}, u32[]{:S(2)}) collective-permute-start(bf16[512,256]{1,0:T(8,128)(2,1)S(1)} %get-tuple-element.99), channel_id=1, source_target_pairs={{0,3},{1,0},{2,1},{3,2},{4,7},{5,4},{6,5},{7,6},{8,11},{9,8},{10,9... | collective-permute-start | bytes 786440 | tf_op jit(solution)/shard_map/ppermute | solution.py:844
  141.7 54.0 %collective-permute-start.32 = (bf16[128,2816]{1,0:T(8,128)(2,1)}, bf16[128,2816]{1,0:T(8,128)(2,1)}, u32[]{:S(2)}, u32[]{:S(2)}) collective-permute-start(bf16[128,2816]{1,0:T(8,128)(2,1)} %all_gather.17.refs_8_), channel_id=1, source_target_pairs={{0,16},{4,20},{8,24},{12,28},{16,0},{20,4},{24,8},{28,12},{1,17},{... | collective-permute-start | bytes 2162696 | tf_op jit(solution)/shard_map/ppermute | solution.py:847
  143.8 22.4 %collective-permute-start.3 = (bf16[4,4,32,256]{3,2,1,0:T(8,128)(2,1)S(1)}, bf16[4,4,32,256]{3,2,1,0:T(8,128)(2,1)S(1)}, u32[]{:S(2)}, u32[]{:S(2)}) collective-permute-start(bf16[4,4,32,256]{3,2,1,0:T(8,128)(2,1)S(1)} %bitcast_dynamic-update-slice_fusion.9), channel_id=1, source_target_pairs={{0,4},{4,0},{8,12},{12,8},{16,20},{20,16},{24,28},{28,24},{1,5},{5... | collective-permute-start | bytes 786440 | tf_op jit(solution)/shard_map/ppermute | solution.py:847
  164.6 37.6 %collective-permute-start.30 = (bf16[128,2816]{1,0:T(8,128)(2,1)}, bf16[128,2816]{1,0:T(8,128)(2,1)}, u32[]{:S(2)}, u32[]{:S(2)}) collective-permute-start(bf16[128,2816]{1,0:T(8,128)(2,1)} %all_gather.17.refs_8_), channel_id=1, source_target_pairs={{0,8},{4,12},{8,0},{12,4},{16,24},{20,28},{24,16},{28,20},{1,9},{5... | collective-permute-start | bytes 2162696 | tf_op jit(solution)/shard_map/ppermute | solution.py:847
  164.9 30.9 %collective-permute-start.39 = (bf16[352,1024]{1,0:T(8,128)(2,1)}, bf16[352,1024]{1,0:T(8,128)(2,1)}, u32[]{:S(2)}, u32[]{:S(2)}) collective-permute-start(bf16[352,1024]{1,0:T(8,128)(2,1)} %all_gather.18.refs_16_), channel_id=1, source_target_pairs={{0,16},{4,20},{8,24},{12,28},{16,0},{20,4},{24,8},{28,12},{1,17},{... | collective-permute-start | bytes 2162696 | tf_op jit(solution)/shard_map/ppermute | solution.py:847
  166.2 20.0 %collective-permute-start.6 = (bf16[4,4,32,256]{3,2,1,0:T(8,128)(2,1)S(1)}, bf16[4,4,32,256]{3,2,1,0:T(8,128)(2,1)S(1)}, u32[]{:S(2)}, u32[]{:S(2)}) collective-permute-start(bf16[4,4,32,256]{3,2,1,0:T(8,128)(2,1)S(1)} %bitcast_dynamic-update-slice_fusion.9), channel_id=1, source_target_pairs={{0,16},{4,20},{8,24},{12,28},{16,0},{20,4},{24,8},{28,12},{1,17},{... | collective-permute-start | bytes 786440 | tf_op jit(solution)/shard_map/ppermute | solution.py:847
  166.5 21.0 %collective-permute-start.5 = (bf16[4,4,32,256]{3,2,1,0:T(8,128)(2,1)S(1)}, bf16[4,4,32,256]{3,2,1,0:T(8,128)(2,1)S(1)}, u32[]{:S(2)}, u32[]{:S(2)}) collective-permute-start(bf16[4,4,32,256]{3,2,1,0:T(8,128)(2,1)S(1)} %collective-permute-done.4), channel_id=1, source_target_pairs={{0,4},{4,0},{8,12},{12,8},{16,20},{20,16},{24,28},{28,24},{1,5},{5... | collective-permute-start | bytes 786440 | tf_op jit(solution)/shard_map/ppermute | solution.py:847
  192.0 17.7 %collective-permute-start.37 = (bf16[352,1024]{1,0:T(8,128)(2,1)}, bf16[352,1024]{1,0:T(8,128)(2,1)}, u32[]{:S(2)}, u32[]{:S(2)}) collective-permute-start(bf16[352,1024]{1,0:T(8,128)(2,1)} %all_gather.18.refs_16_), channel_id=1, source_target_pairs={{0,8},{4,12},{8,0},{12,4},{16,24},{20,28},{24,16},{28,20},{1,9},{5... | collective-permute-start | bytes 2162696 | tf_op jit(solution)/shard_map/ppermute | solution.py:847
  193.2 16.7 %collective-permute-start.29 = (bf16[128,2816]{1,0:T(8,128)(2,1)}, bf16[128,2816]{1,0:T(8,128)(2,1)}, u32[]{:S(2)}, u32[]{:S(2)}) collective-permute-start(bf16[128,2816]{1,0:T(8,128)(2,1)} %all_gather.17.refs_8_), channel_id=1, source_target_pairs={{0,4},{4,0},{8,12},{12,8},{16,20},{20,16},{24,28},{28,24},{1,5},{5... | collective-permute-start | bytes 2162696 | tf_op jit(solution)/shard_map/ppermute | solution.py:847
  195.7 30.8 %collective-permute-start.44 = (bf16[128,3072]{1,0:T(8,128)(2,1)S(1)}, bf16[128,3072]{1,0:T(8,128)(2,1)}, u32[]{:S(2)}, u32[]{:S(2)}) collective-permute-start(bf16[128,3072]{1,0:T(8,128)(2,1)S(1)} %all_gather.19.refs_0_), channel_id=1, source_target_pairs={{0,8},{4,12},{8,0},{12,4},{16,24},{20,28},{24,16},{28,20},{1,9},{5... | collective-permute-start | bytes 2359304 | tf_op jit(solution)/shard_map/ppermute | solution.py:847
  197.7 24.0 %collective-permute-start.36 = (bf16[352,1024]{1,0:T(8,128)(2,1)}, bf16[352,1024]{1,0:T(8,128)(2,1)S(1)}, u32[]{:S(2)}, u32[]{:S(2)}) collective-permute-start(bf16[352,1024]{1,0:T(8,128)(2,1)} %all_gather.18.refs_16_), channel_id=1, source_target_pairs={{0,4},{4,0},{8,12},{12,8},{16,20},{20,16},{24,28},{28,24},{1,5},{5... | collective-permute-start | bytes 2162696 | tf_op jit(solution)/shard_map/ppermute | solution.py:847
  202.2 46.6 %collective-permute-start.23 = (bf16[128,3840]{1,0:T(8,128)(2,1)S(1)}, bf16[128,3840]{1,0:T(8,128)(2,1)}, u32[]{:S(2)}, u32[]{:S(2)}) collective-permute-start(bf16[128,3840]{1,0:T(8,128)(2,1)S(1)} %all_gather.16.refs_0_), channel_id=1, source_target_pairs={{0,8},{4,12},{8,0},{12,4},{16,24},{20,28},{24,16},{28,20},{1,9},{5... | collective-permute-start | bytes 2949128 | tf_op jit(solution)/shard_map/ppermute | solution.py:847
  209.7 39.1 %collective-permute-start.25 = (bf16[128,3840]{1,0:T(8,128)(2,1)S(1)}, bf16[128,3840]{1,0:T(8,128)(2,1)}, u32[]{:S(2)}, u32[]{:S(2)}) collective-permute-start(bf16[128,3840]{1,0:T(8,128)(2,1)S(1)} %all_gather.16.refs_0_), channel_id=1, source_target_pairs={{0,16},{4,20},{8,24},{12,28},{16,0},{20,4},{24,8},{28,12},{1,17},{... | collective-permute-start | bytes 2949128 | tf_op jit(solution)/shard_map/ppermute | solution.py:847
  209.9 39.0 %collective-permute-start.22 = (bf16[128,3840]{1,0:T(8,128)(2,1)S(1)}, bf16[128,3840]{1,0:T(8,128)(2,1)}, u32[]{:S(2)}, u32[]{:S(2)}) collective-permute-start(bf16[128,3840]{1,0:T(8,128)(2,1)S(1)} %all_gather.16.refs_0_), channel_id=1, source_target_pairs={{0,4},{4,0},{8,12},{12,8},{16,20},{20,16},{24,28},{28,24},{1,5},{5... | collective-permute-start | bytes 2949128 | tf_op jit(solution)/shard_map/ppermute | solution.py:847
  221.7 41.3 %collective-permute-start.34 = (bf16[128,2816]{1,0:T(8,128)(2,1)}, bf16[128,2816]{1,0:T(8,128)(2,1)}, u32[]{:S(2)}, u32[]{:S(2)}) collective-permute-start(bf16[128,2816]{1,0:T(8,128)(2,1)} %collective-permute-done.32.refs_12_), channel_id=1, source_target_pairs={{0,8},{4,12},{8,0},{12,4},{16,24},{20,28},{24,16},{28,20},{1,9},{5... | collective-permute-start | bytes 2162696 | tf_op jit(solution)/shard_map/ppermute | solution.py:847
  226.5 52.0 %collective-permute-start.41 = (bf16[352,1024]{1,0:T(8,128)(2,1)}, bf16[352,1024]{1,0:T(8,128)(2,1)}, u32[]{:S(2)}, u32[]{:S(2)}) collective-permute-start(bf16[352,1024]{1,0:T(8,128)(2,1)} %collective-permute-done.39.refs_20_), channel_id=1, source_target_pairs={{0,8},{4,12},{8,0},{12,4},{16,24},{20,28},{24,16},{28,20},{1,9},{5... | collective-permute-start | bytes 2162696 | tf_op jit(solution)/shard_map/ppermute | solution.py:847
  248.8 30.9 %collective-permute-start.16 = (bf16[512,128]{1,0:T(8,128)(2,1)}, bf16[512,128]{1,0:T(8,128)(2,1)S(1)}, u32[]{:S(2)}, u32[]{:S(2)}) collective-permute-start(bf16[512,128]{1,0:T(8,128)(2,1)} %get-tuple-element.115), channel_id=1, source_target_pairs={{0,1},{1,2},{2,3},{3,0},{4,5},{5,6},{6,7},{7,4},{8,9},{9,10},{10,1... | collective-permute-start | bytes 393224 | tf_op jit(solution)/shard_map/ppermute | solution.py:844
  248.8 30.9 %collective-permute-start.17 = (bf16[512,128]{1,0:T(8,128)(2,1)}, bf16[512,128]{1,0:T(8,128)(2,1)S(1)}, u32[]{:S(2)}, u32[]{:S(2)}) collective-permute-start(bf16[512,128]{1,0:T(8,128)(2,1)} %get-tuple-element.114), channel_id=1, source_target_pairs={{0,2},{1,3},{2,0},{3,1},{4,6},{5,7},{6,4},{7,5},{8,10},{9,11},{10,... | collective-permute-start | bytes 393224 | tf_op jit(solution)/shard_map/ppermute | solution.py:844
  248.9 31.3 %collective-permute-start.18 = (bf16[512,128]{1,0:T(8,128)(2,1)}, bf16[512,128]{1,0:T(8,128)(2,1)S(1)}, u32[]{:S(2)}, u32[]{:S(2)}) collective-permute-start(bf16[512,128]{1,0:T(8,128)(2,1)} %get-tuple-element.113), channel_id=1, source_target_pairs={{0,3},{1,0},{2,1},{3,2},{4,7},{5,4},{6,5},{7,6},{8,11},{9,8},{10,9... | collective-permute-start | bytes 393224 | tf_op jit(solution)/shard_map/ppermute | solution.py:844
  263.0 35.8 %collective-permute-start.33 = (bf16[128,2816]{1,0:T(8,128)(2,1)}, bf16[128,2816]{1,0:T(8,128)(2,1)}, u32[]{:S(2)}, u32[]{:S(2)}) collective-permute-start(bf16[128,2816]{1,0:T(8,128)(2,1)} %collective-permute-done.32.refs_12_), channel_id=1, source_target_pairs={{0,4},{4,0},{8,12},{12,8},{16,20},{20,16},{24,28},{28,24},{1,5},{5... | collective-permute-start | bytes 2162696 | tf_op jit(solution)/shard_map/ppermute | solution.py:847
  278.5 20.8 %collective-permute-start.40 = (bf16[352,1024]{1,0:T(8,128)(2,1)}, bf16[352,1024]{1,0:T(8,128)(2,1)}, u32[]{:S(2)}, u32[]{:S(2)}) collective-permute-start(bf16[352,1024]{1,0:T(8,128)(2,1)} %collective-permute-done.39.refs_20_), channel_id=1, source_target_pairs={{0,4},{4,0},{8,12},{12,8},{16,20},{20,16},{24,28},{28,24},{1,5},{5... | collective-permute-start | bytes 2162696 | tf_op jit(solution)/shard_map/ppermute | solution.py:847
  279.7 19.8 %collective-permute-start.31 = (bf16[128,2816]{1,0:T(8,128)(2,1)}, bf16[128,2816]{1,0:T(8,128)(2,1)}, u32[]{:S(2)}, u32[]{:S(2)}) collective-permute-start(bf16[128,2816]{1,0:T(8,128)(2,1)} %collective-permute-done.30.refs_10_), channel_id=1, source_target_pairs={{0,4},{4,0},{8,12},{12,8},{16,20},{20,16},{24,28},{28,24},{1,5},{5... | collective-permute-start | bytes 2162696 | tf_op jit(solution)/shard_map/ppermute | solution.py:847
  279.7 25.0 %collective-permute-start.38 = (bf16[352,1024]{1,0:T(8,128)(2,1)}, bf16[352,1024]{1,0:T(8,128)(2,1)}, u32[]{:S(2)}, u32[]{:S(2)}) collective-permute-start(bf16[352,1024]{1,0:T(8,128)(2,1)} %collective-permute-done.37.refs_18_), channel_id=1, source_target_pairs={{0,4},{4,0},{8,12},{12,8},{16,20},{20,16},{24,28},{28,24},{1,5},{5... | collective-permute-start | bytes 2162696 | tf_op jit(solution)/shard_map/ppermute | solution.py:847
  280.2 23.6 %collective-permute-start.27 = (bf16[128,3840]{1,0:T(8,128)(2,1)}, bf16[128,3840]{1,0:T(8,128)(2,1)}, u32[]{:S(2)}, u32[]{:S(2)}) collective-permute-start(bf16[128,3840]{1,0:T(8,128)(2,1)} %collective-permute-done.23.refs_2_), channel_id=1, source_target_pairs={{0,16},{4,20},{8,24},{12,28},{16,0},{20,4},{24,8},{28,12},{1,17},{... | collective-permute-start | bytes 2949128 | tf_op jit(solution)/shard_map/ppermute | solution.py:847
  298.9 17.5 %collective-permute-start.24 = (bf16[128,3840]{1,0:T(8,128)(2,1)}, bf16[128,3840]{1,0:T(8,128)(2,1)}, u32[]{:S(2)}, u32[]{:S(2)}) collective-permute-start(bf16[128,3840]{1,0:T(8,128)(2,1)} %collective-permute-done.23.refs_2_), channel_id=1, source_target_pairs={{0,4},{4,0},{8,12},{12,8},{16,20},{20,16},{24,28},{28,24},{1,5},{5... | collective-permute-start | bytes 2949128 | tf_op jit(solution)/shard_map/ppermute | solution.py:847
  299.3 17.4 %collective-permute-start.26 = (bf16[128,3840]{1,0:T(8,128)(2,1)}, bf16[128,3840]{1,0:T(8,128)(2,1)}, u32[]{:S(2)}, u32[]{:S(2)}) collective-permute-start(bf16[128,3840]{1,0:T(8,128)(2,1)} %collective-permute-done.25.refs_4_), channel_id=1, source_target_pairs={{0,4},{4,0},{8,12},{12,8},{16,20},{20,16},{24,28},{28,24},{1,5},{5... | collective-permute-start | bytes 2949128 | tf_op jit(solution)/shard_map/ppermute | solution.py:847
  316.4 61.1 %collective-permute-start.46 = (bf16[128,3072]{1,0:T(8,128)(2,1)S(1)}, bf16[128,3072]{1,0:T(8,128)(2,1)}, u32[]{:S(2)}, u32[]{:S(2)}) collective-permute-start(bf16[128,3072]{1,0:T(8,128)(2,1)S(1)} %all_gather.19.refs_0_), channel_id=1, source_target_pairs={{0,16},{4,20},{8,24},{12,28},{16,0},{20,4},{24,8},{28,12},{1,17},{... | collective-permute-start | bytes 2359304 | tf_op jit(solution)/shard_map/ppermute | solution.py:847
  316.7 60.9 %collective-permute-start.48 = (bf16[128,3072]{1,0:T(8,128)(2,1)}, bf16[128,3072]{1,0:T(8,128)(2,1)}, u32[]{:S(2)}, u32[]{:S(2)}) collective-permute-start(bf16[128,3072]{1,0:T(8,128)(2,1)} %collective-permute-done.44.refs_2_), channel_id=1, source_target_pairs={{0,16},{4,20},{8,24},{12,28},{16,0},{20,4},{24,8},{28,12},{1,17},{... | collective-permute-start | bytes 2359304 | tf_op jit(solution)/shard_map/ppermute | solution.py:847
  367.7 22.3 %collective-permute-start.51 = (bf16[512,256]{1,0:T(8,128)(2,1)S(1)}, bf16[512,256]{1,0:T(8,128)(2,1)S(1)}, u32[]{:S(2)}, u32[]{:S(2)}) collective-permute-start(bf16[512,256]{1,0:T(8,128)(2,1)S(1)} %get-tuple-element.96), channel_id=1, source_target_pairs={{0,2},{1,3},{2,0},{3,1},{4,6},{5,7},{6,4},{7,5},{8,10},{9,11},{10,... | collective-permute-start | bytes 786440 | tf_op jit(solution)/shard_map/ppermute | solution.py:844
  367.8 23.7 %collective-permute-start.52 = (bf16[512,256]{1,0:T(8,128)(2,1)S(1)}, bf16[512,256]{1,0:T(8,128)(2,1)S(1)}, u32[]{:S(2)}, u32[]{:S(2)}) collective-permute-start(bf16[512,256]{1,0:T(8,128)(2,1)S(1)} %get-tuple-element.95), channel_id=1, source_target_pairs={{0,3},{1,0},{2,1},{3,2},{4,7},{5,4},{6,5},{7,6},{8,11},{9,8},{10,9... | collective-permute-start | bytes 786440 | tf_op jit(solution)/shard_map/ppermute | solution.py:844
  375.1 76.2 %collective-permute-start.43 = (bf16[128,3072]{1,0:T(8,128)(2,1)S(1)}, bf16[128,3072]{1,0:T(8,128)(2,1)S(1)}, u32[]{:S(2)}, u32[]{:S(2)}) collective-permute-start(bf16[128,3072]{1,0:T(8,128)(2,1)S(1)} %all_gather.19.refs_0_), channel_id=1, source_target_pairs={{0,4},{4,0},{8,12},{12,8},{16,20},{20,16},{24,28},{28,24},{1,5},{5... | collective-permute-start | bytes 2359304 | tf_op jit(solution)/shard_map/ppermute | solution.py:847
  377.6 76.5 %collective-permute-start.45 = (bf16[128,3072]{1,0:T(8,128)(2,1)}, bf16[128,3072]{1,0:T(8,128)(2,1)S(1)}, u32[]{:S(2)}, u32[]{:S(2)}) collective-permute-start(bf16[128,3072]{1,0:T(8,128)(2,1)} %collective-permute-done.44.refs_2_), channel_id=1, source_target_pairs={{0,4},{4,0},{8,12},{12,8},{16,20},{20,16},{24,28},{28,24},{1,5},{5... | collective-permute-start | bytes 2359304 | tf_op jit(solution)/shard_map/ppermute | solution.py:847
  377.6 79.0 %collective-permute-start.47 = (bf16[128,3072]{1,0:T(8,128)(2,1)}, bf16[128,3072]{1,0:T(8,128)(2,1)}, u32[]{:S(2)}, u32[]{:S(2)}) collective-permute-start(bf16[128,3072]{1,0:T(8,128)(2,1)} %collective-permute-done.46.refs_4_), channel_id=1, source_target_pairs={{0,4},{4,0},{8,12},{12,8},{16,20},{20,16},{24,28},{28,24},{1,5},{5... | collective-permute-start | bytes 2359304 | tf_op jit(solution)/shard_map/ppermute | solution.py:847
  390.0 67.5 %collective-permute-start.49 = (bf16[128,3072]{1,0:T(8,128)(2,1)}, bf16[128,3072]{1,0:T(8,128)(2,1)}, u32[]{:S(2)}, u32[]{:S(2)}) collective-permute-start(bf16[128,3072]{1,0:T(8,128)(2,1)} %collective-permute-done.48.refs_6_), channel_id=1, source_target_pairs={{0,4},{4,0},{8,12},{12,8},{16,20},{20,16},{24,28},{28,24},{1,5},{5... | collective-permute-start | bytes 2359304 | tf_op jit(solution)/shard_map/ppermute | solution.py:847
  421.3 30.5 %collective-permute-start.65 = (bf16[4,128,384]{2,1,0:T(8,128)(2,1)S(1)}, bf16[4,128,384]{2,1,0:T(8,128)(2,1)}, u32[]{:S(2)}, u32[]{:S(2)}) collective-permute-start(bf16[4,128,384]{2,1,0:T(8,128)(2,1)S(1)} %slice_bitcast_fusion), channel_id=1, source_target_pairs={{0,4},{4,0},{8,12},{12,8},{16,20},{20,16},{24,28},{28,24},{1,5},{5... | collective-permute-start | bytes 1179656 | tf_op jit(solution)/shard_map/ppermute | solution.py:847
  454.0 34.5 %collective-permute-start.56 = (bf16[512,384]{1,0:T(8,128)(2,1)S(1)}, bf16[512,384]{1,0:T(8,128)(2,1)S(1)}, u32[]{:S(2)}, u32[]{:S(2)}) collective-permute-start(bf16[512,384]{1,0:T(8,128)(2,1)S(1)} %get-tuple-element.79), channel_id=1, source_target_pairs={{0,2},{1,3},{2,0},{3,1},{4,6},{5,7},{6,4},{7,5},{8,10},{9,11},{10,... | collective-permute-start | bytes 1179656 | tf_op jit(solution)/shard_map/ppermute | solution.py:844
  456.7 34.0 %collective-permute-start.58 = (bf16[512,384]{1,0:T(8,128)(2,1)S(1)}, bf16[512,384]{1,0:T(8,128)(2,1)S(1)}, u32[]{:S(2)}, u32[]{:S(2)}) collective-permute-start(bf16[512,384]{1,0:T(8,128)(2,1)S(1)} %get-tuple-element.78), channel_id=1, source_target_pairs={{0,3},{1,0},{2,1},{3,2},{4,7},{5,4},{6,5},{7,6},{8,11},{9,8},{10,9... | collective-permute-start | bytes 1179656 | tf_op jit(solution)/shard_map/ppermute | solution.py:844
  457.6 33.2 %collective-permute-start.53 = (bf16[512,384]{1,0:T(8,128)(2,1)S(1)}, bf16[512,384]{1,0:T(8,128)(2,1)S(1)}, u32[]{:S(2)}, u32[]{:S(2)}) collective-permute-start(bf16[512,384]{1,0:T(8,128)(2,1)S(1)} %get-tuple-element.84), channel_id=1, source_target_pairs={{0,1},{1,2},{2,3},{3,0},{4,5},{5,6},{6,7},{7,4},{8,9},{9,10},{10,1... | collective-permute-start | bytes 1179656 | tf_op jit(solution)/shard_map/ppermute | solution.py:844
  460.0 62.3 %collective-permute-start.55 = (bf16[512,384]{1,0:T(8,128)(2,1)S(1)}, bf16[512,384]{1,0:T(8,128)(2,1)S(1)}, u32[]{:S(2)}, u32[]{:S(2)}) collective-permute-start(bf16[512,384]{1,0:T(8,128)(2,1)S(1)} %get-tuple-element.83), channel_id=1, source_target_pairs={{0,2},{1,3},{2,0},{3,1},{4,6},{5,7},{6,4},{7,5},{8,10},{9,11},{10,... | collective-permute-start | bytes 1179656 | tf_op jit(solution)/shard_map/ppermute | solution.py:844
  462.3 60.5 %collective-permute-start.57 = (bf16[512,384]{1,0:T(8,128)(2,1)S(1)}, bf16[512,384]{1,0:T(8,128)(2,1)S(1)}, u32[]{:S(2)}, u32[]{:S(2)}) collective-permute-start(bf16[512,384]{1,0:T(8,128)(2,1)S(1)} %get-tuple-element.82), channel_id=1, source_target_pairs={{0,3},{1,0},{2,1},{3,2},{4,7},{5,4},{6,5},{7,6},{8,11},{9,8},{10,9... | collective-permute-start | bytes 1179656 | tf_op jit(solution)/shard_map/ppermute | solution.py:844
  489.3 96.0 %collective-permute-start.89 = (bf16[4,352,1024]{2,1,0:T(8,128)(2,1)}, bf16[4,352,1024]{2,1,0:T(8,128)(2,1)S(1)}, u32[]{:S(2)}, u32[]{:S(2)}) collective-permute-start(bf16[4,352,1024]{2,1,0:T(8,128)(2,1)} %get-tuple-element.57), channel_id=1, source_target_pairs={{0,4},{4,0},{8,12},{12,8},{16,20},{20,16},{24,28},{28,24},{1,5},{5... | collective-permute-start | bytes 8650760 | tf_op jit(solution)/shard_map/ppermute | solution.py:847
  490.7 67.9 %collective-permute-start.71 = (bf16[4,128,1024]{2,1,0:T(8,128)(2,1)}, bf16[4,128,1024]{2,1,0:T(8,128)(2,1)}, u32[]{:S(2)}, u32[]{:S(2)}) collective-permute-start(bf16[4,128,1024]{2,1,0:T(8,128)(2,1)} %get-tuple-element.51), channel_id=1, source_target_pairs={{0,4},{4,0},{8,12},{12,8},{16,20},{20,16},{24,28},{28,24},{1,5},{5... | collective-permute-start | bytes 3145736 | tf_op jit(solution)/shard_map/ppermute | solution.py:847
  490.8 46.6 %collective-permute-start.66 = (bf16[2,128,384]{2,1,0:T(8,128)(2,1)}, bf16[2,128,384]{2,1,0:T(8,128)(2,1)}, u32[]{:S(2)}, u32[]{:S(2)}) collective-permute-start(bf16[2,128,384]{2,1,0:T(8,128)(2,1)} %add_convert_fusion.8), channel_id=1, source_target_pairs={{0,8},{4,12},{8,0},{12,4},{16,24},{20,28},{24,16},{28,20},{1,9},{5... | collective-permute-start | bytes 589832 | tf_op jit(solution)/shard_map/ppermute | solution.py:847
  547.6 38.9 %collective-permute-start.83 = (bf16[4,128,2816]{2,1,0:T(8,128)(2,1)}, bf16[4,128,2816]{2,1,0:T(8,128)(2,1)}, u32[]{:S(2)}, u32[]{:S(2)}) collective-permute-start(bf16[4,128,2816]{2,1,0:T(8,128)(2,1)} %get-tuple-element.55), channel_id=1, source_target_pairs={{0,4},{4,0},{8,12},{12,8},{16,20},{20,16},{24,28},{28,24},{1,5},{5... | collective-permute-start | bytes 8650760 | tf_op jit(solution)/shard_map/ppermute | solution.py:847
  552.0 37.5 %collective-permute-start.77 = (bf16[4,128,2816]{2,1,0:T(8,128)(2,1)}, bf16[4,128,2816]{2,1,0:T(8,128)(2,1)}, u32[]{:S(2)}, u32[]{:S(2)}) collective-permute-start(bf16[4,128,2816]{2,1,0:T(8,128)(2,1)} %get-tuple-element.53), channel_id=1, source_target_pairs={{0,4},{4,0},{8,12},{12,8},{16,20},{20,16},{24,28},{28,24},{1,5},{5... | collective-permute-start | bytes 8650760 | tf_op jit(solution)/shard_map/ppermute | solution.py:847
  586.5 29.2 %collective-permute-start.90 = (bf16[2,352,1024]{2,1,0:T(8,128)(2,1)S(1)}, bf16[2,352,1024]{2,1,0:T(8,128)(2,1)S(1)}, u32[]{:S(2)}, u32[]{:S(2)}) collective-permute-start(bf16[2,352,1024]{2,1,0:T(8,128)(2,1)S(1)} %add_convert_fusion), channel_id=1, source_target_pairs={{0,8},{4,12},{8,0},{12,4},{16,24},{20,28},{24,16},{28,20},{1,9},{5... | collective-permute-start | bytes 4325384 | tf_op jit(solution)/shard_map/ppermute | solution.py:847
  589.5 29.2 %collective-permute-start.84 = (bf16[2,128,2816]{2,1,0:T(8,128)(2,1)S(1)}, bf16[2,128,2816]{2,1,0:T(8,128)(2,1)S(1)}, u32[]{:S(2)}, u32[]{:S(2)}) collective-permute-start(bf16[2,128,2816]{2,1,0:T(8,128)(2,1)S(1)} %add_convert_fusion.1), channel_id=1, source_target_pairs={{0,16},{4,20},{8,24},{12,28},{16,0},{20,4},{24,8},{28,12},{1,17},{... | collective-permute-start | bytes 4325384 | tf_op jit(solution)/shard_map/ppermute | solution.py:847
  591.8 54.8 %collective-permute-start.78 = (bf16[2,128,2816]{2,1,0:T(8,128)(2,1)S(1)}, bf16[2,128,2816]{2,1,0:T(8,128)(2,1)S(1)}, u32[]{:S(2)}, u32[]{:S(2)}) collective-permute-start(bf16[2,128,2816]{2,1,0:T(8,128)(2,1)S(1)} %add_convert_fusion.2), channel_id=1, source_target_pairs={{0,8},{4,12},{8,0},{12,4},{16,24},{20,28},{24,16},{28,20},{1,9},{5... | collective-permute-start | bytes 4325384 | tf_op jit(solution)/shard_map/ppermute | solution.py:847
  616.1 32.4 %collective-permute-start.91 = (bf16[1,352,1024]{2,1,0:T(8,128)(2,1)S(1)}, bf16[1,352,1024]{2,1,0:T(8,128)(2,1)S(1)}, u32[]{:S(2)}, u32[]{:S(2)}) collective-permute-start(bf16[1,352,1024]{2,1,0:T(8,128)(2,1)S(1)} %add_convert_fusion.3), channel_id=1, source_target_pairs={{0,16},{4,20},{8,24},{12,28},{16,0},{20,4},{24,8},{28,12},{1,17},{... | collective-permute-start | bytes 2162696 | tf_op jit(solution)/shard_map/ppermute | solution.py:847
  620.0 42.0 %collective-permute-start.85 = (bf16[1,128,2816]{2,1,0:T(8,128)(2,1)S(1)}, bf16[1,128,2816]{2,1,0:T(8,128)(2,1)S(1)}, u32[]{:S(2)}, u32[]{:S(2)}) collective-permute-start(bf16[1,128,2816]{2,1,0:T(8,128)(2,1)S(1)} %add_convert_fusion.4), channel_id=1, source_target_pairs={{0,8},{4,12},{8,0},{12,4},{16,24},{20,28},{24,16},{28,20},{1,9},{5... | collective-permute-start | bytes 2162696 | tf_op jit(solution)/shard_map/ppermute | solution.py:847
  648.0 18.7 %collective-permute-start.79 = (bf16[1,128,2816]{2,1,0:T(8,128)(2,1)S(1)}, bf16[1,128,2816]{2,1,0:T(8,128)(2,1)S(1)}, u32[]{:S(2)}, u32[]{:S(2)}) collective-permute-start(bf16[1,128,2816]{2,1,0:T(8,128)(2,1)S(1)} %add_convert_fusion.5), channel_id=1, source_target_pairs={{0,16},{4,20},{8,24},{12,28},{16,0},{20,4},{24,8},{28,12},{1,17},{... | collective-permute-start | bytes 2162696 | tf_op jit(solution)/shard_map/ppermute | solution.py:847
  649.1 54.7 %collective-permute-start.92 = (bf16[88,1024]{1,0:T(8,128)(2,1)S(1)}, bf16[88,1024]{1,0:T(8,128)(2,1)S(1)}, u32[]{:S(2)}, u32[]{:S(2)}) collective-permute-start(bf16[88,1024]{1,0:T(8,128)(2,1)S(1)} %get-tuple-element.86), channel_id=1, source_target_pairs={{0,1},{1,2},{2,3},{3,0},{4,5},{5,6},{6,7},{7,4},{8,9},{9,10},{10,1... | collective-permute-start | bytes 540680 | tf_op jit(solution)/shard_map/ppermute | solution.py:844
  652.2 51.6 %collective-permute-start.93 = (bf16[88,1024]{1,0:T(8,128)(2,1)S(1)}, bf16[88,1024]{1,0:T(8,128)(2,1)S(1)}, u32[]{:S(2)}, u32[]{:S(2)}) collective-permute-start(bf16[88,1024]{1,0:T(8,128)(2,1)S(1)} %get-tuple-element.88), channel_id=1, source_target_pairs={{0,2},{1,3},{2,0},{3,1},{4,6},{5,7},{6,4},{7,5},{8,10},{9,11},{10,... | collective-permute-start | bytes 540680 | tf_op jit(solution)/shard_map/ppermute | solution.py:844
  669.1 21.3 %collective-permute-start.80 = (bf16[32,2816]{1,0:T(8,128)(2,1)S(1)}, bf16[32,2816]{1,0:T(8,128)(2,1)S(1)}, u32[]{:S(2)}, u32[]{:S(2)}) collective-permute-start(bf16[32,2816]{1,0:T(8,128)(2,1)S(1)} %get-tuple-element.92), channel_id=1, source_target_pairs={{0,1},{1,2},{2,3},{3,0},{4,5},{5,6},{6,7},{7,4},{8,9},{9,10},{10,1... | collective-permute-start | bytes 540680 | tf_op jit(solution)/shard_map/ppermute | solution.py:844
  683.0 19.3 %collective-permute-start.81 = (bf16[32,2816]{1,0:T(8,128)(2,1)S(1)}, bf16[32,2816]{1,0:T(8,128)(2,1)S(1)}, u32[]{:S(2)}, u32[]{:S(2)}) collective-permute-start(bf16[32,2816]{1,0:T(8,128)(2,1)S(1)} %get-tuple-element.94), channel_id=1, source_target_pairs={{0,2},{1,3},{2,0},{3,1},{4,6},{5,7},{6,4},{7,5},{8,10},{9,11},{10,... | collective-permute-start | bytes 540680 | tf_op jit(solution)/shard_map/ppermute | solution.py:844
  683.0 19.3 %collective-permute-start.82 = (bf16[32,2816]{1,0:T(8,128)(2,1)S(1)}, bf16[32,2816]{1,0:T(8,128)(2,1)S(1)}, u32[]{:S(2)}, u32[]{:S(2)}) collective-permute-start(bf16[32,2816]{1,0:T(8,128)(2,1)S(1)} %get-tuple-element.93), channel_id=1, source_target_pairs={{0,3},{1,0},{2,1},{3,2},{4,7},{5,4},{6,5},{7,6},{8,11},{9,8},{10,9... | collective-permute-start | bytes 540680 | tf_op jit(solution)/shard_map/ppermute | solution.py:844
  (75 other events, 1276.0 us)
Sparse Core Ops, SparseCore 0:
  16.0 133.0 all-gather.2

commit v2 on v1

--- a/solution.py
+++ b/solution.py
@@ -13,6 +13,7 @@
 TOKEN_BLOCK = 512
 FF_BLOCK = 256
 NEG = -1e30
+MESH = pl.DeviceIdType.MESH
 F32 = jnp.float32
 LOW = jnp.bfloat16
 BYTES = 60 * 2**20
@@ -429,12 +430,27 @@
     )(x, w, gain, fv, cos, sin)
 
 
-def attend_kernel(q_ref, k_ref, v_ref, sq_ref, sk_ref, o_ref, of_ref, lse_ref, s_ref, m_ref, l_ref, acc_ref):
-    i = pl.program_id(0)
-    tb = q_ref.shape[0]
-    q = q_ref[...]
-    seg_q = sq_ref[:, 0:1]
+def meet_ctx(n_ctx):
+    c = lax.axis_index("ctx")
+    barrier = pltpu.get_barrier_semaphore()
+    for k in range(1, n_ctx):
+        pl.semaphore_signal(barrier, inc=1, device_id={"ctx": lax.rem(c + k, n_ctx)}, device_id_type=MESH)
+    pl.semaphore_wait(barrier, n_ctx - 1)
+
+
+def ctx_copy(src, dst, send, recv, to):
+    return pltpu.make_async_remote_copy(
+        src_ref=src, dst_ref=dst, send_sem=send, recv_sem=recv, device_id={"ctx": to}, device_id_type=MESH
+    )
+
+
+def attend_kernel(n_ctx, q_ref, k_ref, v_ref, sq_ref, sk_ref, att_ref, of_ref, lse_ref,
+                  o_ref, s_ref, m_ref, l_ref, acc_ref, send, recv, own):
+    c = lax.axis_index("ctx")
+    tb = m_ref.shape[0]
+    width = q_ref.shape[1]
     lane = lax.broadcasted_iota(jnp.int32, (tb, LANES), 1)
+    meet_ctx(n_ctx)
 
     def fold(x, op):
         r = x[:, 0:LANES]
@@ -442,182 +458,264 @@
             r = op(r, x[:, b * LANES : (b + 1) * LANES])
         return r
 
-    for head in range(2):
-        qm = head_lanes(q, head)
-        m_ref[...] = jnp.full_like(m_ref, NEG)
-
-        def score(j, causal):
-            at = pl.ds(pl.multiple_of(j * tb, tb), tb)
-            s = dot(qm, k_ref[at, :], 1, 1)
-            ok = seg_q == sk_ref[0:1, at]
-            if causal:
-                r = lax.broadcasted_iota(jnp.int32, (tb, tb), 0)
-                c = lax.broadcasted_iota(jnp.int32, (tb, tb), 1)
-                ok = ok & (r >= c)
-            s = jnp.where(ok, s, NEG)
-            s_ref[:, at] = s
-            m_ref[...] = jnp.maximum(m_ref[...], fold(s, jnp.maximum))
-
-        def score_step(j, carry):
-            score(j, False)
+    def home(pair):
+        return att_ref.at[:, pl.ds(pl.multiple_of(c * width + pair * LANES, LANES), LANES)]
+
+    for pair in range(width // LANES):
+        cols = slice(pair * LANES, (pair + 1) * LANES)
+
+        def query_block(i, carry):
+            mine = pl.ds(pl.multiple_of(i * tb, tb), tb)
+            q = q_ref[mine, cols]
+            seg_q = sq_ref[mine, 0:1]
+            for head in range(2):
+                qm = head_lanes(q, head)
+                m_ref[...] = jnp.full_like(m_ref, NEG)
+
+                def score(j, causal):
+                    at = pl.ds(pl.multiple_of(j * tb, tb), tb)
+                    s = dot(qm, k_ref[at, cols], 1, 1)
+                    ok = seg_q == sk_ref[0:1, at]
+                    if causal:
+                        r = lax.broadcasted_iota(jnp.int32, (tb, tb), 0)
+                        t = lax.broadcasted_iota(jnp.int32, (tb, tb), 1)
+                        ok = ok & (r >= t)
+                    s = jnp.where(ok, s, NEG)
+                    s_ref[:, at] = s
+                    m_ref[...] = jnp.maximum(m_ref[...], fold(s, jnp.maximum))
+
+                def score_step(j, carry):
+                    score(j, False)
+                    return carry
+
+                lax.fori_loop(0, i, score_step, 0)
+                score(i, True)
+                top = jnp.max(m_ref[...], axis=1, keepdims=True)
+                l_ref[...] = jnp.zeros_like(l_ref)
+                acc_ref[...] = jnp.zeros_like(acc_ref)
+
+                def value_step(j, carry):
+                    at = pl.ds(pl.multiple_of(j * tb, tb), tb)
+                    p = jnp.exp(s_ref[:, at] - top)
+                    l_ref[...] += fold(p, jnp.add)
+                    acc_ref[...] += dot(p.astype(LOW), v_ref[at, cols], 1, 0)
+                    return carry
+
+                lax.fori_loop(0, i + 1, value_step, 0)
+                total = jnp.sum(l_ref[...], axis=1, keepdims=True)
+                out = acc_ref[...] / total
+                lse = jnp.broadcast_to(top + jnp.log(total), (tb, LANES))
+                if head == 0:
+                    of_ref[mine, cols] = out
+                    lse_ref[mine, cols] = lse
+                else:
+                    of_ref[mine, cols] = jnp.where(lane < HEAD_DIM, of_ref[mine, cols], out)
+                    lse_ref[mine, cols] = jnp.where(lane < HEAD_DIM, lse_ref[mine, cols], lse)
+            o_ref[mine, cols] = of_ref[mine, cols].astype(LOW)
+
+            @pl.when(i == c)
+            def _():
+                pltpu.make_async_copy(o_ref.at[mine, cols], home(pair), own.at[pair]).start()
+
+            @pl.when(i != c)
+            def _():
+                k = lax.rem(i + n_ctx - c, n_ctx) - 1
+                ctx_copy(o_ref.at[mine, cols], home(pair), send.at[k, pair], recv.at[k, pair], i).start()
+
             return carry
 
-        lax.fori_loop(0, i, score_step, 0)
-        score(i, True)
-        top = jnp.max(m_ref[...], axis=1, keepdims=True)
-        l_ref[...] = jnp.zeros_like(l_ref)
-        acc_ref[...] = jnp.zeros_like(acc_ref)
-
-        def value_step(j, carry):
-            at = pl.ds(pl.multiple_of(j * tb, tb), tb)
-            p = jnp.exp(s_ref[:, at] - top)
-            l_ref[...] += fold(p, jnp.add)
-            acc_ref[...] += dot(p.astype(LOW), v_ref[at, :], 1, 0)
-            return carry
-
-        lax.fori_loop(0, i + 1, value_step, 0)
-        total = jnp.sum(l_ref[...], axis=1, keepdims=True)
-        out = acc_ref[...] / total
-        lse = jnp.broadcast_to(top + jnp.log(total), (tb, LANES))
-        if head == 0:
-            of_ref[...] = out
-            lse_ref[...] = lse
-        else:
-            of_ref[...] = jnp.where(lane < HEAD_DIM, of_ref[...], out)
-            lse_ref[...] = jnp.where(lane < HEAD_DIM, lse_ref[...], lse)
-    o_ref[...] = of_ref[...].astype(LOW)
-
-
-def attend_call(pair, q, k, v, seg_col, seg_row):
-    length = q.shape[0]
+        lax.fori_loop(0, n_ctx, query_block, 0)
+    for pair in range(width // LANES):
+        cols = slice(pair * LANES, (pair + 1) * LANES)
+        pltpu.make_async_copy(o_ref.at[0:tb, cols], home(pair), own.at[pair]).wait()
+        for k in range(n_ctx - 1):
+            ctx_copy(o_ref.at[0:tb, cols], home(pair), send.at[k, pair], recv.at[k, pair], c).wait()
+
+
+def attend_call(n_ctx, q, k, v, seg_col, seg_row):
+    length, width = q.shape
     tb = TOKEN_BLOCK
-    rows = pl.BlockSpec((tb, LANES), lambda i: (i, 0))
-    full = pl.BlockSpec((length, LANES), lambda i: (0, pair))
+    pairs = width // LANES
+    vmem = pl.BlockSpec(memory_space=pltpu.VMEM)
     return pl.pallas_call(
-        attend_kernel,
-        grid=(length // tb,),
-        in_specs=[
-            pl.BlockSpec((tb, LANES), lambda i: (i, pair)),
-            full,
-            full,
-            rows,
-            pl.BlockSpec((8, length), lambda i: (0, 0)),
-        ],
-        out_specs=[rows, rows, rows],
+        functools.partial(attend_kernel, n_ctx),
+        in_specs=[vmem] * 5,
+        out_specs=[pl.BlockSpec(memory_space=pl.ANY), vmem, vmem],
         out_shape=[
-            jax.ShapeDtypeStruct((length, LANES), LOW),
-            jax.ShapeDtypeStruct((length, LANES), F32),
-            jax.ShapeDtypeStruct((length, LANES), F32),
+            jax.ShapeDtypeStruct((tb, n_ctx * width), LOW),
+            jax.ShapeDtypeStruct((length, width), F32),
+            jax.ShapeDtypeStruct((length, width), F32),
         ],
         scratch_shapes=[
+            pltpu.VMEM((length, width), LOW),
             pltpu.VMEM((tb, length), F32),
             pltpu.VMEM((tb, LANES), F32),
             pltpu.VMEM((tb, LANES), F32),
             pltpu.VMEM((tb, LANES), F32),
+            pltpu.SemaphoreType.DMA((n_ctx - 1, pairs)),
+            pltpu.SemaphoreType.DMA((n_ctx - 1, pairs)),
+            pltpu.SemaphoreType.DMA((pairs,)),
         ],
-        compiler_params=params(),
+        compiler_params=params(collective_id=1, has_side_effects=True),
         cost_estimate=pl.CostEstimate(
-            flops=8 * 10**9, bytes_accessed=6 * 2**20, transcendentals=length * length
+            flops=16 * 10**9, bytes_accessed=12 * 2**20, transcendentals=2 * length * length
         ),
         name="attend",
     )(q, k, v, seg_col, seg_row)
 
 
 def attend_back_kernel(
-    q_ref, k_ref, v_ref, g_ref, of_ref, lse_ref, sc_ref, sr_ref, cos_ref, sin_ref, out_ref,
-    lse_row, delta_row, dq_acc, dk_acc, dv_acc,
+    n_ctx, ga_ref, q_ref, k_ref, v_ref, of_ref, lse_ref, sc_ref, sr_ref, cos_ref, sin_ref, out_ref, home_ref,
+    g_ref, lse_row, delta_row, dq_acc, dk_acc, dv_acc, gsend, grecv, send, recv, own,
 ):
-    j = pl.program_id(0)
-    steps = pl.num_programs(0)
+    c = lax.axis_index("ctx")
     tb = dk_acc.shape[0]
-
-    @pl.when(j == 0)
-    def _():
-        dq_acc[...] = jnp.zeros_like(dq_acc)
-        r = lax.broadcasted_iota(jnp.int32, (8, LANES), 0)
-        lane = lax.broadcasted_iota(jnp.int32, (8, LANES), 1)
-        first = jnp.where(lane == r * HEAD_DIM, 1.0, 0.0)
-        group = jnp.where(lane // HEAD_DIM == r, 1.0, 0.0)
-        exact = lax.Precision.HIGHEST
-        for b in range(lse_ref.shape[0] // tb):
-            at = slice(b * tb, (b + 1) * tb)
-            dims = (((1,), (1,)), ((), ()))
-            lse_row[:, at] = lax.dot_general(first, lse_ref[at, :], dims, precision=exact, preferred_element_type=F32)
-            prod = g_ref[at, :].astype(F32) * of_ref[at, :]
+    length, width = q_ref.shape
+    model = n_ctx * width
+    meet_ctx(n_ctx)
+
+    def grad_copy(k, to):
+        rows = pl.ds(pl.multiple_of(c * tb, tb), tb)
+        cols = pl.ds(pl.multiple_of(to * width, width), width)
+        return ctx_copy(ga_ref.at[:, cols], g_ref.at[rows, :], gsend.at[k - 1], grecv.at[k - 1], to)
+
+    def home(pair, t):
+        return home_ref.at[:, pl.ds(pl.multiple_of(t * model + c * width + pair * LANES, LANES), LANES)]
+
+    def part(pair, t, chunk):
+        rows = pl.ds(pl.multiple_of(chunk * tb, tb), tb)
+        return out_ref.at[pair, rows, t * LANES : (t + 1) * LANES]
+
+    def part_copy(pair, t, k):
+        to = lax.rem(c + k, n_ctx)
+        return ctx_copy(part(pair, t, to), home(pair, t), send.at[k - 1, pair, t], recv.at[k - 1, pair, t], to)
+
+    first = [grad_copy(k, lax.rem(c + k, n_ctx)) for k in range(1, n_ctx)]
+    for f in first:
+        f.start()
+    keep = pltpu.make_async_copy(
+        ga_ref.at[:, pl.ds(pl.multiple_of(c * width, width), width)],
+        g_ref.at[pl.ds(pl.multiple_of(c * tb, tb), tb), :],
+        own.at[0, 0],
+    )
+    keep.start()
+    keep.wait()
+    for f in first:
+        f.wait()
+
+    r8 = lax.broadcasted_iota(jnp.int32, (8, LANES), 0)
+    l8 = lax.broadcasted_iota(jnp.int32, (8, LANES), 1)
+    pick = jnp.where(l8 == r8 * HEAD_DIM, 1.0, 0.0)
+    group = jnp.where(l8 // HEAD_DIM == r8, 1.0, 0.0)
+    exact = lax.Precision.HIGHEST
+    dims = (((1,), (1,)), ((), ()))
+    for pair in range(width // LANES):
+        cols = slice(pair * LANES, (pair + 1) * LANES)
+
+        def stats(b, carry):
+            at = pl.ds(pl.multiple_of(b * tb, tb), tb)
+            lse_row[:, at] = lax.dot_general(pick, lse_ref[at, cols], dims, precision=exact, preferred_element_type=F32)
+            prod = g_ref[at, cols].astype(F32) * of_ref[at, cols]
             delta_row[:, at] = lax.dot_general(group, prod, dims, precision=exact, preferred_element_type=F32)
-
-    dk_acc[...] = jnp.zeros_like(dk_acc)
-    dv_acc[...] = jnp.zeros_like(dv_acc)
-    mine = pl.ds(pl.multiple_of(j * tb, tb), tb)
-    k = k_ref[mine, :]
-    v = v_ref[mine, :]
-    seg_k = sc_ref[mine, 0:1]
-
-    def block(i, causal):
-        at = pl.ds(pl.multiple_of(i * tb, tb), tb)
-        q = q_ref[at, :]
-        g = g_ref[at, :]
-        ok = seg_k == sr_ref[0:1, at]
-        if causal:
-            r = lax.broadcasted_iota(jnp.int32, (tb, tb), 0)
-            c = lax.broadcasted_iota(jnp.int32, (tb, tb), 1)
-            ok = ok & (r <= c)
-        for head in range(2):
-            qm = head_lanes(q, head)
-            gm = head_lanes(g, head)
-            s = dot(k, qm, 1, 1)
-            p = jnp.where(ok, jnp.exp(s - lse_row[head : head + 1, at]), 0.0)
-            dp = dot(v, gm, 1, 1)
-            ds = (p * (dp - delta_row[head : head + 1, at])).astype(LOW)
-            dv_acc[...] += dot(p.astype(LOW), gm, 1, 0)
-            dk_acc[...] += dot(ds, qm, 1, 0)
-            dq_acc[at, :] += dot(ds, head_lanes(k, head), 0, 0)
-
-    block(j, True)
-
-    def step(i, carry):
-        block(i, False)
-        return carry
-
-    lax.fori_loop(j + 1, steps, step, 0)
-    dk = dk_acc[...]
-    dk = dk * cos_ref[mine, :] - half_swap(dk) * sin_ref[mine, :]
-    out_ref[mine, LANES : 2 * LANES] = dk.astype(LOW)
-    out_ref[mine, 2 * LANES : 3 * LANES] = dv_acc[...].astype(LOW)
-
-    @pl.when(j == steps - 1)
-    def _():
-        for b in range(dq_acc.shape[0] // tb):
-            at = slice(b * tb, (b + 1) * tb)
+            dq_acc[at, :] = jnp.zeros((tb, LANES), F32)
+            return carry
+
+        lax.fori_loop(0, n_ctx, stats, 0)
+
+        def key_block(j, carry):
+            dk_acc[...] = jnp.zeros_like(dk_acc)
+            dv_acc[...] = jnp.zeros_like(dv_acc)
+            mine = pl.ds(pl.multiple_of(j * tb, tb), tb)
+            k = k_ref[mine, cols]
+            v = v_ref[mine, cols]
+            seg_k = sc_ref[mine, 0:1]
+
+            def block(i, causal):
+                at = pl.ds(pl.multiple_of(i * tb, tb), tb)
+                q = q_ref[at, cols]
+                g = g_ref[at, cols]
+                ok = seg_k == sr_ref[0:1, at]
+                if causal:
+                    r = lax.broadcasted_iota(jnp.int32, (tb, tb), 0)
+                    t = lax.broadcasted_iota(jnp.int32, (tb, tb), 1)
+                    ok = ok & (r <= t)
+                for head in range(2):
+                    qm = head_lanes(q, head)
+                    gm = head_lanes(g, head)
+                    s = dot(k, qm, 1, 1)
+                    p = jnp.where(ok, jnp.exp(s - lse_row[head : head + 1, at]), 0.0)
+                    dp = dot(v, gm, 1, 1)
+                    ds = (p * (dp - delta_row[head : head + 1, at])).astype(LOW)
+                    dv_acc[...] += dot(p.astype(LOW), gm, 1, 0)
+                    dk_acc[...] += dot(ds, qm, 1, 0)
+                    dq_acc[at, :] += dot(ds, head_lanes(k, head), 0, 0)
+
+            block(j, True)
+
+            def step(i, carry):
+                block(i, False)
+                return carry
+
+            lax.fori_loop(j + 1, n_ctx, step, 0)
+            dk = dk_acc[...]
+            dk = dk * cos_ref[mine, :] - half_swap(dk) * sin_ref[mine, :]
+            out_ref[pair, mine, LANES : 2 * LANES] = dk.astype(LOW)
+            out_ref[pair, mine, 2 * LANES : 3 * LANES] = dv_acc[...].astype(LOW)
+            return carry
+
+        lax.fori_loop(0, n_ctx, key_block, 0)
+
+        def query_done(b, carry):
+            at = pl.ds(pl.multiple_of(b * tb, tb), tb)
             dq = dq_acc[at, :] * 0.125
             dq = dq * cos_ref[at, :] - half_swap(dq) * sin_ref[at, :]
-            out_ref[at, 0:LANES] = dq.astype(LOW)
-
-
-def attend_back_call(pair, q, k, v, g, of, lse, seg_col, seg_row, cos, sin):
-    length = q.shape[0]
+            out_ref[pair, at, 0:LANES] = dq.astype(LOW)
+            return carry
+
+        lax.fori_loop(0, n_ctx, query_done, 0)
+        for t in range(3):
+            pltpu.make_async_copy(part(pair, t, c), home(pair, t), own.at[pair, t]).start()
+            for k in range(1, n_ctx):
+                part_copy(pair, t, k).start()
+    for pair in range(width // LANES):
+        for t in range(3):
+            pltpu.make_async_copy(part(pair, t, c), home(pair, t), own.at[pair, t]).wait()
+            for k in range(1, n_ctx):
+                part_copy(pair, t, k).wait()
+
+
+def attend_back_call(n_ctx, ga, q, k, v, of, lse, seg_col, seg_row, cos, sin):
+    length, width = q.shape
     tb = TOKEN_BLOCK
-    full = pl.BlockSpec((length, LANES), lambda j: (0, pair))
-    own = pl.BlockSpec((length, LANES), lambda j: (0, 0))
+    pairs = width // LANES
+    vmem = pl.BlockSpec(memory_space=pltpu.VMEM)
     return pl.pallas_call(
-        attend_back_kernel,
-        grid=(length // tb,),
-        in_specs=[full] * 4 + [own] * 3 + [pl.BlockSpec((8, length), lambda j: (0, 0))] + [own] * 2,
-        out_specs=pl.BlockSpec((length, 3 * LANES), lambda j: (0, 0)),
-        out_shape=jax.ShapeDtypeStruct((length, 3 * LANES), LOW),
+        functools.partial(attend_back_kernel, n_ctx),
+        in_specs=[pl.BlockSpec(memory_space=pl.ANY)] + [vmem] * 9,
+        out_specs=[vmem, pl.BlockSpec(memory_space=pl.ANY)],
+        out_shape=[
+            jax.ShapeDtypeStruct((pairs, length, 3 * LANES), LOW),
+            jax.ShapeDtypeStruct((tb, 3 * n_ctx * width), LOW),
+        ],
         scratch_shapes=[
+            pltpu.VMEM((length, width), LOW),
             pltpu.VMEM((8, length), F32),
             pltpu.VMEM((8, length), F32),
             pltpu.VMEM((length, LANES), F32),
             pltpu.VMEM((tb, LANES), F32),
             pltpu.VMEM((tb, LANES), F32),
+            pltpu.SemaphoreType.DMA((n_ctx - 1,)),
+            pltpu.SemaphoreType.DMA((n_ctx - 1,)),
+            pltpu.SemaphoreType.DMA((n_ctx - 1, pairs, 3)),
+            pltpu.SemaphoreType.DMA((n_ctx - 1, pairs, 3)),
+            pltpu.SemaphoreType.DMA((pairs, 3)),
         ],
-        compiler_params=params(),
+        compiler_params=params(collective_id=2, has_side_effects=True),
         cost_estimate=pl.CostEstimate(
-            flops=20 * 10**9, bytes_accessed=8 * 2**20, transcendentals=length * length
+            flops=40 * 10**9, bytes_accessed=16 * 2**20, transcendentals=2 * length * length
         ),
         name="attend_back",
-    )(q, k, v, g, of, lse, seg_col, seg_row, cos, sin)
+    )(ga, q, k, v, of, lse, seg_col, seg_row, cos, sin)
 
 
 def mlp_kernel(blocks, tok_ref, att_ref, cot_ref, gain_ref, *refs):
@@ -765,24 +863,16 @@
     )(tok, att, cot, gain, *go, *up, *dn)
 
 
-def input_kernel(blocks, parts, tok_ref, gm_ref, v1_ref, gain_ref, *refs):
+def input_kernel(blocks, tok_ref, gm_ref, v1_ref, gain_ref, g, *refs):
     w_in, refs = refs[:blocks], refs[blocks:]
-    g_in, refs = refs[: 2 * parts], refs[2 * parts :]
-    ig_ref, vg_ref, w, g, rel, nat, sem = refs
+    ig_ref, vg_ref, w, rel, nat, sem = refs
     dp = lax.axis_index("dp")
-    c = lax.axis_index("ctx")
     model = tok_ref.shape[1]
     made = [pltpu.make_async_copy(w_in[d], w.at[pl.ds(d * LANES, LANES), :], sem.at[d]) for d in range(blocks)]
     for m in made:
         m.start()
     for d in range(blocks):
         rel[:, d * LANES : (d + 1) * LANES] = tok_ref[:, lane_block(dp ^ d)].astype(F32)
-    for k in range(parts):
-        source = lax.rem(c + parts - k, parts)
-        for pair in range(2):
-            for t in range(3):
-                block = g_in[2 * k + pair][:, t * LANES : (t + 1) * LANES]
-                g[:, pl.ds(pl.multiple_of(t * model + source * 2 * LANES + pair * LANES, LANES), LANES)] = block
     gv = g[:, 2 * model :].astype(F32)
     vg_ref[...] = v1_ref[...] + 0.5 * gv
     x = rel[...]
@@ -800,20 +890,18 @@
     ig_ref[...] = gm_ref[...] + nat[...]
 
 
-def input_call(tok, gm, v1, gain, ws, gs):
+def input_call(tok, gm, v1, gain, g, ws):
     tb, model = tok.shape
     blocks = len(ws)
-    parts = len(gs) // 2
     vmem = pl.BlockSpec(memory_space=pltpu.VMEM)
     shape = jax.ShapeDtypeStruct
     return pl.pallas_call(
-        functools.partial(input_kernel, blocks, parts),
-        in_specs=[vmem] * 4 + [pl.BlockSpec(memory_space=pl.ANY)] * blocks + [vmem] * len(gs),
+        functools.partial(input_kernel, blocks),
+        in_specs=[vmem] * 5 + [pl.BlockSpec(memory_space=pl.ANY)] * blocks,
         out_specs=[vmem, vmem],
         out_shape=[shape((tb, model), F32)] * 2,
         scratch_shapes=[
             pltpu.VMEM((model, 3 * model), LOW),
-            pltpu.VMEM((tb, 3 * model), LOW),
             pltpu.VMEM((tb, model), F32),
             pltpu.VMEM((tb, model), F32),
             pltpu.SemaphoreType.DMA((blocks,)),
@@ -823,7 +911,7 @@
             flops=2 * tb * model * 3 * model, bytes_accessed=20 * 2**20, transcendentals=0
         ),
         name="input_grad",
-    )(tok, gm, v1, gain, *ws, *gs)
+    )(tok, gm, v1, gain, g, *ws)
 
 
 def fast_local(
@@ -905,24 +993,16 @@
     sin = jnp.concatenate([-sin, sin] * 2, axis=1)
     xn, q, k, v = qkv_call(row_tokens, head_weights, gain_rel, head_first, cos, sin)
     pairs = width // LANES
-    outs = [attend_call(p, q, k, v, seg_col, seg_row) for p in range(pairs)]
-    attended = jnp.zeros((seq, model), LOW)
-    for p in range(pairs):
-        for s, slot in enumerate(swap_ctx(outs[p][0], 0)):
-            at = ((c + n_ctx - s) % n_ctx) * width + p * LANES
-            attended = lax.dynamic_update_slice_in_dim(attended, slot, at, 1)
+    attended, out_full, log_total = attend_call(n_ctx, q, k, v, seg_col, seg_row)
     cot = cotangent[0]
     (output, grad_middle, grad_attended, gate_keep, gate_send, up_keep, up_send, out_keep, out_send,
      down_keep, down_send) = mlp_call(tok, attended, cot, gain_two_rel, go, up, dn)
 
-    head_grad = place(swap_ctx(grad_attended, 1), 0)
-
     qkv_all = gather_dp(gather_ctx(jnp.concatenate([w_query, w_key, w_value], axis=1)), plane + bits[:1])
 
-    back = [
-        attend_back_call(p, q, k, v, head_grad, outs[p][1], outs[p][2], seg_col, seg_row, cos, sin)
-        for p in range(pairs)
-    ]
+    back, home_grad = attend_back_call(
+        n_ctx, grad_attended, q, k, v, out_full, log_total, seg_col, seg_row, cos, sin
+    )
 
     def scatter_dp(keep, send, order):
         terms = [keep, flip(send, bits[0])]
@@ -955,7 +1035,6 @@
     down_grad = scatter_ctx(scatter_dp(down_keep, down_send, plane))
     out_grad = scatter_ctx(scatter_dp(out_keep, out_send, plane[::-1]))
 
-    grads = [swap_ctx(b, 0) for b in back]
     qkv_grad = jnp.zeros((3, own_rows, model), F32)
     for p in range(pairs):
         product = lax.dot_general(
@@ -968,9 +1047,7 @@
             qkv_grad = lax.dynamic_update_slice_in_dim(qkv_grad, block, at, 2)
     query_grad, key_grad, value_grad = qkv_grad[0], qkv_grad[1], 0.5 * qkv_grad[2]
 
-    input_grad, v1_grad = input_call(
-        tok, grad_middle, v1_accum[0], gain_rel, qkv_all, [grads[p][s] for s in range(n_ctx) for p in range(pairs)]
-    )
+    input_grad, v1_grad = input_call(tok, grad_middle, v1_accum[0], gain_rel, home_grad, qkv_all)
 
     def row_dot(a, w):
         return jnp.sum(a * w.astype(F32), axis=1)

time: 724 us -> 736 us (1.017)
  Pallas kernels: 151 us -> 247 us
  waiting for transfers between devices: 243 us -> 199 us
  starting transfers between devices: 103 us -> 72.8 us
    pallas_call x5 -> x3, Pallas kernels: 93.7 us -> 176 us  [the longest x1 119 us: attend_back_call(): pl.pallas_call(functools.partial(attend_back_kernel, n_ctx), in_specs=[pl...]
    ppermute x42 -> x27, waiting for transfers between devices: 112 us -> 46.7 us  [shift(): return lax.ppermute(x, 'ctx', [(i, (i + k) % n_ctx) for i in range(n_ctx)])]
    ppermute x53, waiting for transfers between devices: 131 us -> 152 us  [flip(): return lax.ppermute(x, 'dp', [(i, i ^ bit) for i in range(n_dp)])]
    ppermute x53, starting transfers between devices: 57.4 us -> 36.6 us  [flip(): return lax.ppermute(x, 'dp', [(i, i ^ bit) for i in range(n_dp)])]
    pallas_call x1, Pallas kernels: 9.55 us -> 23.9 us  [qkv_call(): pl.pallas_call(functools.partial(qkv_kernel, model // LANES), grid=(lengt...]
    ppermute x42 -> x27, starting transfers between devices: 45.9 us -> 36.2 us  [shift(): return lax.ppermute(x, 'ctx', [(i, (i + k) % n_ctx) for i in range(n_ctx)])]
  transfers between devices with their start and end apart: 96 -> 81, of which waited for: 27 -> 24; matrix products, arithmetic and copies ran while one was open for 12% -> 11% of each run, Pallas kernels for 21% -> 34%
where the time goes in v2:
time: 736 us; the launch traced here: 729 us
  Pallas kernels  247 us (34%)
  waiting for transfers between devices  199 us (27%)
  blocking collectives  110 us (15%)
  starting transfers between devices  72.8 us (10%)
  local copies, waits for them, and re-layouts  40.3 us (5%)
  other arithmetic  37 us (5%)
  between operations  15.3 us (2%)
  matrix products  7.54 us (1%)
    ppermute x53, waiting for transfers between devices, flip(): return lax.ppermute(x, 'dp', [(i, i ^ bit) for i in range(n_dp)])  152 us
    pallas_call x1, Pallas kernels, attend_back_call(): pl.pallas_call(functools.partial(attend_back_kernel, n_ctx), in_specs=[pl...  119 us
    all_gather x4, blocking collectives, gather_ctx(): return lax.all_gather(x, 'ctx', axis=0, tiled=True)  110 us
    pallas_call x1, Pallas kernels, mlp_call(): pl.pallas_call(functools.partial(mlp_kernel, blocks), grid=(ff // FF_BLOC...  47.5 us
    ppermute x27, waiting for transfers between devices, shift(): return lax.ppermute(x, 'ctx', [(i, (i + k) % n_ctx) for i in range(n_ctx)])  46.7 us
    pallas_call x1, Pallas kernels, attend_call(): pl.pallas_call(functools.partial(attend_kernel, n_ctx), in_specs=[vmem] *...  44.4 us
    ppermute x53, starting transfers between devices, flip(): return lax.ppermute(x, 'dp', [(i, i ^ bit) for i in range(n_dp)])  36.6 us
    ppermute x27, starting transfers between devices, shift(): return lax.ppermute(x, 'ctx', [(i, (i + k) % n_ctx) for i in range(n_ctx)])  36.2 us
  transfers between devices with their start and end apart: 81, of which 24 were waited for; matrix products, arithmetic and copies ran while one was open for 11% of the time, Pallas kernels for 34%

profile of v2, /device:TPU:27, one launch (start us, length us, event | category | flops | bytes accessed | tf_op | source)
XLA Modules:
  0.0 728.9 jit_solution(11956390072954421017)
XLA Ops:
  7.3 1.4 pad_add_fusion
  12.7 3.1 collective-permute-start
  16.9 20.0 %all_gather.17.refs_8_ = bf16[128,2816]{1,0:T(8,128)(2,1)} all-gather(bf16[32,2816]{1,0:T(8,128)(2,1)S(1)} %copy-done.15), channel_id=1, replica_groups=mesh['dp'=8,'ctx'=4] {'ctx'}, dimensions={0}, use_global_device_ids=true | all-gather | bytes 901120 | tf_op jit(solution)/shard_map/all_gather | solution.py:961
  37.2 26.3 %all_gather.18.refs_16_ = bf16[352,1024]{1,0:T(8,128)(2,1)S(1)} all-gather(bf16[88,1024]{1,0:T(8,128)(2,1)S(1)} %copy-done.24), channel_id=1, replica_groups=mesh['dp'=8,'ctx'=4] {'ctx'}, dimensions={0}, use_global_device_ids=true | all-gather | bytes 901120 | tf_op jit(solution)/shard_map/all_gather | solution.py:961
  63.5 28.3 %all_gather.19.refs_0_ = bf16[128,3072]{1,0:T(8,128)(2,1)S(1)} all-gather(bf16[32,3072]{1,0:T(8,128)(2,1)S(1)} %pad_maximum_fusion.4), channel_id=1, replica_groups=mesh['dp'=8,'ctx'=4] {'ctx'}, dimensions={0}, use_global_device_ids=true | all-gather | bytes 983040 | tf_op jit(solution)/shard_map/all_gather | solution.py:961
  92.7 35.6 %all_gather.16.refs_0_ = bf16[128,3840]{1,0:T(8,128)(2,1)S(1)} all-gather(bf16[32,3840]{1,0:T(8,128)(2,1)S(1)} %pad_maximum_fusion.3), channel_id=1, replica_groups=mesh['dp'=8,'ctx'=4] {'ctx'}, dimensions={0}, use_global_device_ids=true | all-gather | bytes 1228800 | tf_op jit(solution)/shard_map/all_gather | solution.py:961
  129.4 3.2 collective-permute-start.10
  133.4 2.2 collective-permute-done.2
  142.8 1.5 collective-permute-done.10
  145.5 19.2 %collective-permute-done.11 = bf16[512,256]{1,0:T(8,128)(2,1)S(1)} collective-permute-done((bf16[512,256]{1,0:T(8,128)(2,1)}, bf16[512,256]{1,0:T(8,128)(2,1)S(1)}, u32[]{:S(2)}, u32[]{:S(2)}) %collective-permute-start.11) | collective-permute-done | bytes 262176 | tf_op jit(solution)/shard_map/ppermute | solution.py:932
  166.0 2.0 collective-permute-start.3
  171.1 3.7 fusion.18
  174.8 11.6 %collective-permute-done.8 = bf16[4,4,32,256]{3,2,1,0:T(8,128)(2,1)S(1)} collective-permute-done((bf16[4,4,32,256]{3,2,1,0:T(8,128)(2,1)S(1)}, bf16[4,4,32,256]{3,2,1,0:T(8,128)(2,1)S(1)}, u32[]{:S(2)}, u32[]{:S(2)}) %collective-permute-start.8) | collective-permute-done | bytes 262176 | tf_op jit(solution)/shard_map/ppermute | solution.py:935
  186.4 2.5 collective-permute-start.23
  189.3 3.1 pad_maximum_fusion
  193.7 8.9 %collective-permute-done.31.refs_18_ = bf16[352,1024]{1,0:T(8,128)(2,1)} collective-permute-done((bf16[352,1024]{1,0:T(8,128)(2,1)S(1)}, bf16[352,1024]{1,0:T(8,128)(2,1)}, u32[]{:S(2)}, u32[]{:S(2)}) %collective-permute-start.31) | collective-permute-done | bytes 720928 | tf_op jit(solution)/shard_map/ppermute | solution.py:935
  204.2 2.1 collective-permute-start.16
  206.3 13.1 %collective-permute-done.38.refs_2_ = bf16[128,3072]{1,0:T(8,128)(2,1)} collective-permute-done((bf16[128,3072]{1,0:T(8,128)(2,1)S(1)}, bf16[128,3072]{1,0:T(8,128)(2,1)}, u32[]{:S(2)}, u32[]{:S(2)}) %collective-permute-start.38) | collective-permute-done | bytes 786464 | tf_op jit(solution)/shard_map/ppermute | solution.py:935
  219.4 1.5 collective-permute-start.9
  222.0 3.0 collective-permute-start.27
  225.0 15.4 %collective-permute-done.17.refs_2_ = bf16[128,3840]{1,0:T(8,128)(2,1)} collective-permute-done((bf16[128,3840]{1,0:T(8,128)(2,1)S(1)}, bf16[128,3840]{1,0:T(8,128)(2,1)}, u32[]{:S(2)}, u32[]{:S(2)}) %collective-permute-start.17) | collective-permute-done | bytes 983072 | tf_op jit(solution)/shard_map/ppermute | solution.py:935
  242.7 13.2 %collective-permute-done.28.refs_14_ = bf16[128,2816]{1,0:T(8,128)(2,1)} collective-permute-done((bf16[128,2816]{1,0:T(8,128)(2,1)S(1)}, bf16[128,2816]{1,0:T(8,128)(2,1)}, u32[]{:S(2)}, u32[]{:S(2)}) %collective-permute-start.28) | collective-permute-done | bytes 720928 | tf_op jit(solution)/shard_map/ppermute | solution.py:935
  255.9 1.5 collective-permute-start.34
  257.4 13.9 %collective-permute-done.35.refs_22_ = bf16[352,1024]{1,0:T(8,128)(2,1)} collective-permute-done((bf16[352,1024]{1,0:T(8,128)(2,1)}, bf16[352,1024]{1,0:T(8,128)(2,1)}, u32[]{:S(2)}, u32[]{:S(2)}) %collective-permute-start.35) | collective-permute-done | bytes 720928 | tf_op jit(solution)/shard_map/ppermute | solution.py:935
  273.4 1.5 copy.61
  274.9 1.5 copy.65
  278.4 23.9 %qkv.1 = (bf16[2048,1024]{1,0:T(8,128)(2,1)}, bf16[2048,256]{1,0:T(8,128)(2,1)}, bf16[2048,256]{1,0:T(8,128)(2,1)}, bf16[2048,256]{1,0:T(8,128)(2,1)}) custom-call(bf16[2048,1024]{1,0:T(8,128)(2,1)} %bitcast.229, bf16[1024,768]{1,0:T(8,128)(2,1)} %bitcast.204, f32[1,1024]{1,0:T(1,128)} %reshape.244.gain_ref, bf16[2048,256]{1,0:T(8,128)(2,1)} %copy-done.11, ...), custom_call_target="tpu_custom_call" | custom-call | flops 3221225472 | bytes 10485760 | tf_op jit(solution)/shard_map/qkv/pallas_call | solution.py:417
  305.5 44.4 %attend.1 = (bf16[512,1024]{1,0:T(8,128)(2,1)}, f32[2048,256]{1,0:T(8,128)}, f32[2048,256]{1,0:T(8,128)}) custom-call(bf16[2048,256]{1,0:T(8,128)(2,1)} %get-tuple-element.34.q_ref, bf16[2048,256]{1,0:T(8,128)(2,1)} %get-tuple-element.35.k_ref, bf16[2048,256]{1,0:T(8,128)(2,1)} %get-tuple-element.36.v_ref, s32[2048,128]{1,0:T(8,128)} %broadcast_in_dim.39.sq_ref.sc_ref, ...), custom_call_target="tpu_custom_call" | custom-call | flops 16000000000 | bytes 12582912 | tf_op jit(solution)/shard_map/attend/pallas_call | solution.py:540
  351.9 47.5 %mlp.1 = (bf16[512,1024]{1,0:T(8,128)(2,1)}, f32[512,1024]{1,0:T(8,128)}, bf16[512,1024]{1,0:T(8,128)(2,1)}, bf16[4,128,2816]{2,1,0:T(8,128)(2,1)}, bf16[4,128,2...) custom-call(bf16[512,1024]{1,0:T(8,128)(2,1)} %bitcast.199, ...), custom_call_target="tpu_custom_call" | custom-call | flops 26843545600 | bytes 52428800 | tf_op jit(solution)/shard_map/mlp/pallas_call | solution.py:832
  399.3 118.9 %attend_back.1 = (bf16[2,2048,384]{2,1,0:T(8,128)(2,1)}, bf16[512,3072]{1,0:T(8,128)(2,1)}) custom-call(bf16[512,1024]{1,0:T(8,128)(2,1)} %get-tuple-element.40.ga_ref, bf16[2048,256]{1,0:T(8,128)(2,1)} %get-tuple-element.34.q_ref, bf16[2048,256]{1,0:T(8,128)(2,1)} %get-tuple-element.35.k_ref, bf16[2048,256]{1,0:T(8,128)(2,1)} %get-tuple-element.36.v_ref, ...), custom_call_target="tpu_custom_call" | custom-call | flops 40000000000 | bytes 16777216 | tf_op jit(solution)/shard_map/attend_back/pallas_call | solution.py:692
  518.3 5.2 fusion.9
  523.5 2.4 fusion.6
  530.7 12.4 %input_grad.1 = (f32[512,1024]{1,0:T(8,128)}, f32[512,1024]{1,0:T(8,128)}) custom-call(bf16[512,1024]{1,0:T(8,128)(2,1)} %bitcast.200, f32[512,1024]{1,0:T(8,128)} %get-tuple-element.39.gm_ref, f32[512,1024]{1,0:T(8,128)} %bitcast.203, f32[1,1024]{1,0:T(1,128)} %reshape.244.gain_ref, bf16[512,3072]{1,0:T(8,128)(2,1)} %get-tuple-element.43.g, ...), custom_call_target="tpu_custom_call" | custom-call | flops 3221225472 | bytes 20971520 | tf_op jit(solution)/shard_map/input_grad/pallas_call | solution.py:898
  546.9 3.5 collective-permute-done.45
  551.6 3.0 collective-permute-done.51
  562.4 3.1 collective-permute-start.68
  566.9 1.4 reshape.258
  568.2 1.8 collective-permute-start.53
  570.0 1.4 reshape.259
  573.9 2.2 add_convert_fusion.6
  579.2 1.4 reshape.261
  580.6 1.4 reshape.262
  581.9 1.4 reshape.263
  585.0 4.5 collective-permute-done.57
  591.9 1.8 multiply_reduce_fusion.3
  593.7 2.3 collective-permute-done.58
  597.4 3.2 collective-permute-start.59
  601.4 1.4 fusion.43
  604.7 1.7 add_convert_fusion.1
  609.8 23.1 %collective-permute-done.75 = bf16[2,352,1024]{2,1,0:T(8,128)(2,1)S(1)} collective-permute-done((bf16[2,352,1024]{2,1,0:T(8,128)(2,1)S(1)}, bf16[2,352,1024]{2,1,0:T(8,128)(2,1)S(1)}, u32[]{:S(2)}, u32[]{:S(2)}) %collective-permute-start.75) | collective-permute-done | bytes 1441824 | tf_op jit(solution)/shard_map/ppermute | solution.py:935
  632.9 1.5 add_convert_fusion.3
  635.8 1.4 add_convert_fusion.4
  637.4 26.4 %collective-permute-done.63 = bf16[2,128,2816]{2,1,0:T(8,128)(2,1)S(1)} collective-permute-done((bf16[2,128,2816]{2,1,0:T(8,128)(2,1)S(1)}, bf16[2,128,2816]{2,1,0:T(8,128)(2,1)S(1)}, u32[]{:S(2)}, u32[]{:S(2)}) %collective-permute-start.63) | collective-permute-done | bytes 1441824 | tf_op jit(solution)/shard_map/ppermute | solution.py:935
  664.2 1.6 convert_add_fusion
  665.9 2.7 collective-permute-start.77
  669.2 10.1 %collective-permute-done.70 = bf16[1,128,2816]{2,1,0:T(8,128)(2,1)S(1)} collective-permute-done((bf16[1,128,2816]{2,1,0:T(8,128)(2,1)S(1)}, bf16[1,128,2816]{2,1,0:T(8,128)(2,1)S(1)}, u32[]{:S(2)}, u32[]{:S(2)}) %collective-permute-start.70) | collective-permute-done | bytes 720928 | tf_op jit(solution)/shard_map/ppermute | solution.py:935
  679.2 1.4 convert_add_fusion.1
  680.8 2.4 collective-permute-start.71
  684.8 2.9 collective-permute-done.71
  687.6 1.8 collective-permute-start.65
  689.4 10.8 %collective-permute-done.72 = bf16[32,2816]{1,0:T(8,128)(2,1)S(1)} collective-permute-done((bf16[32,2816]{1,0:T(8,128)(2,1)S(1)}, bf16[32,2816]{1,0:T(8,128)(2,1)S(1)}, u32[]{:S(2)}, u32[]{:S(2)}) %collective-permute-start.72) | collective-permute-done | bytes 180256 | tf_op jit(solution)/shard_map/ppermute | solution.py:932
  700.2 5.8 collective-permute-start.67
  707.0 3.1 collective-permute-start.79
  710.1 9.4 %collective-permute-done.66 = bf16[32,2816]{1,0:T(8,128)(2,1)S(1)} collective-permute-done((bf16[32,2816]{1,0:T(8,128)(2,1)S(1)}, bf16[32,2816]{1,0:T(8,128)(2,1)S(1)}, u32[]{:S(2)}, u32[]{:S(2)}) %collective-permute-start.66) | collective-permute-done | bytes 180256 | tf_op jit(solution)/shard_map/ppermute | solution.py:932
  (291 shorter events, 79.8 us)
Async XLA Ops:
  7.2 271.2 %all-gather.3.cloned.1.call-start = ((), (), s32[]{:S(2)}) async-start(), calls=%async_computation | async-start | bytes 5242880 | tf_op jit(solution)/shard_map/all_gather | solution.py:961
  8.7 128.2 %collective-permute-start.13 = (s32[2,512]{1,0:T(2,128)}, s32[2,512]{1,0:T(2,128)}, u32[]{:S(2)}, u32[]{:S(2)}) collective-permute-start(s32[2,512]{1,0:T(2,128)} %get-tuple-element.119), channel_id=1, source_target_pairs={{0,1},{1,2},{2,3},{3,0},{4,5},{5,6},{6,7},{7,4},{8,9},{9,10},{10,1... | collective-permute-start | bytes 12296 | tf_op jit(solution)/shard_map/ppermute | solution.py:932
  8.7 128.7 %collective-permute-start.14 = (s32[2,512]{1,0:T(2,128)}, s32[2,512]{1,0:T(2,128)}, u32[]{:S(2)}, u32[]{:S(2)}) collective-permute-start(s32[2,512]{1,0:T(2,128)} %get-tuple-element.119), channel_id=1, source_target_pairs={{0,2},{1,3},{2,0},{3,1},{4,6},{5,7},{6,4},{7,5},{8,10},{9,11},{10,... | collective-permute-start | bytes 12296 | tf_op jit(solution)/shard_map/ppermute | solution.py:932
  10.1 127.7 %collective-permute-start.15 = (s32[2,512]{1,0:T(2,128)}, s32[2,512]{1,0:T(2,128)}, u32[]{:S(2)}, u32[]{:S(2)}) collective-permute-start(s32[2,512]{1,0:T(2,128)} %get-tuple-element.119), channel_id=1, source_target_pairs={{0,3},{1,0},{2,1},{3,2},{4,7},{5,4},{6,5},{7,6},{8,11},{9,8},{10,9... | collective-permute-start | bytes 12296 | tf_op jit(solution)/shard_map/ppermute | solution.py:932
  12.7 115.6 %collective-permute-start = (bf16[4,32,256]{2,1,0:T(8,128)(2,1)}, bf16[4,32,256]{2,1,0:T(8,128)(2,1)}, u32[]{:S(2)}, u32[]{:S(2)}) collective-permute-start(bf16[4,32,256]{2,1,0:T(8,128)(2,1)} %get-tuple-element.105), channel_id=1, source_target_pairs={{0,1},{1,2},{2,3},{3,0},{4,5},{5,6},{6,7},{7,4},{8,9},{9,10},{10,1... | collective-permute-start | bytes 196616 | tf_op jit(solution)/shard_map/ppermute | solution.py:932
  15.8 113.5 %collective-permute-start.1 = (bf16[4,32,256]{2,1,0:T(8,128)(2,1)}, bf16[4,32,256]{2,1,0:T(8,128)(2,1)}, u32[]{:S(2)}, u32[]{:S(2)}) collective-permute-start(bf16[4,32,256]{2,1,0:T(8,128)(2,1)} %get-tuple-element.104), channel_id=1, source_target_pairs={{0,2},{1,3},{2,0},{3,1},{4,6},{5,7},{6,4},{7,5},{8,10},{9,11},{10,... | collective-permute-start | bytes 196616 | tf_op jit(solution)/shard_map/ppermute | solution.py:932
  129.4 15.0 %collective-permute-start.10 = (bf16[512,256]{1,0:T(8,128)(2,1)}, bf16[512,256]{1,0:T(8,128)(2,1)S(1)}, u32[]{:S(2)}, u32[]{:S(2)}) collective-permute-start(bf16[512,256]{1,0:T(8,128)(2,1)} %get-tuple-element.86), channel_id=1, source_target_pairs={{0,1},{1,2},{2,3},{3,0},{4,5},{5,6},{6,7},{7,4},{8,9},{9,10},{10,1... | collective-permute-start | bytes 786440 | tf_op jit(solution)/shard_map/ppermute | solution.py:932
  135.6 29.1 %collective-permute-start.11 = (bf16[512,256]{1,0:T(8,128)(2,1)}, bf16[512,256]{1,0:T(8,128)(2,1)S(1)}, u32[]{:S(2)}, u32[]{:S(2)}) collective-permute-start(bf16[512,256]{1,0:T(8,128)(2,1)} %get-tuple-element.87), channel_id=1, source_target_pairs={{0,2},{1,3},{2,0},{3,1},{4,6},{5,7},{6,4},{7,5},{8,10},{9,11},{10,... | collective-permute-start | bytes 786440 | tf_op jit(solution)/shard_map/ppermute | solution.py:932
  137.0 29.0 %collective-permute-start.12 = (bf16[512,256]{1,0:T(8,128)(2,1)}, bf16[512,256]{1,0:T(8,128)(2,1)S(1)}, u32[]{:S(2)}, u32[]{:S(2)}) collective-permute-start(bf16[512,256]{1,0:T(8,128)(2,1)} %get-tuple-element.85), channel_id=1, source_target_pairs={{0,3},{1,0},{2,1},{3,2},{4,7},{5,4},{6,5},{7,6},{8,11},{9,8},{10,9... | collective-permute-start | bytes 786440 | tf_op jit(solution)/shard_map/ppermute | solution.py:932
  137.5 30.5 %collective-permute-start.4 = (bf16[4,4,32,256]{3,2,1,0:T(8,128)(2,1)S(1)}, bf16[4,4,32,256]{3,2,1,0:T(8,128)(2,1)S(1)}, u32[]{:S(2)}, u32[]{:S(2)}) collective-permute-start(bf16[4,4,32,256]{3,2,1,0:T(8,128)(2,1)S(1)} %bitcast_dynamic-update-slice_fusion.9), channel_id=1, source_target_pairs={{0,8},{4,12},{8,0},{12,4},{16,24},{20,28},{24,16},{28,20},{1,9},{5... | collective-permute-start | bytes 786440 | tf_op jit(solution)/shard_map/ppermute | solution.py:935
  137.8 30.3 %collective-permute-start.6 = (bf16[4,4,32,256]{3,2,1,0:T(8,128)(2,1)S(1)}, bf16[4,4,32,256]{3,2,1,0:T(8,128)(2,1)S(1)}, u32[]{:S(2)}, u32[]{:S(2)}) collective-permute-start(bf16[4,4,32,256]{3,2,1,0:T(8,128)(2,1)S(1)} %bitcast_dynamic-update-slice_fusion.9), channel_id=1, source_target_pairs={{0,16},{4,20},{8,24},{12,28},{16,0},{20,4},{24,8},{28,12},{1,17},{... | collective-permute-start | bytes 786440 | tf_op jit(solution)/shard_map/ppermute | solution.py:935
  144.4 44.5 %collective-permute-start.26 = (bf16[128,2816]{1,0:T(8,128)(2,1)S(1)}, bf16[128,2816]{1,0:T(8,128)(2,1)S(1)}, u32[]{:S(2)}, u32[]{:S(2)}) collective-permute-start(bf16[128,2816]{1,0:T(8,128)(2,1)S(1)} %copy-done.18), channel_id=1, source_target_pairs={{0,16},{4,20},{8,24},{12,28},{16,0},{20,4},{24,8},{28,12},{1,17},{... | collective-permute-start | bytes 2162696 | tf_op jit(solution)/shard_map/ppermute | solution.py:935
  164.7 24.3 %collective-permute-start.33 = (bf16[352,1024]{1,0:T(8,128)(2,1)S(1)}, bf16[352,1024]{1,0:T(8,128)(2,1)}, u32[]{:S(2)}, u32[]{:S(2)}) collective-permute-start(bf16[352,1024]{1,0:T(8,128)(2,1)S(1)} %all_gather.18.refs_16_), channel_id=1, source_target_pairs={{0,16},{4,20},{8,24},{12,28},{16,0},{20,4},{24,8},{28,12},{1,17},{... | collective-permute-start | bytes 2162696 | tf_op jit(solution)/shard_map/ppermute | solution.py:935
  169.3 23.1 %collective-permute-start.24 = (bf16[128,2816]{1,0:T(8,128)(2,1)S(1)}, bf16[128,2816]{1,0:T(8,128)(2,1)}, u32[]{:S(2)}, u32[]{:S(2)}) collective-permute-start(bf16[128,2816]{1,0:T(8,128)(2,1)S(1)} %copy-done.18), channel_id=1, source_target_pairs={{0,8},{4,12},{8,0},{12,4},{16,24},{20,28},{24,16},{28,20},{1,9},{5... | collective-permute-start | bytes 2162696 | tf_op jit(solution)/shard_map/ppermute | solution.py:935
  169.6 32.9 %collective-permute-start.31 = (bf16[352,1024]{1,0:T(8,128)(2,1)S(1)}, bf16[352,1024]{1,0:T(8,128)(2,1)}, u32[]{:S(2)}, u32[]{:S(2)}) collective-permute-start(bf16[352,1024]{1,0:T(8,128)(2,1)S(1)} %all_gather.18.refs_16_), channel_id=1, source_target_pairs={{0,8},{4,12},{8,0},{12,4},{16,24},{20,28},{24,16},{28,20},{1,9},{5... | collective-permute-start | bytes 2162696 | tf_op jit(solution)/shard_map/ppermute | solution.py:935
  170.8 15.5 %collective-permute-start.8 = (bf16[4,4,32,256]{3,2,1,0:T(8,128)(2,1)S(1)}, bf16[4,4,32,256]{3,2,1,0:T(8,128)(2,1)S(1)}, u32[]{:S(2)}, u32[]{:S(2)}) collective-permute-start(bf16[4,4,32,256]{3,2,1,0:T(8,128)(2,1)S(1)} %collective-permute-done.4), channel_id=1, source_target_pairs={{0,16},{4,20},{8,24},{12,28},{16,0},{20,4},{24,8},{28,12},{1,17},{... | collective-permute-start | bytes 786440 | tf_op jit(solution)/shard_map/ppermute | solution.py:935
  186.4 16.5 %collective-permute-start.23 = (bf16[128,2816]{1,0:T(8,128)(2,1)S(1)}, bf16[128,2816]{1,0:T(8,128)(2,1)S(1)}, u32[]{:S(2)}, u32[]{:S(2)}) collective-permute-start(bf16[128,2816]{1,0:T(8,128)(2,1)S(1)} %copy-done.18), channel_id=1, source_target_pairs={{0,4},{4,0},{8,12},{12,8},{16,20},{20,16},{24,28},{28,24},{1,5},{5... | collective-permute-start | bytes 2162696 | tf_op jit(solution)/shard_map/ppermute | solution.py:935
  188.9 15.3 %collective-permute-start.30 = (bf16[352,1024]{1,0:T(8,128)(2,1)S(1)}, bf16[352,1024]{1,0:T(8,128)(2,1)S(1)}, u32[]{:S(2)}, u32[]{:S(2)}) collective-permute-start(bf16[352,1024]{1,0:T(8,128)(2,1)S(1)} %all_gather.18.refs_16_), channel_id=1, source_target_pairs={{0,4},{4,0},{8,12},{12,8},{16,20},{20,16},{24,28},{28,24},{1,5},{5... | collective-permute-start | bytes 2162696 | tf_op jit(solution)/shard_map/ppermute | solution.py:935
  189.0 30.4 %collective-permute-start.38 = (bf16[128,3072]{1,0:T(8,128)(2,1)S(1)}, bf16[128,3072]{1,0:T(8,128)(2,1)}, u32[]{:S(2)}, u32[]{:S(2)}) collective-permute-start(bf16[128,3072]{1,0:T(8,128)(2,1)S(1)} %all_gather.19.refs_0_), channel_id=1, source_target_pairs={{0,8},{4,12},{8,0},{12,4},{16,24},{20,28},{24,16},{28,20},{1,9},{5... | collective-permute-start | bytes 2359304 | tf_op jit(solution)/shard_map/ppermute | solution.py:935
  192.4 48.0 %collective-permute-start.17 = (bf16[128,3840]{1,0:T(8,128)(2,1)S(1)}, bf16[128,3840]{1,0:T(8,128)(2,1)}, u32[]{:S(2)}, u32[]{:S(2)}) collective-permute-start(bf16[128,3840]{1,0:T(8,128)(2,1)S(1)} %all_gather.16.refs_0_), channel_id=1, source_target_pairs={{0,8},{4,12},{8,0},{12,4},{16,24},{20,28},{24,16},{28,20},{1,9},{5... | collective-permute-start | bytes 2949128 | tf_op jit(solution)/shard_map/ppermute | solution.py:935
  202.5 18.4 %collective-permute-start.40 = (bf16[128,3072]{1,0:T(8,128)(2,1)S(1)}, bf16[128,3072]{1,0:T(8,128)(2,1)S(1)}, u32[]{:S(2)}, u32[]{:S(2)}) collective-permute-start(bf16[128,3072]{1,0:T(8,128)(2,1)S(1)} %all_gather.19.refs_0_), channel_id=1, source_target_pairs={{0,16},{4,20},{8,24},{12,28},{16,0},{20,4},{24,8},{28,12},{1,17},{... | collective-permute-start | bytes 2359304 | tf_op jit(solution)/shard_map/ppermute | solution.py:935
  202.9 38.4 %collective-permute-start.19 = (bf16[128,3840]{1,0:T(8,128)(2,1)S(1)}, bf16[128,3840]{1,0:T(8,128)(2,1)}, u32[]{:S(2)}, u32[]{:S(2)}) collective-permute-start(bf16[128,3840]{1,0:T(8,128)(2,1)S(1)} %all_gather.16.refs_0_), channel_id=1, source_target_pairs={{0,16},{4,20},{8,24},{12,28},{16,0},{20,4},{24,8},{28,12},{1,17},{... | collective-permute-start | bytes 2949128 | tf_op jit(solution)/shard_map/ppermute | solution.py:935
  204.2 37.3 %collective-permute-start.16 = (bf16[128,3840]{1,0:T(8,128)(2,1)S(1)}, bf16[128,3840]{1,0:T(8,128)(2,1)S(1)}, u32[]{:S(2)}, u32[]{:S(2)}) collective-permute-start(bf16[128,3840]{1,0:T(8,128)(2,1)S(1)} %all_gather.16.refs_0_), channel_id=1, source_target_pairs={{0,4},{4,0},{8,12},{12,8},{16,20},{20,16},{24,28},{28,24},{1,5},{5... | collective-permute-start | bytes 2949128 | tf_op jit(solution)/shard_map/ppermute | solution.py:935
  220.9 34.9 %collective-permute-start.28 = (bf16[128,2816]{1,0:T(8,128)(2,1)S(1)}, bf16[128,2816]{1,0:T(8,128)(2,1)}, u32[]{:S(2)}, u32[]{:S(2)}) collective-permute-start(bf16[128,2816]{1,0:T(8,128)(2,1)S(1)} %collective-permute-done.26.refs_12_), channel_id=1, source_target_pairs={{0,8},{4,12},{8,0},{12,4},{16,24},{20,28},{24,16},{28,20},{1,9},{5... | collective-permute-start | bytes 2162696 | tf_op jit(solution)/shard_map/ppermute | solution.py:935
  222.0 50.3 %collective-permute-start.27 = (bf16[128,2816]{1,0:T(8,128)(2,1)S(1)}, bf16[128,2816]{1,0:T(8,128)(2,1)S(1)}, u32[]{:S(2)}, u32[]{:S(2)}) collective-permute-start(bf16[128,2816]{1,0:T(8,128)(2,1)S(1)} %collective-permute-done.26.refs_12_), channel_id=1, source_target_pairs={{0,4},{4,0},{8,12},{12,8},{16,20},{20,16},{24,28},{28,24},{1,5},{5... | collective-permute-start | bytes 2162696 | tf_op jit(solution)/shard_map/ppermute | solution.py:935
  240.4 30.9 %collective-permute-start.35 = (bf16[352,1024]{1,0:T(8,128)(2,1)}, bf16[352,1024]{1,0:T(8,128)(2,1)}, u32[]{:S(2)}, u32[]{:S(2)}) collective-permute-start(bf16[352,1024]{1,0:T(8,128)(2,1)} %collective-permute-done.33.refs_20_), channel_id=1, source_target_pairs={{0,8},{4,12},{8,0},{12,4},{16,24},{20,28},{24,16},{28,20},{1,9},{5... | collective-permute-start | bytes 2162696 | tf_op jit(solution)/shard_map/ppermute | solution.py:935
  241.2 61.8 %collective-permute-start.42 = (bf16[128,3072]{1,0:T(8,128)(2,1)}, bf16[128,3072]{1,0:T(8,128)(2,1)}, u32[]{:S(2)}, u32[]{:S(2)}) collective-permute-start(bf16[128,3072]{1,0:T(8,128)(2,1)} %collective-permute-done.38.refs_2_), channel_id=1, source_target_pairs={{0,16},{4,20},{8,24},{12,28},{16,0},{20,4},{24,8},{28,12},{1,17},{... | collective-permute-start | bytes 2359304 | tf_op jit(solution)/shard_map/ppermute | solution.py:935
  241.5 62.0 %collective-permute-start.21 = (bf16[128,3840]{1,0:T(8,128)(2,1)}, bf16[128,3840]{1,0:T(8,128)(2,1)}, u32[]{:S(2)}, u32[]{:S(2)}) collective-permute-start(bf16[128,3840]{1,0:T(8,128)(2,1)} %collective-permute-done.17.refs_2_), channel_id=1, source_target_pairs={{0,16},{4,20},{8,24},{12,28},{16,0},{20,4},{24,8},{28,12},{1,17},{... | collective-permute-start | bytes 2949128 | tf_op jit(solution)/shard_map/ppermute | solution.py:935
  255.9 46.5 %collective-permute-start.34 = (bf16[352,1024]{1,0:T(8,128)(2,1)}, bf16[352,1024]{1,0:T(8,128)(2,1)}, u32[]{:S(2)}, u32[]{:S(2)}) collective-permute-start(bf16[352,1024]{1,0:T(8,128)(2,1)} %collective-permute-done.33.refs_20_), channel_id=1, source_target_pairs={{0,4},{4,0},{8,12},{12,8},{16,20},{20,16},{24,28},{28,24},{1,5},{5... | collective-permute-start | bytes 2162696 | tf_op jit(solution)/shard_map/ppermute | solution.py:935
  271.3 31.1 %collective-permute-start.25 = (bf16[128,2816]{1,0:T(8,128)(2,1)}, bf16[128,2816]{1,0:T(8,128)(2,1)}, u32[]{:S(2)}, u32[]{:S(2)}) collective-permute-start(bf16[128,2816]{1,0:T(8,128)(2,1)} %collective-permute-done.24.refs_10_), channel_id=1, source_target_pairs={{0,4},{4,0},{8,12},{12,8},{16,20},{20,16},{24,28},{28,24},{1,5},{5... | collective-permute-start | bytes 2162696 | tf_op jit(solution)/shard_map/ppermute | solution.py:935
  272.3 30.6 %collective-permute-start.32 = (bf16[352,1024]{1,0:T(8,128)(2,1)}, bf16[352,1024]{1,0:T(8,128)(2,1)}, u32[]{:S(2)}, u32[]{:S(2)}) collective-permute-start(bf16[352,1024]{1,0:T(8,128)(2,1)} %collective-permute-done.31.refs_18_), channel_id=1, source_target_pairs={{0,4},{4,0},{8,12},{12,8},{16,20},{20,16},{24,28},{28,24},{1,5},{5... | collective-permute-start | bytes 2162696 | tf_op jit(solution)/shard_map/ppermute | solution.py:935
  302.4 47.5 %collective-permute-start.18 = (bf16[128,3840]{1,0:T(8,128)(2,1)}, bf16[128,3840]{1,0:T(8,128)(2,1)S(1)}, u32[]{:S(2)}, u32[]{:S(2)}) collective-permute-start(bf16[128,3840]{1,0:T(8,128)(2,1)} %collective-permute-done.17.refs_2_), channel_id=1, source_target_pairs={{0,4},{4,0},{8,12},{12,8},{16,20},{20,16},{24,28},{28,24},{1,5},{5... | collective-permute-start | bytes 2949128 | tf_op jit(solution)/shard_map/ppermute | solution.py:935
  302.5 48.8 %collective-permute-start.20 = (bf16[128,3840]{1,0:T(8,128)(2,1)}, bf16[128,3840]{1,0:T(8,128)(2,1)}, u32[]{:S(2)}, u32[]{:S(2)}) collective-permute-start(bf16[128,3840]{1,0:T(8,128)(2,1)} %collective-permute-done.19.refs_4_), channel_id=1, source_target_pairs={{0,4},{4,0},{8,12},{12,8},{16,20},{20,16},{24,28},{28,24},{1,5},{5... | collective-permute-start | bytes 2949128 | tf_op jit(solution)/shard_map/ppermute | solution.py:935
  302.9 48.4 %collective-permute-start.29 = (bf16[128,2816]{1,0:T(8,128)(2,1)}, bf16[128,2816]{1,0:T(8,128)(2,1)}, u32[]{:S(2)}, u32[]{:S(2)}) collective-permute-start(bf16[128,2816]{1,0:T(8,128)(2,1)} %collective-permute-done.28.refs_14_), channel_id=1, source_target_pairs={{0,4},{4,0},{8,12},{12,8},{16,20},{20,16},{24,28},{28,24},{1,5},{5... | collective-permute-start | bytes 2162696 | tf_op jit(solution)/shard_map/ppermute | solution.py:935
  303.0 48.7 %collective-permute-start.36 = (bf16[352,1024]{1,0:T(8,128)(2,1)}, bf16[352,1024]{1,0:T(8,128)(2,1)}, u32[]{:S(2)}, u32[]{:S(2)}) collective-permute-start(bf16[352,1024]{1,0:T(8,128)(2,1)} %collective-permute-done.35.refs_22_), channel_id=1, source_target_pairs={{0,4},{4,0},{8,12},{12,8},{16,20},{20,16},{24,28},{28,24},{1,5},{5... | collective-permute-start | bytes 2162696 | tf_op jit(solution)/shard_map/ppermute | solution.py:935
  303.5 48.4 %collective-permute-start.22 = (bf16[128,3840]{1,0:T(8,128)(2,1)}, bf16[128,3840]{1,0:T(8,128)(2,1)}, u32[]{:S(2)}, u32[]{:S(2)}) collective-permute-start(bf16[128,3840]{1,0:T(8,128)(2,1)} %collective-permute-done.21.refs_6_), channel_id=1, source_target_pairs={{0,4},{4,0},{8,12},{12,8},{16,20},{20,16},{24,28},{28,24},{1,5},{5... | collective-permute-start | bytes 2949128 | tf_op jit(solution)/shard_map/ppermute | solution.py:935
  349.9 180.2 %collective-permute-start.37 = (bf16[128,3072]{1,0:T(8,128)(2,1)S(1)}, bf16[128,3072]{1,0:T(8,128)(2,1)}, u32[]{:S(2)}, u32[]{:S(2)}) collective-permute-start(bf16[128,3072]{1,0:T(8,128)(2,1)S(1)} %all_gather.19.refs_0_), channel_id=1, source_target_pairs={{0,4},{4,0},{8,12},{12,8},{16,20},{20,16},{24,28},{28,24},{1,5},{5... | collective-permute-start | bytes 2359304 | tf_op jit(solution)/shard_map/ppermute | solution.py:935
  351.3 178.9 %collective-permute-start.39 = (bf16[128,3072]{1,0:T(8,128)(2,1)}, bf16[128,3072]{1,0:T(8,128)(2,1)}, u32[]{:S(2)}, u32[]{:S(2)}) collective-permute-start(bf16[128,3072]{1,0:T(8,128)(2,1)} %collective-permute-done.38.refs_2_), channel_id=1, source_target_pairs={{0,4},{4,0},{8,12},{12,8},{16,20},{20,16},{24,28},{28,24},{1,5},{5... | collective-permute-start | bytes 2359304 | tf_op jit(solution)/shard_map/ppermute | solution.py:935
  351.4 179.3 %collective-permute-start.41 = (bf16[128,3072]{1,0:T(8,128)(2,1)S(1)}, bf16[128,3072]{1,0:T(8,128)(2,1)}, u32[]{:S(2)}, u32[]{:S(2)}) collective-permute-start(bf16[128,3072]{1,0:T(8,128)(2,1)S(1)} %copy-done.14), channel_id=1, source_target_pairs={{0,4},{4,0},{8,12},{12,8},{16,20},{20,16},{24,28},{28,24},{1,5},{5... | collective-permute-start | bytes 2359304 | tf_op jit(solution)/shard_map/ppermute | solution.py:935
  351.8 178.9 %collective-permute-start.43 = (bf16[128,3072]{1,0:T(8,128)(2,1)}, bf16[128,3072]{1,0:T(8,128)(2,1)}, u32[]{:S(2)}, u32[]{:S(2)}) collective-permute-start(bf16[128,3072]{1,0:T(8,128)(2,1)} %collective-permute-done.42.refs_6_), channel_id=1, source_target_pairs={{0,4},{4,0},{8,12},{12,8},{16,20},{20,16},{24,28},{28,24},{1,5},{5... | collective-permute-start | bytes 2359304 | tf_op jit(solution)/shard_map/ppermute | solution.py:935
  525.9 74.7 %collective-permute-start.74 = (bf16[4,352,1024]{2,1,0:T(8,128)(2,1)}, bf16[4,352,1024]{2,1,0:T(8,128)(2,1)}, u32[]{:S(2)}, u32[]{:S(2)}) collective-permute-start(bf16[4,352,1024]{2,1,0:T(8,128)(2,1)} %get-tuple-element.55), channel_id=1, source_target_pairs={{0,4},{4,0},{8,12},{12,8},{16,20},{20,16},{24,28},{28,24},{1,5},{5... | collective-permute-start | bytes 8650760 | tf_op jit(solution)/shard_map/ppermute | solution.py:935
  530.1 14.4 %collective-permute-start.50 = (bf16[4,128,384]{2,1,0:T(8,128)(2,1)S(1)}, bf16[4,128,384]{2,1,0:T(8,128)(2,1)}, u32[]{:S(2)}, u32[]{:S(2)}) collective-permute-start(bf16[4,128,384]{2,1,0:T(8,128)(2,1)S(1)} %slice_bitcast_fusion), channel_id=1, source_target_pairs={{0,4},{4,0},{8,12},{12,8},{16,20},{20,16},{24,28},{28,24},{1,5},{5... | collective-permute-start | bytes 1179656 | tf_op jit(solution)/shard_map/ppermute | solution.py:935
  530.2 13.0 %collective-permute-start.44 = (bf16[4,128,384]{2,1,0:T(8,128)(2,1)}, bf16[4,128,384]{2,1,0:T(8,128)(2,1)}, u32[]{:S(2)}, u32[]{:S(2)}) collective-permute-start(bf16[4,128,384]{2,1,0:T(8,128)(2,1)} %slice_bitcast_fusion.1), channel_id=1, source_target_pairs={{0,4},{4,0},{8,12},{12,8},{16,20},{20,16},{24,28},{28,24},{1,5},{5... | collective-permute-start | bytes 1179656 | tf_op jit(solution)/shard_map/ppermute | solution.py:935
  543.1 30.8 %collective-permute-start.56 = (bf16[4,128,1024]{2,1,0:T(8,128)(2,1)}, bf16[4,128,1024]{2,1,0:T(8,128)(2,1)}, u32[]{:S(2)}, u32[]{:S(2)}) collective-permute-start(bf16[4,128,1024]{2,1,0:T(8,128)(2,1)} %get-tuple-element.49), channel_id=1, source_target_pairs={{0,4},{4,0},{8,12},{12,8},{16,20},{20,16},{24,28},{28,24},{1,5},{5... | collective-permute-start | bytes 3145736 | tf_op jit(solution)/shard_map/ppermute | solution.py:935
  545.6 9.0 %collective-permute-start.51 = (bf16[2,128,384]{2,1,0:T(8,128)(2,1)S(1)}, bf16[2,128,384]{2,1,0:T(8,128)(2,1)S(1)}, u32[]{:S(2)}, u32[]{:S(2)}) collective-permute-start(bf16[2,128,384]{2,1,0:T(8,128)(2,1)S(1)} %add_convert_fusion.8), channel_id=1, source_target_pairs={{0,8},{4,12},{8,0},{12,4},{16,24},{20,28},{24,16},{28,20},{1,9},{5... | collective-permute-start | bytes 589832 | tf_op jit(solution)/shard_map/ppermute | solution.py:935
  559.1 9.2 %collective-permute-start.49 = (bf16[32,384]{1,0:T(8,128)(2,1)}, bf16[32,384]{1,0:T(8,128)(2,1)}, u32[]{:S(2)}, u32[]{:S(2)}) collective-permute-start(bf16[32,384]{1,0:T(8,128)(2,1)} %get-tuple-element.110), channel_id=1, source_target_pairs={{0,3},{1,0},{2,1},{3,2},{4,7},{5,4},{6,5},{7,6},{8,11},{9,8},{10,9... | collective-permute-start | bytes 73736 | tf_op jit(solution)/shard_map/ppermute | solution.py:932
  562.4 41.1 %collective-permute-start.68 = (bf16[4,128,2816]{2,1,0:T(8,128)(2,1)}, bf16[4,128,2816]{2,1,0:T(8,128)(2,1)}, u32[]{:S(2)}, u32[]{:S(2)}) collective-permute-start(bf16[4,128,2816]{2,1,0:T(8,128)(2,1)} %get-tuple-element.53), channel_id=1, source_target_pairs={{0,4},{4,0},{8,12},{12,8},{16,20},{20,16},{24,28},{28,24},{1,5},{5... | collective-permute-start | bytes 8650760 | tf_op jit(solution)/shard_map/ppermute | solution.py:935
  566.8 39.6 %collective-permute-start.62 = (bf16[4,128,2816]{2,1,0:T(8,128)(2,1)}, bf16[4,128,2816]{2,1,0:T(8,128)(2,1)S(1)}, u32[]{:S(2)}, u32[]{:S(2)}) collective-permute-start(bf16[4,128,2816]{2,1,0:T(8,128)(2,1)} %get-tuple-element.51), channel_id=1, source_target_pairs={{0,4},{4,0},{8,12},{12,8},{16,20},{20,16},{24,28},{28,24},{1,5},{5... | collective-permute-start | bytes 8650760 | tf_op jit(solution)/shard_map/ppermute | solution.py:935
  577.7 11.8 %collective-permute-start.57 = (bf16[2,128,1024]{2,1,0:T(8,128)(2,1)}, bf16[2,128,1024]{2,1,0:T(8,128)(2,1)}, u32[]{:S(2)}, u32[]{:S(2)}) collective-permute-start(bf16[2,128,1024]{2,1,0:T(8,128)(2,1)} %add_convert_fusion.6), channel_id=1, source_target_pairs={{0,16},{4,20},{8,24},{12,28},{16,0},{20,4},{24,8},{28,12},{1,17},{... | collective-permute-start | bytes 1572872 | tf_op jit(solution)/shard_map/ppermute | solution.py:935
  597.4 10.7 %collective-permute-start.59 = (bf16[32,1024]{1,0:T(8,128)(2,1)S(1)}, bf16[32,1024]{1,0:T(8,128)(2,1)S(1)}, u32[]{:S(2)}, u32[]{:S(2)}) collective-permute-start(bf16[32,1024]{1,0:T(8,128)(2,1)S(1)} %get-tuple-element.92), channel_id=1, source_target_pairs={{0,1},{1,2},{2,3},{3,0},{4,5},{5,6},{6,7},{7,4},{8,9},{9,10},{10,1... | collective-permute-start | bytes 196616 | tf_op jit(solution)/shard_map/ppermute | solution.py:932
  603.5 29.4 %collective-permute-start.75 = (bf16[2,352,1024]{2,1,0:T(8,128)(2,1)S(1)}, bf16[2,352,1024]{2,1,0:T(8,128)(2,1)S(1)}, u32[]{:S(2)}, u32[]{:S(2)}) collective-permute-start(bf16[2,352,1024]{2,1,0:T(8,128)(2,1)S(1)} %add_convert_fusion), channel_id=1, source_target_pairs={{0,8},{4,12},{8,0},{12,4},{16,24},{20,28},{24,16},{28,20},{1,9},{5... | collective-permute-start | bytes 4325384 | tf_op jit(solution)/shard_map/ppermute | solution.py:935
  606.4 29.4 %collective-permute-start.69 = (bf16[2,128,2816]{2,1,0:T(8,128)(2,1)S(1)}, bf16[2,128,2816]{2,1,0:T(8,128)(2,1)S(1)}, u32[]{:S(2)}, u32[]{:S(2)}) collective-permute-start(bf16[2,128,2816]{2,1,0:T(8,128)(2,1)S(1)} %add_convert_fusion.1), channel_id=1, source_target_pairs={{0,16},{4,20},{8,24},{12,28},{16,0},{20,4},{24,8},{28,12},{1,17},{... | collective-permute-start | bytes 4325384 | tf_op jit(solution)/shard_map/ppermute | solution.py:935
  608.1 55.7 %collective-permute-start.63 = (bf16[2,128,2816]{2,1,0:T(8,128)(2,1)S(1)}, bf16[2,128,2816]{2,1,0:T(8,128)(2,1)S(1)}, u32[]{:S(2)}, u32[]{:S(2)}) collective-permute-start(bf16[2,128,2816]{2,1,0:T(8,128)(2,1)S(1)} %add_convert_fusion.2), channel_id=1, source_target_pairs={{0,8},{4,12},{8,0},{12,4},{16,24},{20,28},{24,16},{28,20},{1,9},{5... | collective-permute-start | bytes 4325384 | tf_op jit(solution)/shard_map/ppermute | solution.py:935
  634.4 29.8 %collective-permute-start.76 = (bf16[1,352,1024]{2,1,0:T(8,128)(2,1)S(1)}, bf16[1,352,1024]{2,1,0:T(8,128)(2,1)S(1)}, u32[]{:S(2)}, u32[]{:S(2)}) collective-permute-start(bf16[1,352,1024]{2,1,0:T(8,128)(2,1)S(1)} %add_convert_fusion.3), channel_id=1, source_target_pairs={{0,16},{4,20},{8,24},{12,28},{16,0},{20,4},{24,8},{28,12},{1,17},{... | collective-permute-start | bytes 2162696 | tf_op jit(solution)/shard_map/ppermute | solution.py:935
  637.2 42.0 %collective-permute-start.70 = (bf16[1,128,2816]{2,1,0:T(8,128)(2,1)S(1)}, bf16[1,128,2816]{2,1,0:T(8,128)(2,1)S(1)}, u32[]{:S(2)}, u32[]{:S(2)}) collective-permute-start(bf16[1,128,2816]{2,1,0:T(8,128)(2,1)S(1)} %add_convert_fusion.4), channel_id=1, source_target_pairs={{0,8},{4,12},{8,0},{12,4},{16,24},{20,28},{24,16},{28,20},{1,9},{5... | collective-permute-start | bytes 2162696 | tf_op jit(solution)/shard_map/ppermute | solution.py:935
  664.1 19.9 %collective-permute-start.64 = (bf16[1,128,2816]{2,1,0:T(8,128)(2,1)S(1)}, bf16[1,128,2816]{2,1,0:T(8,128)(2,1)S(1)}, u32[]{:S(2)}, u32[]{:S(2)}) collective-permute-start(bf16[1,128,2816]{2,1,0:T(8,128)(2,1)S(1)} %add_convert_fusion.5), channel_id=1, source_target_pairs={{0,16},{4,20},{8,24},{12,28},{16,0},{20,4},{24,8},{28,12},{1,17},{... | collective-permute-start | bytes 2162696 | tf_op jit(solution)/shard_map/ppermute | solution.py:935
  665.9 55.1 %collective-permute-start.77 = (bf16[88,1024]{1,0:T(8,128)(2,1)S(1)}, bf16[88,1024]{1,0:T(8,128)(2,1)S(1)}, u32[]{:S(2)}, u32[]{:S(2)}) collective-permute-start(bf16[88,1024]{1,0:T(8,128)(2,1)S(1)} %get-tuple-element.76), channel_id=1, source_target_pairs={{0,1},{1,2},{2,3},{3,0},{4,5},{5,6},{6,7},{7,4},{8,9},{9,10},{10,1... | collective-permute-start | bytes 540680 | tf_op jit(solution)/shard_map/ppermute | solution.py:932
  668.5 52.5 %collective-permute-start.78 = (bf16[88,1024]{1,0:T(8,128)(2,1)S(1)}, bf16[88,1024]{1,0:T(8,128)(2,1)S(1)}, u32[]{:S(2)}, u32[]{:S(2)}) collective-permute-start(bf16[88,1024]{1,0:T(8,128)(2,1)S(1)} %get-tuple-element.78), channel_id=1, source_target_pairs={{0,2},{1,3},{2,0},{3,1},{4,6},{5,7},{6,4},{7,5},{8,10},{9,11},{10,... | collective-permute-start | bytes 540680 | tf_op jit(solution)/shard_map/ppermute | solution.py:932
  683.2 17.0 %collective-permute-start.72 = (bf16[32,2816]{1,0:T(8,128)(2,1)S(1)}, bf16[32,2816]{1,0:T(8,128)(2,1)S(1)}, u32[]{:S(2)}, u32[]{:S(2)}) collective-permute-start(bf16[32,2816]{1,0:T(8,128)(2,1)S(1)} %get-tuple-element.81), channel_id=1, source_target_pairs={{0,2},{1,3},{2,0},{3,1},{4,6},{5,7},{6,4},{7,5},{8,10},{9,11},{10,... | collective-permute-start | bytes 540680 | tf_op jit(solution)/shard_map/ppermute | solution.py:932
  684.0 16.2 %collective-permute-start.73 = (bf16[32,2816]{1,0:T(8,128)(2,1)S(1)}, bf16[32,2816]{1,0:T(8,128)(2,1)S(1)}, u32[]{:S(2)}, u32[]{:S(2)}) collective-permute-start(bf16[32,2816]{1,0:T(8,128)(2,1)S(1)} %get-tuple-element.80), channel_id=1, source_target_pairs={{0,3},{1,0},{2,1},{3,2},{4,7},{5,4},{6,5},{7,6},{8,11},{9,8},{10,9... | collective-permute-start | bytes 540680 | tf_op jit(solution)/shard_map/ppermute | solution.py:932
  687.6 19.3 %collective-permute-start.65 = (bf16[32,2816]{1,0:T(8,128)(2,1)S(1)}, bf16[32,2816]{1,0:T(8,128)(2,1)S(1)}, u32[]{:S(2)}, u32[]{:S(2)}) collective-permute-start(bf16[32,2816]{1,0:T(8,128)(2,1)S(1)} %get-tuple-element.82), channel_id=1, source_target_pairs={{0,1},{1,2},{2,3},{3,0},{4,5},{5,6},{6,7},{7,4},{8,9},{9,10},{10,1... | collective-permute-start | bytes 540680 | tf_op jit(solution)/shard_map/ppermute | solution.py:932
  700.2 19.3 %collective-permute-start.66 = (bf16[32,2816]{1,0:T(8,128)(2,1)S(1)}, bf16[32,2816]{1,0:T(8,128)(2,1)S(1)}, u32[]{:S(2)}, u32[]{:S(2)}) collective-permute-start(bf16[32,2816]{1,0:T(8,128)(2,1)S(1)} %get-tuple-element.84), channel_id=1, source_target_pairs={{0,2},{1,3},{2,0},{3,1},{4,6},{5,7},{6,4},{7,5},{8,10},{9,11},{10,... | collective-permute-start | bytes 540680 | tf_op jit(solution)/shard_map/ppermute | solution.py:932
  700.2 19.3 %collective-permute-start.67 = (bf16[32,2816]{1,0:T(8,128)(2,1)S(1)}, bf16[32,2816]{1,0:T(8,128)(2,1)S(1)}, u32[]{:S(2)}, u32[]{:S(2)}) collective-permute-start(bf16[32,2816]{1,0:T(8,128)(2,1)S(1)} %get-tuple-element.83), channel_id=1, source_target_pairs={{0,3},{1,0},{2,1},{3,2},{4,7},{5,4},{6,5},{7,6},{8,11},{9,8},{10,9... | collective-permute-start | bytes 540680 | tf_op jit(solution)/shard_map/ppermute | solution.py:932
  707.0 14.0 %collective-permute-start.79 = (bf16[88,1024]{1,0:T(8,128)(2,1)S(1)}, bf16[88,1024]{1,0:T(8,128)(2,1)S(1)}, u32[]{:S(2)}, u32[]{:S(2)}) collective-permute-start(bf16[88,1024]{1,0:T(8,128)(2,1)S(1)} %get-tuple-element.77), channel_id=1, source_target_pairs={{0,3},{1,0},{2,1},{3,2},{4,7},{5,4},{6,5},{7,6},{8,11},{9,8},{10,9... | collective-permute-start | bytes 540680 | tf_op jit(solution)/shard_map/ppermute | solution.py:932
  (55 other events, 1349.1 us)
Sparse Core Ops, SparseCore 0:
  16.0 132.9 all-gather.2

commit v3 on v2

--- a/solution.py
+++ b/solution.py
@@ -388,54 +388,14 @@
     return jnp.where(lane // HEAD_DIM == head, x, jnp.zeros_like(x))
 
 
-def qkv_kernel(blocks, x_ref, w_ref, gain_ref, fv_ref, cos_ref, sin_ref, xn_ref, q_ref, k_ref, v_ref, rel):
-    dp = lax.axis_index("dp")
-    for d in range(blocks):
-        rel[:, d * LANES : (d + 1) * LANES] = x_ref[:, lane_block(dp ^ d)].astype(F32)
-    x = rel[...]
-    inv = lax.rsqrt(jnp.mean(x * x, axis=-1, keepdims=True) + epsilon)
-    xn = (x * inv * gain_ref[...]).astype(LOW)
-    xn_ref[...] = xn
-    width = q_ref.shape[1]
-    proj = dot(xn, w_ref[...], 1, 0)
-    cos, sin = cos_ref[...], sin_ref[...]
-    for b in range(width // LANES):
-        at = slice(b * LANES, (b + 1) * LANES)
-        qb = proj[:, b * LANES : (b + 1) * LANES]
-        q_ref[:, at] = ((qb * cos + half_swap(qb) * sin) * 0.125).astype(LOW)
-        kb = proj[:, width + b * LANES : width + (b + 1) * LANES]
-        k_ref[:, at] = (kb * cos + half_swap(kb) * sin).astype(LOW)
-    v_ref[...] = (0.5 * proj[:, 2 * width :] + 0.5 * fv_ref[...].astype(F32)).astype(LOW)
-
-
-def qkv_call(x, w, gain, fv, cos, sin):
-    length, model = x.shape
-    width = fv.shape[1]
-    tb = TOKEN_BLOCK
-    row = lambda cols: pl.BlockSpec((tb, cols), lambda i: (i, 0))
-    whole = lambda a: pl.BlockSpec(a.shape, lambda i: (0, 0))
-    return pl.pallas_call(
-        functools.partial(qkv_kernel, model // LANES),
-        grid=(length // tb,),
-        in_specs=[row(model), whole(w), whole(gain), row(width), row(LANES), row(LANES)],
-        out_specs=[row(model), row(width), row(width), row(width)],
-        out_shape=[jax.ShapeDtypeStruct((length, model), LOW)]
-        + [jax.ShapeDtypeStruct((length, width), LOW)] * 3,
-        scratch_shapes=[pltpu.VMEM((tb, model), F32)],
-        compiler_params=params(),
-        cost_estimate=pl.CostEstimate(
-            flops=2 * length * model * 3 * width, bytes_accessed=10 * 2**20, transcendentals=0
-        ),
-        name="qkv",
-    )(x, w, gain, fv, cos, sin)
-
-
-def meet_ctx(n_ctx):
-    c = lax.axis_index("ctx")
+def meet(n_ctx, bits):
+    c, dp = lax.axis_index("ctx"), lax.axis_index("dp")
     barrier = pltpu.get_barrier_semaphore()
     for k in range(1, n_ctx):
         pl.semaphore_signal(barrier, inc=1, device_id={"ctx": lax.rem(c + k, n_ctx)}, device_id_type=MESH)
-    pl.semaphore_wait(barrier, n_ctx - 1)
+    for bit in bits:
+        pl.semaphore_signal(barrier, inc=1, device_id={"dp": dp ^ bit}, device_id_type=MESH)
+    pl.semaphore_wait(barrier, n_ctx - 1 + len(bits))
 
 
 def ctx_copy(src, dst, send, recv, to):
@@ -444,13 +404,239 @@
     )
 
 
-def attend_kernel(n_ctx, q_ref, k_ref, v_ref, sq_ref, sk_ref, att_ref, of_ref, lse_ref,
-                  o_ref, s_ref, m_ref, l_ref, acc_ref, send, recv, own):
-    c = lax.axis_index("ctx")
+def dp_copy(src, dst, send, recv, bit):
+    to = lax.axis_index("dp") ^ bit
+    return pltpu.make_async_remote_copy(
+        src_ref=src, dst_ref=dst, send_sem=send, recv_sem=recv, device_id={"dp": to}, device_id_type=MESH
+    )
+
+
+def rows_of(index, size):
+    return pl.ds(pl.multiple_of(index * size, size), size)
+
+
+CORE, NEAR, FAR = 1, 2, 4
+
+
+class Gather:
+    def __init__(self, n_ctx, src, dst, send, recv, order):
+        self.n, self.src, self.dst, self.send, self.recv = n_ctx, src, dst, send, recv
+        self.first, self.second = order
+        self.rows = src.shape[0]
+
+    def along(self, k):
+        c = lax.axis_index("ctx")
+        to = lax.rem(c + k, self.n)
+        return ctx_copy(self.src, self.dst.at[0, pl.ds(c * self.rows, self.rows), :], self.send.at[k - 1], self.recv.at[k - 1], to)
+
+    def plane(self, slot, bit, at):
+        return dp_copy(self.dst.at[slot], self.dst.at[slot ^ bit], self.send.at[at], self.recv.at[at], bit)
+
+    def own(self):
+        c = lax.axis_index("ctx")
+        return pltpu.make_async_copy(self.src, self.dst.at[0, pl.ds(c * self.rows, self.rows), :], self.send.at[10])
+
+    def hop(self, at):
+        one, two = self.first, self.second
+        slot, bit = [(0, one), (0, two), (one, two), (0, CORE), (one, CORE), (two, CORE), (one | two, CORE)][at]
+        return self.plane(slot, bit, 3 + at)
+
+    def start(self):
+        self.own().start()
+        for k in range(1, self.n):
+            self.along(k).start()
+
+    def spread(self):
+        self.own().wait()
+        for k in range(1, self.n):
+            self.along(k).wait_recv()
+        for at in (0, 1, 3):
+            self.hop(at).start()
+
+    def forward(self):
+        self.hop(0).wait_recv()
+        self.hop(2).start()
+        self.hop(4).start()
+
+    def cross(self):
+        self.hop(1).wait_recv()
+        self.hop(5).start()
+        self.hop(2).wait_recv()
+        self.hop(6).start()
+
+    def finish(self):
+        for k in range(1, self.n):
+            self.along(k).wait_send()
+        for at in range(7):
+            self.hop(at).wait_send()
+        for at in range(3, 7):
+            self.hop(at).wait_recv()
+
+
+def front_kernel(
+    n_ctx, tok_ref, fv_ref, mark_ref, pack_ref, freq_ref, wg_ref, wu_ref, wo_ref, wd_ref,
+    xn_ref, q_ref, k_ref, v_ref, of_ref, lse_ref, cos_ref, sin_ref, seg_ref, marks, gain_ref,
+    att_ref, wg_all, wu_all, wo_all, wd_all,
+    x_all, fvs, packs, whead, rel, o_ref, s_ref, m_ref, l_ref, acc_ref,
+    mark_send, mark_recv, pack_send, pack_recv, tok_send, tok_recv, fv_send, fv_recv, w_send, w_recv,
+    o_send, o_recv, own, own_o,
+):
+    c, dp = lax.axis_index("ctx"), lax.axis_index("dp")
     tb = m_ref.shape[0]
+    half = tb // 2
+    model = tok_ref.shape[1]
+    blocks = model // LANES
     width = q_ref.shape[1]
+    own_rows = wg_ref.shape[0]
     lane = lax.broadcasted_iota(jnp.int32, (tb, LANES), 1)
-    meet_ctx(n_ctx)
+    right, left = lax.rem(c + 1, n_ctx), lax.rem(c + n_ctx - 1, n_ctx)
+    exact = lax.Precision.HIGHEST
+
+    weights = [
+        Gather(n_ctx, src, dst, w_send.at[i], w_recv.at[i], order)
+        for i, (src, dst, order) in enumerate(
+            [
+                (wg_ref, wg_all, (NEAR, FAR)),
+                (wo_ref, wo_all, (FAR, NEAR)),
+                (wu_ref, wu_all, (FAR, NEAR)),
+                (wd_ref, wd_all, (NEAR, FAR)),
+            ]
+        )
+    ]
+    early, late = weights[:2], weights[2:]
+
+    def mark_copy(k):
+        at = rows_of(c, tb)
+        return ctx_copy(mark_ref, marks.at[:, at], mark_send.at[k - 1], mark_recv.at[k - 1], lax.rem(c + k, n_ctx))
+
+    def pack_copy(k):
+        to = lax.rem(c + k, n_ctx)
+        return ctx_copy(pack_ref.at[to], packs.at[0, c], pack_send.at[k - 1], pack_recv.at[k - 1], to)
+
+    def pack_hop(slot, bit, at):
+        return dp_copy(packs.at[slot], packs.at[slot ^ bit], pack_send.at[at], pack_recv.at[at], bit)
+
+    def fv_copy(k):
+        to = lax.rem(c + k, n_ctx)
+        return ctx_copy(fv_ref.at[:, rows_of(to, width)], fvs.at[rows_of(c, tb), :], fv_send.at[k - 1], fv_recv.at[k - 1], to)
+
+    def tok_copy(way, step):
+        block = lax.rem(c + n_ctx - step, n_ctx) if way == 0 else lax.rem(c + step, n_ctx)
+        at = pl.ds(pl.multiple_of(block * tb + way * half, half), half)
+        src = tok_ref.at[pl.ds(way * half, half), :] if step == 0 else x_all.at[at, :]
+        return ctx_copy(src, x_all.at[at, :], tok_send.at[way, step], tok_recv.at[way, step], left if way else right)
+
+    locals_ = [
+        pltpu.make_async_copy(tok_ref, x_all.at[rows_of(c, tb), :], own.at[0]),
+        pltpu.make_async_copy(fv_ref.at[:, rows_of(c, width)], fvs.at[rows_of(c, tb), :], own.at[1]),
+        pltpu.make_async_copy(pack_ref.at[c], packs.at[0, c], own.at[2]),
+        pltpu.make_async_copy(mark_ref, marks.at[:, rows_of(c, tb)], own.at[3]),
+    ]
+
+    meet(n_ctx, (CORE, NEAR, FAR))
+    for k in range(1, n_ctx):
+        mark_copy(k).start()
+        pack_copy(k).start()
+    for way in range(2):
+        tok_copy(way, 0).start()
+    for w in early:
+        w.start()
+    for m in locals_:
+        m.start()
+    for k in range(1, n_ctx):
+        fv_copy(k).start()
+
+    locals_[3].wait()
+    for k in range(1, n_ctx):
+        mark_copy(k).wait_recv()
+    row8 = lax.broadcasted_iota(jnp.int32, (8, LANES), 0)
+    pick_seg = jnp.where(row8 == 0, 1.0, 0.0)
+    pick_pos = jnp.where(row8 == 1, 1.0, 0.0)
+
+    def table(b, carry):
+        at = rows_of(b, tb)
+        m = marks[:, at].astype(F32)
+        dims = (((0,), (0,)), ((), ()))
+        seg_ref[at, :] = lax.dot_general(m, pick_seg, dims, precision=exact, preferred_element_type=F32)
+        pos = lax.dot_general(m, pick_pos, dims, precision=exact, preferred_element_type=F32)
+        angle = pos * freq_ref[0:1, :]
+        cos_ref[at, :] = jnp.cos(angle)
+        sin_ref[at, :] = jnp.sin(angle) * freq_ref[1:2, :]
+        return carry
+
+    locals_[2].wait()
+    for k in range(1, n_ctx):
+        pack_copy(k).wait_recv()
+    pack_hop(0, NEAR, 3).start()
+    lax.fori_loop(0, n_ctx, table, 0)
+    pack_hop(0, NEAR, 3).wait_recv()
+    pack_hop(0, FAR, 4).start()
+    pack_hop(NEAR, FAR, 5).start()
+    pack_hop(0, CORE, 6).start()
+    pack_hop(NEAR, CORE, 7).start()
+
+    for way in range(2):
+        tok_copy(way, 0).wait_recv()
+        tok_copy(way, 1).start()
+    pack_hop(0, FAR, 4).wait_recv()
+    pack_hop(FAR, CORE, 8).start()
+    pack_hop(NEAR, FAR, 5).wait_recv()
+    pack_hop(NEAR | FAR, CORE, 9).start()
+    for w in early:
+        w.spread()
+    for at, (slot, bit) in enumerate([(0, CORE), (NEAR, CORE), (FAR, CORE), (NEAR | FAR, CORE)]):
+        pack_hop(slot, bit, 6 + at).wait_recv()
+    count = packs.shape[0]
+    for t in range(3):
+        block = packs[:, :, t * own_rows : (t + 1) * own_rows, :]
+        whead[:, t * width : (t + 1) * width] = block.reshape(model, width)
+    gains = packs[:, :, 3 * own_rows : 4 * own_rows, 0:LANES].reshape(model, LANES).astype(F32)
+    gain_ref[...] = gains.T[0:8, :]
+    locals_[0].wait()
+    locals_[1].wait()
+
+    def project(chunk, part):
+        at = pl.ds(pl.multiple_of(chunk * tb + part * half, half), half)
+        for d in range(blocks):
+            rel[:, d * LANES : (d + 1) * LANES] = x_all[at, lane_block(dp ^ d)].astype(F32)
+        x = rel[...]
+        inv = lax.rsqrt(jnp.mean(x * x, axis=-1, keepdims=True) + epsilon)
+        xn = (x * inv * gain_ref[0:1, :]).astype(LOW)
+        xn_ref[at, :] = xn
+        proj = dot(xn, whead[...], 1, 0)
+        cos, sin = cos_ref[at, :], sin_ref[at, :]
+        for b in range(width // LANES):
+            cols = slice(b * LANES, (b + 1) * LANES)
+            qb = proj[:, b * LANES : (b + 1) * LANES]
+            q_ref[at, cols] = ((qb * cos + half_swap(qb) * sin) * 0.125).astype(LOW)
+            kb = proj[:, width + b * LANES : width + (b + 1) * LANES]
+            k_ref[at, cols] = (kb * cos + half_swap(kb) * sin).astype(LOW)
+        v_ref[at, :] = (0.5 * proj[:, 2 * width :] + 0.5 * fvs[at, :].astype(F32)).astype(LOW)
+
+    def project_pair(step):
+        def one(part, carry):
+            project(lax.rem(c + (2 * part - 1) * step + n_ctx, n_ctx), part)
+            return carry
+
+        lax.fori_loop(0, 2, one, 0)
+
+    project_pair(0)
+    for w in early:
+        w.forward()
+    for way in range(2):
+        tok_copy(way, 1).wait_recv()
+        tok_copy(way, 2).start()
+    for k in range(1, n_ctx):
+        fv_copy(k).wait_recv()
+    project_pair(1)
+    project_pair(2)
+    for w in early:
+        w.cross()
+    for way in range(2):
+        tok_copy(way, 2).wait_recv()
+    for w in late:
+        w.start()
+    project_pair(3)
 
     def fold(x, op):
         r = x[:, 0:LANES]
@@ -461,107 +647,145 @@
     def home(pair):
         return att_ref.at[:, pl.ds(pl.multiple_of(c * width + pair * LANES, LANES), LANES)]
 
+    def query_block(pair, i):
+        cols = slice(pair * LANES, (pair + 1) * LANES)
+        mine = rows_of(i, tb)
+        q = q_ref[mine, cols]
+        seg_q = seg_ref[mine, 0:1]
+        for head in range(2):
+            qm = head_lanes(q, head)
+            m_ref[...] = jnp.full_like(m_ref, NEG)
+
+            def score(j, causal):
+                at = rows_of(j, tb)
+                s = dot(qm, k_ref[at, cols], 1, 1)
+                ok = seg_q == marks[0:1, at].astype(F32)
+                if causal:
+                    r = lax.broadcasted_iota(jnp.int32, (tb, tb), 0)
+                    t = lax.broadcasted_iota(jnp.int32, (tb, tb), 1)
+                    ok = ok & (r >= t)
+                s = jnp.where(ok, s, NEG)
+                s_ref[:, at] = s
+                m_ref[...] = jnp.maximum(m_ref[...], fold(s, jnp.maximum))
+
+            def score_step(j, carry):
+                score(j, False)
+                return carry
+
+            lax.fori_loop(0, i, score_step, 0)
+            score(i, True)
+            top = jnp.max(m_ref[...], axis=1, keepdims=True)
+            l_ref[...] = jnp.zeros_like(l_ref)
+            acc_ref[...] = jnp.zeros_like(acc_ref)
+
+            def value_step(j, carry):
+                at = rows_of(j, tb)
+                p = jnp.exp(s_ref[:, at] - top)
+                l_ref[...] += fold(p, jnp.add)
+                acc_ref[...] += dot(p.astype(LOW), v_ref[at, cols], 1, 0)
+                return carry
+
+            lax.fori_loop(0, i + 1, value_step, 0)
+            total = jnp.sum(l_ref[...], axis=1, keepdims=True)
+            out = acc_ref[...] / total
+            lse = jnp.broadcast_to(top + jnp.log(total), (tb, LANES))
+            if head == 0:
+                of_ref[mine, cols] = out
+                lse_ref[mine, cols] = lse
+            else:
+                of_ref[mine, cols] = jnp.where(lane < HEAD_DIM, of_ref[mine, cols], out)
+                lse_ref[mine, cols] = jnp.where(lane < HEAD_DIM, lse_ref[mine, cols], lse)
+        o_ref[mine, cols] = of_ref[mine, cols].astype(LOW)
+
+        @pl.when(i == c)
+        def _():
+            pltpu.make_async_copy(o_ref.at[mine, cols], home(pair), own_o.at[pair]).start()
+
+        @pl.when(i != c)
+        def _():
+            k = lax.rem(i + n_ctx - c, n_ctx) - 1
+            ctx_copy(o_ref.at[mine, cols], home(pair), o_send.at[k, pair], o_recv.at[k, pair], i).start()
+
+    def query_blocks(pair, lo, hi):
+        def one(i, carry):
+            query_block(pair, i)
+            return carry
+
+        lax.fori_loop(lo, hi, one, 0)
+
+    query_blocks(0, 0, n_ctx)
+    for w in late:
+        w.spread()
+    query_blocks(1, 0, n_ctx)
+    for w in late:
+        w.forward()
     for pair in range(width // LANES):
         cols = slice(pair * LANES, (pair + 1) * LANES)
-
-        def query_block(i, carry):
-            mine = pl.ds(pl.multiple_of(i * tb, tb), tb)
-            q = q_ref[mine, cols]
-            seg_q = sq_ref[mine, 0:1]
-            for head in range(2):
-                qm = head_lanes(q, head)
-                m_ref[...] = jnp.full_like(m_ref, NEG)
-
-                def score(j, causal):
-                    at = pl.ds(pl.multiple_of(j * tb, tb), tb)
-                    s = dot(qm, k_ref[at, cols], 1, 1)
-                    ok = seg_q == sk_ref[0:1, at]
-                    if causal:
-                        r = lax.broadcasted_iota(jnp.int32, (tb, tb), 0)
-                        t = lax.broadcasted_iota(jnp.int32, (tb, tb), 1)
-                        ok = ok & (r >= t)
-                    s = jnp.where(ok, s, NEG)
-                    s_ref[:, at] = s
-                    m_ref[...] = jnp.maximum(m_ref[...], fold(s, jnp.maximum))
-
-                def score_step(j, carry):
-                    score(j, False)
-                    return carry
-
-                lax.fori_loop(0, i, score_step, 0)
-                score(i, True)
-                top = jnp.max(m_ref[...], axis=1, keepdims=True)
-                l_ref[...] = jnp.zeros_like(l_ref)
-                acc_ref[...] = jnp.zeros_like(acc_ref)
-
-                def value_step(j, carry):
-                    at = pl.ds(pl.multiple_of(j * tb, tb), tb)
-                    p = jnp.exp(s_ref[:, at] - top)
-                    l_ref[...] += fold(p, jnp.add)
-                    acc_ref[...] += dot(p.astype(LOW), v_ref[at, cols], 1, 0)
-                    return carry
-
-                lax.fori_loop(0, i + 1, value_step, 0)
-                total = jnp.sum(l_ref[...], axis=1, keepdims=True)
-                out = acc_ref[...] / total
-                lse = jnp.broadcast_to(top + jnp.log(total), (tb, LANES))
-                if head == 0:
-                    of_ref[mine, cols] = out
-                    lse_ref[mine, cols] = lse
-                else:
-                    of_ref[mine, cols] = jnp.where(lane < HEAD_DIM, of_ref[mine, cols], out)
-                    lse_ref[mine, cols] = jnp.where(lane < HEAD_DIM, lse_ref[mine, cols], lse)
-            o_ref[mine, cols] = of_ref[mine, cols].astype(LOW)
-
-            @pl.when(i == c)
-            def _():
-                pltpu.make_async_copy(o_ref.at[mine, cols], home(pair), own.at[pair]).start()
-
-            @pl.when(i != c)
-            def _():
-                k = lax.rem(i + n_ctx - c, n_ctx) - 1
-                ctx_copy(o_ref.at[mine, cols], home(pair), send.at[k, pair], recv.at[k, pair], i).start()
-
-            return carry
-
-        lax.fori_loop(0, n_ctx, query_block, 0)
-    for pair in range(width // LANES):
-        cols = slice(pair * LANES, (pair + 1) * LANES)
-        pltpu.make_async_copy(o_ref.at[0:tb, cols], home(pair), own.at[pair]).wait()
+        pltpu.make_async_copy(o_ref.at[0:tb, cols], home(pair), own_o.at[pair]).wait()
         for k in range(n_ctx - 1):
-            ctx_copy(o_ref.at[0:tb, cols], home(pair), send.at[k, pair], recv.at[k, pair], c).wait()
-
-
-def attend_call(n_ctx, q, k, v, seg_col, seg_row):
-    length, width = q.shape
-    tb = TOKEN_BLOCK
+            ctx_copy(o_ref.at[0:tb, cols], home(pair), o_send.at[k, pair], o_recv.at[k, pair], c).wait()
+    for w in late:
+        w.cross()
+    for k in range(1, n_ctx):
+        mark_copy(k).wait_send()
+        pack_copy(k).wait_send()
+        fv_copy(k).wait_send()
+    for at, (slot, bit) in enumerate(
+        [(0, NEAR), (0, FAR), (NEAR, FAR), (0, CORE), (NEAR, CORE), (FAR, CORE), (NEAR | FAR, CORE)]
+    ):
+        pack_hop(slot, bit, 3 + at).wait_send()
+    for way in range(2):
+        for step in range(3):
+            tok_copy(way, step).wait_send()
+    for w in weights:
+        w.finish()
+
+
+def front_call(n_dp, n_ctx, tok, fv, mark, pack, freq, wg, wu, wo, wd):
+    tb, model = tok.shape
+    width = model // n_ctx
+    length = n_ctx * tb
     pairs = width // LANES
     vmem = pl.BlockSpec(memory_space=pltpu.VMEM)
+    anyspace = pl.BlockSpec(memory_space=pl.ANY)
+    shape = jax.ShapeDtypeStruct
+    dma = pltpu.SemaphoreType.DMA
     return pl.pallas_call(
-        functools.partial(attend_kernel, n_ctx),
-        in_specs=[vmem] * 5,
-        out_specs=[pl.BlockSpec(memory_space=pl.ANY), vmem, vmem],
-        out_shape=[
-            jax.ShapeDtypeStruct((tb, n_ctx * width), LOW),
-            jax.ShapeDtypeStruct((length, width), F32),
-            jax.ShapeDtypeStruct((length, width), F32),
-        ],
+        functools.partial(front_kernel, n_ctx),
+        in_specs=[anyspace] * 4 + [vmem] + [anyspace] * 4,
+        out_specs=[vmem] * 11 + [anyspace] * 5,
+        out_shape=[shape((length, model), LOW)]
+        + [shape((length, width), LOW)] * 3
+        + [shape((length, width), F32)] * 2
+        + [shape((length, LANES), F32)] * 3
+        + [shape((8, length), jnp.int32), shape((8, model), F32)]
+        + [shape((tb, model), LOW)]
+        + [shape((n_dp, n_ctx * w.shape[0], w.shape[1]), LOW) for w in (wg, wu, wo, wd)],
         scratch_shapes=[
+            pltpu.VMEM((length, model), LOW),
+            pltpu.VMEM((length, width), LOW),
+            pltpu.VMEM((n_dp,) + pack.shape, LOW),
+            pltpu.VMEM((model, 3 * width), LOW),
+            pltpu.VMEM((tb // 2, model), F32),
             pltpu.VMEM((length, width), LOW),
             pltpu.VMEM((tb, length), F32),
             pltpu.VMEM((tb, LANES), F32),
             pltpu.VMEM((tb, LANES), F32),
             pltpu.VMEM((tb, LANES), F32),
-            pltpu.SemaphoreType.DMA((n_ctx - 1, pairs)),
-            pltpu.SemaphoreType.DMA((n_ctx - 1, pairs)),
-            pltpu.SemaphoreType.DMA((pairs,)),
+            dma((n_ctx - 1,)), dma((n_ctx - 1,)),
+            dma((n_ctx + 6,)), dma((n_ctx + 6,)),
+            dma((2, n_ctx - 1)), dma((2, n_ctx - 1)),
+            dma((n_ctx - 1,)), dma((n_ctx - 1,)),
+            dma((4, 11)), dma((4, 11)),
+            dma((n_ctx - 1, pairs)), dma((n_ctx - 1, pairs)),
+            dma((4,)), dma((pairs,)),
         ],
         compiler_params=params(collective_id=1, has_side_effects=True),
         cost_estimate=pl.CostEstimate(
-            flops=16 * 10**9, bytes_accessed=12 * 2**20, transcendentals=2 * length * length
+            flops=24 * 10**9, bytes_accessed=60 * 2**20, transcendentals=2 * length * length
         ),
-        name="attend",
-    )(q, k, v, seg_col, seg_row)
+        name="front",
+    )(tok, fv, mark, pack, freq, wg, wu, wo, wd)
 
 
 def attend_back_kernel(
@@ -572,7 +796,7 @@
     tb = dk_acc.shape[0]
     length, width = q_ref.shape
     model = n_ctx * width
-    meet_ctx(n_ctx)
+    meet(n_ctx, ())
 
     def grad_copy(k, to):
         rows = pl.ds(pl.multiple_of(c * tb, tb), tb)
@@ -634,7 +858,7 @@
                 at = pl.ds(pl.multiple_of(i * tb, tb), tb)
                 q = q_ref[at, cols]
                 g = g_ref[at, cols]
-                ok = seg_k == sr_ref[0:1, at]
+                ok = seg_k == sr_ref[0:1, at].astype(F32)
                 if causal:
                     r = lax.broadcasted_iota(jnp.int32, (tb, tb), 0)
                     t = lax.broadcasted_iota(jnp.int32, (tb, tb), 1)
@@ -719,27 +943,25 @@
 
 
 def mlp_kernel(blocks, tok_ref, att_ref, cot_ref, gain_ref, *refs):
-    pieces, refs = refs[: 3 * blocks], refs[3 * blocks :]
-    go_in, up_in, dn_in = pieces[:blocks], pieces[blocks : 2 * blocks], pieces[2 * blocks :]
+    (wo_in, wg_in, wu_in, wd_in), refs = refs[:4], refs[4:]
     out_ref, gm_ref, ga_ref, gk, gs, uk, us, ok, os, dk, ds = refs[:11]
     wo, wg, wu, wd, att, nat, n2, mi, mit, inv_ref, oacc, dacc, dwd, sem, osem = refs[11:]
     dp = lax.axis_index("dp")
     u = pl.program_id(0)
     last = pl.num_programs(0) - 1
-    ff = wu.shape[1]
-    down = dn_in[0].shape[0]
+    down = wd_in.shape[1]
 
     def copies():
         made = []
         for d in range(blocks):
             at = pl.ds(d * LANES, LANES)
-            made.append(pltpu.make_async_copy(go_in[d].at[:, pl.ds(ff, wo.shape[1])], wo.at[at, :], sem.at[0, d]))
+            made.append(pltpu.make_async_copy(wo_in.at[d], wo.at[at, :], sem.at[0, d]))
         for d in range(blocks):
             at = pl.ds(d * LANES, LANES)
-            made.append(pltpu.make_async_copy(go_in[d].at[:, pl.ds(0, ff)], wg.at[at, :], sem.at[1, d]))
-            made.append(pltpu.make_async_copy(up_in[d], wu.at[at, :], sem.at[2, d]))
+            made.append(pltpu.make_async_copy(wg_in.at[d], wg.at[at, :], sem.at[1, d]))
+            made.append(pltpu.make_async_copy(wu_in.at[d], wu.at[at, :], sem.at[2, d]))
             rows = pl.ds(pl.multiple_of((dp ^ d) * down, 32), down)
-            made.append(pltpu.make_async_copy(dn_in[d], wd.at[rows, :], sem.at[3, d]))
+            made.append(pltpu.make_async_copy(wd_in.at[d], wd.at[rows, :], sem.at[3, d]))
         return made
 
     def out_copies():
@@ -817,12 +1039,11 @@
             c.wait()
 
 
-def mlp_call(tok, att, cot, gain, go, up, dn):
+def mlp_call(tok, att, cot, gain, wo, wg, wu, wd):
     tb, model = tok.shape
-    blocks = len(go)
-    ff = up[0].shape[1]
+    blocks, _, ff = wg.shape
     half = blocks // 2
-    down = dn[0].shape[0]
+    down = wd.shape[1]
     whole = lambda a: pl.BlockSpec(a.shape, lambda u: (0, 0))
     anyspace = pl.BlockSpec(memory_space=pl.ANY)
     half_cols = pl.BlockSpec((half, LANES, FF_BLOCK), lambda u: (0, 0, u))
@@ -832,7 +1053,7 @@
     return pl.pallas_call(
         functools.partial(mlp_kernel, blocks),
         grid=(ff // FF_BLOCK,),
-        in_specs=[whole(tok), whole(att), whole(cot), whole(gain)] + [anyspace] * (3 * blocks),
+        in_specs=[whole(tok), whole(att), whole(cot), whole(gain)] + [anyspace] * 4,
         out_specs=[tokens, tokens, tokens] + [half_cols] * 4 + [half_out] * 2 + [anyspace] * 2,
         out_shape=[shape((tb, model), LOW), shape((tb, model), F32), shape((tb, model), LOW)]
         + [shape((half, LANES, ff), LOW)] * 4
@@ -860,7 +1081,7 @@
             flops=2 * tb * model * (8 * ff + 3 * model), bytes_accessed=50 * 2**20, transcendentals=0
         ),
         name="mlp",
-    )(tok, att, cot, gain, *go, *up, *dn)
+    )(tok, att, cot, gain, wo, wg, wu, wd)
 
 
 def input_kernel(blocks, tok_ref, gm_ref, v1_ref, gain_ref, g, *refs):
@@ -960,43 +1181,25 @@
     def gather_ctx(x):
         return lax.all_gather(x, "ctx", axis=0, tiled=True)
 
+    pairs = width // LANES
     tok = tokens[0]
-    row_tokens = gather_ctx(tok)
-    marks = jnp.concatenate([segment_ids, positions], axis=0)
-    marks = place([marks] + [shift(marks, k) for k in range(1, n_ctx)], 1)
-    head_first = place(swap_ctx(first_values[0], 1), 0)
-
+    mark = jnp.concatenate([segment_ids, positions, jnp.zeros((6, seq), jnp.int32)], axis=0)
     gains = jnp.stack([attn_gain, mlp_gain], axis=1)
     gains = jnp.tile(jnp.pad(gains, ((0, 0), (0, width - 2))), (1, n_ctx))
-    packed = jnp.stack([w_query, w_key, w_value, gains])
-    slots = jnp.stack(swap_ctx(packed, 2))
-    slots = place([slots[k : k + 1] for k in range(n_ctx)], 0)
-    slots = jnp.stack(gather_dp(slots, plane + bits[:1]))
-    packed_all = slots.reshape(n_dp * n_ctx, 4, own_rows, width)
-    head_weights = packed_all[:, :3].transpose(0, 2, 1, 3).reshape(model, 3 * width)
-    gain_rel = packed_all[:, 3, :, 0].reshape(1, model).astype(F32)
-    gain_two_rel = packed_all[:, 3, :, 1].reshape(1, model).astype(F32)
-
-    go = gather_ctx(jnp.concatenate([w_gate, w_out], axis=1))
-    up = gather_ctx(w_up)
-    dn = gather_ctx(w_down)
-    go = gather_dp(go, plane + bits[:1])
-    up = gather_dp(up, plane[::-1] + bits[:1])
-    dn = gather_dp(dn, plane[::-1] + bits[:1])
-
-    seg_row = jnp.broadcast_to(marks[0:1], (8, length))
-    seg_col = jnp.broadcast_to(marks[0][:, None], (length, LANES))
+    pack = jnp.concatenate([w_query, w_key, w_value, gains], axis=0)
+    pack = pack.reshape(4 * own_rows, n_ctx, width).transpose(1, 0, 2)
     freqs = 10000.0 ** (-jnp.arange(HEAD_DIM // 2).astype(F32) * (2.0 / HEAD_DIM))
-    angles = marks[1].astype(F32)[:, None] * freqs
-    cos, sin = jnp.cos(angles), jnp.sin(angles)
-    cos = jnp.concatenate([cos] * 4, axis=1)
-    sin = jnp.concatenate([-sin, sin] * 2, axis=1)
-    xn, q, k, v = qkv_call(row_tokens, head_weights, gain_rel, head_first, cos, sin)
-    pairs = width // LANES
-    attended, out_full, log_total = attend_call(n_ctx, q, k, v, seg_col, seg_row)
+    turn = jnp.ones((HEAD_DIM // 2,), F32)
+    freq = jnp.stack([jnp.tile(freqs, 4), jnp.tile(jnp.concatenate([-turn, turn]), 2)])
+    freq = jnp.pad(freq, ((0, 6), (0, 0)))
+    (xn, q, k, v, out_full, log_total, cos, sin, seg_col, seg_row, gain_rows, attended,
+     gate_all, up_all, out_all, down_all) = front_call(
+        n_dp, n_ctx, tok, first_values[0], mark, pack, freq, w_gate, w_up, w_out, w_down
+    )
+    gain_rel, gain_two_rel = gain_rows[0:1], gain_rows[1:2]
     cot = cotangent[0]
     (output, grad_middle, grad_attended, gate_keep, gate_send, up_keep, up_send, out_keep, out_send,
-     down_keep, down_send) = mlp_call(tok, attended, cot, gain_two_rel, go, up, dn)
+     down_keep, down_send) = mlp_call(tok, attended, cot, gain_two_rel, out_all, gate_all, up_all, down_all)
 
     qkv_all = gather_dp(gather_ctx(jnp.concatenate([w_query, w_key, w_value], axis=1)), plane + bits[:1])
 

time: 736 us -> 650 us (0.88)
  Pallas kernels: 247 us -> 385 us
  waiting for transfers between devices: 199 us -> 104 us
  blocking collectives: 110 us -> 16.6 us
  starting transfers between devices: 72.8 us -> 54.8 us
  between operations: 15.3 us -> 1.56 us
  local copies, waits for them, and re-layouts: 40.3 us -> 31.4 us
    pallas_call x2 -> x1, Pallas kernels: 68.3 us -> 204 us  [front_call(): pl.pallas_call(functools.partial(front_kernel, n_ctx), in_specs=[anyspace...]
    all_gather x4 -> x1, blocking collectives: 110 us -> 16.6 us  [gather_ctx(): return lax.all_gather(x, 'ctx', axis=0, tiled=True)]
    ppermute x53 -> x25, waiting for transfers between devices: 152 us -> 80.8 us  [flip(): return lax.ppermute(x, 'dp', [(i, i ^ bit) for i in range(n_dp)])]
    ppermute x27 -> x18, waiting for transfers between devices: 46.7 us -> 23.1 us  [shift(): return lax.ppermute(x, 'ctx', [(i, (i + k) % n_ctx) for i in range(n_ctx)])]
    ppermute x27 -> x18, starting transfers between devices: 36.2 us -> 27.1 us  [shift(): return lax.ppermute(x, 'ctx', [(i, (i + k) % n_ctx) for i in range(n_ctx)])]
    ppermute x53 -> x25, starting transfers between devices: 36.6 us -> 27.6 us  [flip(): return lax.ppermute(x, 'dp', [(i, i ^ bit) for i in range(n_dp)])]
  transfers between devices with their start and end apart: 81 -> 43, of which waited for: 24 -> 14; matrix products, arithmetic and copies ran while one was open for 11% -> 10% of each run, Pallas kernels for 34% -> 21%
where the time goes in v3:
time: 650 us; the launch traced here: 637 us
  Pallas kernels  385 us (59%)
  waiting for transfers between devices  104 us (16%)
  starting transfers between devices  54.8 us (8%)
  other arithmetic  36.9 us (6%)
  local copies, waits for them, and re-layouts  31.4 us (5%)
  blocking collectives  16.6 us (3%)
  matrix products  7.54 us (1%)
    pallas_call x1, Pallas kernels, front_call(): pl.pallas_call(functools.partial(front_kernel, n_ctx), in_specs=[anyspace...  204 us
    pallas_call x1, Pallas kernels, attend_back_call(): pl.pallas_call(functools.partial(attend_back_kernel, n_ctx), in_specs=[pl...  120 us
    ppermute x25, waiting for transfers between devices, flip(): return lax.ppermute(x, 'dp', [(i, i ^ bit) for i in range(n_dp)])  80.8 us
    pallas_call x1, Pallas kernels, mlp_call(): pl.pallas_call(functools.partial(mlp_kernel, blocks), grid=(ff // FF_BLOC...  47.5 us
    ppermute x25, starting transfers between devices, flip(): return lax.ppermute(x, 'dp', [(i, i ^ bit) for i in range(n_dp)])  27.6 us
    ppermute x18, starting transfers between devices, shift(): return lax.ppermute(x, 'ctx', [(i, (i + k) % n_ctx) for i in range(n_ctx)])  27.1 us
    ppermute x18, waiting for transfers between devices, shift(): return lax.ppermute(x, 'ctx', [(i, (i + k) % n_ctx) for i in range(n_ctx)])  23.1 us
    convert_element_type x12, other arithmetic, scatter_dp(): got = flip(pick(leave).astype(LOW), bit)  18.3 us
  transfers between devices with their start and end apart: 43, of which 14 were waited for; matrix products, arithmetic and copies ran while one was open for 10% of the time, Pallas kernels for 21%

profile of v3, /device:TPU:27, one launch (start us, length us, event | category | flops | bytes accessed | tf_op | source)
XLA Modules:
  0.0 637.4 jit_solution(4490283542487522383)
XLA Ops:
  4.7 1.4 add_add_fusion.mark_ref
  6.8 204.2 %front.1 = (bf16[2048,1024]{1,0:T(8,128)(2,1)}, bf16[2048,256]{1,0:T(8,128)(2,1)}, bf16[2048,256]{1,0:T(8,128)(2,1)}, bf16[2048,256]{1,0:T(8,128)(2,1)}, f32[204...) custom-call(bf16[512,1024]{1,0:T(8,128)(2,1)} %bitcast.161, ...), custom_call_target="tpu_custom_call" | custom-call | flops 24000000000 | bytes 62914560 | tf_op jit(solution)/shard_map/front/pallas_call | solution.py:753
  211.0 1.4 fusion.48
  212.4 47.5 %mlp.1 = (bf16[512,1024]{1,0:T(8,128)(2,1)}, f32[512,1024]{1,0:T(8,128)}, bf16[512,1024]{1,0:T(8,128)(2,1)}, bf16[4,128,2816]{2,1,0:T(8,128)(2,1)}, bf16[4,128,2...) custom-call(bf16[512,1024]{1,0:T(8,128)(2,1)} %bitcast.162, ...), custom_call_target="tpu_custom_call" | custom-call | flops 26843545600 | bytes 52428800 | tf_op jit(solution)/shard_map/mlp/pallas_call | solution.py:1053
  260.7 120.5 %attend_back.1 = (bf16[2,2048,384]{2,1,0:T(8,128)(2,1)}, bf16[512,3072]{1,0:T(8,128)(2,1)}) custom-call(bf16[512,1024]{1,0:T(8,128)(2,1)} %get-tuple-element.51.ga_ref, bf16[2048,256]{1,0:T(8,128)(2,1)} %get-tuple-element.52.q_ref, bf16[2048,256]{1,0:T(8,128)(2,1)} %get-tuple-element.53.k_ref, bf16[2048,256]{1,0:T(8,128)(2,1)} %get-tuple-element.54.v_ref, ...), custom_call_target="tpu_custom_call" | custom-call | flops 40000000000 | bytes 16777216 | tf_op jit(solution)/shard_map/attend_back/pallas_call | solution.py:916
  381.2 5.2 fusion.9
  387.2 2.4 fusion.6
  391.5 1.1 copy-done.1
  392.7 16.6 %all_gather.3.refs_0_ = bf16[128,3072]{1,0:T(8,128)(2,1)S(1)} all-gather(bf16[32,3072]{1,0:T(8,128)(2,1)S(1)} %pad_maximum_fusion), channel_id=1, replica_groups=mesh['dp'=8,'ctx'=4] {'ctx'}, dimensions={0}, use_global_device_ids=true | all-gather | bytes 983040 | tf_op jit(solution)/shard_map/all_gather | solution.py:1182
  412.7 1.3 collective-permute-start.8
  415.4 1.9 collective-permute-done.8
  418.3 1.3 collective-permute-start.9
  419.6 2.4 collective-permute-done.14
  422.1 1.6 fusion.20
  423.7 1.2 collective-permute-start.15
  427.1 1.5 collective-permute-done.15
  428.7 1.0 fusion.18
  431.3 1.4 reshape.215
  432.7 1.4 reshape.212
  434.1 3.3 collective-permute-start.16
  437.4 1.4 reshape.213
  440.5 3.8 collective-permute-start.25
  444.3 1.4 reshape.214
  446.1 1.4 reshape.216
  449.2 1.6 collective-permute-start.18
  450.8 2.2 add_convert_fusion.6
  453.0 1.2 collective-permute-start.20
  454.2 1.4 reshape.217
  456.4 1.4 reshape.218
  459.4 6.8 %collective-permute-done.20 = bf16[2,128,1024]{2,1,0:T(8,128)(2,1)} collective-permute-done((bf16[2,128,1024]{2,1,0:T(8,128)(2,1)}, bf16[2,128,1024]{2,1,0:T(8,128)(2,1)}, u32[]{:S(2)}, u32[]{:S(2)}) %collective-permute-start.20) | collective-permute-done | bytes 524320 | tf_op jit(solution)/shard_map/ppermute | solution.py:1156
  466.2 1.2 add_convert_fusion.7
  469.7 9.7 %collective-permute-done.21 = bf16[1,128,1024]{2,1,0:T(8,128)(2,1)S(1)} collective-permute-done((bf16[1,128,1024]{2,1,0:T(8,128)(2,1)S(1)}, bf16[1,128,1024]{2,1,0:T(8,128)(2,1)S(1)}, u32[]{:S(2)}, u32[]{:S(2)}) %collective-permute-start.21) | collective-permute-done | bytes 262176 | tf_op jit(solution)/shard_map/ppermute | solution.py:1156
  479.7 1.3 convert_add_fusion.3
  481.1 2.1 collective-permute-start
  483.1 1.2 collective-permute-start.5
  484.3 1.4 fusion.42
  486.2 3.0 add_convert_fusion.1
  489.2 7.6 %collective-permute-done.3.refs_4_ = bf16[128,3072]{1,0:T(8,128)(2,1)S(1)} collective-permute-done((bf16[128,3072]{1,0:T(8,128)(2,1)S(1)}, bf16[128,3072]{1,0:T(8,128)(2,1)S(1)}, u32[]{:S(2)}, u32[]{:S(2)}) %collective-permute-start.3) | collective-permute-done | bytes 786464 | tf_op jit(solution)/shard_map/ppermute | solution.py:1156
  496.7 1.8 collective-permute-start.22
  498.5 1.8 add_convert_fusion
  500.2 5.3 collective-permute-start.4
  505.5 8.1 %collective-permute-done.5.refs_6_ = bf16[128,3072]{1,0:T(8,128)(2,1)S(1)} collective-permute-done((bf16[128,3072]{1,0:T(8,128)(2,1)}, bf16[128,3072]{1,0:T(8,128)(2,1)S(1)}, u32[]{:S(2)}, u32[]{:S(2)}) %collective-permute-start.5) | collective-permute-done | bytes 786464 | tf_op jit(solution)/shard_map/ppermute | solution.py:1156
  513.6 2.7 collective-permute-start.6
  518.1 1.4 fusion.44
  519.5 2.8 collective-permute-done.23
  522.3 1.4 add_convert_fusion.2
  523.8 3.5 collective-permute-done.24
  529.8 12.5 %input_grad.1 = (f32[512,1024]{1,0:T(8,128)}, f32[512,1024]{1,0:T(8,128)}) custom-call(bf16[512,1024]{1,0:T(8,128)(2,1)} %bitcast.163, f32[512,1024]{1,0:T(8,128)} %get-tuple-element.50.gm_ref, f32[512,1024]{1,0:T(8,128)} %bitcast.160, f32[1,1024]{1,0:T(1,128)} %get-tuple-element.124.gain_ref, bf16[512,3072]{1,0:T(8,128)(2,1)} %get-tuple-element.61.g, ...), custom_call_target="tpu_custom_call" | custom-call | flops 3221225472 | bytes 20971520 | tf_op jit(solution)/shard_map/input_grad/pallas_call | solution.py:1119
  542.3 7.7 %collective-permute-done.38 = bf16[2,352,1024]{2,1,0:T(8,128)(2,1)} collective-permute-done((bf16[2,352,1024]{2,1,0:T(8,128)(2,1)}, bf16[2,352,1024]{2,1,0:T(8,128)(2,1)}, u32[]{:S(2)}, u32[]{:S(2)}) %collective-permute-start.38) | collective-permute-done | bytes 1441824 | tf_op jit(solution)/shard_map/ppermute | solution.py:1156
  550.1 1.7 add_convert_fusion.3
  552.2 1.8 add_convert_fusion.4
  554.9 26.1 %collective-permute-done.26 = bf16[2,128,2816]{2,1,0:T(8,128)(2,1)} collective-permute-done((bf16[2,128,2816]{2,1,0:T(8,128)(2,1)}, bf16[2,128,2816]{2,1,0:T(8,128)(2,1)}, u32[]{:S(2)}, u32[]{:S(2)}) %collective-permute-start.26) | collective-permute-done | bytes 1441824 | tf_op jit(solution)/shard_map/ppermute | solution.py:1156
  581.0 1.6 add_convert_fusion.5
  582.9 1.8 convert_add_fusion
  584.8 2.1 collective-permute-start.40
  587.3 9.0 %collective-permute-done.33 = bf16[1,128,2816]{2,1,0:T(8,128)(2,1)S(1)} collective-permute-done((bf16[1,128,2816]{2,1,0:T(8,128)(2,1)S(1)}, bf16[1,128,2816]{2,1,0:T(8,128)(2,1)S(1)}, u32[]{:S(2)}, u32[]{:S(2)}) %collective-permute-start.33) | collective-permute-done | bytes 720928 | tf_op jit(solution)/shard_map/ppermute | solution.py:1156
  596.3 1.7 convert_add_fusion.1
  598.1 2.1 collective-permute-start.34
  601.3 1.7 convert_add_fusion.2
  603.1 3.8 collective-permute-start.28
  606.9 8.4 %collective-permute-done.35 = bf16[32,2816]{1,0:T(8,128)(2,1)S(1)} collective-permute-done((bf16[32,2816]{1,0:T(8,128)(2,1)S(1)}, bf16[32,2816]{1,0:T(8,128)(2,1)S(1)}, u32[]{:S(2)}, u32[]{:S(2)}) %collective-permute-start.35) | collective-permute-done | bytes 180256 | tf_op jit(solution)/shard_map/ppermute | solution.py:1153
  615.3 7.6 %collective-permute-start.30 = (bf16[32,2816]{1,0:T(8,128)(2,1)S(1)}, bf16[32,2816]{1,0:T(8,128)(2,1)S(1)}, u32[]{:S(2)}, u32[]{:S(2)}) collective-permute-start(bf16[32,2816]{1,0:T(8,128)(2,1)S(1)} %get-tuple-element.99), channel_id=1, source_target_pairs={{0,3},{1,0},{2,1},{3,2},{4,7},{5,4},{6,5},{7,6},{8,11},{9,8},{10,9... | collective-permute-start | bytes 540680 | tf_op jit(solution)/shard_map/ppermute | solution.py:1153
  623.9 2.3 collective-permute-start.42
  626.2 8.5 %collective-permute-done.29 = bf16[32,2816]{1,0:T(8,128)(2,1)S(1)} collective-permute-done((bf16[32,2816]{1,0:T(8,128)(2,1)S(1)}, bf16[32,2816]{1,0:T(8,128)(2,1)S(1)}, u32[]{:S(2)}, u32[]{:S(2)}) %collective-permute-start.29) | collective-permute-done | bytes 180256 | tf_op jit(solution)/shard_map/ppermute | solution.py:1153
  (161 shorter events, 38.4 us)
Async XLA Ops:
  259.9 223.2 %collective-permute-start.37 = (bf16[4,352,1024]{2,1,0:T(8,128)(2,1)}, bf16[4,352,1024]{2,1,0:T(8,128)(2,1)}, u32[]{:S(2)}, u32[]{:S(2)}) collective-permute-start(bf16[4,352,1024]{2,1,0:T(8,128)(2,1)} %get-tuple-element.73), channel_id=1, source_target_pairs={{0,4},{4,0},{8,12},{12,8},{16,20},{20,16},{24,28},{28,24},{1,5},{5... | collective-permute-start | bytes 8650760 | tf_op jit(solution)/shard_map/ppermute | solution.py:1156
  260.2 225.6 %collective-permute-start.31 = (bf16[4,128,2816]{2,1,0:T(8,128)(2,1)}, bf16[4,128,2816]{2,1,0:T(8,128)(2,1)}, u32[]{:S(2)}, u32[]{:S(2)}) collective-permute-start(bf16[4,128,2816]{2,1,0:T(8,128)(2,1)} %get-tuple-element.71), channel_id=1, source_target_pairs={{0,4},{4,0},{8,12},{12,8},{16,20},{20,16},{24,28},{28,24},{1,5},{5... | collective-permute-start | bytes 8650760 | tf_op jit(solution)/shard_map/ppermute | solution.py:1156
  260.5 188.7 %collective-permute-start.19 = (bf16[4,128,1024]{2,1,0:T(8,128)(2,1)}, bf16[4,128,1024]{2,1,0:T(8,128)(2,1)}, u32[]{:S(2)}, u32[]{:S(2)}) collective-permute-start(bf16[4,128,1024]{2,1,0:T(8,128)(2,1)} %get-tuple-element.67), channel_id=1, source_target_pairs={{0,4},{4,0},{8,12},{12,8},{16,20},{20,16},{24,28},{28,24},{1,5},{5... | collective-permute-start | bytes 3145736 | tf_op jit(solution)/shard_map/ppermute | solution.py:1156
  381.1 6.0 copy-start.26
  381.2 6.0 copy-start.27
  386.4 22.9 %copy-start.8 = (bf16[1024,384]{1,0:T(8,128)(2,1)}, bf16[1024,384]{1,0:T(8,128)(2,1)S(1)}, u32[]{:S(2)}) copy-start(bf16[1024,384]{1,0:T(8,128)(2,1)S(1)} %fusion.9) | copy-start | bytes 2359300
  386.4 4.1 copy-start.16
  386.4 4.1 copy-start.17
  386.4 27.6 %collective-permute-start.13 = (bf16[4,128,384]{2,1,0:T(8,128)(2,1)S(1)}, bf16[4,128,384]{2,1,0:T(8,128)(2,1)}, u32[]{:S(2)}, u32[]{:S(2)}) collective-permute-start(bf16[4,128,384]{2,1,0:T(8,128)(2,1)S(1)} %slice_bitcast_fusion), channel_id=1, source_target_pairs={{0,4},{4,0},{8,12},{12,8},{16,20},{20,16},{24,28},{28,24},{1,5},{5... | collective-permute-start | bytes 1179656 | tf_op jit(solution)/shard_map/ppermute | solution.py:1156
  389.5 20.5 %copy-start.9 = (bf16[1024,384]{1,0:T(8,128)(2,1)}, bf16[1024,384]{1,0:T(8,128)(2,1)S(1)}, u32[]{:S(2)}) copy-start(bf16[1024,384]{1,0:T(8,128)(2,1)S(1)} %fusion.6) | copy-start | bytes 2359300
  390.4 20.3 %collective-permute-start.7 = (bf16[4,128,384]{2,1,0:T(8,128)(2,1)}, bf16[4,128,384]{2,1,0:T(8,128)(2,1)}, u32[]{:S(2)}, u32[]{:S(2)}) collective-permute-start(bf16[4,128,384]{2,1,0:T(8,128)(2,1)} %slice_bitcast_fusion.1), channel_id=1, source_target_pairs={{0,4},{4,0},{8,12},{12,8},{16,20},{20,16},{24,28},{28,24},{1,5},{5... | collective-permute-start | bytes 1179656 | tf_op jit(solution)/shard_map/ppermute | solution.py:1156
  409.3 71.8 %copy-start = (bf16[128,3072]{1,0:T(8,128)(2,1)}, bf16[128,3072]{1,0:T(8,128)(2,1)S(1)}, u32[]{:S(2)}) copy-start(bf16[128,3072]{1,0:T(8,128)(2,1)S(1)} %all_gather.3.refs_0_) | copy-start | bytes 2359300
  410.7 4.3 copy-start.19
  410.7 4.3 copy-start.20
  412.7 4.6 collective-permute-start.8
  415.1 7.0 %collective-permute-start.14 = (bf16[2,128,384]{2,1,0:T(8,128)(2,1)S(1)}, bf16[2,128,384]{2,1,0:T(8,128)(2,1)S(1)}, u32[]{:S(2)}, u32[]{:S(2)}) collective-permute-start(bf16[2,128,384]{2,1,0:T(8,128)(2,1)S(1)} %add_convert_fusion.8), channel_id=1, source_target_pairs={{0,8},{4,12},{8,0},{12,4},{16,24},{20,28},{24,16},{28,20},{1,9},{5... | collective-permute-start | bytes 589832 | tf_op jit(solution)/shard_map/ppermute | solution.py:1156
  418.3 6.5 %collective-permute-start.9 = (bf16[1,128,384]{2,1,0:T(8,128)(2,1)S(1)}, bf16[1,128,384]{2,1,0:T(8,128)(2,1)S(1)}, u32[]{:S(2)}, u32[]{:S(2)}) collective-permute-start(bf16[1,128,384]{2,1,0:T(8,128)(2,1)S(1)} %fusion.23), channel_id=1, source_target_pairs={{0,16},{4,20},{8,24},{12,28},{16,0},{20,4},{24,8},{28,12},{1,17},{... | collective-permute-start | bytes 294920 | tf_op jit(solution)/shard_map/ppermute | solution.py:1156
  423.7 5.0 collective-permute-start.15
  427.1 5.6 collective-permute-start.10
  428.7 5.4 collective-permute-start.11
  432.7 7.7 %collective-permute-start.12 = (bf16[32,384]{1,0:T(8,128)(2,1)}, bf16[32,384]{1,0:T(8,128)(2,1)}, u32[]{:S(2)}, u32[]{:S(2)}) collective-permute-start(bf16[32,384]{1,0:T(8,128)(2,1)} %get-tuple-element.120), channel_id=1, source_target_pairs={{0,3},{1,0},{2,1},{3,2},{4,7},{5,4},{6,5},{7,6},{8,11},{9,8},{10,9... | collective-permute-start | bytes 73736 | tf_op jit(solution)/shard_map/ppermute | solution.py:1153
  434.1 11.6 %collective-permute-start.16 = (bf16[32,384]{1,0:T(8,128)(2,1)}, bf16[32,384]{1,0:T(8,128)(2,1)}, u32[]{:S(2)}, u32[]{:S(2)}) collective-permute-start(bf16[32,384]{1,0:T(8,128)(2,1)} %get-tuple-element.118), channel_id=1, source_target_pairs={{0,1},{1,2},{2,3},{3,0},{4,5},{5,6},{6,7},{7,4},{8,9},{9,10},{10,1... | collective-permute-start | bytes 73736 | tf_op jit(solution)/shard_map/ppermute | solution.py:1153
  440.5 77.2 %collective-permute-start.25 = (bf16[4,128,2816]{2,1,0:T(8,128)(2,1)}, bf16[4,128,2816]{2,1,0:T(8,128)(2,1)}, u32[]{:S(2)}, u32[]{:S(2)}) collective-permute-start(bf16[4,128,2816]{2,1,0:T(8,128)(2,1)} %get-tuple-element.69), channel_id=1, source_target_pairs={{0,4},{4,0},{8,12},{12,8},{16,20},{20,16},{24,28},{28,24},{1,5},{5... | collective-permute-start | bytes 8650760 | tf_op jit(solution)/shard_map/ppermute | solution.py:1156
  445.7 7.3 %collective-permute-start.17 = (bf16[32,384]{1,0:T(8,128)(2,1)}, bf16[32,384]{1,0:T(8,128)(2,1)}, u32[]{:S(2)}, u32[]{:S(2)}) collective-permute-start(bf16[32,384]{1,0:T(8,128)(2,1)} %get-tuple-element.117), channel_id=1, source_target_pairs={{0,2},{1,3},{2,0},{3,1},{4,6},{5,7},{6,4},{7,5},{8,10},{9,11},{10,... | collective-permute-start | bytes 73736 | tf_op jit(solution)/shard_map/ppermute | solution.py:1153
  447.5 6.7 %copy-start.21 = (f32[32,3,128]{2,1,0:T(4,128)S(1)}, f32[32,3,128]{2,1,0:T(4,128)}, u32[]{:S(2)}) copy-start(f32[32,3,128]{2,1,0:T(4,128)} %reshape.216) | copy-start | bytes 147460
  449.2 6.4 %collective-permute-start.18 = (bf16[32,384]{1,0:T(8,128)(2,1)}, bf16[32,384]{1,0:T(8,128)(2,1)}, u32[]{:S(2)}, u32[]{:S(2)}) collective-permute-start(bf16[32,384]{1,0:T(8,128)(2,1)} %get-tuple-element.116), channel_id=1, source_target_pairs={{0,3},{1,0},{2,1},{3,2},{4,7},{5,4},{6,5},{7,6},{8,11},{9,8},{10,9... | collective-permute-start | bytes 73736 | tf_op jit(solution)/shard_map/ppermute | solution.py:1153
  453.0 16.2 %copy-start.24 = (bf16[32]{0:T(256)(128)(2,1)S(1)}, bf16[32]{0:T(256)(128)(2,1)}, u32[]{:S(2)}) copy-start(bf16[32]{0:T(256)(128)(2,1)} %param.21) | copy-start | bytes 196
  453.0 13.2 %collective-permute-start.20 = (bf16[2,128,1024]{2,1,0:T(8,128)(2,1)}, bf16[2,128,1024]{2,1,0:T(8,128)(2,1)}, u32[]{:S(2)}, u32[]{:S(2)}) collective-permute-start(bf16[2,128,1024]{2,1,0:T(8,128)(2,1)} %add_convert_fusion.6), channel_id=1, source_target_pairs={{0,16},{4,20},{8,24},{12,28},{16,0},{20,4},{24,8},{28,12},{1,17},{... | collective-permute-start | bytes 1572872 | tf_op jit(solution)/shard_map/ppermute | solution.py:1156
  455.6 25.5 %collective-permute-start.1 = (bf16[128,3072]{1,0:T(8,128)(2,1)S(1)}, bf16[128,3072]{1,0:T(8,128)(2,1)}, u32[]{:S(2)}, u32[]{:S(2)}) collective-permute-start(bf16[128,3072]{1,0:T(8,128)(2,1)S(1)} %all_gather.3.refs_0_), channel_id=1, source_target_pairs={{0,8},{4,12},{8,0},{12,4},{16,24},{20,28},{24,16},{28,20},{1,9},{5... | collective-permute-start | bytes 2359304 | tf_op jit(solution)/shard_map/ppermute | solution.py:1156
  467.5 11.9 %collective-permute-start.21 = (bf16[1,128,1024]{2,1,0:T(8,128)(2,1)S(1)}, bf16[1,128,1024]{2,1,0:T(8,128)(2,1)S(1)}, u32[]{:S(2)}, u32[]{:S(2)}) collective-permute-start(bf16[1,128,1024]{2,1,0:T(8,128)(2,1)S(1)} %add_convert_fusion.7), channel_id=1, source_target_pairs={{0,8},{4,12},{8,0},{12,4},{16,24},{20,28},{24,16},{28,20},{1,9},{5... | collective-permute-start | bytes 786440 | tf_op jit(solution)/shard_map/ppermute | solution.py:1156
  479.4 17.3 %collective-permute-start.3 = (bf16[128,3072]{1,0:T(8,128)(2,1)S(1)}, bf16[128,3072]{1,0:T(8,128)(2,1)S(1)}, u32[]{:S(2)}, u32[]{:S(2)}) collective-permute-start(bf16[128,3072]{1,0:T(8,128)(2,1)S(1)} %all_gather.3.refs_0_), channel_id=1, source_target_pairs={{0,16},{4,20},{8,24},{12,28},{16,0},{20,4},{24,8},{28,12},{1,17},{... | collective-permute-start | bytes 2359304 | tf_op jit(solution)/shard_map/ppermute | solution.py:1156
  481.0 5.2 copy-start.3
  481.1 19.2 %collective-permute-start = (bf16[128,3072]{1,0:T(8,128)(2,1)S(1)}, bf16[128,3072]{1,0:T(8,128)(2,1)S(1)}, u32[]{:S(2)}, u32[]{:S(2)}) collective-permute-start(bf16[128,3072]{1,0:T(8,128)(2,1)S(1)} %all_gather.3.refs_0_), channel_id=1, source_target_pairs={{0,4},{4,0},{8,12},{12,8},{16,20},{20,16},{24,28},{28,24},{1,5},{5... | collective-permute-start | bytes 2359304 | tf_op jit(solution)/shard_map/ppermute | solution.py:1156
  483.1 30.4 %collective-permute-start.5 = (bf16[128,3072]{1,0:T(8,128)(2,1)}, bf16[128,3072]{1,0:T(8,128)(2,1)S(1)}, u32[]{:S(2)}, u32[]{:S(2)}) collective-permute-start(bf16[128,3072]{1,0:T(8,128)(2,1)} %collective-permute-done.1.refs_2_), channel_id=1, source_target_pairs={{0,16},{4,20},{8,24},{12,28},{16,0},{20,4},{24,8},{28,12},{1,17},{... | collective-permute-start | bytes 2359304 | tf_op jit(solution)/shard_map/ppermute | solution.py:1156
  485.8 30.5 %collective-permute-start.2 = (bf16[128,3072]{1,0:T(8,128)(2,1)}, bf16[128,3072]{1,0:T(8,128)(2,1)S(1)}, u32[]{:S(2)}, u32[]{:S(2)}) collective-permute-start(bf16[128,3072]{1,0:T(8,128)(2,1)} %collective-permute-done.1.refs_2_), channel_id=1, source_target_pairs={{0,4},{4,0},{8,12},{12,8},{16,20},{20,16},{24,28},{28,24},{1,5},{5... | collective-permute-start | bytes 2359304 | tf_op jit(solution)/shard_map/ppermute | solution.py:1156
  486.2 12.3 %copy-start.7 = (bf16[1,352,1024]{2,1,0:T(8,128)(2,1)S(1)}, bf16[1,352,1024]{2,1,0:T(8,128)(2,1)}, u32[]{:S(2)}) copy-start(bf16[1,352,1024]{2,1,0:T(8,128)(2,1)} %get-tuple-element.87) | copy-start | bytes 2162692
  496.7 20.2 %collective-permute-start.22 = (bf16[32,1024]{1,0:T(8,128)(2,1)S(1)}, bf16[32,1024]{1,0:T(8,128)(2,1)S(1)}, u32[]{:S(2)}, u32[]{:S(2)}) collective-permute-start(bf16[32,1024]{1,0:T(8,128)(2,1)S(1)} %get-tuple-element.105), channel_id=1, source_target_pairs={{0,1},{1,2},{2,3},{3,0},{4,5},{5,6},{6,7},{7,4},{8,9},{9,10},{10,1... | collective-permute-start | bytes 196616 | tf_op jit(solution)/shard_map/ppermute | solution.py:1153
  500.2 19.2 %copy-start.11 = (bf16[128,3072]{1,0:T(8,128)(2,1)}, bf16[128,3072]{1,0:T(8,128)(2,1)S(1)}, u32[]{:S(2)}) copy-start(bf16[128,3072]{1,0:T(8,128)(2,1)S(1)} %collective-permute-done.refs_1_) | copy-start | bytes 2359300
  500.2 28.4 %collective-permute-start.4 = (bf16[128,3072]{1,0:T(8,128)(2,1)S(1)}, bf16[128,3072]{1,0:T(8,128)(2,1)S(1)}, u32[]{:S(2)}, u32[]{:S(2)}) collective-permute-start(bf16[128,3072]{1,0:T(8,128)(2,1)S(1)} %collective-permute-done.3.refs_4_), channel_id=1, source_target_pairs={{0,4},{4,0},{8,12},{12,8},{16,20},{20,16},{24,28},{28,24},{1,5},{5... | collective-permute-start | bytes 2359304 | tf_op jit(solution)/shard_map/ppermute | solution.py:1156
  513.6 5.9 copy-start.12
  513.6 15.1 %collective-permute-start.6 = (bf16[128,3072]{1,0:T(8,128)(2,1)S(1)}, bf16[128,3072]{1,0:T(8,128)(2,1)S(1)}, u32[]{:S(2)}, u32[]{:S(2)}) collective-permute-start(bf16[128,3072]{1,0:T(8,128)(2,1)S(1)} %collective-permute-done.5.refs_6_), channel_id=1, source_target_pairs={{0,4},{4,0},{8,12},{12,8},{16,20},{20,16},{24,28},{28,24},{1,5},{5... | collective-permute-start | bytes 2359304 | tf_op jit(solution)/shard_map/ppermute | solution.py:1156
  516.2 6.1 collective-permute-start.23
  516.9 33.1 %collective-permute-start.38 = (bf16[2,352,1024]{2,1,0:T(8,128)(2,1)}, bf16[2,352,1024]{2,1,0:T(8,128)(2,1)}, u32[]{:S(2)}, u32[]{:S(2)}) collective-permute-start(bf16[2,352,1024]{2,1,0:T(8,128)(2,1)} %add_convert_fusion), channel_id=1, source_target_pairs={{0,8},{4,12},{8,0},{12,4},{16,24},{20,28},{24,16},{28,20},{1,9},{5... | collective-permute-start | bytes 4325384 | tf_op jit(solution)/shard_map/ppermute | solution.py:1156
  517.7 34.5 %collective-permute-start.32 = (bf16[2,128,2816]{2,1,0:T(8,128)(2,1)}, bf16[2,128,2816]{2,1,0:T(8,128)(2,1)}, u32[]{:S(2)}, u32[]{:S(2)}) collective-permute-start(bf16[2,128,2816]{2,1,0:T(8,128)(2,1)} %add_convert_fusion.1), channel_id=1, source_target_pairs={{0,16},{4,20},{8,24},{12,28},{16,0},{20,4},{24,8},{28,12},{1,17},{... | collective-permute-start | bytes 4325384 | tf_op jit(solution)/shard_map/ppermute | solution.py:1156
  522.3 4.9 collective-permute-start.24
  527.2 53.7 %collective-permute-start.26 = (bf16[2,128,2816]{2,1,0:T(8,128)(2,1)}, bf16[2,128,2816]{2,1,0:T(8,128)(2,1)}, u32[]{:S(2)}, u32[]{:S(2)}) collective-permute-start(bf16[2,128,2816]{2,1,0:T(8,128)(2,1)} %add_convert_fusion.2), channel_id=1, source_target_pairs={{0,8},{4,12},{8,0},{12,4},{16,24},{20,28},{24,16},{28,20},{1,9},{5... | collective-permute-start | bytes 4325384 | tf_op jit(solution)/shard_map/ppermute | solution.py:1156
  529.8 20.2 %copy-start.6 = (bf16[4,352,1024]{2,1,0:T(8,128)(2,1)S(1)}, bf16[4,352,1024]{2,1,0:T(8,128)(2,1)}, u32[]{:S(2)}) copy-start(bf16[4,352,1024]{2,1,0:T(8,128)(2,1)} %get-tuple-element.72) | copy-start | bytes 8650756
  542.3 9.8 %copy-start.4 = (bf16[4,128,2816]{2,1,0:T(8,128)(2,1)S(1)}, bf16[4,128,2816]{2,1,0:T(8,128)(2,1)}, u32[]{:S(2)}) copy-start(bf16[4,128,2816]{2,1,0:T(8,128)(2,1)} %get-tuple-element.70) | copy-start | bytes 8650756
  551.8 29.2 %copy-start.2 = (bf16[4,128,2816]{2,1,0:T(8,128)(2,1)S(1)}, bf16[4,128,2816]{2,1,0:T(8,128)(2,1)}, u32[]{:S(2)}) copy-start(bf16[4,128,2816]{2,1,0:T(8,128)(2,1)} %get-tuple-element.68) | copy-start | bytes 8650756
  551.8 31.1 %collective-permute-start.39 = (bf16[1,352,1024]{2,1,0:T(8,128)(2,1)S(1)}, bf16[1,352,1024]{2,1,0:T(8,128)(2,1)S(1)}, u32[]{:S(2)}, u32[]{:S(2)}) collective-permute-start(bf16[1,352,1024]{2,1,0:T(8,128)(2,1)S(1)} %add_convert_fusion.3), channel_id=1, source_target_pairs={{0,16},{4,20},{8,24},{12,28},{16,0},{20,4},{24,8},{28,12},{1,17},{... | collective-permute-start | bytes 2162696 | tf_op jit(solution)/shard_map/ppermute | solution.py:1156
  553.9 42.4 %collective-permute-start.33 = (bf16[1,128,2816]{2,1,0:T(8,128)(2,1)S(1)}, bf16[1,128,2816]{2,1,0:T(8,128)(2,1)S(1)}, u32[]{:S(2)}, u32[]{:S(2)}) collective-permute-start(bf16[1,128,2816]{2,1,0:T(8,128)(2,1)S(1)} %add_convert_fusion.4), channel_id=1, source_target_pairs={{0,8},{4,12},{8,0},{12,4},{16,24},{20,28},{24,16},{28,20},{1,9},{5... | collective-permute-start | bytes 2162696 | tf_op jit(solution)/shard_map/ppermute | solution.py:1156
  582.6 17.9 %collective-permute-start.27 = (bf16[1,128,2816]{2,1,0:T(8,128)(2,1)S(1)}, bf16[1,128,2816]{2,1,0:T(8,128)(2,1)S(1)}, u32[]{:S(2)}, u32[]{:S(2)}) collective-permute-start(bf16[1,128,2816]{2,1,0:T(8,128)(2,1)S(1)} %add_convert_fusion.5), channel_id=1, source_target_pairs={{0,16},{4,20},{8,24},{12,28},{16,0},{20,4},{24,8},{28,12},{1,17},{... | collective-permute-start | bytes 2162696 | tf_op jit(solution)/shard_map/ppermute | solution.py:1156
  584.8 51.3 %collective-permute-start.40 = (bf16[88,1024]{1,0:T(8,128)(2,1)S(1)}, bf16[88,1024]{1,0:T(8,128)(2,1)S(1)}, u32[]{:S(2)}, u32[]{:S(2)}) collective-permute-start(bf16[88,1024]{1,0:T(8,128)(2,1)S(1)} %get-tuple-element.92), channel_id=1, source_target_pairs={{0,1},{1,2},{2,3},{3,0},{4,5},{5,6},{6,7},{7,4},{8,9},{9,10},{10,1... | collective-permute-start | bytes 540680 | tf_op jit(solution)/shard_map/ppermute | solution.py:1153
  586.9 49.2 %collective-permute-start.41 = (bf16[88,1024]{1,0:T(8,128)(2,1)S(1)}, bf16[88,1024]{1,0:T(8,128)(2,1)S(1)}, u32[]{:S(2)}, u32[]{:S(2)}) collective-permute-start(bf16[88,1024]{1,0:T(8,128)(2,1)S(1)} %get-tuple-element.94), channel_id=1, source_target_pairs={{0,2},{1,3},{2,0},{3,1},{4,6},{5,7},{6,4},{7,5},{8,10},{9,11},{10,... | collective-permute-start | bytes 540680 | tf_op jit(solution)/shard_map/ppermute | solution.py:1153
  598.1 5.0 collective-permute-start.34
  600.2 15.1 %collective-permute-start.35 = (bf16[32,2816]{1,0:T(8,128)(2,1)S(1)}, bf16[32,2816]{1,0:T(8,128)(2,1)S(1)}, u32[]{:S(2)}, u32[]{:S(2)}) collective-permute-start(bf16[32,2816]{1,0:T(8,128)(2,1)S(1)} %get-tuple-element.97), channel_id=1, source_target_pairs={{0,2},{1,3},{2,0},{3,1},{4,6},{5,7},{6,4},{7,5},{8,10},{9,11},{10,... | collective-permute-start | bytes 540680 | tf_op jit(solution)/shard_map/ppermute | solution.py:1153
  600.5 22.5 %copy-start.22 = (bf16[32,2816]{1,0:T(8,128)(2,1)S(1)}, bf16[32,2816]{1,0:T(8,128)(2,1)}, u32[]{:S(2)}) copy-start(bf16[32,2816]{1,0:T(8,128)(2,1)} %wu_ref.1) | copy-start | bytes 540676
  600.5 14.8 %collective-permute-start.36 = (bf16[32,2816]{1,0:T(8,128)(2,1)S(1)}, bf16[32,2816]{1,0:T(8,128)(2,1)S(1)}, u32[]{:S(2)}, u32[]{:S(2)}) collective-permute-start(bf16[32,2816]{1,0:T(8,128)(2,1)S(1)} %get-tuple-element.96), channel_id=1, source_target_pairs={{0,3},{1,0},{2,1},{3,2},{4,7},{5,4},{6,5},{7,6},{8,11},{9,8},{10,9... | collective-permute-start | bytes 540680 | tf_op jit(solution)/shard_map/ppermute | solution.py:1153
  603.0 31.6 %copy-start.23 = (bf16[32,2816]{1,0:T(8,128)(2,1)S(1)}, bf16[32,2816]{1,0:T(8,128)(2,1)}, u32[]{:S(2)}) copy-start(bf16[32,2816]{1,0:T(8,128)(2,1)} %wg_ref.1) | copy-start | bytes 540676
  603.1 20.8 %collective-permute-start.28 = (bf16[32,2816]{1,0:T(8,128)(2,1)S(1)}, bf16[32,2816]{1,0:T(8,128)(2,1)S(1)}, u32[]{:S(2)}, u32[]{:S(2)}) collective-permute-start(bf16[32,2816]{1,0:T(8,128)(2,1)S(1)} %get-tuple-element.98), channel_id=1, source_target_pairs={{0,1},{1,2},{2,3},{3,0},{4,5},{5,6},{6,7},{7,4},{8,9},{9,10},{10,1... | collective-permute-start | bytes 540680 | tf_op jit(solution)/shard_map/ppermute | solution.py:1153
  615.3 19.3 %collective-permute-start.29 = (bf16[32,2816]{1,0:T(8,128)(2,1)S(1)}, bf16[32,2816]{1,0:T(8,128)(2,1)S(1)}, u32[]{:S(2)}, u32[]{:S(2)}) collective-permute-start(bf16[32,2816]{1,0:T(8,128)(2,1)S(1)} %get-tuple-element.100), channel_id=1, source_target_pairs={{0,2},{1,3},{2,0},{3,1},{4,6},{5,7},{6,4},{7,5},{8,10},{9,11},{10,... | collective-permute-start | bytes 540680 | tf_op jit(solution)/shard_map/ppermute | solution.py:1153
  615.3 20.3 %copy-start.25 = (bf16[32]{0:T(256)(128)(2,1)S(1)}, bf16[32]{0:T(256)(128)(2,1)}, u32[]{:S(2)}) copy-start(bf16[32]{0:T(256)(128)(2,1)} %param.26) | copy-start | bytes 196
  615.3 19.3 %collective-permute-start.30 = (bf16[32,2816]{1,0:T(8,128)(2,1)S(1)}, bf16[32,2816]{1,0:T(8,128)(2,1)S(1)}, u32[]{:S(2)}, u32[]{:S(2)}) collective-permute-start(bf16[32,2816]{1,0:T(8,128)(2,1)S(1)} %get-tuple-element.99), channel_id=1, source_target_pairs={{0,3},{1,0},{2,1},{3,2},{4,7},{5,4},{6,5},{7,6},{8,11},{9,8},{10,9... | collective-permute-start | bytes 540680 | tf_op jit(solution)/shard_map/ppermute | solution.py:1153
  623.9 12.2 %collective-permute-start.42 = (bf16[88,1024]{1,0:T(8,128)(2,1)S(1)}, bf16[88,1024]{1,0:T(8,128)(2,1)S(1)}, u32[]{:S(2)}, u32[]{:S(2)}) collective-permute-start(bf16[88,1024]{1,0:T(8,128)(2,1)S(1)} %get-tuple-element.93), channel_id=1, source_target_pairs={{0,3},{1,0},{2,1},{3,2},{4,7},{5,4},{6,5},{7,6},{8,11},{9,8},{10,9... | collective-permute-start | bytes 540680 | tf_op jit(solution)/shard_map/ppermute | solution.py:1153
  (7 other events, 18.3 us)

commit v4 on v3

--- a/solution.py
+++ b/solution.py
@@ -16,7 +16,7 @@
 MESH = pl.DeviceIdType.MESH
 F32 = jnp.float32
 LOW = jnp.bfloat16
-BYTES = 60 * 2**20
+BYTES = 63 * 2**20
 epsilon = 1e-05
 
 
@@ -788,44 +788,129 @@
     )(tok, fv, mark, pack, freq, wg, wu, wo, wd)
 
 
-def attend_back_kernel(
-    n_ctx, ga_ref, q_ref, k_ref, v_ref, of_ref, lse_ref, sc_ref, sr_ref, cos_ref, sin_ref, out_ref, home_ref,
-    g_ref, lse_row, delta_row, dq_acc, dk_acc, dv_acc, gsend, grecv, send, recv, own,
-):
+class Reduce:
+    def __init__(self, n_ctx, keep, gone, acc, rc, rx, ry, rz, out, send, recv, order):
+        self.n, self.keep, self.gone, self.acc, self.rc, self.rx, self.ry, self.rz = n_ctx, keep, gone, acc, rc, rx, ry, rz
+        self.out, self.send, self.recv = out, send, recv
+        self.one, self.two = order
+        self.leave = (self.one >> 1, 3)
+        self.stay = self.two >> 1
+
+    def hop(self, at):
+        src, dst, bit = [
+            (self.gone, self.rc, CORE),
+            (self.acc.at[self.leave[0]], self.rx.at[0], self.one),
+            (self.acc.at[self.leave[1]], self.rx.at[1], self.one),
+            (self.acc.at[self.stay], self.ry, self.two),
+        ][at]
+        return dp_copy(src, dst, self.send.at[at], self.recv.at[at], bit)
+
+    def held(self):
+        return pltpu.make_async_copy(self.keep, self.acc, self.send.at[7])
+
+    def along(self, k):
+        to = lax.rem(lax.axis_index("ctx") + k, self.n)
+        return ctx_copy(self.acc.at[0, to], self.rz.at[k - 1], self.send.at[3 + k], self.recv.at[3 + k], to)
+
+    def begin(self):
+        self.hop(0).start()
+        self.held().start()
+
+    def add(self, block, terms):
+        def one(j, carry):
+            total = self.acc[block, j].astype(F32)
+            for t in terms:
+                total = total + t(j).astype(F32)
+            self.acc[block, j] = total.astype(LOW)
+            return carry
+
+        lax.fori_loop(0, self.acc.shape[1], one, 0)
+
+    def step_one(self):
+        self.held().wait()
+        self.hop(0).wait_recv()
+        for at in (1, 0):
+            block = self.leave[at]
+            self.add(block, [lambda j, block=block: self.rc[block, j]])
+            self.hop(1 + at).start()
+
+    def step_two(self):
+        self.hop(2).wait_recv()
+        self.add(self.stay, [lambda j: self.rc[self.stay, j], lambda j: self.rx[1, j]])
+        self.hop(3).start()
+
+    def step_ctx(self):
+        c = lax.axis_index("ctx")
+        self.hop(1).wait_recv()
+        self.hop(3).wait_recv()
+        self.out[...] = (
+            self.acc[0, c].astype(F32) + self.rc[0, c].astype(F32) + self.rx[0, c].astype(F32) + self.ry[c].astype(F32)
+        )
+        self.add(0, [lambda j: self.rc[0, j], lambda j: self.rx[0, j], lambda j: self.ry[j]])
+        for k in range(1, self.n):
+            self.along(k).start()
+
+    def finish(self):
+        for k in range(1, self.n):
+            self.along(k).wait_recv()
+            self.out[...] += self.rz[k - 1].astype(F32)
+        for at in range(4):
+            self.hop(at).wait_send()
+        for k in range(1, self.n):
+            self.along(k).wait_send()
+
+
+def back_kernel(n_ctx, *refs):
+    ga_ref, q_ref, k_ref, v_ref, of_ref, lse_ref, sc_ref, sr_ref, cos_ref, sin_ref, xn_ref = refs[:11]
+    sides = refs[11:19]
+    home_ref, qkv_out = refs[19:21]
+    outs = refs[21:25]
+    (g_ref, part_ref, lse_row, delta_row, dq_acc, dk_acc, dv_acc, prod) = refs[25:33]
+    rest = refs[33:]
+    buffers, rest = rest[:20], rest[20:]
+    (pk, ps, prc, prx, pry, pz, qz) = rest[:7]
+    (gsend, grecv, send, recv, own, r_send, r_recv, p_send, p_recv, z_send, z_recv) = rest[7:]
     c = lax.axis_index("ctx")
     tb = dk_acc.shape[0]
     length, width = q_ref.shape
     model = n_ctx * width
-    meet(n_ctx, ())
-
-    def grad_copy(k, to):
-        rows = pl.ds(pl.multiple_of(c * tb, tb), tb)
-        cols = pl.ds(pl.multiple_of(to * width, width), width)
-        return ctx_copy(ga_ref.at[:, cols], g_ref.at[rows, :], gsend.at[k - 1], grecv.at[k - 1], to)
+    pairs = width // LANES
+    blocks = model // LANES
+    near_first, far_first = (NEAR, FAR), (FAR, NEAR)
+    gate, up, out, down = [
+        Reduce(n_ctx, sides[2 * i], sides[2 * i + 1], *buffers[5 * i : 5 * i + 5], outs[i], r_send.at[i], r_recv.at[i], order)
+        for i, order in enumerate([near_first, far_first, near_first, far_first])
+    ]
+
+    def grad_copy(k):
+        to = lax.rem(c + k, n_ctx)
+        return ctx_copy(ga_ref.at[:, rows_of(to, width)], g_ref.at[rows_of(c, tb), :], gsend.at[k - 1], grecv.at[k - 1], to)
 
     def home(pair, t):
         return home_ref.at[:, pl.ds(pl.multiple_of(t * model + c * width + pair * LANES, LANES), LANES)]
 
     def part(pair, t, chunk):
-        rows = pl.ds(pl.multiple_of(chunk * tb, tb), tb)
-        return out_ref.at[pair, rows, t * LANES : (t + 1) * LANES]
+        return part_ref.at[pair, rows_of(chunk, tb), pl.ds(t * LANES, LANES)]
 
     def part_copy(pair, t, k):
         to = lax.rem(c + k, n_ctx)
         return ctx_copy(part(pair, t, to), home(pair, t), send.at[k - 1, pair, t], recv.at[k - 1, pair, t], to)
 
-    first = [grad_copy(k, lax.rem(c + k, n_ctx)) for k in range(1, n_ctx)]
-    for f in first:
-        f.start()
-    keep = pltpu.make_async_copy(
-        ga_ref.at[:, pl.ds(pl.multiple_of(c * width, width), width)],
-        g_ref.at[pl.ds(pl.multiple_of(c * tb, tb), tb), :],
-        own.at[0, 0],
-    )
+    def part_own(pair, t):
+        return pltpu.make_async_copy(part(pair, t, c), home(pair, t), own.at[pair, t])
+
+    meet(n_ctx, (CORE, NEAR, FAR))
+    for k in range(1, n_ctx):
+        grad_copy(k).start()
+    keep = pltpu.make_async_copy(ga_ref.at[:, rows_of(c, width)], g_ref.at[rows_of(c, tb), :], own.at[0, 0])
     keep.start()
+    for r in (gate, up, out, down):
+        r.begin()
+    for r in (gate, up, out, down):
+        r.step_one()
     keep.wait()
-    for f in first:
-        f.wait()
+    for k in range(1, n_ctx):
+        grad_copy(k).wait_recv()
 
     r8 = lax.broadcasted_iota(jnp.int32, (8, LANES), 0)
     l8 = lax.broadcasted_iota(jnp.int32, (8, LANES), 1)
@@ -833,29 +918,33 @@
     group = jnp.where(l8 // HEAD_DIM == r8, 1.0, 0.0)
     exact = lax.Precision.HIGHEST
     dims = (((1,), (1,)), ((), ()))
-    for pair in range(width // LANES):
+
+    def stats(pair):
         cols = slice(pair * LANES, (pair + 1) * LANES)
 
-        def stats(b, carry):
-            at = pl.ds(pl.multiple_of(b * tb, tb), tb)
+        def one(b, carry):
+            at = rows_of(b, tb)
             lse_row[:, at] = lax.dot_general(pick, lse_ref[at, cols], dims, precision=exact, preferred_element_type=F32)
-            prod = g_ref[at, cols].astype(F32) * of_ref[at, cols]
-            delta_row[:, at] = lax.dot_general(group, prod, dims, precision=exact, preferred_element_type=F32)
+            mixed = g_ref[at, cols].astype(F32) * of_ref[at, cols]
+            delta_row[:, at] = lax.dot_general(group, mixed, dims, precision=exact, preferred_element_type=F32)
             dq_acc[at, :] = jnp.zeros((tb, LANES), F32)
             return carry
 
-        lax.fori_loop(0, n_ctx, stats, 0)
+        lax.fori_loop(0, n_ctx, one, 0)
+
+    def key_blocks(pair, lo, hi):
+        cols = slice(pair * LANES, (pair + 1) * LANES)
 
         def key_block(j, carry):
             dk_acc[...] = jnp.zeros_like(dk_acc)
             dv_acc[...] = jnp.zeros_like(dv_acc)
-            mine = pl.ds(pl.multiple_of(j * tb, tb), tb)
+            mine = rows_of(j, tb)
             k = k_ref[mine, cols]
             v = v_ref[mine, cols]
             seg_k = sc_ref[mine, 0:1]
 
             def block(i, causal):
-                at = pl.ds(pl.multiple_of(i * tb, tb), tb)
+                at = rows_of(i, tb)
                 q = q_ref[at, cols]
                 g = g_ref[at, cols]
                 ok = seg_k == sr_ref[0:1, at].astype(F32)
@@ -883,69 +972,184 @@
             lax.fori_loop(j + 1, n_ctx, step, 0)
             dk = dk_acc[...]
             dk = dk * cos_ref[mine, :] - half_swap(dk) * sin_ref[mine, :]
-            out_ref[pair, mine, LANES : 2 * LANES] = dk.astype(LOW)
-            out_ref[pair, mine, 2 * LANES : 3 * LANES] = dv_acc[...].astype(LOW)
+            part_ref[pair, mine, LANES : 2 * LANES] = dk.astype(LOW)
+            part_ref[pair, mine, 2 * LANES : 3 * LANES] = dv_acc[...].astype(LOW)
             return carry
 
-        lax.fori_loop(0, n_ctx, key_block, 0)
-
+        lax.fori_loop(lo, hi, key_block, 0)
+
+    def send_home(pair):
         def query_done(b, carry):
-            at = pl.ds(pl.multiple_of(b * tb, tb), tb)
+            at = rows_of(b, tb)
             dq = dq_acc[at, :] * 0.125
             dq = dq * cos_ref[at, :] - half_swap(dq) * sin_ref[at, :]
-            out_ref[pair, at, 0:LANES] = dq.astype(LOW)
+            part_ref[pair, at, 0:LANES] = dq.astype(LOW)
             return carry
 
         lax.fori_loop(0, n_ctx, query_done, 0)
         for t in range(3):
-            pltpu.make_async_copy(part(pair, t, c), home(pair, t), own.at[pair, t]).start()
+            part_own(pair, t).start()
             for k in range(1, n_ctx):
                 part_copy(pair, t, k).start()
-    for pair in range(width // LANES):
+
+    def pair_hop(pair, at):
+        src, dst, bit = [
+            (ps.at[pair], prc.at[pair], CORE),
+            (pk.at[pair, 1], prx.at[pair, 0], NEAR),
+            (pk.at[pair, 3], prx.at[pair, 1], NEAR),
+            (pk.at[pair, 2], pry.at[pair], FAR),
+        ][at]
+        return dp_copy(src, dst, p_send.at[pair, at], p_recv.at[pair, at], bit)
+
+    def pair_ctx(pair, k):
+        to = lax.rem(c + k, n_ctx)
+        return ctx_copy(pz.at[pair, to], qz.at[c, pair], z_send.at[pair, k - 1], z_recv.at[pair, k - 1], to)
+
+    def pair_product(pair):
+        prod[...] = jnp.zeros_like(prod)
+
+        def one(b, carry):
+            at = rows_of(b, tb)
+            prod[...] += dot(part_ref[pair, at, :], xn_ref[at, :], 0, 0)
+            return carry
+
+        lax.fori_loop(0, n_ctx, one, 0)
+        for d in range(blocks):
+            (ps if d % 2 else pk)[pair, d // 2] = prod[:, d * LANES : (d + 1) * LANES].astype(LOW)
+        pair_hop(pair, 0).start()
+
+    def pair_one(pair):
+        pair_hop(pair, 0).wait_recv()
+        for i in (3, 1):
+            pk[pair, i] = (pk[pair, i].astype(F32) + prc[pair, i].astype(F32)).astype(LOW)
+            pair_hop(pair, 1 + i // 2).start()
+
+    def pair_two(pair):
+        pair_hop(pair, 2).wait_recv()
+        total = pk[pair, 2].astype(F32) + prc[pair, 2].astype(F32) + prx[pair, 1].astype(F32)
+        pk[pair, 2] = total.astype(LOW)
+        pair_hop(pair, 3).start()
+
+    def pair_three(pair):
+        pair_hop(pair, 1).wait_recv()
+        pair_hop(pair, 3).wait_recv()
+        total = pk[pair, 0].astype(F32) + prc[pair, 0].astype(F32) + prx[pair, 0].astype(F32) + pry[pair].astype(F32)
+        pz[pair] = total.T.reshape(pz.shape[1:]).astype(LOW)
+        qz[c, pair] = pz[pair, c]
+        for k in range(1, n_ctx):
+            pair_ctx(pair, k).start()
+
+    def pair_finish(pair):
+        for k in range(1, n_ctx):
+            pair_ctx(pair, k).wait()
+        for at in range(4):
+            pair_hop(pair, at).wait_send()
+
+    stats(0)
+    key_blocks(0, 0, n_ctx)
+    send_home(0)
+    pair_product(0)
+    stats(1)
+    key_blocks(1, 0, n_ctx // 2)
+    pair_one(0)
+    gate.step_two()
+    out.step_two()
+    key_blocks(1, n_ctx // 2, n_ctx)
+    send_home(1)
+    pair_product(1)
+    pair_two(0)
+    up.step_two()
+    down.step_two()
+    pair_one(1)
+    pair_three(0)
+    gate.step_ctx()
+    out.step_ctx()
+    pair_two(1)
+    up.step_ctx()
+    down.step_ctx()
+    pair_three(1)
+    for pair in range(pairs):
+        pair_finish(pair)
+        for s in range(n_ctx):
+            for t in range(3):
+                at = t * model + s * width + pair * LANES
+                qkv_out[:, at : at + LANES] = qz[s, pair, :, t * LANES : (t + 1) * LANES].astype(F32)
+    for k in range(1, n_ctx):
+        grad_copy(k).wait_send()
+    for r in (gate, out, up, down):
+        r.finish()
+    for pair in range(pairs):
         for t in range(3):
-            pltpu.make_async_copy(part(pair, t, c), home(pair, t), own.at[pair, t]).wait()
+            part_own(pair, t).wait()
             for k in range(1, n_ctx):
                 part_copy(pair, t, k).wait()
 
 
-def attend_back_call(n_ctx, ga, q, k, v, of, lse, seg_col, seg_row, cos, sin):
+def back_call(n_ctx, ga, q, k, v, of, lse, seg_col, seg_row, cos, sin, xn, sides):
     length, width = q.shape
+    model = n_ctx * width
     tb = TOKEN_BLOCK
     pairs = width // LANES
+    own_rows = model // (model // LANES) // n_ctx
     vmem = pl.BlockSpec(memory_space=pltpu.VMEM)
+    anyspace = pl.BlockSpec(memory_space=pl.ANY)
+    shape = jax.ShapeDtypeStruct
+    dma = pltpu.SemaphoreType.DMA
+    buffers = []
+    for keep in sides[::2]:
+        four, parts, rows, cols = keep.shape
+        buffers += [
+            pltpu.VMEM((four, parts, rows, cols), LOW),
+            pltpu.VMEM((four, parts, rows, cols), LOW),
+            pltpu.VMEM((2, parts, rows, cols), LOW),
+            pltpu.VMEM((parts, rows, cols), LOW),
+            pltpu.VMEM((parts - 1, rows, cols), LOW),
+        ]
+    wide = 3 * LANES
     return pl.pallas_call(
-        functools.partial(attend_back_kernel, n_ctx),
-        in_specs=[pl.BlockSpec(memory_space=pl.ANY)] + [vmem] * 9,
-        out_specs=[vmem, pl.BlockSpec(memory_space=pl.ANY)],
-        out_shape=[
-            jax.ShapeDtypeStruct((pairs, length, 3 * LANES), LOW),
-            jax.ShapeDtypeStruct((tb, 3 * n_ctx * width), LOW),
-        ],
+        functools.partial(back_kernel, n_ctx),
+        in_specs=[anyspace] + [vmem] * 10 + [anyspace] * 8,
+        out_specs=[anyspace] + [vmem] * 5,
+        out_shape=[shape((tb, 3 * model), LOW), shape((own_rows, 3 * model), F32)]
+        + [shape(keep.shape[2:], F32) for keep in sides[::2]],
         scratch_shapes=[
             pltpu.VMEM((length, width), LOW),
+            pltpu.VMEM((pairs, length, wide), LOW),
             pltpu.VMEM((8, length), F32),
             pltpu.VMEM((8, length), F32),
             pltpu.VMEM((length, LANES), F32),
             pltpu.VMEM((tb, LANES), F32),
             pltpu.VMEM((tb, LANES), F32),
-            pltpu.SemaphoreType.DMA((n_ctx - 1,)),
-            pltpu.SemaphoreType.DMA((n_ctx - 1,)),
-            pltpu.SemaphoreType.DMA((n_ctx - 1, pairs, 3)),
-            pltpu.SemaphoreType.DMA((n_ctx - 1, pairs, 3)),
-            pltpu.SemaphoreType.DMA((pairs, 3)),
+            pltpu.VMEM((wide, model), F32),
+        ]
+        + buffers
+        + [
+            pltpu.VMEM((pairs, 4, wide, LANES), LOW),
+            pltpu.VMEM((pairs, 4, wide, LANES), LOW),
+            pltpu.VMEM((pairs, 4, wide, LANES), LOW),
+            pltpu.VMEM((pairs, 2, wide, LANES), LOW),
+            pltpu.VMEM((pairs, wide, LANES), LOW),
+            pltpu.VMEM((pairs, n_ctx, own_rows, wide), LOW),
+            pltpu.VMEM((n_ctx, pairs, own_rows, wide), LOW),
+            dma((n_ctx - 1,)), dma((n_ctx - 1,)),
+            dma((n_ctx - 1, pairs, 3)), dma((n_ctx - 1, pairs, 3)),
+            dma((pairs, 3)),
+            dma((4, 8)), dma((4, 8)),
+            dma((pairs, 4)), dma((pairs, 4)),
+            dma((pairs, n_ctx - 1)), dma((pairs, n_ctx - 1)),
         ],
-        compiler_params=params(collective_id=2, has_side_effects=True),
+        compiler_params=params(collective_id=3, has_side_effects=True),
         cost_estimate=pl.CostEstimate(
-            flops=40 * 10**9, bytes_accessed=16 * 2**20, transcendentals=2 * length * length
+            flops=40 * 10**9, bytes_accessed=60 * 2**20, transcendentals=2 * length * length
         ),
-        name="attend_back",
-    )(ga, q, k, v, of, lse, seg_col, seg_row, cos, sin)
-
-
-def mlp_kernel(blocks, tok_ref, att_ref, cot_ref, gain_ref, *refs):
-    (wo_in, wg_in, wu_in, wd_in), refs = refs[:4], refs[4:]
-    out_ref, gm_ref, ga_ref, gk, gs, uk, us, ok, os, dk, ds = refs[:11]
-    wo, wg, wu, wd, att, nat, n2, mi, mit, inv_ref, oacc, dacc, dwd, sem, osem = refs[11:]
+        name="back",
+    )(ga, q, k, v, of, lse, seg_col, seg_row, cos, sin, xn, *sides)
+
+
+def mlp_kernel(blocks, n_ctx, tok_ref, att_ref, cot_ref, gain_ref, *refs):
+    (wo_in, wg_in, wu_in, wd_in, wq_ref), refs = refs[:5], refs[5:]
+    out_ref, gm_ref, ga_ref, gk, gs, uk, us, ok, os, dk, ds, wq_all = refs[:12]
+    wo, wg, wu, wd, att, nat, n2, mi, mit, inv_ref, oacc, dacc, dwd, sem, osem, q_send, q_recv = refs[12:]
     dp = lax.axis_index("dp")
     u = pl.program_id(0)
     last = pl.num_programs(0) - 1
@@ -971,8 +1175,12 @@
             made.append(pltpu.make_async_copy(dwd.at[rows, :], (ds if d % 2 else dk).at[d // 2], osem.at[d]))
         return made
 
+    attn = Gather(n_ctx, wq_ref, wq_all, q_send, q_recv, (NEAR, FAR))
+
     @pl.when(u == 0)
     def _():
+        meet(n_ctx, (CORE, NEAR, FAR))
+        attn.start()
         made = copies()
         for c in made:
             c.start()
@@ -1014,6 +1222,9 @@
         (us if d % 2 else uk)[d // 2] = dwu[d * LANES : (d + 1) * LANES]
     dwd[cols, :] = dot(hidden, cot, 0, 0).astype(LOW)
 
+    for at, move in ((3, attn.spread), (5, attn.forward), (8, attn.cross)):
+        pl.when(u == at)(move)
+
     @pl.when(u == last)
     def _():
         made = out_copies()
@@ -1032,6 +1243,7 @@
         n2[...] = dot(gb, wo[...], 1, 1)
         for d in range(blocks):
             ga_ref[:, lane_block(dp ^ d)] = n2[:, d * LANES : (d + 1) * LANES].astype(LOW)
+        attn.finish()
         dwo = dot(att[...], gb, 0, 0).astype(LOW)
         for d in range(blocks):
             (os if d % 2 else ok)[d // 2] = dwo[d * LANES : (d + 1) * LANES]
@@ -1039,7 +1251,7 @@
             c.wait()
 
 
-def mlp_call(tok, att, cot, gain, wo, wg, wu, wd):
+def mlp_call(n_ctx, tok, att, cot, gain, wo, wg, wu, wd, wq):
     tb, model = tok.shape
     blocks, _, ff = wg.shape
     half = blocks // 2
@@ -1051,14 +1263,15 @@
     tokens = pl.BlockSpec((tb, model), lambda u: (0, 0))
     shape = jax.ShapeDtypeStruct
     return pl.pallas_call(
-        functools.partial(mlp_kernel, blocks),
+        functools.partial(mlp_kernel, blocks, n_ctx),
         grid=(ff // FF_BLOCK,),
-        in_specs=[whole(tok), whole(att), whole(cot), whole(gain)] + [anyspace] * 4,
-        out_specs=[tokens, tokens, tokens] + [half_cols] * 4 + [half_out] * 2 + [anyspace] * 2,
+        in_specs=[whole(tok), whole(att), whole(cot), whole(gain)] + [anyspace] * 5,
+        out_specs=[tokens, tokens, tokens] + [half_cols] * 4 + [half_out] * 2 + [anyspace] * 3,
         out_shape=[shape((tb, model), LOW), shape((tb, model), F32), shape((tb, model), LOW)]
         + [shape((half, LANES, ff), LOW)] * 4
         + [shape((half, LANES, model), LOW)] * 2
-        + [shape((half, down, model), LOW)] * 2,
+        + [shape((half, down, model), LOW)] * 2
+        + [shape((blocks, n_ctx * wq.shape[0], wq.shape[1]), LOW)],
         scratch_shapes=[
             pltpu.VMEM((model, model), LOW),
             pltpu.VMEM((model, ff), LOW),
@@ -1075,21 +1288,21 @@
             pltpu.VMEM((ff, model), LOW),
             pltpu.SemaphoreType.DMA((4, blocks)),
             pltpu.SemaphoreType.DMA((blocks,)),
+            pltpu.SemaphoreType.DMA((11,)),
+            pltpu.SemaphoreType.DMA((11,)),
         ],
-        compiler_params=params(),
+        compiler_params=params(collective_id=2, has_side_effects=True),
         cost_estimate=pl.CostEstimate(
             flops=2 * tb * model * (8 * ff + 3 * model), bytes_accessed=50 * 2**20, transcendentals=0
         ),
         name="mlp",
-    )(tok, att, cot, gain, wo, wg, wu, wd)
-
-
-def input_kernel(blocks, tok_ref, gm_ref, v1_ref, gain_ref, g, *refs):
-    w_in, refs = refs[:blocks], refs[blocks:]
-    ig_ref, vg_ref, w, rel, nat, sem = refs
+    )(tok, att, cot, gain, wo, wg, wu, wd, wq)
+
+
+def input_kernel(blocks, tok_ref, gm_ref, v1_ref, gain_ref, g, w_in, ig_ref, vg_ref, w, rel, nat, sem):
     dp = lax.axis_index("dp")
     model = tok_ref.shape[1]
-    made = [pltpu.make_async_copy(w_in[d], w.at[pl.ds(d * LANES, LANES), :], sem.at[d]) for d in range(blocks)]
+    made = [pltpu.make_async_copy(w_in.at[d], w.at[pl.ds(d * LANES, LANES), :], sem.at[d]) for d in range(blocks)]
     for m in made:
         m.start()
     for d in range(blocks):
@@ -1113,12 +1326,12 @@
 
 def input_call(tok, gm, v1, gain, g, ws):
     tb, model = tok.shape
-    blocks = len(ws)
+    blocks = ws.shape[0]
     vmem = pl.BlockSpec(memory_space=pltpu.VMEM)
     shape = jax.ShapeDtypeStruct
     return pl.pallas_call(
         functools.partial(input_kernel, blocks),
-        in_specs=[vmem] * 5 + [pl.BlockSpec(memory_space=pl.ANY)] * blocks,
+        in_specs=[vmem] * 5 + [pl.BlockSpec(memory_space=pl.ANY)],
         out_specs=[vmem, vmem],
         out_shape=[shape((tb, model), F32)] * 2,
         scratch_shapes=[
@@ -1132,56 +1345,16 @@
             flops=2 * tb * model * 3 * model, bytes_accessed=20 * 2**20, transcendentals=0
         ),
         name="input_grad",
-    )(tok, gm, v1, gain, g, *ws)
+    )(tok, gm, v1, gain, g, ws)
 
 
 def fast_local(
     n_dp, n_ctx, tokens, first_values, v1_accum, segment_ids, positions, cotangent,
     attn_gain, w_query, w_key, w_value, w_out, mlp_gain, w_gate, w_up, w_down,
 ):
-    c = lax.axis_index("ctx")
     seq, model = tokens.shape[1:]
     width = model // n_ctx
-    length = seq * n_ctx
-    ff = w_gate.shape[1]
     own_rows = w_query.shape[0]
-    down_rows = w_down.shape[0]
-    bits = [1 << b for b in range(n_dp.bit_length() - 1)]
-    plane = bits[1:]
-
-    def shift(x, k):
-        return lax.ppermute(x, "ctx", [(i, (i + k) % n_ctx) for i in range(n_ctx)])
-
-    def flip(x, bit):
-        return lax.ppermute(x, "dp", [(i, i ^ bit) for i in range(n_dp)])
-
-    def cut(x, index, size, axis):
-        return lax.dynamic_slice_in_dim(x, index * size, size, axis)
-
-    def swap_ctx(x, axis):
-        size = x.shape[axis] // n_ctx
-        return [cut(x, c, size, axis)] + [shift(cut(x, (c + k) % n_ctx, size, axis), k) for k in range(1, n_ctx)]
-
-    def place(slots, axis):
-        size = slots[0].shape[axis]
-        dims = list(slots[0].shape)
-        dims[axis] = size * n_ctx
-        out = jnp.zeros(dims, slots[0].dtype)
-        for k, slot in enumerate(slots):
-            out = lax.dynamic_update_slice_in_dim(out, slot, ((c + n_ctx - k) % n_ctx) * size, axis)
-        return out
-
-    def gather_dp(x, order):
-        got = {0: x}
-        for bit in order:
-            for d in sorted(got):
-                got[d ^ bit] = flip(got[d], bit)
-        return [got[d] for d in range(n_dp)]
-
-    def gather_ctx(x):
-        return lax.all_gather(x, "ctx", axis=0, tiled=True)
-
-    pairs = width // LANES
     tok = tokens[0]
     mark = jnp.concatenate([segment_ids, positions, jnp.zeros((6, seq), jnp.int32)], axis=0)
     gains = jnp.stack([attn_gain, mlp_gain], axis=1)
@@ -1196,61 +1369,21 @@
      gate_all, up_all, out_all, down_all) = front_call(
         n_dp, n_ctx, tok, first_values[0], mark, pack, freq, w_gate, w_up, w_out, w_down
     )
-    gain_rel, gain_two_rel = gain_rows[0:1], gain_rows[1:2]
-    cot = cotangent[0]
+    qkv = jnp.concatenate([w_query, w_key, w_value], axis=1)
     (output, grad_middle, grad_attended, gate_keep, gate_send, up_keep, up_send, out_keep, out_send,
-     down_keep, down_send) = mlp_call(tok, attended, cot, gain_two_rel, out_all, gate_all, up_all, down_all)
-
-    qkv_all = gather_dp(gather_ctx(jnp.concatenate([w_query, w_key, w_value], axis=1)), plane + bits[:1])
-
-    back, home_grad = attend_back_call(
-        n_ctx, grad_attended, q, k, v, out_full, log_total, seg_col, seg_row, cos, sin
-    )
-
-    def scatter_dp(keep, send, order):
-        terms = [keep, flip(send, bits[0])]
-        count = keep.shape[0]
-        names = list(range(count))
-        for bit in order:
-            near = bit >> 1
-            stay = [n for n in names if not n & near]
-            leave = [n for n in names if n & near]
-
-            def pick(which):
-                return sum(
-                    jnp.stack([t[names.index(n)] for n in which]).astype(F32) for t in terms
-                )
-
-            got = flip(pick(leave).astype(LOW), bit)
-            terms = [jnp.stack([t[names.index(n)] for n in stay]) for t in terms] + [got]
-            names = stay
-        return sum(t[0].astype(F32) for t in terms)
-
-    def scatter_ctx(x):
-        size = x.shape[0] // n_ctx
-        got = cut(x, c, size, 0)
-        for k in range(1, n_ctx):
-            got = got + shift(cut(x, (c + k) % n_ctx, size, 0).astype(LOW), k).astype(F32)
-        return got
-
-    gate_grad = scatter_ctx(scatter_dp(gate_keep, gate_send, plane))
-    up_grad = scatter_ctx(scatter_dp(up_keep, up_send, plane[::-1]))
-    down_grad = scatter_ctx(scatter_dp(down_keep, down_send, plane))
-    out_grad = scatter_ctx(scatter_dp(out_keep, out_send, plane[::-1]))
-
-    qkv_grad = jnp.zeros((3, own_rows, model), F32)
-    for p in range(pairs):
-        product = lax.dot_general(
-            xn, back[p], (((0,), (0,)), ((), ())), preferred_element_type=F32
-        ).astype(LOW).reshape(n_dp // 2, 2, model // n_dp, 3 * LANES)
-        total = scatter_dp(product[:, 0], product[:, 1], plane)
-        for s, slot in enumerate(swap_ctx(total.astype(LOW), 0)):
-            block = slot.astype(F32).reshape(own_rows, 3, LANES).transpose(1, 0, 2)
-            at = ((c + n_ctx - s) % n_ctx) * width + p * LANES
-            qkv_grad = lax.dynamic_update_slice_in_dim(qkv_grad, block, at, 2)
-    query_grad, key_grad, value_grad = qkv_grad[0], qkv_grad[1], 0.5 * qkv_grad[2]
-
-    input_grad, v1_grad = input_call(tok, grad_middle, v1_accum[0], gain_rel, home_grad, qkv_all)
+     down_keep, down_send, qkv_all) = mlp_call(
+        n_ctx, tok, attended, cotangent[0], gain_rows[1:2], out_all, gate_all, up_all, down_all, qkv
+    )
+    sides = [
+        x.reshape(x.shape[0], n_ctx, x.shape[1] // n_ctx, x.shape[2])
+        for x in (gate_keep, gate_send, up_keep, up_send, out_keep, out_send, down_keep, down_send)
+    ]
+    home_grad, qkv_grad, gate_grad, up_grad, out_grad, down_grad = back_call(
+        n_ctx, grad_attended, q, k, v, out_full, log_total, seg_col, seg_row, cos, sin, xn, sides
+    )
+    query_grad, key_grad = qkv_grad[:, :model], qkv_grad[:, model : 2 * model]
+    value_grad = 0.5 * qkv_grad[:, 2 * model :]
+    input_grad, v1_grad = input_call(tok, grad_middle, v1_accum[0], gain_rows[0:1], home_grad, qkv_all)
 
     def row_dot(a, w):
         return jnp.sum(a * w.astype(F32), axis=1)

time: 650 us -> 497 us (0.76)
  waiting for transfers between devices: 104 us -> 0 us
  Pallas kernels: 385 us -> 468 us
  starting transfers between devices: 54.8 us -> 0 us
  other arithmetic: 36.9 us -> 10.2 us
  local copies, waits for them, and re-layouts: 31.4 us -> 9.43 us
  blocking collectives: 16.6 us -> 0 us
  matrix products: 7.54 us -> 0 us
    ppermute x43 -> x0, waiting for transfers between devices: 104 us -> none  [the longest x25 80.8 us: flip(): return lax.ppermute(x, 'dp', [(i, i ^ bit) for i in range(n_dp)])]
    pallas_call x2, Pallas kernels: 168 us -> 252 us  [the longest x1 178 us: back_call(): pl.pallas_call(functools.partial(back_kernel, n_ctx), in_specs=[anyspace]...]
    ppermute x43 -> x0, starting transfers between devices: 54.8 us -> none  [the longest x25 27.6 us: flip(): return lax.ppermute(x, 'dp', [(i, i ^ bit) for i in range(n_dp)])]
    convert_element_type x14 -> x0, other arithmetic: 20.4 us -> none  [the longest x12 18.3 us: scatter_dp(): got = flip(pick(leave).astype(LOW), bit)]
    all_gather x1 -> x0, blocking collectives: 16.6 us -> none  [gather_ctx(): return lax.all_gather(x, 'ctx', axis=0, tiled=True)]
    transpose x8 -> x0, local copies, waits for them, and re-layouts: 10.4 us -> none  [fast_local(): block = slot.astype(F32).reshape(own_rows, 3, LANES).transpose(1, 0, 2)]
    add x6 -> x0, other arithmetic: 8.02 us -> none  [the longest x4 6.51 us: scatter_dp(): return sum((t[0].astype(F32) for t in terms))]
    dot_general x2 -> x0, matrix products: 7.54 us -> none  [fast_local(): lax.dot_general(xn, back[p], (((0,), (0,)), ((), ())), preferred_element_...]
  transfers between devices with their start and end apart: 43 -> 0, of which waited for: 14 -> 0; matrix products, arithmetic and copies ran while one was open for 10% -> 0% of each run, Pallas kernels for 21% -> 0%
where the time goes in v4:
time: 497 us; the launch traced here: 489 us
  Pallas kernels  468 us (94%)
  other arithmetic  10.2 us (2%)
  local copies, waits for them, and re-layouts  9.43 us (2%)
    pallas_call x1, Pallas kernels, front_call(): pl.pallas_call(functools.partial(front_kernel, n_ctx), in_specs=[anyspace...  204 us
    pallas_call x1, Pallas kernels, back_call(): pl.pallas_call(functools.partial(back_kernel, n_ctx), in_specs=[anyspace]...  178 us
    pallas_call x1, Pallas kernels, mlp_call(): pl.pallas_call(functools.partial(mlp_kernel, blocks, n_ctx), grid=(ff //...  73.7 us
    pallas_call x1, Pallas kernels, input_call(): pl.pallas_call(functools.partial(input_kernel, blocks), in_specs=[vmem] *...  12.4 us

profile of v4, /device:TPU:27, one launch (start us, length us, event | category | flops | bytes accessed | tf_op | source)
XLA Modules:
  0.0 489.2 jit_solution(4204579851379113199)
XLA Ops:
  0.6 0.7 pad_maximum_fusion.1
  1.3 0.1 pad.23.clone
  1.4 0.7 tile.8
  2.1 0.1 stack_tile.7
  2.2 0.1 stack_tile.6
  2.2 0.6 select_maximum_fusion.freq_ref
  2.9 0.1 copy.32
  3.0 1.4 add_add_fusion.mark_ref
  4.3 0.8 copy.39
  5.2 0.9 copy_bitcast_fusion
  6.1 0.7 maximum_bitcast_fusion.pack_ref
  6.8 1.6 pad_maximum_fusion.refs_4_
  8.4 204.1 %front.1 = (bf16[2048,1024]{1,0:T(8,128)(2,1)}, bf16[2048,256]{1,0:T(8,128)(2,1)}, bf16[2048,256]{1,0:T(8,128)(2,1)}, bf16[2048,256]{1,0:T(8,128)(2,1)}, f32[204...) custom-call(bf16[512,1024]{1,0:T(8,128)(2,1)} %bitcast.31, ...), custom_call_target="tpu_custom_call" | custom-call | flops 24000000000 | bytes 62914560 | tf_op jit(solution)/shard_map/front/pallas_call | solution.py:753
  212.5 1.4 fusion
  213.9 73.7 %mlp.1 = (bf16[512,1024]{1,0:T(8,128)(2,1)}, f32[512,1024]{1,0:T(8,128)}, bf16[512,1024]{1,0:T(8,128)(2,1)}, bf16[4,128,2816]{2,1,0:T(8,128)(2,1)}, bf16[4,128,2...) custom-call(bf16[512,1024]{1,0:T(8,128)(2,1)} %bitcast.32, ...), custom_call_target="tpu_custom_call" | custom-call | flops 26843545600 | bytes 52428800 | tf_op jit(solution)/shard_map/mlp/pallas_call | solution.py:1265
  287.6 0.0 copy-start.6
  287.6 0.0 copy-start.7
  287.7 0.0 copy-start.10
  287.7 0.0 copy-start.2
  287.7 0.0 copy-start.3
  287.7 0.0 copy-start.4
  287.7 0.0 copy-start.9
  287.7 178.1 %back.1 = (bf16[512,3072]{1,0:T(8,128)(2,1)}, f32[32,3072]{1,0:T(8,128)}, f32[32,2816]{1,0:T(8,128)}, f32[32,2816]{1,0:T(8,128)}, f32[32,1024]{1,0:T(8,128)}, /*index=5*/f32[88,1024]{1,0:T(8,128)}) custom-call(bf16[512,1024]{1,0:T(8,128)(2,1)} %get-tuple-element.56.refs_0_, bf16[2048,256]{1,0:T(8,128)(2,1)} %get-tuple-element.57.refs_1_, ...), custom_call_target="tpu_custom_call" | custom-call | flops 40000000000 | bytes 62914560 | tf_op jit(solution)/shard_map/back/pallas_call | solution.py:1109
  465.8 0.0 copy-done.6
  465.8 1.1 multiply_reduce_fusion.1
  467.0 0.0 copy-done.7
  467.0 1.1 multiply_reduce_fusion
  468.1 0.0 copy-done.10
  468.1 0.5 convert_divide_fusion
  468.6 0.0 copy-done.2
  468.6 0.0 copy-done.3
  468.6 0.0 copy-done.4
  468.6 1.9 multiply_reduce_fusion.3
  470.6 0.0 copy-done.9
  470.6 0.5 convert_divide_fusion.1
  471.1 0.0 copy-start.8
  471.1 0.0 copy-start.1
  471.1 12.4 %input_grad.1 = (f32[512,1024]{1,0:T(8,128)}, f32[512,1024]{1,0:T(8,128)}) custom-call(bf16[512,1024]{1,0:T(8,128)(2,1)} %bitcast.33, f32[512,1024]{1,0:T(8,128)} %get-tuple-element.55.gm_ref, f32[512,1024]{1,0:T(8,128)} %bitcast.29, f32[1,1024]{1,0:T(1,128)} %get-tuple-element.94.gain_ref, bf16[512,3072]{1,0:T(8,128)(2,1)} %get-tuple-element.75.g, ...), custom_call_target="tpu_custom_call" | custom-call | flops 3221225472 | bytes 20971520 | tf_op jit(solution)/shard_map/input_grad/pallas_call | solution.py:1332
  483.5 0.0 copy-start
  483.5 0.0 copy-start.5
  483.5 2.3 copy.45
  485.9 0.0 copy-done.8
  485.9 0.7 copy.46
  486.5 0.0 copy-done.1
  486.5 0.7 copy.47
  487.3 0.0 copy-done
  487.3 0.7 copy.48
  488.0 0.0 copy-done.5
  488.0 0.7 copy.49
  (5 shorter events, 0.0 us)
Async XLA Ops:
  287.6 178.2 %copy-start.6 = (bf16[32,2816]{1,0:T(8,128)(2,1)S(1)}, bf16[32,2816]{1,0:T(8,128)(2,1)}, u32[]{:S(2)}) copy-start(bf16[32,2816]{1,0:T(8,128)(2,1)} %wg_ref.1) | copy-start | bytes 540676
  287.6 179.3 %copy-start.7 = (bf16[32,2816]{1,0:T(8,128)(2,1)S(1)}, bf16[32,2816]{1,0:T(8,128)(2,1)}, u32[]{:S(2)}) copy-start(bf16[32,2816]{1,0:T(8,128)(2,1)} %wu_ref.1) | copy-start | bytes 540676
  287.7 180.4 %copy-start.10 = (bf16[32]{0:T(256)(128)(2,1)S(1)}, bf16[32]{0:T(256)(128)(2,1)}, u32[]{:S(2)}) copy-start(bf16[32]{0:T(256)(128)(2,1)} %param.26) | copy-start | bytes 196
  287.7 181.0 %copy-start.2 = (bf16[32,1024]{1,0:T(8,128)(2,1)S(1)}, bf16[32,1024]{1,0:T(8,128)(2,1)}, u32[]{:S(2)}) copy-start(bf16[32,1024]{1,0:T(8,128)(2,1)} %param.22) | copy-start | bytes 196612
  287.7 181.0 %copy-start.3 = (bf16[32,1024]{1,0:T(8,128)(2,1)S(1)}, bf16[32,1024]{1,0:T(8,128)(2,1)}, u32[]{:S(2)}) copy-start(bf16[32,1024]{1,0:T(8,128)(2,1)} %param.24) | copy-start | bytes 196612
  287.7 180.9 %copy-start.4 = (bf16[32,1024]{1,0:T(8,128)(2,1)S(1)}, bf16[32,1024]{1,0:T(8,128)(2,1)}, u32[]{:S(2)}) copy-start(bf16[32,1024]{1,0:T(8,128)(2,1)} %param.23) | copy-start | bytes 196612
  287.7 182.9 %copy-start.9 = (bf16[32]{0:T(256)(128)(2,1)S(1)}, bf16[32]{0:T(256)(128)(2,1)}, u32[]{:S(2)}) copy-start(bf16[32]{0:T(256)(128)(2,1)} %param.21) | copy-start | bytes 196
  471.1 14.8 %copy-start.8 = (f32[32,1024]{1,0:T(8,128)S(1)}, f32[32,1024]{1,0:T(8,128)}, u32[]{:S(2)}) copy-start(f32[32,1024]{1,0:T(8,128)} %get-tuple-element.117) | copy-start | bytes 393220
  471.1 15.4 %copy-start.1 = (f32[32,2816]{1,0:T(8,128)S(1)}, f32[32,2816]{1,0:T(8,128)}, u32[]{:S(2)}) copy-start(f32[32,2816]{1,0:T(8,128)} %get-tuple-element.119) | copy-start | bytes 1081348
  483.5 3.7 copy-start
  483.5 4.5 copy-start.5

commit v5 on v4

--- a/solution.py
+++ b/solution.py
@@ -424,10 +424,16 @@
         self.first, self.second = order
         self.rows = src.shape[0]
 
-    def along(self, k):
+    def place(self, c):
+        return self.dst.at[0, pl.ds(c * self.rows, self.rows), :]
+
+    def along(self, bit):
         c = lax.axis_index("ctx")
-        to = lax.rem(c + k, self.n)
-        return ctx_copy(self.src, self.dst.at[0, pl.ds(c * self.rows, self.rows), :], self.send.at[k - 1], self.recv.at[k - 1], to)
+        return ctx_copy(self.src, self.place(c), self.send.at[bit - 1], self.recv.at[bit - 1], c ^ bit)
+
+    def pass_on(self):
+        c = lax.axis_index("ctx")
+        return ctx_copy(self.place(c ^ 2), self.place(c ^ 2), self.send.at[2], self.recv.at[2], c ^ 1)
 
     def plane(self, slot, bit, at):
         return dp_copy(self.dst.at[slot], self.dst.at[slot ^ bit], self.send.at[at], self.recv.at[at], bit)
@@ -443,13 +449,17 @@
 
     def start(self):
         self.own().start()
-        for k in range(1, self.n):
-            self.along(k).start()
+        self.along(2).start()
+        self.along(1).start()
+
+    def relay(self):
+        self.along(2).wait_recv()
+        self.pass_on().start()
 
     def spread(self):
         self.own().wait()
-        for k in range(1, self.n):
-            self.along(k).wait_recv()
+        self.along(1).wait_recv()
+        self.pass_on().wait_recv()
         for at in (0, 1, 3):
             self.hop(at).start()
 
@@ -465,8 +475,9 @@
         self.hop(6).start()
 
     def finish(self):
-        for k in range(1, self.n):
-            self.along(k).wait_send()
+        self.along(1).wait_send()
+        self.along(2).wait_send()
+        self.pass_on().wait_send()
         for at in range(7):
             self.hop(at).wait_send()
         for at in range(3, 7):
@@ -489,7 +500,6 @@
     width = q_ref.shape[1]
     own_rows = wg_ref.shape[0]
     lane = lax.broadcasted_iota(jnp.int32, (tb, LANES), 1)
-    right, left = lax.rem(c + 1, n_ctx), lax.rem(c + n_ctx - 1, n_ctx)
     exact = lax.Precision.HIGHEST
 
     weights = [
@@ -503,7 +513,7 @@
             ]
         )
     ]
-    early, late = weights[:2], weights[2:]
+    early, late = weights[:3], weights[3:]
 
     def mark_copy(k):
         at = rows_of(c, tb)
@@ -520,11 +530,12 @@
         to = lax.rem(c + k, n_ctx)
         return ctx_copy(fv_ref.at[:, rows_of(to, width)], fvs.at[rows_of(c, tb), :], fv_send.at[k - 1], fv_recv.at[k - 1], to)
 
-    def tok_copy(way, step):
-        block = lax.rem(c + n_ctx - step, n_ctx) if way == 0 else lax.rem(c + step, n_ctx)
-        at = pl.ds(pl.multiple_of(block * tb + way * half, half), half)
-        src = tok_ref.at[pl.ds(way * half, half), :] if step == 0 else x_all.at[at, :]
-        return ctx_copy(src, x_all.at[at, :], tok_send.at[way, step], tok_recv.at[way, step], left if way else right)
+    def tok_copy(bit):
+        return ctx_copy(tok_ref, x_all.at[rows_of(c, tb), :], tok_send.at[bit - 1], tok_recv.at[bit - 1], c ^ bit)
+
+    def tok_pass():
+        at = rows_of(c ^ 2, tb)
+        return ctx_copy(x_all.at[at, :], x_all.at[at, :], tok_send.at[2], tok_recv.at[2], c ^ 1)
 
     locals_ = [
         pltpu.make_async_copy(tok_ref, x_all.at[rows_of(c, tb), :], own.at[0]),
@@ -537,14 +548,10 @@
     for k in range(1, n_ctx):
         mark_copy(k).start()
         pack_copy(k).start()
-    for way in range(2):
-        tok_copy(way, 0).start()
     for w in early:
         w.start()
     for m in locals_:
         m.start()
-    for k in range(1, n_ctx):
-        fv_copy(k).start()
 
     locals_[3].wait()
     for k in range(1, n_ctx):
@@ -575,15 +582,14 @@
     pack_hop(0, CORE, 6).start()
     pack_hop(NEAR, CORE, 7).start()
 
-    for way in range(2):
-        tok_copy(way, 0).wait_recv()
-        tok_copy(way, 1).start()
+    for w in early:
+        w.relay()
+    tok_copy(2).start()
+    tok_copy(1).start()
     pack_hop(0, FAR, 4).wait_recv()
     pack_hop(FAR, CORE, 8).start()
     pack_hop(NEAR, FAR, 5).wait_recv()
     pack_hop(NEAR | FAR, CORE, 9).start()
-    for w in early:
-        w.spread()
     for at, (slot, bit) in enumerate([(0, CORE), (NEAR, CORE), (FAR, CORE), (NEAR | FAR, CORE)]):
         pack_hop(slot, bit, 6 + at).wait_recv()
     count = packs.shape[0]
@@ -613,30 +619,33 @@
             k_ref[at, cols] = (kb * cos + half_swap(kb) * sin).astype(LOW)
         v_ref[at, :] = (0.5 * proj[:, 2 * width :] + 0.5 * fvs[at, :].astype(F32)).astype(LOW)
 
-    def project_pair(step):
+    def project_chunk(bit):
         def one(part, carry):
-            project(lax.rem(c + (2 * part - 1) * step + n_ctx, n_ctx), part)
+            project(c ^ bit, part)
             return carry
 
         lax.fori_loop(0, 2, one, 0)
 
-    project_pair(0)
+    for w in early:
+        w.spread()
+    project_chunk(0)
+    tok_copy(2).wait_recv()
+    tok_pass().start()
+    for k in range(1, n_ctx):
+        fv_copy(k).start()
     for w in early:
         w.forward()
-    for way in range(2):
-        tok_copy(way, 1).wait_recv()
-        tok_copy(way, 2).start()
+    tok_copy(1).wait_recv()
     for k in range(1, n_ctx):
         fv_copy(k).wait_recv()
-    project_pair(1)
-    project_pair(2)
+    project_chunk(1)
+    project_chunk(2)
+    tok_pass().wait_recv()
+    for w in late:
+        w.start()
+    project_chunk(3)
     for w in early:
         w.cross()
-    for way in range(2):
-        tok_copy(way, 2).wait_recv()
-    for w in late:
-        w.start()
-    project_pair(3)
 
     def fold(x, op):
         r = x[:, 0:LANES]
@@ -713,7 +722,10 @@
 
         lax.fori_loop(lo, hi, one, 0)
 
-    query_blocks(0, 0, n_ctx)
+    query_blocks(0, 0, 3)
+    for w in late:
+        w.relay()
+    query_blocks(0, 3, n_ctx)
     for w in late:
         w.spread()
     query_blocks(1, 0, n_ctx)
@@ -734,9 +746,9 @@
         [(0, NEAR), (0, FAR), (NEAR, FAR), (0, CORE), (NEAR, CORE), (FAR, CORE), (NEAR | FAR, CORE)]
     ):
         pack_hop(slot, bit, 3 + at).wait_send()
-    for way in range(2):
-        for step in range(3):
-            tok_copy(way, step).wait_send()
+    tok_copy(1).wait_send()
+    tok_copy(2).wait_send()
+    tok_pass().wait_send()
     for w in weights:
         w.finish()
 
@@ -774,7 +786,7 @@
             pltpu.VMEM((tb, LANES), F32),
             dma((n_ctx - 1,)), dma((n_ctx - 1,)),
             dma((n_ctx + 6,)), dma((n_ctx + 6,)),
-            dma((2, n_ctx - 1)), dma((2, n_ctx - 1)),
+            dma((3,)), dma((3,)),
             dma((n_ctx - 1,)), dma((n_ctx - 1,)),
             dma((4, 11)), dma((4, 11)),
             dma((n_ctx - 1, pairs)), dma((n_ctx - 1, pairs)),
@@ -789,8 +801,8 @@
 
 
 class Reduce:
-    def __init__(self, n_ctx, keep, gone, acc, rc, rx, ry, rz, out, send, recv, order):
-        self.n, self.keep, self.gone, self.acc, self.rc, self.rx, self.ry, self.rz = n_ctx, keep, gone, acc, rc, rx, ry, rz
+    def __init__(self, n_ctx, keep, came, acc, rc, rx, ry, rz, out, send, recv, order):
+        self.n, self.keep, self.came, self.acc, self.rc, self.rx, self.ry, self.rz = n_ctx, keep, came, acc, rc, rx, ry, rz
         self.out, self.send, self.recv = out, send, recv
         self.one, self.two = order
         self.leave = (self.one >> 1, 3)
@@ -798,22 +810,25 @@
 
     def hop(self, at):
         src, dst, bit = [
-            (self.gone, self.rc, CORE),
             (self.acc.at[self.leave[0]], self.rx.at[0], self.one),
             (self.acc.at[self.leave[1]], self.rx.at[1], self.one),
             (self.acc.at[self.stay], self.ry, self.two),
-        ][at]
+        ][at - 1]
         return dp_copy(src, dst, self.send.at[at], self.recv.at[at], bit)
 
     def held(self):
         return pltpu.make_async_copy(self.keep, self.acc, self.send.at[7])
 
-    def along(self, k):
-        to = lax.rem(lax.axis_index("ctx") + k, self.n)
-        return ctx_copy(self.acc.at[0, to], self.rz.at[k - 1], self.send.at[3 + k], self.recv.at[3 + k], to)
+    def partner(self):
+        return pltpu.make_async_copy(self.came, self.rc, self.send.at[0])
+
+    def along(self, at):
+        c = lax.axis_index("ctx")
+        block, to = ((c ^ 1, c ^ 1), (c ^ 3, c ^ 1), (c ^ 2, c ^ 2))[at]
+        return ctx_copy(self.acc.at[0, block], self.rz.at[at], self.send.at[4 + at], self.recv.at[4 + at], to)
 
     def begin(self):
-        self.hop(0).start()
+        self.partner().start()
         self.held().start()
 
     def add(self, block, terms):
@@ -828,7 +843,7 @@
 
     def step_one(self):
         self.held().wait()
-        self.hop(0).wait_recv()
+        self.partner().wait()
         for at in (1, 0):
             block = self.leave[at]
             self.add(block, [lambda j, block=block: self.rc[block, j]])
@@ -847,44 +862,60 @@
             self.acc[0, c].astype(F32) + self.rc[0, c].astype(F32) + self.rx[0, c].astype(F32) + self.ry[c].astype(F32)
         )
         self.add(0, [lambda j: self.rc[0, j], lambda j: self.rx[0, j], lambda j: self.ry[j]])
-        for k in range(1, self.n):
-            self.along(k).start()
+        self.along(1).start()
+        self.along(0).start()
+
+    def step_far(self):
+        block = lax.axis_index("ctx") ^ 2
+        self.along(1).wait_recv()
+        self.acc[0, block] = (self.acc[0, block].astype(F32) + self.rz[1].astype(F32)).astype(LOW)
+        self.along(2).start()
 
     def finish(self):
-        for k in range(1, self.n):
-            self.along(k).wait_recv()
-            self.out[...] += self.rz[k - 1].astype(F32)
-        for at in range(4):
+        self.along(0).wait_recv()
+        self.along(2).wait_recv()
+        self.out[...] += self.rz[0].astype(F32) + self.rz[2].astype(F32)
+        for at in range(1, 4):
             self.hop(at).wait_send()
-        for k in range(1, self.n):
-            self.along(k).wait_send()
+        for at in range(3):
+            self.along(at).wait_send()
 
 
 def back_kernel(n_ctx, *refs):
-    ga_ref, q_ref, k_ref, v_ref, of_ref, lse_ref, sc_ref, sr_ref, cos_ref, sin_ref, xn_ref = refs[:11]
+    g_ref, q_ref, k_ref, v_ref, of_ref, lse_ref, sc_ref, sr_ref, cos_ref, sin_ref, xn_ref = refs[:11]
     sides = refs[11:19]
     home_ref, qkv_out = refs[19:21]
     outs = refs[21:25]
-    (g_ref, part_ref, lse_row, delta_row, dq_acc, dk_acc, dv_acc, prod) = refs[25:33]
-    rest = refs[33:]
-    buffers, rest = rest[:20], rest[20:]
+    (part_ref, lse_row, delta_row, dq_acc, dk_acc, dv_acc, prod) = refs[25:32]
+    rest = refs[32:]
+    buffers, rest = rest[:40], rest[40:]
     (pk, ps, prc, prx, pry, pz, qz) = rest[:7]
-    (gsend, grecv, send, recv, own, r_send, r_recv, p_send, p_recv, z_send, z_recv) = rest[7:]
+    (send, recv, own, r_send, r_recv, p_send, p_recv, z_send, z_recv) = rest[7:]
     c = lax.axis_index("ctx")
     tb = dk_acc.shape[0]
     length, width = q_ref.shape
     model = n_ctx * width
     pairs = width // LANES
     blocks = model // LANES
-    near_first, far_first = (NEAR, FAR), (FAR, NEAR)
-    gate, up, out, down = [
-        Reduce(n_ctx, sides[2 * i], sides[2 * i + 1], *buffers[5 * i : 5 * i + 5], outs[i], r_send.at[i], r_recv.at[i], order)
-        for i, order in enumerate([near_first, far_first, near_first, far_first])
-    ]
-
-    def grad_copy(k):
-        to = lax.rem(c + k, n_ctx)
-        return ctx_copy(ga_ref.at[:, rows_of(to, width)], g_ref.at[rows_of(c, tb), :], gsend.at[k - 1], grecv.at[k - 1], to)
+    orders = ((NEAR, FAR), (FAR, NEAR))
+    groups = []
+    for i in range(4):
+        keep, came = sides[2 * i], sides[2 * i + 1]
+        wide = keep.shape[3] // 2
+        groups.append([])
+        for h, order in enumerate(orders):
+            cols = pl.ds(h * wide, wide)
+            unit = 2 * i + h
+            groups[i].append(
+                Reduce(
+                    n_ctx, keep.at[:, :, :, cols], came.at[:, :, :, cols], *buffers[5 * unit : 5 * unit + 5],
+                    outs[i].at[:, cols], r_send.at[unit], r_recv.at[unit], order,
+                )
+            )
+
+    def each(i, what):
+        for unit in groups[i]:
+            getattr(unit, what)()
 
     def home(pair, t):
         return home_ref.at[:, pl.ds(pl.multiple_of(t * model + c * width + pair * LANES, LANES), LANES)]
@@ -900,17 +931,9 @@
         return pltpu.make_async_copy(part(pair, t, c), home(pair, t), own.at[pair, t])
 
     meet(n_ctx, (CORE, NEAR, FAR))
-    for k in range(1, n_ctx):
-        grad_copy(k).start()
-    keep = pltpu.make_async_copy(ga_ref.at[:, rows_of(c, width)], g_ref.at[rows_of(c, tb), :], own.at[0, 0])
-    keep.start()
-    for r in (gate, up, out, down):
-        r.begin()
-    for r in (gate, up, out, down):
-        r.step_one()
-    keep.wait()
-    for k in range(1, n_ctx):
-        grad_copy(k).wait_recv()
+    for i in range(4):
+        each(i, "begin")
+    each(0, "step_one")
 
     r8 = lax.broadcasted_iota(jnp.int32, (8, LANES), 0)
     l8 = lax.broadcasted_iota(jnp.int32, (8, LANES), 1)
@@ -1045,39 +1068,46 @@
         for at in range(4):
             pair_hop(pair, at).wait_send()
 
+    middle = n_ctx // 2
     stats(0)
-    key_blocks(0, 0, n_ctx)
+    key_blocks(0, 0, middle)
+    each(0, "step_two")
+    each(1, "step_one")
+    key_blocks(0, middle, n_ctx)
     send_home(0)
     pair_product(0)
+    each(0, "step_ctx")
     stats(1)
-    key_blocks(1, 0, n_ctx // 2)
+    key_blocks(1, 0, middle)
+    each(1, "step_two")
+    each(2, "step_one")
     pair_one(0)
-    gate.step_two()
-    out.step_two()
-    key_blocks(1, n_ctx // 2, n_ctx)
+    each(0, "step_far")
+    key_blocks(1, middle, n_ctx)
     send_home(1)
+    each(1, "step_ctx")
     pair_product(1)
     pair_two(0)
-    up.step_two()
-    down.step_two()
+    each(2, "step_two")
+    each(3, "step_one")
     pair_one(1)
     pair_three(0)
-    gate.step_ctx()
-    out.step_ctx()
+    each(1, "step_far")
+    each(2, "step_ctx")
     pair_two(1)
-    up.step_ctx()
-    down.step_ctx()
+    each(3, "step_two")
+    each(2, "step_far")
     pair_three(1)
+    each(3, "step_ctx")
+    each(3, "step_far")
     for pair in range(pairs):
         pair_finish(pair)
         for s in range(n_ctx):
             for t in range(3):
                 at = t * model + s * width + pair * LANES
                 qkv_out[:, at : at + LANES] = qz[s, pair, :, t * LANES : (t + 1) * LANES].astype(F32)
-    for k in range(1, n_ctx):
-        grad_copy(k).wait_send()
-    for r in (gate, out, up, down):
-        r.finish()
+    for i in range(4):
+        each(i, "finish")
     for pair in range(pairs):
         for t in range(3):
             part_own(pair, t).wait()
@@ -1085,7 +1115,7 @@
                 part_copy(pair, t, k).wait()
 
 
-def back_call(n_ctx, ga, q, k, v, of, lse, seg_col, seg_row, cos, sin, xn, sides):
+def back_call(n_ctx, g, q, k, v, of, lse, seg_col, seg_row, cos, sin, xn, sides):
     length, width = q.shape
     model = n_ctx * width
     tb = TOKEN_BLOCK
@@ -1098,22 +1128,16 @@
     buffers = []
     for keep in sides[::2]:
         four, parts, rows, cols = keep.shape
-        buffers += [
-            pltpu.VMEM((four, parts, rows, cols), LOW),
-            pltpu.VMEM((four, parts, rows, cols), LOW),
-            pltpu.VMEM((2, parts, rows, cols), LOW),
-            pltpu.VMEM((parts, rows, cols), LOW),
-            pltpu.VMEM((parts - 1, rows, cols), LOW),
-        ]
+        for lead in ((four, parts), (four, parts), (2, parts), (parts,), (3,)) * 2:
+            buffers.append(pltpu.VMEM(lead + (rows, cols // 2), LOW))
     wide = 3 * LANES
     return pl.pallas_call(
         functools.partial(back_kernel, n_ctx),
-        in_specs=[anyspace] + [vmem] * 10 + [anyspace] * 8,
+        in_specs=[vmem] * 11 + [anyspace] * 8,
         out_specs=[anyspace] + [vmem] * 5,
         out_shape=[shape((tb, 3 * model), LOW), shape((own_rows, 3 * model), F32)]
         + [shape(keep.shape[2:], F32) for keep in sides[::2]],
         scratch_shapes=[
-            pltpu.VMEM((length, width), LOW),
             pltpu.VMEM((pairs, length, wide), LOW),
             pltpu.VMEM((8, length), F32),
             pltpu.VMEM((8, length), F32),
@@ -1131,10 +1155,9 @@
             pltpu.VMEM((pairs, wide, LANES), LOW),
             pltpu.VMEM((pairs, n_ctx, own_rows, wide), LOW),
             pltpu.VMEM((n_ctx, pairs, own_rows, wide), LOW),
-            dma((n_ctx - 1,)), dma((n_ctx - 1,)),
             dma((n_ctx - 1, pairs, 3)), dma((n_ctx - 1, pairs, 3)),
             dma((pairs, 3)),
-            dma((4, 8)), dma((4, 8)),
+            dma((8, 8)), dma((8, 8)),
             dma((pairs, 4)), dma((pairs, 4)),
             dma((pairs, n_ctx - 1)), dma((pairs, n_ctx - 1)),
         ],
@@ -1143,135 +1166,209 @@
             flops=40 * 10**9, bytes_accessed=60 * 2**20, transcendentals=2 * length * length
         ),
         name="back",
-    )(ga, q, k, v, of, lse, seg_col, seg_row, cos, sin, xn, *sides)
-
-
-def mlp_kernel(blocks, n_ctx, tok_ref, att_ref, cot_ref, gain_ref, *refs):
-    (wo_in, wg_in, wu_in, wd_in, wq_ref), refs = refs[:5], refs[5:]
-    out_ref, gm_ref, ga_ref, gk, gs, uk, us, ok, os, dk, ds, wq_all = refs[:12]
-    wo, wg, wu, wd, att, nat, n2, mi, mit, inv_ref, oacc, dacc, dwd, sem, osem, q_send, q_recv = refs[12:]
-    dp = lax.axis_index("dp")
-    u = pl.program_id(0)
-    last = pl.num_programs(0) - 1
+    )(g, q, k, v, of, lse, seg_col, seg_row, cos, sin, xn, *sides)
+
+
+def mlp_kernel(
+    blocks, n_ctx, tok_ref, att_ref, cot_ref, gain_ref, wo_in, wg_in, wu_in, wd_in, wq_ref, wr_ref,
+    out_ref, gm_ref, gh_ref, gk, gc, uk, uc, ok, oc, dk, dc, wq_all, wr_all,
+    wo, wg, wu, wd, att, nat, n2, mi, mit, oacc, dacc, hid_all, dg_all, du_all, stage, ostage,
+    sem, hop_send, hop_recv, st_own, st_send, st_recv, o_sem, d_own, d_send, d_recv, g_send, g_recv,
+):
+    c, dp = lax.axis_index("ctx"), lax.axis_index("dp")
+    tb, model = tok_ref.shape
+    width = model // n_ctx
+    ff = wu.shape[1]
+    steps = ff // FF_BLOCK
     down = wd_in.shape[1]
-
-    def copies():
-        made = []
-        for d in range(blocks):
-            at = pl.ds(d * LANES, LANES)
-            made.append(pltpu.make_async_copy(wo_in.at[d], wo.at[at, :], sem.at[0, d]))
-        for d in range(blocks):
-            at = pl.ds(d * LANES, LANES)
-            made.append(pltpu.make_async_copy(wg_in.at[d], wg.at[at, :], sem.at[1, d]))
-            made.append(pltpu.make_async_copy(wu_in.at[d], wu.at[at, :], sem.at[2, d]))
-            rows = pl.ds(pl.multiple_of((dp ^ d) * down, 32), down)
-            made.append(pltpu.make_async_copy(wd_in.at[d], wd.at[rows, :], sem.at[3, d]))
-        return made
-
-    def out_copies():
-        made = []
-        for d in range(blocks):
-            rows = pl.ds(pl.multiple_of((dp ^ d) * down, 32), down)
-            made.append(pltpu.make_async_copy(dwd.at[rows, :], (ds if d % 2 else dk).at[d // 2], osem.at[d]))
-        return made
-
-    attn = Gather(n_ctx, wq_ref, wq_all, q_send, q_recv, (NEAR, FAR))
-
-    @pl.when(u == 0)
-    def _():
-        meet(n_ctx, (CORE, NEAR, FAR))
-        attn.start()
-        made = copies()
-        for c in made:
-            c.start()
-        for d in range(blocks):
-            att[:, d * LANES : (d + 1) * LANES] = att_ref[:, lane_block(dp ^ d)]
-        for c in made[:blocks]:
-            c.wait()
-        mid = tok_ref[...].astype(F32) + dot(att[...], wo[...], 1, 0)
-        inv = lax.rsqrt(jnp.mean(mid * mid, axis=-1, keepdims=True) + epsilon)
-        oacc[...] = mid
-        nat[...] = mid * inv
-        inv_ref[...] = jnp.broadcast_to(inv, inv_ref.shape)
-        for d in range(blocks):
-            n2[:, d * LANES : (d + 1) * LANES] = nat[:, lane_block(dp ^ d)]
-        mi[...] = (n2[...] * gain_ref[...]).astype(LOW)
-        mit[...] = mi[...].T
-        dacc[...] = jnp.zeros_like(dacc)
-        for c in made[blocks:]:
-            c.wait()
-
-    cols = pl.ds(pl.multiple_of(u * FF_BLOCK, FF_BLOCK), FF_BLOCK)
-    x = mi[...]
-    cot = cot_ref[...]
-    wgu, wuu, wdu = wg[:, cols], wu[:, cols], wd[cols, :]
-    gate = dot(x, wgu, 1, 0)
-    up = dot(x, wuu, 1, 0)
-    grad_hidden = dot(cot, wdu, 1, 1)
-    sig = jax.nn.sigmoid(gate)
-    hidden = (gate * sig * up).astype(LOW)
-    dg = (grad_hidden * up * sig * (1.0 + gate * (1.0 - sig))).astype(LOW)
-    du = (grad_hidden * gate * sig).astype(LOW)
-    oacc[...] += dot(hidden, wdu, 1, 0)
-    dacc[...] += dot(dg, wgu, 1, 1) + dot(du, wuu, 1, 1)
-    xt = mit[...]
-    dwg = dot(xt, dg, 1, 0).astype(LOW)
-    dwu = dot(xt, du, 1, 0).astype(LOW)
+    half = blocks // 2
+    attn = [
+        Gather(n_ctx, wq_ref, wq_all, hop_send.at[0], hop_recv.at[0], (NEAR, FAR)),
+        Gather(n_ctx, wr_ref, wr_all, hop_send.at[1], hop_recv.at[1], (FAR, NEAR)),
+    ]
+
+    loads = []
     for d in range(blocks):
-        (gs if d % 2 else gk)[d // 2] = dwg[d * LANES : (d + 1) * LANES]
-        (us if d % 2 else uk)[d // 2] = dwu[d * LANES : (d + 1) * LANES]
-    dwd[cols, :] = dot(hidden, cot, 0, 0).astype(LOW)
-
-    for at, move in ((3, attn.spread), (5, attn.forward), (8, attn.cross)):
-        pl.when(u == at)(move)
-
-    @pl.when(u == last)
-    def _():
-        made = out_copies()
-        for c in made:
-            c.start()
-        out_ref[...] = oacc[...].astype(LOW)
-        scaled = dacc[...] * gain_ref[...]
-        norm = n2[...]
-        mean = jnp.mean(scaled * norm, axis=-1, keepdims=True)
-        n2[...] = inv_ref[:, 0:1] * (scaled - norm * mean)
-        for d in range(blocks):
-            nat[:, lane_block(dp ^ d)] = n2[:, d * LANES : (d + 1) * LANES]
-        gm = cot.astype(F32) + nat[...]
-        gm_ref[...] = gm
-        gb = gm.astype(LOW)
-        n2[...] = dot(gb, wo[...], 1, 1)
-        for d in range(blocks):
-            ga_ref[:, lane_block(dp ^ d)] = n2[:, d * LANES : (d + 1) * LANES].astype(LOW)
-        attn.finish()
-        dwo = dot(att[...], gb, 0, 0).astype(LOW)
-        for d in range(blocks):
-            (os if d % 2 else ok)[d // 2] = dwo[d * LANES : (d + 1) * LANES]
-        for c in made:
-            c.wait()
-
-
-def mlp_call(n_ctx, tok, att, cot, gain, wo, wg, wu, wd, wq):
+        at = pl.ds(d * LANES, LANES)
+        loads.append(pltpu.make_async_copy(wo_in.at[d], wo.at[at, :], sem.at[0, d]))
+    for d in range(blocks):
+        at = pl.ds(d * LANES, LANES)
+        rows = pl.ds(pl.multiple_of((dp ^ d) * down, 32), down)
+        loads.append(pltpu.make_async_copy(wg_in.at[d], wg.at[at, :], sem.at[1, d]))
+        loads.append(pltpu.make_async_copy(wu_in.at[d], wu.at[at, :], sem.at[2, d]))
+        loads.append(pltpu.make_async_copy(wd_in.at[d], wd.at[rows, :], sem.at[3, d]))
+    for m in loads:
+        m.start()
+    for d in range(blocks):
+        att[:, d * LANES : (d + 1) * LANES] = att_ref[:, lane_block(dp ^ d)]
+    meet(n_ctx, (CORE, NEAR, FAR))
+    for w in attn:
+        w.start()
+    for m in loads[:blocks]:
+        m.wait()
+    mid = tok_ref[...].astype(F32) + dot(att[...], wo[...], 1, 0)
+    inv = lax.rsqrt(jnp.mean(mid * mid, axis=-1, keepdims=True) + epsilon)
+    oacc[...] = mid
+    nat[...] = mid * inv
+    for d in range(blocks):
+        n2[:, d * LANES : (d + 1) * LANES] = nat[:, lane_block(dp ^ d)]
+    mi[...] = (n2[...] * gain_ref[...]).astype(LOW)
+    mit[...] = mi[...].T
+    dacc[...] = jnp.zeros_like(dacc)
+    for m in loads[blocks:]:
+        m.wait()
+
+    def columns(u):
+        return pl.ds(pl.multiple_of(u * FF_BLOCK, FF_BLOCK), FF_BLOCK)
+
+    def data_step(u, carry):
+        cols = columns(u)
+        x = mi[...]
+        cot = cot_ref[...]
+        wgu, wuu, wdu = wg[:, cols], wu[:, cols], wd[cols, :]
+        gate = dot(x, wgu, 1, 0)
+        up = dot(x, wuu, 1, 0)
+        grad_hidden = dot(cot, wdu, 1, 1)
+        sig = jax.nn.sigmoid(gate)
+        hidden = (gate * sig * up).astype(LOW)
+        dg = (grad_hidden * up * sig * (1.0 + gate * (1.0 - sig))).astype(LOW)
+        du = (grad_hidden * gate * sig).astype(LOW)
+        hid_all[:, cols] = hidden
+        dg_all[:, cols] = dg
+        du_all[:, cols] = du
+        oacc[...] += dot(hidden, wdu, 1, 0)
+        dacc[...] += dot(dg, wgu, 1, 1) + dot(du, wuu, 1, 1)
+        return carry
+
+    lax.fori_loop(0, 3, data_step, 0)
+    for w in attn:
+        w.relay()
+    lax.fori_loop(3, 6, data_step, 0)
+    for w in attn:
+        w.spread()
+    lax.fori_loop(6, steps, data_step, 0)
+
+    out_ref[...] = oacc[...].astype(LOW)
+    scaled = dacc[...] * gain_ref[...]
+    norm = n2[...]
+    mean = jnp.mean(scaled * norm, axis=-1, keepdims=True)
+    n2[...] = inv * (scaled - norm * mean)
+    for d in range(blocks):
+        nat[:, lane_block(dp ^ d)] = n2[:, d * LANES : (d + 1) * LANES]
+    gm = cot_ref[...].astype(F32) + nat[...]
+    gm_ref[...] = gm
+    gb = gm.astype(LOW)
+    n2[...] = dot(gb, wo[...], 1, 1)
+    for d in range(blocks):
+        mi[:, lane_block(dp ^ d)] = n2[:, d * LANES : (d + 1) * LANES].astype(LOW)
+
+    def grad_copy(k):
+        to = lax.rem(c + k, n_ctx)
+        return ctx_copy(mi.at[:, rows_of(to, width)], gh_ref.at[rows_of(c, tb), :], g_send.at[k - 1], g_recv.at[k - 1], to)
+
+    grad_own = pltpu.make_async_copy(mi.at[:, rows_of(c, width)], gh_ref.at[rows_of(c, tb), :], o_sem.at[2])
+    for k in range(1, n_ctx):
+        grad_copy(k).start()
+    grad_own.start()
+    for w in attn:
+        w.forward()
+
+    def down_step(u, carry):
+        cols = columns(u)
+        wd[cols, :] = dot(hid_all[:, cols], cot_ref[...], 0, 0).astype(LOW)
+        return carry
+
+    lax.fori_loop(0, steps, down_step, 0)
+
+    def down_copy(d):
+        rows = pl.ds(pl.multiple_of((dp ^ d) * down, 32), down)
+        if d % 2:
+            return dp_copy(wd.at[rows, :], dc.at[d // 2], d_send.at[d // 2], d_recv.at[d // 2], CORE)
+        return pltpu.make_async_copy(wd.at[rows, :], dk.at[d // 2], d_own.at[d // 2])
+
+    for d in range(blocks):
+        down_copy(d).start()
+
+    dwo = dot(att[...], gb, 0, 0).astype(LOW)
+    for d in range(blocks):
+        ostage[d % 2, d // 2] = dwo[d * LANES : (d + 1) * LANES]
+    out_own = pltpu.make_async_copy(ostage.at[0], ok, o_sem.at[0])
+    out_gone = dp_copy(ostage.at[1], oc, o_sem.at[1], o_sem.at[3], CORE)
+    out_own.start()
+    out_gone.start()
+
+    def side(u, t, which):
+        slot = lax.rem(u, 2)
+        cols = columns(u)
+        keep, came = ((gk, gc), (uk, uc))[t]
+        if which == 0:
+            return pltpu.make_async_copy(stage.at[slot, t, 0], keep.at[:, :, cols], st_own.at[slot, t])
+        return dp_copy(stage.at[slot, t, 1], came.at[:, :, cols], st_send.at[slot, t], st_recv.at[t, u], CORE)
+
+    def weight_step(u, carry):
+        cols = columns(u)
+
+        @pl.when(u >= 2)
+        def _():
+            for t in range(2):
+                side(u - 2, t, 0).wait()
+                side(u - 2, t, 1).wait_send()
+
+        slot = lax.rem(u, 2)
+        for t, grad in enumerate((dg_all, du_all)):
+            dw = dot(mit[...], grad[:, cols], 1, 0).astype(LOW)
+            for d in range(blocks):
+                stage[slot, t, d % 2, d // 2] = dw[d * LANES : (d + 1) * LANES]
+            side(u, t, 0).start()
+            side(u, t, 1).start()
+        return carry
+
+    lax.fori_loop(0, 5, weight_step, 0)
+    for w in attn:
+        w.cross()
+    lax.fori_loop(5, steps, weight_step, 0)
+
+    for u in (steps - 2, steps - 1):
+        for t in range(2):
+            side(u, t, 0).wait()
+            side(u, t, 1).wait_send()
+
+    def arrived(u, carry):
+        for t in range(2):
+            side(u, t, 1).wait_recv()
+        return carry
+
+    lax.fori_loop(0, steps, arrived, 0)
+    out_own.wait()
+    out_gone.wait()
+    for d in range(blocks):
+        down_copy(d).wait()
+    grad_own.wait()
+    for k in range(1, n_ctx):
+        grad_copy(k).wait()
+    for w in attn:
+        w.finish()
+
+
+def mlp_call(n_ctx, tok, att, cot, gain, wo, wg, wu, wd, wq, wr):
     tb, model = tok.shape
     blocks, _, ff = wg.shape
     half = blocks // 2
     down = wd.shape[1]
-    whole = lambda a: pl.BlockSpec(a.shape, lambda u: (0, 0))
+    width = model // n_ctx
+    vmem = pl.BlockSpec(memory_space=pltpu.VMEM)
     anyspace = pl.BlockSpec(memory_space=pl.ANY)
-    half_cols = pl.BlockSpec((half, LANES, FF_BLOCK), lambda u: (0, 0, u))
-    half_out = pl.BlockSpec((half, LANES, model), lambda u: (0, 0, 0))
-    tokens = pl.BlockSpec((tb, model), lambda u: (0, 0))
     shape = jax.ShapeDtypeStruct
+    dma = pltpu.SemaphoreType.DMA
     return pl.pallas_call(
         functools.partial(mlp_kernel, blocks, n_ctx),
-        grid=(ff // FF_BLOCK,),
-        in_specs=[whole(tok), whole(att), whole(cot), whole(gain)] + [anyspace] * 5,
-        out_specs=[tokens, tokens, tokens] + [half_cols] * 4 + [half_out] * 2 + [anyspace] * 3,
-        out_shape=[shape((tb, model), LOW), shape((tb, model), F32), shape((tb, model), LOW)]
+        in_specs=[vmem] * 4 + [anyspace] * 6,
+        out_specs=[vmem] * 2 + [anyspace] * 11,
+        out_shape=[shape((tb, model), LOW), shape((tb, model), F32), shape((n_ctx * tb, width), LOW)]
         + [shape((half, LANES, ff), LOW)] * 4
         + [shape((half, LANES, model), LOW)] * 2
         + [shape((half, down, model), LOW)] * 2
-        + [shape((blocks, n_ctx * wq.shape[0], wq.shape[1]), LOW)],
+        + [shape((blocks, n_ctx * w.shape[0], w.shape[1]), LOW) for w in (wq, wr)],
         scratch_shapes=[
             pltpu.VMEM((model, model), LOW),
             pltpu.VMEM((model, ff), LOW),
@@ -1282,33 +1379,65 @@
             pltpu.VMEM((tb, model), F32),
             pltpu.VMEM((tb, model), LOW),
             pltpu.VMEM((model, tb), LOW),
-            pltpu.VMEM((tb, LANES), F32),
             pltpu.VMEM((tb, model), F32),
             pltpu.VMEM((tb, model), F32),
-            pltpu.VMEM((ff, model), LOW),
-            pltpu.SemaphoreType.DMA((4, blocks)),
-            pltpu.SemaphoreType.DMA((blocks,)),
-            pltpu.SemaphoreType.DMA((11,)),
-            pltpu.SemaphoreType.DMA((11,)),
+            pltpu.VMEM((tb, ff), LOW),
+            pltpu.VMEM((tb, ff), LOW),
+            pltpu.VMEM((tb, ff), LOW),
+            pltpu.VMEM((2, 2, 2, half, LANES, FF_BLOCK), LOW),
+            pltpu.VMEM((2, half, LANES, model), LOW),
+            dma((4, blocks)),
+            dma((2, 11)), dma((2, 11)),
+            dma((2, 2)), dma((2, 2)), dma((2, ff // FF_BLOCK)),
+            dma((4,)),
+            dma((half,)), dma((half,)), dma((half,)),
+            dma((n_ctx - 1,)), dma((n_ctx - 1,)),
         ],
         compiler_params=params(collective_id=2, has_side_effects=True),
         cost_estimate=pl.CostEstimate(
             flops=2 * tb * model * (8 * ff + 3 * model), bytes_accessed=50 * 2**20, transcendentals=0
         ),
         name="mlp",
-    )(tok, att, cot, gain, wo, wg, wu, wd, wq)
-
-
-def input_kernel(blocks, tok_ref, gm_ref, v1_ref, gain_ref, g, w_in, ig_ref, vg_ref, w, rel, nat, sem):
+    )(tok, att, cot, gain, wo, wg, wu, wd, wq, wr)
+
+
+def input_kernel(
+    blocks, tok_ref, gm_ref, v1_ref, gain_ref, g, own_gain, qkv_ref, gate_ref, up_ref, out_ref, down_ref,
+    wq_ref, wr_ref, wgate_ref, wup_ref, wq_all, wr_all,
+    ig_ref, vg_ref, gq_ref, gk_ref, gv_ref, go_ref, gg_ref, gu_ref, gd_ref, gains_ref, w, rel, nat, sem,
+):
     dp = lax.axis_index("dp")
     model = tok_ref.shape[1]
-    made = [pltpu.make_async_copy(w_in.at[d], w.at[pl.ds(d * LANES, LANES), :], sem.at[d]) for d in range(blocks)]
+    cut = wq_ref.shape[1]
+    made = []
+    for d in range(blocks):
+        at = pl.ds(d * LANES, LANES)
+        made.append(pltpu.make_async_copy(wq_all.at[d], w.at[at, pl.ds(0, cut)], sem.at[0, d]))
+        made.append(pltpu.make_async_copy(wr_all.at[d], w.at[at, pl.ds(cut, 3 * model - cut)], sem.at[1, d]))
     for m in made:
         m.start()
     for d in range(blocks):
         rel[:, d * LANES : (d + 1) * LANES] = tok_ref[:, lane_block(dp ^ d)].astype(F32)
     gv = g[:, 2 * model :].astype(F32)
     vg_ref[...] = v1_ref[...] + 0.5 * gv
+
+    def row_dot(a, b):
+        return jnp.sum(a * b.astype(F32), axis=1, keepdims=True)
+
+    gq_ref[...] = qkv_ref[:, :model]
+    gk_ref[...] = qkv_ref[:, model : 2 * model]
+    gv_ref[...] = 0.5 * qkv_ref[:, 2 * model :]
+    go_ref[...] = out_ref[...]
+    gg_ref[...] = gate_ref[...]
+    gu_ref[...] = up_ref[...]
+    gd_ref[...] = down_ref[...]
+    both = 2 * model - cut
+    one = row_dot(qkv_ref[:, :cut], wq_ref[...]) + row_dot(qkv_ref[:, cut : 2 * model], wr_ref[:, :both])
+    one = one + row_dot(gv_ref[...], wr_ref[:, both:])
+    two = row_dot(gate_ref[...], wgate_ref[...]) + row_dot(up_ref[...], wup_ref[...])
+    lane = lax.broadcasted_iota(jnp.int32, gains_ref.shape, 1)
+    gains_ref[...] = jnp.where(lane == 0, one, two) / own_gain[...]
+
     x = rel[...]
     inv = lax.rsqrt(jnp.mean(x * x, axis=-1, keepdims=True) + epsilon)
     norm = x * inv
@@ -1324,28 +1453,32 @@
     ig_ref[...] = gm_ref[...] + nat[...]
 
 
-def input_call(tok, gm, v1, gain, g, ws):
+def input_call(tok, gm, v1, gain, g, own_gain, qkv, grads, wq, wr, wgate, wup, wq_all, wr_all):
     tb, model = tok.shape
-    blocks = ws.shape[0]
+    blocks = wq_all.shape[0]
+    rows = qkv.shape[0]
     vmem = pl.BlockSpec(memory_space=pltpu.VMEM)
     shape = jax.ShapeDtypeStruct
     return pl.pallas_call(
         functools.partial(input_kernel, blocks),
-        in_specs=[vmem] * 5 + [pl.BlockSpec(memory_space=pl.ANY)],
-        out_specs=[vmem, vmem],
-        out_shape=[shape((tb, model), F32)] * 2,
+        in_specs=[vmem] * 15 + [pl.BlockSpec(memory_space=pl.ANY)] * 2,
+        out_specs=[vmem] * 10,
+        out_shape=[shape((tb, model), F32)] * 2
+        + [shape((rows, model), F32)] * 4
+        + [shape(x.shape, F32) for x in (grads[0], grads[1], grads[3])]
+        + [shape((rows, LANES), F32)],
         scratch_shapes=[
             pltpu.VMEM((model, 3 * model), LOW),
             pltpu.VMEM((tb, model), F32),
             pltpu.VMEM((tb, model), F32),
-            pltpu.SemaphoreType.DMA((blocks,)),
+            pltpu.SemaphoreType.DMA((2, blocks)),
         ],
         compiler_params=params(),
         cost_estimate=pl.CostEstimate(
             flops=2 * tb * model * 3 * model, bytes_accessed=20 * 2**20, transcendentals=0
         ),
         name="input_grad",
-    )(tok, gm, v1, gain, g, ws)
+    )(tok, gm, v1, gain, g, own_gain, qkv, *grads, wq, wr, wgate, wup, wq_all, wr_all)
 
 
 def fast_local(
@@ -1369,32 +1502,29 @@
      gate_all, up_all, out_all, down_all) = front_call(
         n_dp, n_ctx, tok, first_values[0], mark, pack, freq, w_gate, w_up, w_out, w_down
     )
-    qkv = jnp.concatenate([w_query, w_key, w_value], axis=1)
-    (output, grad_middle, grad_attended, gate_keep, gate_send, up_keep, up_send, out_keep, out_send,
-     down_keep, down_send, qkv_all) = mlp_call(
-        n_ctx, tok, attended, cotangent[0], gain_rows[1:2], out_all, gate_all, up_all, down_all, qkv
+    cut = model // 2
+    wq = jnp.concatenate([w_query, w_key[:, :cut]], axis=1)
+    wr = jnp.concatenate([w_key[:, cut:], w_value], axis=1)
+    (output, grad_middle, head_grad, gate_keep, gate_came, up_keep, up_came, out_keep, out_came,
+     down_keep, down_came, wq_all, wr_all) = mlp_call(
+        n_ctx, tok, attended, cotangent[0], gain_rows[1:2], out_all, gate_all, up_all, down_all, wq, wr
     )
     sides = [
         x.reshape(x.shape[0], n_ctx, x.shape[1] // n_ctx, x.shape[2])
-        for x in (gate_keep, gate_send, up_keep, up_send, out_keep, out_send, down_keep, down_send)
+        for x in (gate_keep, gate_came, up_keep, up_came, out_keep, out_came, down_keep, down_came)
     ]
-    home_grad, qkv_grad, gate_grad, up_grad, out_grad, down_grad = back_call(
-        n_ctx, grad_attended, q, k, v, out_full, log_total, seg_col, seg_row, cos, sin, xn, sides
-    )
-    query_grad, key_grad = qkv_grad[:, :model], qkv_grad[:, model : 2 * model]
-    value_grad = 0.5 * qkv_grad[:, 2 * model :]
-    input_grad, v1_grad = input_call(tok, grad_middle, v1_accum[0], gain_rows[0:1], home_grad, qkv_all)
-
-    def row_dot(a, w):
-        return jnp.sum(a * w.astype(F32), axis=1)
-
-    gain_one = (
-        row_dot(query_grad, w_query) + row_dot(key_grad, w_key) + row_dot(value_grad, w_value)
-    ) / attn_gain.astype(F32)
-    gain_two = (row_dot(gate_grad, w_gate) + row_dot(up_grad, w_up)) / mlp_gain.astype(F32)
+    home_grad, qkv_grad, *grads = back_call(
+        n_ctx, head_grad, q, k, v, out_full, log_total, seg_col, seg_row, cos, sin, xn, sides
+    )
+    own_gain = jnp.stack([attn_gain.astype(F32)] + [mlp_gain.astype(F32)] * (LANES - 1), axis=1)
+    (input_grad, v1_grad, query_grad, key_grad, value_grad, out_grad, gate_grad, up_grad, down_grad,
+     gain_grads) = input_call(
+        tok, grad_middle, v1_accum[0], gain_rows[0:1], home_grad, own_gain, qkv_grad, grads,
+        wq, wr, w_gate, w_up, wq_all, wr_all
+    )
     return (
-        output[None], input_grad[None], v1_grad[None], gain_one, query_grad, key_grad, value_grad,
-        out_grad, gain_two, gate_grad, up_grad, down_grad,
+        output[None], input_grad[None], v1_grad[None], gain_grads[:, 0], query_grad, key_grad, value_grad,
+        out_grad, gain_grads[:, 1], gate_grad, up_grad, down_grad,
     )
 
 
@@ -1424,6 +1554,7 @@
             rows == 1
             and seq == TOKEN_BLOCK
             and model == n_dp * LANES
+            and n_ctx == 4
             and model == 2 * LANES * n_ctx
             and args[12].shape[1] % FF_BLOCK == 0
         )

time: 497 us -> 434 us (0.87)
  the two profiles are of different devices: /device:TPU:27 before, /device:TPU:8 now
where the time goes in v5:
time: 434 us; the launch traced here: 425 us
  Pallas kernels  410 us (94%)
  local copies, waits for them, and re-layouts  8.99 us (2%)
  other arithmetic  4.68 us (1%)
    pallas_call x1, Pallas kernels, front_call(): pl.pallas_call(functools.partial(front_kernel, n_ctx), in_specs=[anyspace...  184 us
    pallas_call x1, Pallas kernels, back_call(): pl.pallas_call(functools.partial(back_kernel, n_ctx), in_specs=[vmem] * 1...  140 us
    pallas_call x1, Pallas kernels, mlp_call(): pl.pallas_call(functools.partial(mlp_kernel, blocks, n_ctx), in_specs=[vm...  72.8 us
    pallas_call x1, Pallas kernels, input_call(): pl.pallas_call(functools.partial(input_kernel, blocks), in_specs=[vmem] *...  13.3 us

profile of v5, /device:TPU:8, one launch (start us, length us, event | category | flops | bytes accessed | tf_op | source)
XLA Modules:
  0.0 425.0 jit_solution(4637614374698333253)
XLA Ops:
  0.6 0.7 pad_maximum_fusion.2
  1.3 0.1 copy.288
  1.4 0.9 copy_bitcast_fusion
  2.3 0.8 copy.295
  3.2 0.7 maximum_bitcast_fusion.pack_ref
  3.9 0.1 pad.24.clone
  4.0 1.4 add_add_fusion.mark_ref
  5.4 0.1 stack_tile.6
  5.5 0.7 tile.8
  6.1 0.1 stack_tile.7
  6.2 0.6 select_maximum_fusion.freq_ref
  6.8 0.0 copy-start
  6.8 0.0 copy-start.1
  6.8 0.0 copy-start.2
  6.8 184.0 %front.1 = (bf16[2048,1024]{1,0:T(8,128)(2,1)}, bf16[2048,256]{1,0:T(8,128)(2,1)}, bf16[2048,256]{1,0:T(8,128)(2,1)}, bf16[2048,256]{1,0:T(8,128)(2,1)}, f32[204...) custom-call(bf16[512,1024]{1,0:T(8,128)(2,1)} %bitcast.31, ...), custom_call_target="tpu_custom_call" | custom-call | flops 24000000000 | bytes 62914560 | tf_op jit(solution)/shard_map/front/pallas_call | solution.py:765
  190.8 1.4 fusion.1
  192.2 0.0 copy-done
  192.2 0.0 copy-done.1
  192.2 0.0 copy-done.2
  192.3 0.7 pad_maximum_fusion
  193.0 72.8 %mlp.1 = (bf16[512,1024]{1,0:T(8,128)(2,1)}, f32[512,1024]{1,0:T(8,128)}, bf16[2048,256]{1,0:T(8,128)(2,1)}, bf16[4,128,2816]{2,1,0:T(8,128)(2,1)}, bf16[4,128,2...) custom-call(bf16[512,1024]{1,0:T(8,128)(2,1)} %bitcast.32, ...), custom_call_target="tpu_custom_call" | custom-call | flops 26843545600 | bytes 52428800 | tf_op jit(solution)/shard_map/mlp/pallas_call | solution.py:1363
  265.7 0.0 copy-start.3
  265.7 0.0 copy-start.4
  265.8 140.4 %back.1 = (bf16[512,3072]{1,0:T(8,128)(2,1)}, f32[32,3072]{1,0:T(8,128)}, f32[32,2816]{1,0:T(8,128)}, f32[32,2816]{1,0:T(8,128)}, f32[32,1024]{1,0:T(8,128)}, /*index=5*/f32[88,1024]{1,0:T(8,128)}) custom-call(bf16[2048,256]{1,0:T(8,128)(2,1)} %get-tuple-element.65.refs_0_, bf16[2048,256]{1,0:T(8,128)(2,1)} %get-tuple-element.66.refs_1_, ...), custom_call_target="tpu_custom_call" | custom-call | flops 40000000000 | bytes 62914560 | tf_op jit(solution)/shard_map/back/pallas_call | solution.py:1134
  406.1 0.0 copy-done.3
  406.1 0.1 copy.160
  406.2 0.0 copy-done.4
  406.2 0.1 copy.161
  406.3 0.8 stack.18
  407.2 0.6 stack.19.own_gain
  407.8 13.3 %input_grad.1 = (f32[512,1024]{1,0:T(8,128)}, f32[512,1024]{1,0:T(8,128)}, f32[32,1024]{1,0:T(8,128)}, f32[32,1024]{1,0:T(8,128)}, f32[32,1024]{1,0:T(8,128)}, /...) custom-call(bf16[512,1024]{1,0:T(8,128)(2,1)} %bitcast.33, ...), custom_call_target="tpu_custom_call" | custom-call | flops 3221225472 | bytes 20971520 | tf_op jit(solution)/shard_map/input_grad/pallas_call | solution.py:1462
  421.0 1.5 slice_reduce_fusion
  422.5 2.3 copy.297
  (6 shorter events, 0.0 us)
Async XLA Ops:
  6.8 185.4 %copy-start = (bf16[32,1024]{1,0:T(8,128)(2,1)S(1)}, bf16[32,1024]{1,0:T(8,128)(2,1)}, u32[]{:S(2)}) copy-start(bf16[32,1024]{1,0:T(8,128)(2,1)} %param.23) | copy-start | bytes 196612
  6.8 185.4 %copy-start.1 = (bf16[32,1024]{1,0:T(8,128)(2,1)S(1)}, bf16[32,1024]{1,0:T(8,128)(2,1)}, u32[]{:S(2)}) copy-start(bf16[32,1024]{1,0:T(8,128)(2,1)} %param.22) | copy-start | bytes 196612
  6.8 185.4 %copy-start.2 = (bf16[32,1024]{1,0:T(8,128)(2,1)S(1)}, bf16[32,1024]{1,0:T(8,128)(2,1)}, u32[]{:S(2)}) copy-start(bf16[32,1024]{1,0:T(8,128)(2,1)} %param.24) | copy-start | bytes 196612
  265.7 140.4 %copy-start.3 = (bf16[32]{0:T(256)(128)(2,1)S(1)}, bf16[32]{0:T(256)(128)(2,1)}, u32[]{:S(2)}) copy-start(bf16[32]{0:T(256)(128)(2,1)} %param.21) | copy-start | bytes 196
  265.7 140.5 %copy-start.4 = (bf16[32]{0:T(256)(128)(2,1)S(1)}, bf16[32]{0:T(256)(128)(2,1)}, u32[]{:S(2)}) copy-start(bf16[32]{0:T(256)(128)(2,1)} %param.26) | copy-start | bytes 196

commit v6 on v5

--- a/solution.py
+++ b/solution.py
@@ -2,6 +2,7 @@
 
 import jax
 import jax.numpy as jnp
+import numpy as np
 from jax import lax
 from jax.experimental import pallas as pl
 from jax.experimental.pallas import tpu as pltpu
@@ -488,7 +489,7 @@
     n_ctx, tok_ref, fv_ref, mark_ref, pack_ref, freq_ref, wg_ref, wu_ref, wo_ref, wd_ref,
     xn_ref, q_ref, k_ref, v_ref, of_ref, lse_ref, cos_ref, sin_ref, seg_ref, marks, gain_ref,
     att_ref, wg_all, wu_all, wo_all, wd_all,
-    x_all, fvs, packs, whead, rel, o_ref, s_ref, m_ref, l_ref, acc_ref,
+    x_all, fvs, packs, whead, rel, o_ref, s_ref, m_ref, l_ref, acc_ref, p_all, total_ref,
     mark_send, mark_recv, pack_send, pack_recv, tok_send, tok_recv, fv_send, fv_recv, w_send, w_recv,
     o_send, o_recv, own, own_o,
 ):
@@ -502,18 +503,22 @@
     lane = lax.broadcasted_iota(jnp.int32, (tb, LANES), 1)
     exact = lax.Precision.HIGHEST
 
-    weights = [
-        Gather(n_ctx, src, dst, w_send.at[i], w_recv.at[i], order)
-        for i, (src, dst, order) in enumerate(
-            [
-                (wg_ref, wg_all, (NEAR, FAR)),
-                (wo_ref, wo_all, (FAR, NEAR)),
-                (wu_ref, wu_all, (FAR, NEAR)),
-                (wd_ref, wd_all, (NEAR, FAR)),
-            ]
-        )
-    ]
-    early, late = weights[:3], weights[3:]
+    weights = []
+    for i, (src, dst) in enumerate(((wg_ref, wg_all), (wo_ref, wo_all), (wu_ref, wu_all), (wd_ref, wd_all))):
+        wide = src.shape[1] // 2
+        weights.append([])
+        for h, order in enumerate(((NEAR, FAR), (FAR, NEAR))):
+            cols = pl.ds(h * wide, wide)
+            unit = 2 * i + h
+            weights[i].append(
+                Gather(n_ctx, src.at[:, cols], dst.at[:, :, cols], w_send.at[unit], w_recv.at[unit], order)
+            )
+    gate, out, up, down = weights
+
+    def each(what, *arrays):
+        for array in arrays:
+            for half_way in array:
+                getattr(half_way, what)()
 
     def mark_copy(k):
         at = rows_of(c, tb)
@@ -548,8 +553,7 @@
     for k in range(1, n_ctx):
         mark_copy(k).start()
         pack_copy(k).start()
-    for w in early:
-        w.start()
+    each("start", gate, out)
     for m in locals_:
         m.start()
 
@@ -575,17 +579,17 @@
     for k in range(1, n_ctx):
         pack_copy(k).wait_recv()
     pack_hop(0, NEAR, 3).start()
+    each("relay", gate, out)
+    tok_copy(2).start()
+    tok_copy(1).start()
+    each("start", up)
     lax.fori_loop(0, n_ctx, table, 0)
     pack_hop(0, NEAR, 3).wait_recv()
     pack_hop(0, FAR, 4).start()
     pack_hop(NEAR, FAR, 5).start()
     pack_hop(0, CORE, 6).start()
     pack_hop(NEAR, CORE, 7).start()
-
-    for w in early:
-        w.relay()
-    tok_copy(2).start()
-    tok_copy(1).start()
+    each("spread", gate, out)
     pack_hop(0, FAR, 4).wait_recv()
     pack_hop(FAR, CORE, 8).start()
     pack_hop(NEAR, FAR, 5).wait_recv()
@@ -617,7 +621,7 @@
             q_ref[at, cols] = ((qb * cos + half_swap(qb) * sin) * 0.125).astype(LOW)
             kb = proj[:, width + b * LANES : width + (b + 1) * LANES]
             k_ref[at, cols] = (kb * cos + half_swap(kb) * sin).astype(LOW)
-        v_ref[at, :] = (0.5 * proj[:, 2 * width :] + 0.5 * fvs[at, :].astype(F32)).astype(LOW)
+        of_ref[at, :] = 0.5 * proj[:, 2 * width :]
 
     def project_chunk(bit):
         def one(part, carry):
@@ -626,26 +630,24 @@
 
         lax.fori_loop(0, 2, one, 0)
 
-    for w in early:
-        w.spread()
     project_chunk(0)
+    each("forward", gate, out)
     tok_copy(2).wait_recv()
     tok_pass().start()
+    each("relay", up)
+    each("start", down)
+    each("cross", gate, out)
+    tok_copy(1).wait_recv()
+    project_chunk(1)
+    project_chunk(2)
+    each("spread", up)
+    each("relay", down)
     for k in range(1, n_ctx):
         fv_copy(k).start()
-    for w in early:
-        w.forward()
-    tok_copy(1).wait_recv()
-    for k in range(1, n_ctx):
-        fv_copy(k).wait_recv()
-    project_chunk(1)
-    project_chunk(2)
     tok_pass().wait_recv()
-    for w in late:
-        w.start()
     project_chunk(3)
-    for w in early:
-        w.cross()
+    each("forward", up)
+    each("spread", down)
 
     def fold(x, op):
         r = x[:, 0:LANES]
@@ -656,11 +658,12 @@
     def home(pair):
         return att_ref.at[:, pl.ds(pl.multiple_of(c * width + pair * LANES, LANES), LANES)]
 
-    def query_block(pair, i):
+    def weigh(pair, i):
         cols = slice(pair * LANES, (pair + 1) * LANES)
         mine = rows_of(i, tb)
         q = q_ref[mine, cols]
         seg_q = seg_ref[mine, 0:1]
+        base = i * (i + 1) // 2
         for head in range(2):
             qm = head_lanes(q, head)
             m_ref[...] = jnp.full_like(m_ref, NEG)
@@ -685,25 +688,39 @@
             score(i, True)
             top = jnp.max(m_ref[...], axis=1, keepdims=True)
             l_ref[...] = jnp.zeros_like(l_ref)
-            acc_ref[...] = jnp.zeros_like(acc_ref)
-
-            def value_step(j, carry):
-                at = rows_of(j, tb)
-                p = jnp.exp(s_ref[:, at] - top)
+
+            def weight_step(j, carry):
+                p = jnp.exp(s_ref[:, rows_of(j, tb)] - top)
                 l_ref[...] += fold(p, jnp.add)
-                acc_ref[...] += dot(p.astype(LOW), v_ref[at, cols], 1, 0)
+                p_all[2 * pair + head, base + j] = p.astype(LOW)
                 return carry
 
-            lax.fori_loop(0, i + 1, value_step, 0)
+            lax.fori_loop(0, i + 1, weight_step, 0)
             total = jnp.sum(l_ref[...], axis=1, keepdims=True)
-            out = acc_ref[...] / total
+            total_ref[mine, :] = jnp.where(lane == 2 * pair + head, total, total_ref[mine, :])
             lse = jnp.broadcast_to(top + jnp.log(total), (tb, LANES))
             if head == 0:
-                of_ref[mine, cols] = out
                 lse_ref[mine, cols] = lse
             else:
+                lse_ref[mine, cols] = jnp.where(lane < HEAD_DIM, lse_ref[mine, cols], lse)
+
+    def mix(pair, i):
+        cols = slice(pair * LANES, (pair + 1) * LANES)
+        mine = rows_of(i, tb)
+        base = i * (i + 1) // 2
+        for head in range(2):
+            acc_ref[...] = jnp.zeros_like(acc_ref)
+
+            def value_step(j, carry):
+                acc_ref[...] += dot(p_all[2 * pair + head, base + j], v_ref[rows_of(j, tb), cols], 1, 0)
+                return carry
+
+            lax.fori_loop(0, i + 1, value_step, 0)
+            out = acc_ref[...] / total_ref[mine, 2 * pair + head : 2 * pair + head + 1]
+            if head == 0:
+                of_ref[mine, cols] = out
+            else:
                 of_ref[mine, cols] = jnp.where(lane < HEAD_DIM, of_ref[mine, cols], out)
-                lse_ref[mine, cols] = jnp.where(lane < HEAD_DIM, lse_ref[mine, cols], lse)
         o_ref[mine, cols] = of_ref[mine, cols].astype(LOW)
 
         @pl.when(i == c)
@@ -715,29 +732,35 @@
             k = lax.rem(i + n_ctx - c, n_ctx) - 1
             ctx_copy(o_ref.at[mine, cols], home(pair), o_send.at[k, pair], o_recv.at[k, pair], i).start()
 
-    def query_blocks(pair, lo, hi):
+    def over_queries(what, pair):
         def one(i, carry):
-            query_block(pair, i)
+            what(pair, i)
             return carry
 
-        lax.fori_loop(lo, hi, one, 0)
-
-    query_blocks(0, 0, 3)
-    for w in late:
-        w.relay()
-    query_blocks(0, 3, n_ctx)
-    for w in late:
-        w.spread()
-    query_blocks(1, 0, n_ctx)
-    for w in late:
-        w.forward()
+        lax.fori_loop(0, n_ctx, one, 0)
+
+    total_ref[...] = jnp.ones_like(total_ref)
+    over_queries(weigh, 0)
+    each("cross", up)
+    over_queries(weigh, 1)
+    each("forward", down)
+    for k in range(1, n_ctx):
+        fv_copy(k).wait_recv()
+
+    def values(b, carry):
+        at = rows_of(b, tb)
+        v_ref[at, :] = (of_ref[at, :] + 0.5 * fvs[at, :].astype(F32)).astype(LOW)
+        return carry
+
+    lax.fori_loop(0, n_ctx, values, 0)
+    over_queries(mix, 0)
+    each("cross", down)
+    over_queries(mix, 1)
     for pair in range(width // LANES):
         cols = slice(pair * LANES, (pair + 1) * LANES)
         pltpu.make_async_copy(o_ref.at[0:tb, cols], home(pair), own_o.at[pair]).wait()
         for k in range(n_ctx - 1):
             ctx_copy(o_ref.at[0:tb, cols], home(pair), o_send.at[k, pair], o_recv.at[k, pair], c).wait()
-    for w in late:
-        w.cross()
     for k in range(1, n_ctx):
         mark_copy(k).wait_send()
         pack_copy(k).wait_send()
@@ -749,8 +772,7 @@
     tok_copy(1).wait_send()
     tok_copy(2).wait_send()
     tok_pass().wait_send()
-    for w in weights:
-        w.finish()
+    each("finish", *weights)
 
 
 def front_call(n_dp, n_ctx, tok, fv, mark, pack, freq, wg, wu, wo, wd):
@@ -784,11 +806,13 @@
             pltpu.VMEM((tb, LANES), F32),
             pltpu.VMEM((tb, LANES), F32),
             pltpu.VMEM((tb, LANES), F32),
+            pltpu.VMEM((2 * pairs, n_ctx * (n_ctx + 1) // 2, tb, tb), LOW),
+            pltpu.VMEM((length, LANES), F32),
             dma((n_ctx - 1,)), dma((n_ctx - 1,)),
             dma((n_ctx + 6,)), dma((n_ctx + 6,)),
             dma((3,)), dma((3,)),
             dma((n_ctx - 1,)), dma((n_ctx - 1,)),
-            dma((4, 11)), dma((4, 11)),
+            dma((8, 11)), dma((8, 11)),
             dma((n_ctx - 1, pairs)), dma((n_ctx - 1, pairs)),
             dma((4,)), dma((pairs,)),
         ],
@@ -923,8 +947,7 @@
     def part(pair, t, chunk):
         return part_ref.at[pair, rows_of(chunk, tb), pl.ds(t * LANES, LANES)]
 
-    def part_copy(pair, t, k):
-        to = lax.rem(c + k, n_ctx)
+    def part_copy(pair, t, k, to):
         return ctx_copy(part(pair, t, to), home(pair, t), send.at[k - 1, pair, t], recv.at[k - 1, pair, t], to)
 
     def part_own(pair, t):
@@ -997,23 +1020,23 @@
             dk = dk * cos_ref[mine, :] - half_swap(dk) * sin_ref[mine, :]
             part_ref[pair, mine, LANES : 2 * LANES] = dk.astype(LOW)
             part_ref[pair, mine, 2 * LANES : 3 * LANES] = dv_acc[...].astype(LOW)
+            dq = dq_acc[mine, :] * 0.125
+            dq = dq * cos_ref[mine, :] - half_swap(dq) * sin_ref[mine, :]
+            part_ref[pair, mine, 0:LANES] = dq.astype(LOW)
+
+            @pl.when(j == c)
+            def _():
+                for t in range(3):
+                    part_own(pair, t).start()
+
+            @pl.when(j != c)
+            def _():
+                for t in range(3):
+                    part_copy(pair, t, lax.rem(j + n_ctx - c, n_ctx), j).start()
+
             return carry
 
         lax.fori_loop(lo, hi, key_block, 0)
-
-    def send_home(pair):
-        def query_done(b, carry):
-            at = rows_of(b, tb)
-            dq = dq_acc[at, :] * 0.125
-            dq = dq * cos_ref[at, :] - half_swap(dq) * sin_ref[at, :]
-            part_ref[pair, at, 0:LANES] = dq.astype(LOW)
-            return carry
-
-        lax.fori_loop(0, n_ctx, query_done, 0)
-        for t in range(3):
-            part_own(pair, t).start()
-            for k in range(1, n_ctx):
-                part_copy(pair, t, k).start()
 
     def pair_hop(pair, at):
         src, dst, bit = [
@@ -1074,7 +1097,6 @@
     each(0, "step_two")
     each(1, "step_one")
     key_blocks(0, middle, n_ctx)
-    send_home(0)
     pair_product(0)
     each(0, "step_ctx")
     stats(1)
@@ -1084,7 +1106,6 @@
     pair_one(0)
     each(0, "step_far")
     key_blocks(1, middle, n_ctx)
-    send_home(1)
     each(1, "step_ctx")
     pair_product(1)
     pair_two(0)
@@ -1112,7 +1133,7 @@
         for t in range(3):
             part_own(pair, t).wait()
             for k in range(1, n_ctx):
-                part_copy(pair, t, k).wait()
+                part_copy(pair, t, k, lax.rem(c + k, n_ctx)).wait()
 
 
 def back_call(n_ctx, g, q, k, v, of, lse, seg_col, seg_row, cos, sin, xn, sides):
@@ -1402,9 +1423,9 @@
 
 
 def input_kernel(
-    blocks, tok_ref, gm_ref, v1_ref, gain_ref, g, own_gain, qkv_ref, gate_ref, up_ref, out_ref, down_ref,
+    blocks, tok_ref, gm_ref, v1_ref, y_ref, g, gain_ref, own_gain, qkv_ref, gate_ref, up_ref, out_ref, down_ref,
     wq_ref, wr_ref, wgate_ref, wup_ref, wq_all, wr_all,
-    ig_ref, vg_ref, gq_ref, gk_ref, gv_ref, go_ref, gg_ref, gu_ref, gd_ref, gains_ref, w, rel, nat, sem,
+    ig_ref, vg_ref, yo_ref, gq_ref, gk_ref, gv_ref, go_ref, gg_ref, gu_ref, gd_ref, gains_ref, w, rel, nat, sem,
 ):
     dp = lax.axis_index("dp")
     model = tok_ref.shape[1]
@@ -1414,35 +1435,43 @@
         at = pl.ds(d * LANES, LANES)
         made.append(pltpu.make_async_copy(wq_all.at[d], w.at[at, pl.ds(0, cut)], sem.at[0, d]))
         made.append(pltpu.make_async_copy(wr_all.at[d], w.at[at, pl.ds(cut, 3 * model - cut)], sem.at[1, d]))
-    for m in made:
-        m.start()
+
+    def row_dot(a, b):
+        return jnp.sum(a * b.astype(F32), axis=1, keepdims=True)
+
+    @pl.when(pl.program_id(0) == 0)
+    def _():
+        for m in made:
+            m.start()
+        gq_ref[...] = qkv_ref[:, :model]
+        gk_ref[...] = qkv_ref[:, model : 2 * model]
+        gv_ref[...] = 0.5 * qkv_ref[:, 2 * model :]
+        go_ref[...] = out_ref[...]
+        gg_ref[...] = gate_ref[...]
+        gu_ref[...] = up_ref[...]
+        gd_ref[...] = down_ref[...]
+        both = 2 * model - cut
+        one = row_dot(qkv_ref[:, :cut], wq_ref[...]) + row_dot(qkv_ref[:, cut : 2 * model], wr_ref[:, :both])
+        one = one + row_dot(gv_ref[...], wr_ref[:, both:])
+        two = row_dot(gate_ref[...], wgate_ref[...]) + row_dot(up_ref[...], wup_ref[...])
+        lane = lax.broadcasted_iota(jnp.int32, gains_ref.shape, 1)
+        gains_ref[...] = jnp.where(lane == 0, one, two) / own_gain[...]
+
+    yo_ref[...] = y_ref[...]
     for d in range(blocks):
         rel[:, d * LANES : (d + 1) * LANES] = tok_ref[:, lane_block(dp ^ d)].astype(F32)
     gv = g[:, 2 * model :].astype(F32)
     vg_ref[...] = v1_ref[...] + 0.5 * gv
 
-    def row_dot(a, b):
-        return jnp.sum(a * b.astype(F32), axis=1, keepdims=True)
-
-    gq_ref[...] = qkv_ref[:, :model]
-    gk_ref[...] = qkv_ref[:, model : 2 * model]
-    gv_ref[...] = 0.5 * qkv_ref[:, 2 * model :]
-    go_ref[...] = out_ref[...]
-    gg_ref[...] = gate_ref[...]
-    gu_ref[...] = up_ref[...]
-    gd_ref[...] = down_ref[...]
-    both = 2 * model - cut
-    one = row_dot(qkv_ref[:, :cut], wq_ref[...]) + row_dot(qkv_ref[:, cut : 2 * model], wr_ref[:, :both])
-    one = one + row_dot(gv_ref[...], wr_ref[:, both:])
-    two = row_dot(gate_ref[...], wgate_ref[...]) + row_dot(up_ref[...], wup_ref[...])
-    lane = lax.broadcasted_iota(jnp.int32, gains_ref.shape, 1)
-    gains_ref[...] = jnp.where(lane == 0, one, two) / own_gain[...]
-
     x = rel[...]
     inv = lax.rsqrt(jnp.mean(x * x, axis=-1, keepdims=True) + epsilon)
     norm = x * inv
-    for m in made:
-        m.wait()
+
+    @pl.when(pl.program_id(0) == 0)
+    def _():
+        for m in made:
+            m.wait()
+
     grad = dot(g[:, : 2 * model], w[:, : 2 * model], 1, 1)
     grad = grad + 0.5 * dot(g[:, 2 * model :], w[:, 2 * model :], 1, 1)
     scaled = grad * gain_ref[...]
@@ -1453,24 +1482,27 @@
     ig_ref[...] = gm_ref[...] + nat[...]
 
 
-def input_call(tok, gm, v1, gain, g, own_gain, qkv, grads, wq, wr, wgate, wup, wq_all, wr_all):
+def input_call(tok, gm, v1, y, g, gain, own_gain, qkv, grads, wq, wr, wgate, wup, wq_all, wr_all):
     tb, model = tok.shape
     blocks = wq_all.shape[0]
     rows = qkv.shape[0]
-    vmem = pl.BlockSpec(memory_space=pltpu.VMEM)
+    part = tb // 2
     shape = jax.ShapeDtypeStruct
+    token = lambda cols: pl.BlockSpec((part, cols), lambda i: (i, 0))
+    whole = lambda a: pl.BlockSpec(a.shape, lambda i: (0, 0))
+    small = [gain, own_gain, qkv, *grads, wq, wr, wgate, wup]
+    ends = [shape((rows, model), F32)] * 4 + [shape(x.shape, F32) for x in (grads[0], grads[1], grads[3])]
+    ends.append(shape((rows, LANES), F32))
     return pl.pallas_call(
         functools.partial(input_kernel, blocks),
-        in_specs=[vmem] * 15 + [pl.BlockSpec(memory_space=pl.ANY)] * 2,
-        out_specs=[vmem] * 10,
-        out_shape=[shape((tb, model), F32)] * 2
-        + [shape((rows, model), F32)] * 4
-        + [shape(x.shape, F32) for x in (grads[0], grads[1], grads[3])]
-        + [shape((rows, LANES), F32)],
+        grid=(tb // part,),
+        in_specs=[token(model)] * 4 + [token(3 * model)] + [whole(x) for x in small] + [pl.BlockSpec(memory_space=pl.ANY)] * 2,
+        out_specs=[token(model)] * 3 + [whole(x) for x in ends],
+        out_shape=[shape((tb, model), F32)] * 2 + [shape((tb, model), LOW)] + ends,
         scratch_shapes=[
             pltpu.VMEM((model, 3 * model), LOW),
-            pltpu.VMEM((tb, model), F32),
-            pltpu.VMEM((tb, model), F32),
+            pltpu.VMEM((part, model), F32),
+            pltpu.VMEM((part, model), F32),
             pltpu.SemaphoreType.DMA((2, blocks)),
         ],
         compiler_params=params(),
@@ -1478,7 +1510,7 @@
             flops=2 * tb * model * 3 * model, bytes_accessed=20 * 2**20, transcendentals=0
         ),
         name="input_grad",
-    )(tok, gm, v1, gain, g, own_gain, qkv, *grads, wq, wr, wgate, wup, wq_all, wr_all)
+    )(tok, gm, v1, y, g, *small, wq_all, wr_all)
 
 
 def fast_local(
@@ -1494,10 +1526,11 @@
     gains = jnp.tile(jnp.pad(gains, ((0, 0), (0, width - 2))), (1, n_ctx))
     pack = jnp.concatenate([w_query, w_key, w_value, gains], axis=0)
     pack = pack.reshape(4 * own_rows, n_ctx, width).transpose(1, 0, 2)
-    freqs = 10000.0 ** (-jnp.arange(HEAD_DIM // 2).astype(F32) * (2.0 / HEAD_DIM))
-    turn = jnp.ones((HEAD_DIM // 2,), F32)
-    freq = jnp.stack([jnp.tile(freqs, 4), jnp.tile(jnp.concatenate([-turn, turn]), 2)])
-    freq = jnp.pad(freq, ((0, 6), (0, 0)))
+    freqs = 10000.0 ** (-np.arange(HEAD_DIM // 2).astype(np.float32) * np.float32(2.0 / HEAD_DIM))
+    freq = np.zeros((8, LANES), np.float32)
+    freq[0] = np.tile(freqs.astype(np.float32), LANES // (HEAD_DIM // 2))
+    freq[1] = np.where(np.arange(LANES) % HEAD_DIM < HEAD_DIM // 2, -1.0, 1.0)
+    freq = jnp.asarray(freq)
     (xn, q, k, v, out_full, log_total, cos, sin, seg_col, seg_row, gain_rows, attended,
      gate_all, up_all, out_all, down_all) = front_call(
         n_dp, n_ctx, tok, first_values[0], mark, pack, freq, w_gate, w_up, w_out, w_down
@@ -1517,9 +1550,9 @@
         n_ctx, head_grad, q, k, v, out_full, log_total, seg_col, seg_row, cos, sin, xn, sides
     )
     own_gain = jnp.stack([attn_gain.astype(F32)] + [mlp_gain.astype(F32)] * (LANES - 1), axis=1)
-    (input_grad, v1_grad, query_grad, key_grad, value_grad, out_grad, gate_grad, up_grad, down_grad,
+    (input_grad, v1_grad, output, query_grad, key_grad, value_grad, out_grad, gate_grad, up_grad, down_grad,
      gain_grads) = input_call(
-        tok, grad_middle, v1_accum[0], gain_rows[0:1], home_grad, own_gain, qkv_grad, grads,
+        tok, grad_middle, v1_accum[0], output, home_grad, gain_rows[0:1], own_gain, qkv_grad, grads,
         wq, wr, w_gate, w_up, wq_all, wr_all
     )
     return (

time: 434 us -> 414 us (0.954)
  the two profiles are of different devices: /device:TPU:8 before, /device:TPU:27 now
where the time goes in v6:
time: 414 us; the launch traced here: 406 us
  Pallas kernels  395 us (95%)
  local copies, waits for them, and re-layouts  5.68 us (1%)
    pallas_call x1, Pallas kernels, front_call(): pl.pallas_call(functools.partial(front_kernel, n_ctx), in_specs=[anyspace...  178 us
    pallas_call x1, Pallas kernels, back_call(): pl.pallas_call(functools.partial(back_kernel, n_ctx), in_specs=[vmem] * 1...  130 us
    pallas_call x1, Pallas kernels, mlp_call(): pl.pallas_call(functools.partial(mlp_kernel, blocks, n_ctx), in_specs=[vm...  74.2 us
    pallas_call x1, Pallas kernels, input_call(): pl.pallas_call(functools.partial(input_kernel, blocks), grid=(tb // part,...  12.7 us

profile of v6, /device:TPU:27, one launch (start us, length us, event | category | flops | bytes accessed | tf_op | source)
XLA Modules:
  0.0 406.2 jit_solution(11480250935587018192)
XLA Ops:
  0.6 0.7 pad_maximum_fusion.2
  1.3 0.1 copy.289
  1.4 0.9 copy_bitcast_fusion
  2.3 0.8 copy.296
  3.2 0.7 maximum_bitcast_fusion.pack_ref
  3.9 0.1 pad.17.clone
  4.0 1.4 add_add_fusion.mark_ref
  5.4 0.0 copy-start
  5.4 0.0 copy-start.1
  5.4 0.0 copy-start.2
  5.4 177.8 %front.1 = (bf16[2048,1024]{1,0:T(8,128)(2,1)}, bf16[2048,256]{1,0:T(8,128)(2,1)}, bf16[2048,256]{1,0:T(8,128)(2,1)}, bf16[2048,256]{1,0:T(8,128)(2,1)}, f32[204...) custom-call(bf16[512,1024]{1,0:T(8,128)(2,1)} %bitcast.30, ...), custom_call_target="tpu_custom_call" | custom-call | flops 24000000000 | bytes 62914560 | tf_op jit(solution)/shard_map/front/pallas_call | solution.py:787
  183.1 1.4 fusion.1
  184.6 0.0 copy-done
  184.6 0.0 copy-done.1
  184.6 0.0 copy-done.2
  184.6 0.7 pad_maximum_fusion
  185.3 74.2 %mlp.1 = (bf16[512,1024]{1,0:T(8,128)(2,1)}, f32[512,1024]{1,0:T(8,128)}, bf16[2048,256]{1,0:T(8,128)(2,1)}, bf16[4,128,2816]{2,1,0:T(8,128)(2,1)}, bf16[4,128,2...) custom-call(bf16[512,1024]{1,0:T(8,128)(2,1)} %bitcast.31, ...), custom_call_target="tpu_custom_call" | custom-call | flops 26843545600 | bytes 52428800 | tf_op jit(solution)/shard_map/mlp/pallas_call | solution.py:1384
  259.5 0.0 copy-start.3
  259.6 0.0 copy-start.4
  259.6 130.4 %back.1 = (bf16[512,3072]{1,0:T(8,128)(2,1)}, f32[32,3072]{1,0:T(8,128)}, f32[32,2816]{1,0:T(8,128)}, f32[32,2816]{1,0:T(8,128)}, f32[32,1024]{1,0:T(8,128)}, /*index=5*/f32[88,1024]{1,0:T(8,128)}) custom-call(bf16[2048,256]{1,0:T(8,128)(2,1)} %get-tuple-element.66.refs_0_, bf16[2048,256]{1,0:T(8,128)(2,1)} %get-tuple-element.67.refs_1_, ...), custom_call_target="tpu_custom_call" | custom-call | flops 40000000000 | bytes 62914560 | tf_op jit(solution)/shard_map/back/pallas_call | solution.py:1155
  390.0 0.0 copy-done.3
  390.0 0.1 copy.161
  390.1 0.0 copy-done.4
  390.1 0.1 copy.162
  390.2 0.6 stack.15
  390.8 0.6 stack.16.own_gain
  391.4 12.7 %input_grad.1 = (f32[512,1024]{1,0:T(8,128)}, f32[512,1024]{1,0:T(8,128)}, bf16[512,1024]{1,0:T(8,128)(2,1)}, f32[32,1024]{1,0:T(8,128)}, f32[32,1024]{1,0:T(8,1...) custom-call(bf16[512,1024]{1,0:T(8,128)(2,1)} %bitcast.32, ...), custom_call_target="tpu_custom_call" | custom-call | flops 3221225472 | bytes 20971520 | tf_op jit(solution)/shard_map/input_grad/pallas_call | solution.py:1496
  404.2 1.5 slice_reduce_fusion
  (4 shorter events, 0.0 us)
Async XLA Ops:
  5.4 179.2 %copy-start = (bf16[32,1024]{1,0:T(8,128)(2,1)S(1)}, bf16[32,1024]{1,0:T(8,128)(2,1)}, u32[]{:S(2)}) copy-start(bf16[32,1024]{1,0:T(8,128)(2,1)} %param.24) | copy-start | bytes 196612
  5.4 179.2 %copy-start.1 = (bf16[32,1024]{1,0:T(8,128)(2,1)S(1)}, bf16[32,1024]{1,0:T(8,128)(2,1)}, u32[]{:S(2)}) copy-start(bf16[32,1024]{1,0:T(8,128)(2,1)} %param.23) | copy-start | bytes 196612
  5.4 179.2 %copy-start.2 = (bf16[32,1024]{1,0:T(8,128)(2,1)S(1)}, bf16[32,1024]{1,0:T(8,128)(2,1)}, u32[]{:S(2)}) copy-start(bf16[32,1024]{1,0:T(8,128)(2,1)} %param.25) | copy-start | bytes 196612
  259.5 130.5 %copy-start.3 = (bf16[32]{0:T(256)(128)(2,1)S(1)}, bf16[32]{0:T(256)(128)(2,1)}, u32[]{:S(2)}) copy-start(bf16[32]{0:T(256)(128)(2,1)} %param.22) | copy-start | bytes 196
  259.6 130.6 %copy-start.4 = (bf16[32]{0:T(256)(128)(2,1)S(1)}, bf16[32]{0:T(256)(128)(2,1)}, u32[]{:S(2)}) copy-start(bf16[32]{0:T(256)(128)(2,1)} %param.27) | copy-start | bytes 196
